TPU v7x, 32 devices: a whole 2x2x4 slice. The times are simulated.
32 devices in a mesh: fsdp: 16 (over z, y, core), tp: 2 (over x).
Axes of the slice: x: 2, y: 2, z: 4, core: 2. Of those that a mesh axis runs over, the one named last changes fastest.
Arguments:
- tokens: bfloat16 [3, 16, 1280, 1024], P(None, 'fsdp', 'tp'), may hold values from -6 to 6
- segments: int32 [3, 16, 1280], P(None, 'fsdp', 'tp'), may hold values from 0 to 12, as said below
- parents: int32 [3, 16, 13], P(None, 'fsdp'), may hold values from 0 to 4, as said below
- norm_gains: float32 [4, 1024], replicated, may hold values from 0.5 to 1.5
- norm_biases: float32 [4, 1024], replicated, may hold values from -1.8 to 1.8
- w_qkv: bfloat16 [1024, 3, 1024], P('fsdp', None, 'tp'), may hold values from -0.1875 to 0.1875
- w_out: bfloat16 [1024, 1024], P('tp', 'fsdp'), may hold values from -0.1875 to 0.1875
- w_up: bfloat16 [1024, 4096], P('fsdp', 'tp'), may hold values from -0.1875 to 0.1875
- w_down: bfloat16 [4096, 1024], P('tp', 'fsdp'), may hold values from -0.09375 to 0.09375
- cotangent: bfloat16 [3, 16, 1280, 1024], P(None, 'fsdp', 'tp'), may hold values from -12 to 12
Outputs:
- out: bfloat16 [3, 16, 1280, 1024], P(None, 'fsdp', 'tp')
- input_grad: float32 [3, 16, 1280, 1024], P(None, 'fsdp', 'tp')
- grad_w_qkv: float32 [1024, 3, 1024], P('fsdp', None, 'tp')
- grad_w_out: float32 [1024, 1024], P('tp', 'fsdp')
- grad_w_up: float32 [1024, 4096], P('fsdp', 'tp')
- grad_w_down: float32 [4096, 1024], P('tp', 'fsdp')
- grad_gains: float32 [4, 1024], replicated
- grad_biases: float32 [4, 1024], replicated
Inputs may be any that keep to these rules, and one draw needn't show every extreme that they name: Along each tree the segment number never falls; segment 0, the trunk, begins the tree and holds between 384 and 768 tokens; segments 1 to 4 are branches and 5 to 12 leaves, each after its parent. parents[m, t, s] is the parent segment of segment s: 0 for segments 0 to 4 (the trunk is its own), a branch for each leaf, each branch the parent of exactly two leaves.
All inputs are finite; a program needn't handle non-finite values.
Results may differ from a plain program's by a relative error of at most 0.017.
Values may be sent and summed in bfloat16 or wider, within the bound.
A program may use at most 512 MiB of HBM per device.

v0:
```python
import math

import jax
import jax.numpy as jnp
from jax import lax
from jax.sharding import PartitionSpec as P

HEAD_DIM = 64


relax_alpha = 32.0
norm_eps = 1e-05
masked_value = -1e30


def layer_norm(values, gain, shift):
    mean_row = jnp.mean(values, axis=-1, keepdims=True)
    centered = values - mean_row
    variance = jnp.mean(centered * centered, axis=-1, keepdims=True)
    return centered * lax.rsqrt(variance + norm_eps) * gain + shift


def gelu_tanh(values):
    return jax.nn.gelu(values, approximate=True)


def path_allowed(seg_rows, row_start, seg_all, parents):
    seg_count = parents.shape[0]
    labels = jnp.arange(seg_count, dtype=jnp.int32)
    parent_row = jnp.sum(
        jnp.where(seg_rows[:, None] == labels[None, :], parents[None, :], 0), axis=1
    )
    grand_row = jnp.sum(
        jnp.where(parent_row[:, None] == labels[None, :], parents[None, :], 0), axis=1
    )
    column = seg_all[None, :]
    on_path = (
        (column == seg_rows[:, None])
        | (column == parent_row[:, None])
        | (column == grand_row[:, None])
    )
    row_pos = row_start + jnp.arange(seg_rows.shape[0], dtype=jnp.int32)
    col_pos = jnp.arange(seg_all.shape[0], dtype=jnp.int32)
    return on_path & (col_pos[None, :] <= row_pos[:, None])


def contract_rows(left, right):
    return lax.dot_general(
        left, right, (((0,), (0,)), ((), ())), preferred_element_type=jnp.float32
    )


def contract_cols(left, right):
    return lax.dot_general(
        left, right, (((1,), (1,)), ((), ())), preferred_element_type=jnp.float32
    )


def gather_weights(w_qkv, w_out, w_up, w_down):
    return (
        lax.all_gather(w_qkv, "fsdp", axis=0, tiled=True),
        lax.all_gather(w_out, "fsdp", axis=1, tiled=True),
        lax.all_gather(w_up, "fsdp", axis=0, tiled=True),
        lax.all_gather(w_down, "fsdp", axis=1, tiled=True),
    )


def scatter_grads(grad_tuple):
    return (
        lax.psum_scatter(
            grad_tuple[0].astype(jnp.bfloat16), "fsdp", scatter_dimension=0, tiled=True
        ).astype(jnp.float32),
        lax.psum_scatter(
            grad_tuple[1].astype(jnp.bfloat16), "fsdp", scatter_dimension=1, tiled=True
        ).astype(jnp.float32),
        lax.psum_scatter(
            grad_tuple[2].astype(jnp.bfloat16), "fsdp", scatter_dimension=0, tiled=True
        ).astype(jnp.float32),
        lax.psum_scatter(
            grad_tuple[3].astype(jnp.bfloat16), "fsdp", scatter_dimension=1, tiled=True
        ).astype(jnp.float32),
    )


def block_scores(qry_blk, key_all, seg_all, parents, row_start):
    scores = relax_alpha * jnp.einsum(
        "hqd,hkd->hqk", qry_blk, key_all, preferred_element_type=jnp.float32
    )
    seg_rows = seg_all[row_start : row_start + qry_blk.shape[1]]
    allowed = path_allowed(seg_rows, row_start, seg_all, parents)
    return jnp.where(allowed[None], scores, masked_value)


def attention_forward(query_low, key_all, val_all, seg_all, parents):
    block_rows = query_low.shape[1] // 2
    outputs = []
    top_rows = []
    totals = []
    for row_start in range(0, query_low.shape[1], block_rows):
        qry_blk = query_low[:, row_start : row_start + block_rows]
        masked = block_scores(qry_blk, key_all, seg_all, parents, row_start)
        top_row = jnp.max(masked, axis=-1, keepdims=True)
        exp_rows = jnp.exp(masked - top_row)
        sum_row = jnp.sum(exp_rows, axis=-1, keepdims=True)
        prob_low = (exp_rows / sum_row).astype(jnp.bfloat16)
        outputs.append(
            jnp.einsum("hqk,hkd->hqd", prob_low, val_all, preferred_element_type=jnp.float32)
        )
        top_rows.append(top_row)
        totals.append(sum_row)
    return (jnp.concatenate(outputs, axis=1), top_rows, totals)


def attention_backward(query_low, key_all, val_all, seg_all, parents, top_rows, totals, grad_att):
    block_rows = query_low.shape[1] // 2
    grad_query = []
    grad_keys = jnp.zeros(key_all.shape, jnp.float32)
    grad_vals = jnp.zeros(val_all.shape, jnp.float32)
    for block_number, row_start in enumerate(range(0, query_low.shape[1], block_rows)):
        qry_blk = query_low[:, row_start : row_start + block_rows]
        grad_blk = grad_att[:, row_start : row_start + block_rows]
        masked = block_scores(qry_blk, key_all, seg_all, parents, row_start)
        prob_rows = jnp.exp(masked - top_rows[block_number]) / totals[block_number]
        prob_low = prob_rows.astype(jnp.bfloat16)
        grad_vals = grad_vals + jnp.einsum(
            "hqk,hqd->hkd", prob_low, grad_blk, preferred_element_type=jnp.float32
        )
        grad_probs = jnp.einsum(
            "hqd,hkd->hqk", grad_blk, val_all, preferred_element_type=jnp.float32
        )
        row_dot = jnp.sum(prob_rows * grad_probs, axis=-1, keepdims=True)
        grad_scores = (prob_rows * (grad_probs - row_dot)).astype(jnp.bfloat16)
        grad_query.append(
            relax_alpha
            * jnp.einsum("hqk,hkd->hqd", grad_scores, key_all, preferred_element_type=jnp.float32)
        )
        grad_keys = grad_keys + relax_alpha * jnp.einsum(
            "hqk,hqd->hkd", grad_scores, qry_blk, preferred_element_type=jnp.float32
        )
    return (jnp.concatenate(grad_query, axis=1), grad_keys, grad_vals)


def on_device(
    tokens, segments, parents, norm_gains, norm_biases, w_qkv, w_out, w_up, w_down, cotangent
):
    micro_count = tokens.shape[0]
    local_rows = tokens.shape[2]
    model_width = tokens.shape[3]
    tree_len = local_rows * lax.axis_size("tp")
    local_width = w_qkv.shape[2]
    heads_local = local_width // HEAD_DIM
    query_scale = 1.0 / (relax_alpha * math.sqrt(HEAD_DIM))
    grad_gains = jnp.zeros((4, model_width), jnp.float32)
    grad_biases = jnp.zeros((4, model_width), jnp.float32)
    out_list = []
    input_list = []
    for micro_index in range(micro_count):
        weight_set = gather_weights(w_qkv, w_out, w_up, w_down)
        full_qkv, full_out, full_up, full_down = weight_set
        qkv_matrix = full_qkv.reshape(model_width, 3 * local_width)
        path_par = parents[micro_index, 0]
        tree_input = tokens[micro_index, 0].astype(jnp.float32)
        normed_val, pull_a1 = jax.vjp(layer_norm, tree_input, norm_gains[0], norm_biases[0])
        normed_a = normed_val.astype(jnp.bfloat16)
        normed_full, seg_all = (
            lax.all_gather(normed_a, "tp", axis=0, tiled=True),
            lax.all_gather(segments[micro_index, 0], "tp", axis=0, tiled=True),
        )
        qkv_proj = jnp.dot(normed_full, qkv_matrix, preferred_element_type=jnp.float32)
        qkv_proj = qkv_proj.reshape(tree_len, 3, heads_local, HEAD_DIM)
        query_low = (qkv_proj[:, 0] * query_scale).astype(jnp.bfloat16).transpose(1, 0, 2)
        key_all = qkv_proj[:, 1].astype(jnp.bfloat16).transpose(1, 0, 2)
        val_all = qkv_proj[:, 2].astype(jnp.bfloat16).transpose(1, 0, 2)
        attended, top_rows, totals = attention_forward(
            query_low, key_all, val_all, seg_all, path_par
        )
        attended_low = (
            attended.transpose(1, 0, 2).reshape(tree_len, local_width).astype(jnp.bfloat16)
        )
        branch_a = lax.psum_scatter(
            jnp.dot(attended_low, full_out, preferred_element_type=jnp.float32),
            "tp",
            scatter_dimension=0,
            tiled=True,
        )
        post_a, pull_a2 = jax.vjp(layer_norm, branch_a, norm_gains[1], norm_biases[1])
        residual = tree_input + post_a
        normed_fval, pull_f1 = jax.vjp(layer_norm, residual, norm_gains[2], norm_biases[2])
        normed_f_full = lax.all_gather(normed_fval.astype(jnp.bfloat16), "tp", axis=0, tiled=True)
        up_proj = jnp.dot(normed_f_full, full_up, preferred_element_type=jnp.float32)
        hidden_val, pull_gelu = jax.vjp(gelu_tanh, up_proj)
        hidden = hidden_val.astype(jnp.bfloat16)
        branch_f = lax.psum_scatter(
            jnp.dot(hidden, full_down, preferred_element_type=jnp.float32),
            "tp",
            scatter_dimension=0,
            tiled=True,
        )
        post_f, pull_f2 = jax.vjp(layer_norm, branch_f, norm_gains[3], norm_biases[3])
        out_list.append((residual + post_f).astype(jnp.bfloat16))
        grad_out = cotangent[micro_index, 0].astype(jnp.float32)
        grad_branch_f, gain_f2, bias_f2 = pull_f2(grad_out)
        grad_branch_full = lax.all_gather(
            grad_branch_f.astype(jnp.bfloat16), "tp", axis=0, tiled=True
        )
        grad_down_local = contract_rows(hidden, grad_branch_full)
        grad_hidden = contract_cols(grad_branch_full, full_down)
        grad_up = pull_gelu(grad_hidden)[0].astype(jnp.bfloat16)
        grad_up_local = contract_rows(normed_f_full, grad_up)
        grad_normed_f = lax.psum_scatter(
            contract_cols(grad_up, full_up), "tp", scatter_dimension=0, tiled=True
        )
        grad_resid_part, gain_f1, bias_f1 = pull_f1(grad_normed_f)
        grad_residual = grad_out + grad_resid_part
        grad_branch_a, gain_a2, bias_a2 = pull_a2(grad_residual)
        grad_branch_low = grad_branch_a.astype(jnp.bfloat16)
        grad_branch_a_full = lax.all_gather(grad_branch_low, "tp", axis=0, tiled=True)
        grad_out_local = contract_rows(attended_low, grad_branch_a_full)
        grad_attended = contract_cols(grad_branch_a_full, full_out).astype(jnp.bfloat16)
        grad_attended = grad_attended.reshape(tree_len, heads_local, HEAD_DIM).transpose(1, 0, 2)
        grad_query, grad_keys, grad_vals = attention_backward(
            query_low, key_all, val_all, seg_all, path_par, top_rows, totals, grad_attended
        )
        grad_query_low = grad_query.astype(jnp.bfloat16) * jnp.asarray(query_scale, jnp.bfloat16)
        grad_stack = jnp.stack(
            [grad_query_low, grad_keys.astype(jnp.bfloat16), grad_vals.astype(jnp.bfloat16)], axis=0
        )
        grad_qkv = grad_stack.transpose(2, 0, 1, 3).reshape(tree_len, 3 * local_width)
        grad_qkv_local = contract_rows(normed_full, grad_qkv).reshape(model_width, 3, local_width)
        grad_normed_a = lax.psum_scatter(
            contract_cols(grad_qkv, qkv_matrix).astype(jnp.bfloat16),
            "tp",
            scatter_dimension=0,
            tiled=True,
        ).astype(jnp.float32)
        grad_input_part, gain_a1, bias_a1 = pull_a1(grad_normed_a)
        input_list.append(grad_residual + grad_input_part)
        grad_gains = grad_gains + jnp.stack([gain_a1, gain_a2, gain_f1, gain_f2], axis=0)
        grad_biases = grad_biases + jnp.stack([bias_a1, bias_a2, bias_f1, bias_f2], axis=0)
        locals_now = (grad_qkv_local, grad_out_local, grad_up_local, grad_down_local)
        shards_now = scatter_grads(locals_now)
        if micro_index == 0:
            grad_shards = shards_now
        else:
            grad_shards = jax.tree.map(jnp.add, grad_shards, shards_now)
    gains_sum, biases_sum = lax.psum((grad_gains, grad_biases), ("fsdp", "tp"))
    out_rows = jnp.stack(out_list, axis=0)[:, None]
    input_rows = jnp.stack(input_list, axis=0)[:, None]
    return (
        out_rows,
        input_rows,
        grad_shards[0],
        grad_shards[1],
        grad_shards[2],
        grad_shards[3],
        gains_sum,
        biases_sum,
    )


def solution(mesh):
    in_specs = (
        P(None, "fsdp", "tp", None),
        P(None, "fsdp", "tp"),
        P(None, "fsdp", None),
        P(),
        P(),
        P("fsdp", None, "tp"),
        P("tp", "fsdp"),
        P("fsdp", "tp"),
        P("tp", "fsdp"),
        P(None, "fsdp", "tp", None),
    )
    out_specs = (
        P(None, "fsdp", "tp", None),
        P(None, "fsdp", "tp", None),
        P("fsdp", None, "tp"),
        P("tp", "fsdp"),
        P("fsdp", "tp"),
        P("tp", "fsdp"),
        P(),
        P(),
    )
    return jax.shard_map(
        on_device, mesh=mesh, in_specs=in_specs, out_specs=out_specs, check_vma=False
    )
```

profile of v0, /device:TPU:0, one launch (start us, length us, event | category | flops | bytes accessed | tf_op | source)
XLA Modules:
  0.0 2374.1 jit_solution(3958163826461033322)
XLA Ops:
  27.9 30.6 %all-gather.22.cloned.1.call-done = bf16[1024,3,512]{2,0,1:T(8,128)(2,1)} async-done(((bf16[64,3,512]{2,0,1:T(8,128)(2,1)}), bf16[1024,3,512]{2,0,1:T(8,128)(2,1)}) %all-gather.22.cloned.1.call-update) | async-done | bytes 3145744 | tf_op jit(solution)/shard_map/all_gather | solution.py:61
  61.6 36.3 %all-gather.20.cloned.1.call-done = bf16[1280,1024]{1,0:T(8,128)(2,1)} async-done(((bf16[640,1024]{1,0:T(8,128)(2,1)}), bf16[1280,1024]{1,0:T(8,128)(2,1)}) %all-gather.20.cloned.1.call-update) | async-done | bytes 2621456 | tf_op jit(solution)/shard_map/all_gather | solution.py:166
  107.2 15.0 fusion.405
  135.4 15.3 fusion.402
  193.3 15.1 fusion.412
  221.6 14.9 fusion.409
  269.0 15.0 fusion.419
  334.7 19.8 reduce-scatter.29.cloned.1.call-done
  356.4 66.2 %reduce-scatter.33.cloned.1.call-done = f32[640,1024]{1,0:T(8,128)} async-done(((f32[1280,1024]{1,0:T(8,128)}), f32[640,1024]{1,0:T(8,128)}) %reduce-scatter.33.cloned.1.call-update) | async-done | bytes 2621456 | tf_op jit(solution)/shard_map/reduce_scatter | solution.py:180
  444.5 30.6 %all-gather.28.cloned.1.call-done = bf16[1024,2048]{1,0:T(8,128)(2,1)} async-done(((bf16[64,2048]{1,0:T(8,128)(2,1)}), bf16[1024,2048]{1,0:T(8,128)(2,1)}) %all-gather.28.cloned.1.call-update) | async-done | bytes 4194320 | tf_op jit(solution)/shard_map/all_gather | solution.py:63
  475.1 38.9 %all-gather.38.cloned.1.call-done = bf16[1280,1024]{1,0:T(8,128)(2,1)} async-done(((bf16[640,1024]{1,0:T(8,128)(2,1)}), bf16[1280,1024]{1,0:T(8,128)(2,1)}) %all-gather.38.cloned.1.call-update) | async-done | bytes 2621456 | tf_op jit(solution)/shard_map/all_gather | solution.py:189
  524.8 41.9 %all-gather.30.cloned.1.call-done = bf16[2048,1024]{0,1:T(8,128)(2,1)} async-done(((bf16[2048,64]{0,1:T(8,128)(2,1)}), bf16[2048,1024]{0,1:T(8,128)(2,1)}) %all-gather.30.cloned.1.call-update) | async-done | bytes 4194320 | tf_op jit(solution)/shard_map/all_gather | solution.py:64
  579.0 26.6 %all-gather.34.cloned.1.call-done = bf16[1280,1024]{1,0:T(8,128)(2,1)} async-done(((bf16[640,1024]{1,0:T(8,128)(2,1)}), bf16[1280,1024]{1,0:T(8,128)(2,1)}) %all-gather.34.cloned.1.call-update) | async-done | bytes 2621456 | tf_op jit(solution)/shard_map/all_gather | solution.py:189
  626.6 20.1 all-gather.26.cloned.1.call-done
  667.3 47.4 %reduce-scatter.35.cloned.1.call-done = f32[640,1024]{1,0:T(8,128)} async-done(((f32[1280,1024]{1,0:T(8,128)}), f32[640,1024]{1,0:T(8,128)}) %reduce-scatter.35.cloned.1.call-update) | async-done | bytes 2621456 | tf_op jit(solution)/shard_map/reduce_scatter | solution.py:193
  716.7 66.0 %reduce-scatter.31.cloned.1.call-done = f32[640,1024]{1,0:T(8,128)} async-done(((f32[1280,1024]{1,0:T(8,128)}), f32[640,1024]{1,0:T(8,128)}) %reduce-scatter.31.cloned.1.call-update) | async-done | bytes 2621456 | tf_op jit(solution)/shard_map/reduce_scatter | solution.py:193
  787.6 63.6 %reduce-scatter.27.cloned.1.call-done = f32[640,1024]{1,0:T(8,128)} async-done(((f32[1280,1024]{1,0:T(8,128)}), f32[640,1024]{1,0:T(8,128)}) %reduce-scatter.27.cloned.1.call-update) | async-done | bytes 2621456 | tf_op jit(solution)/shard_map/reduce_scatter | solution.py:193
  877.9 32.9 %all-gather.48.cloned.1.call-done = bf16[1280,1024]{1,0:T(8,128)(2,1)} async-done(((bf16[640,1024]{1,0:T(8,128)(2,1)}), bf16[1280,1024]{1,0:T(8,128)(2,1)}) %all-gather.48.cloned.1.call-update) | async-done | bytes 2621456 | tf_op jit(solution)/shard_map/all_gather | solution.py:203
  910.7 15.4 fusion.50
  936.1 15.1 all-gather.44.cloned.1.call-done
  951.2 15.4 fusion.43
  976.8 15.0 all-gather.40.cloned.1.call-done
  991.7 15.4 fusion.36
  1017.2 42.5 %reduce-scatter.45.cloned.1.call-done = f32[640,1024]{1,0:T(8,128)} async-done(((f32[1280,1024]{1,0:T(8,128)}), f32[640,1024]{1,0:T(8,128)}) %reduce-scatter.45.cloned.1.call-update) | async-done | bytes 2621456 | tf_op jit(solution)/shard_map/reduce_scatter | solution.py:210
  1059.7 68.7 %reduce-scatter.41.cloned.1.call-done = f32[640,1024]{1,0:T(8,128)} async-done(((f32[1280,1024]{1,0:T(8,128)}), f32[640,1024]{1,0:T(8,128)}) %reduce-scatter.41.cloned.1.call-update) | async-done | bytes 2621456 | tf_op jit(solution)/shard_map/reduce_scatter | solution.py:210
  1128.4 68.1 %reduce-scatter.37.cloned.1.call-done = f32[640,1024]{1,0:T(8,128)} async-done(((f32[1280,1024]{1,0:T(8,128)}), f32[640,1024]{1,0:T(8,128)}) %reduce-scatter.37.cloned.1.call-update) | async-done | bytes 2621456 | tf_op jit(solution)/shard_map/reduce_scatter | solution.py:210
  1346.0 20.4 multiply_reduce_fusion
  1366.3 20.9 multiply_reduce_fusion.1
  1387.2 17.4 multiply_convert_fusion.1
  1409.3 18.4 multiply_reduce_fusion.5
  1427.6 19.1 multiply_convert_fusion
  1452.0 22.6 multiply_convert_fusion.5
  1522.7 20.9 multiply_reduce_fusion.4
  1543.7 22.7 multiply_convert_fusion.4
  1591.3 18.8 multiply_reduce_fusion.2
  1610.1 22.8 multiply_convert_fusion.2
  1675.6 20.8 multiply_reduce_fusion.3
  1696.5 22.6 multiply_convert_fusion.3
  1814.9 43.8 %reduce-scatter.57.cloned.1.call-done = bf16[512,64]{0,1:T(8,128)(2,1)} async-done(((bf16[512,1024]{0,1:T(8,128)(2,1)}), bf16[512,64]{0,1:T(8,128)(2,1)}) %reduce-scatter.57.cloned.1.call-update) | async-done | bytes 65552 | tf_op jit(solution)/shard_map/reduce_scatter | solution.py:73
  1858.8 60.0 %reduce-scatter.55.cloned.1.call-done = bf16[512,64]{0,1:T(8,128)(2,1)} async-done(((bf16[512,1024]{0,1:T(8,128)(2,1)}), bf16[512,64]{0,1:T(8,128)(2,1)}) %reduce-scatter.55.cloned.1.call-update) | async-done | bytes 65552 | tf_op jit(solution)/shard_map/reduce_scatter | solution.py:73
  1918.8 60.3 %reduce-scatter.59.cloned.1.call-done = bf16[512,64]{0,1:T(8,128)(2,1)} async-done(((bf16[512,1024]{0,1:T(8,128)(2,1)}), bf16[512,64]{0,1:T(8,128)(2,1)}) %reduce-scatter.59.cloned.1.call-update) | async-done | bytes 65552 | tf_op jit(solution)/shard_map/reduce_scatter | solution.py:73
  1980.7 67.7 %reduce-scatter.53.cloned.1.call-done = bf16[64,3,512]{2,0,1:T(8,128)(2,1)} async-done(((bf16[1024,3,512]{2,0,1:T(8,128)(2,1)}), bf16[64,3,512]{2,0,1:T(8,128)(2,1)}) %reduce-scatter.53.cloned.1.call-update) | async-done | bytes 196624 | tf_op jit(solution)/shard_map/reduce_scatter | solution.py:70
  2048.4 68.9 %reduce-scatter.49.cloned.1.call-done = bf16[64,3,512]{2,0,1:T(8,128)(2,1)} async-done(((bf16[1024,3,512]{2,0,1:T(8,128)(2,1)}), bf16[64,3,512]{2,0,1:T(8,128)(2,1)}) %reduce-scatter.49.cloned.1.call-update) | async-done | bytes 196624 | tf_op jit(solution)/shard_map/reduce_scatter | solution.py:70
  2117.2 68.9 %reduce-scatter.51.cloned.1.call-done = bf16[64,3,512]{2,0,1:T(8,128)(2,1)} async-done(((bf16[1024,3,512]{2,0,1:T(8,128)(2,1)}), bf16[64,3,512]{2,0,1:T(8,128)(2,1)}) %reduce-scatter.51.cloned.1.call-update) | async-done | bytes 196624 | tf_op jit(solution)/shard_map/reduce_scatter | solution.py:70
  2188.1 36.8 %reduce-scatter.47.cloned.1.call-done = bf16[640,1024]{1,0:T(8,128)(2,1)} async-done(((bf16[1280,1024]{1,0:T(8,128)(2,1)}), bf16[640,1024]{1,0:T(8,128)(2,1)}) %reduce-scatter.47.cloned.1.call-update) | async-done | bytes 1310736 | tf_op jit(solution)/shard_map/reduce_scatter | solution.py:230
  2224.9 39.8 %reduce-scatter.39.cloned.1.call-done = bf16[640,1024]{1,0:T(8,128)(2,1)} async-done(((bf16[1280,1024]{1,0:T(8,128)(2,1)}), bf16[640,1024]{1,0:T(8,128)(2,1)}) %reduce-scatter.39.cloned.1.call-update) | async-done | bytes 1310736 | tf_op jit(solution)/shard_map/reduce_scatter | solution.py:230
  2264.6 40.0 %reduce-scatter.43.cloned.1.call-done = bf16[640,1024]{1,0:T(8,128)(2,1)} async-done(((bf16[1280,1024]{1,0:T(8,128)(2,1)}), bf16[640,1024]{1,0:T(8,128)(2,1)}) %reduce-scatter.43.cloned.1.call-update) | async-done | bytes 1310736 | tf_op jit(solution)/shard_map/reduce_scatter | solution.py:230
  2315.1 40.1 %all-reduce = (f32[4,1024]{1,0:T(4,128)}, f32[4,1024]{1,0:T(4,128)}) all-reduce(f32[4,1024]{1,0:T(4,128)S(1)} %fusion.303, f32[4,1024]{1,0:T(4,128)S(1)} %fusion.304), channel_id=1, replica_groups=mesh['fsdp'=16,'tp'=2] {'fsdp','tp'}, use_global_device_ids=true, to_apply=%region_114.115 | all-reduce | flops 8192 | bytes 65536 | tf_op jit(solution)/shard_map/psum | solution.py:246
  (674 shorter events, 731.5 us)
Async XLA Ops:
  7.2 51.3 %all-gather.22.cloned.1.call-start = ((), (), s32[]{:S(2)}) async-start(), calls=%async_computation.25 | async-start | bytes 3342336 | tf_op jit(solution)/shard_map/all_gather | solution.py:61
  7.9 90.0 %all-gather.20.cloned.1.call-start = ((), (), s32[]{:S(2)}) async-start(), calls=%async_computation.24 | async-start | bytes 3932160 | tf_op jit(solution)/shard_map/all_gather | solution.py:166
  16.8 148.3 %all-gather.24.cloned.1.call-start = ((), (), s32[]{:S(2)}) async-start(), calls=%async_computation.26 | async-start | bytes 1114112 | tf_op jit(solution)/shard_map/all_gather | solution.py:62
  17.5 166.4 %all-gather.32.cloned.1.call-start = ((), (), s32[]{:S(2)}) async-start(), calls=%async_computation.32 | async-start | bytes 3932160 | tf_op jit(solution)/shard_map/all_gather | solution.py:166
  18.1 241.8 %all-gather.36.cloned.1.call-start = ((), (), s32[]{:S(2)}) async-start(), calls=%async_computation.36 | async-start | bytes 3932160 | tf_op jit(solution)/shard_map/all_gather | solution.py:166
  18.7 314.0 %reduce-scatter.25.cloned.1.call-start = ((), (), s32[]{:S(2)}) async-start(), calls=%async_computation.27 | async-start | bytes 7864320 | tf_op jit(solution)/shard_map/reduce_scatter | solution.py:180
  170.7 183.7 %reduce-scatter.29.cloned.1.call-start = ((), (), s32[]{:S(2)}) async-start(), calls=%async_computation.33 | async-start | bytes 7864320 | tf_op jit(solution)/shard_map/reduce_scatter | solution.py:180
  256.2 166.3 %reduce-scatter.33.cloned.1.call-start = ((), (), s32[]{:S(2)}) async-start(), calls=%async_computation.37 | async-start | bytes 7864320 | tf_op jit(solution)/shard_map/reduce_scatter | solution.py:180
  331.6 143.5 %all-gather.28.cloned.1.call-start = ((), (), s32[]{:S(2)}) async-start(), calls=%async_computation.29 | async-start | bytes 4456448 | tf_op jit(solution)/shard_map/all_gather | solution.py:63
  332.4 181.7 %all-gather.38.cloned.1.call-start = ((), (), s32[]{:S(2)}) async-start(), calls=%async_computation.38 | async-start | bytes 3932160 | tf_op jit(solution)/shard_map/all_gather | solution.py:189
  442.4 124.3 %all-gather.30.cloned.1.call-start = ((), (), s32[]{:S(2)}) async-start(), calls=%async_computation.30 | async-start | bytes 4456448 | tf_op jit(solution)/shard_map/all_gather | solution.py:64
  443.1 162.5 %all-gather.34.cloned.1.call-start = ((), (), s32[]{:S(2)}) async-start(), calls=%async_computation.34 | async-start | bytes 3932160 | tf_op jit(solution)/shard_map/all_gather | solution.py:189
  443.7 203.1 %all-gather.26.cloned.1.call-start = ((), (), s32[]{:S(2)}) async-start(), calls=%async_computation.28 | async-start | bytes 3932160 | tf_op jit(solution)/shard_map/all_gather | solution.py:189
  444.5 270.3 %reduce-scatter.35.cloned.1.call-start = ((), (), s32[]{:S(2)}) async-start(), calls=%async_computation.39 | async-start | bytes 7864320 | tf_op jit(solution)/shard_map/reduce_scatter | solution.py:193
  578.5 204.1 %reduce-scatter.31.cloned.1.call-start = ((), (), s32[]{:S(2)}) async-start(), calls=%async_computation.35 | async-start | bytes 7864320 | tf_op jit(solution)/shard_map/reduce_scatter | solution.py:193
  626.6 224.6 %reduce-scatter.27.cloned.1.call-start = ((), (), s32[]{:S(2)}) async-start(), calls=%async_computation.31 | async-start | bytes 7864320 | tf_op jit(solution)/shard_map/reduce_scatter | solution.py:193
  667.1 243.6 %all-gather.48.cloned.1.call-start = ((), (), s32[]{:S(2)}) async-start(), calls=%async_computation.48 | async-start | bytes 3932160 | tf_op jit(solution)/shard_map/all_gather | solution.py:203
  871.6 79.6 %all-gather.44.cloned.1.call-start = ((), (), s32[]{:S(2)}) async-start(), calls=%async_computation.44 | async-start | bytes 3932160 | tf_op jit(solution)/shard_map/all_gather | solution.py:203
  874.7 117.1 %all-gather.40.cloned.1.call-start = ((), (), s32[]{:S(2)}) async-start(), calls=%async_computation.40 | async-start | bytes 3932160 | tf_op jit(solution)/shard_map/all_gather | solution.py:203
  877.8 181.9 %reduce-scatter.45.cloned.1.call-start = ((), (), s32[]{:S(2)}) async-start(), calls=%async_computation.49 | async-start | bytes 7864320 | tf_op jit(solution)/shard_map/reduce_scatter | solution.py:210
  935.8 192.5 %reduce-scatter.41.cloned.1.call-start = ((), (), s32[]{:S(2)}) async-start(), calls=%async_computation.45 | async-start | bytes 7864320 | tf_op jit(solution)/shard_map/reduce_scatter | solution.py:210
  976.3 220.1 %reduce-scatter.37.cloned.1.call-start = ((), (), s32[]{:S(2)}) async-start(), calls=%async_computation.41 | async-start | bytes 7864320 | tf_op jit(solution)/shard_map/reduce_scatter | solution.py:210
  1016.9 179.6 %copy-start.109 = (f32[640]{0:T(1024)S(1)}, f32[640]{0:T(1024)}, u32[]{:S(2)}) copy-start(f32[640]{0:T(1024)} %copy-done.108) | copy-start | bytes 7684
  1016.9 186.5 %copy-start.125 = (f32[640]{0:T(1024)S(1)}, f32[640]{0:T(1024)}, u32[]{:S(2)}) copy-start(f32[640]{0:T(1024)} %copy-done.124) | copy-start | bytes 7684
  1016.9 186.5 %copy-start.123 = (f32[640]{0:T(1024)S(1)}, f32[640]{0:T(1024)}, u32[]{:S(2)}) copy-start(f32[640]{0:T(1024)} %copy-done.122) | copy-start | bytes 7684
  1016.9 186.6 %copy-start.121 = (f32[640]{0:T(1024)S(1)}, f32[640]{0:T(1024)}, u32[]{:S(2)}) copy-start(f32[640]{0:T(1024)} %copy-done.120) | copy-start | bytes 7684
  1016.9 281.1 %all-gather.50.cloned.1.call-start = ((), (), s32[]{:S(2)}) async-start(), calls=%async_computation.50 | async-start | bytes 3932160 | tf_op jit(solution)/shard_map/all_gather | solution.py:217
  1222.5 106.5 %all-gather.42.cloned.1.call-start = ((), (), s32[]{:S(2)}) async-start(), calls=%async_computation.42 | async-start | bytes 3932160 | tf_op jit(solution)/shard_map/all_gather | solution.py:217
  1225.6 249.0 %all-gather.46.cloned.1.call-start = ((), (), s32[]{:S(2)}) async-start(), calls=%async_computation.46 | async-start | bytes 3932160 | tf_op jit(solution)/shard_map/all_gather | solution.py:217
  1227.0 583.9 %reduce-scatter.71.cloned.1.call-start = ((), (), s32[]{:S(2)}) async-start(), calls=%async_computation.63 | async-start | bytes 4456448 | tf_op jit(solution)/shard_map/reduce_scatter | solution.py:79
  1239.0 571.9 %reduce-scatter.67.cloned.1.call-start = ((), (), s32[]{:S(2)}) async-start(), calls=%async_computation.61 | async-start | bytes 4456448 | tf_op jit(solution)/shard_map/reduce_scatter | solution.py:79
  1251.0 559.9 %reduce-scatter.69.cloned.1.call-start = ((), (), s32[]{:S(2)}) async-start(), calls=%async_computation.62 | async-start | bytes 4456448 | tf_op jit(solution)/shard_map/reduce_scatter | solution.py:79
  1263.1 549.9 %reduce-scatter.65.cloned.1.call-start = ((), (), s32[]{:S(2)}) async-start(), calls=%async_computation.60 | async-start | bytes 4456448 | tf_op jit(solution)/shard_map/reduce_scatter | solution.py:76
  1274.5 538.4 %reduce-scatter.63.cloned.1.call-start = ((), (), s32[]{:S(2)}) async-start(), calls=%async_computation.59 | async-start | bytes 4456448 | tf_op jit(solution)/shard_map/reduce_scatter | solution.py:76
  1286.0 526.9 %reduce-scatter.61.cloned.1.call-start = ((), (), s32[]{:S(2)}) async-start(), calls=%async_computation.58 | async-start | bytes 4456448 | tf_op jit(solution)/shard_map/reduce_scatter | solution.py:76
  1297.5 561.3 %reduce-scatter.57.cloned.1.call-start = ((), (), s32[]{:S(2)}) async-start(), calls=%async_computation.56 | async-start | bytes 1114112 | tf_op jit(solution)/shard_map/reduce_scatter | solution.py:73
  1543.6 375.2 %reduce-scatter.55.cloned.1.call-start = ((), (), s32[]{:S(2)}) async-start(), calls=%async_computation.55 | async-start | bytes 1114112 | tf_op jit(solution)/shard_map/reduce_scatter | solution.py:73
  1586.4 392.7 %reduce-scatter.59.cloned.1.call-start = ((), (), s32[]{:S(2)}) async-start(), calls=%async_computation.57 | async-start | bytes 1114112 | tf_op jit(solution)/shard_map/reduce_scatter | solution.py:73
  1653.9 394.5 %reduce-scatter.53.cloned.1.call-start = ((), (), s32[]{:S(2)}) async-start(), calls=%async_computation.54 | async-start | bytes 3342336 | tf_op jit(solution)/shard_map/reduce_scatter | solution.py:70
  1664.9 452.3 %reduce-scatter.49.cloned.1.call-start = ((), (), s32[]{:S(2)}) async-start(), calls=%async_computation.52 | async-start | bytes 3342336 | tf_op jit(solution)/shard_map/reduce_scatter | solution.py:70
  1696.4 489.7 %reduce-scatter.51.cloned.1.call-start = ((), (), s32[]{:S(2)}) async-start(), calls=%async_computation.53 | async-start | bytes 3342336 | tf_op jit(solution)/shard_map/reduce_scatter | solution.py:70
  1779.7 445.2 %reduce-scatter.47.cloned.1.call-start = ((), (), s32[]{:S(2)}) async-start(), calls=%async_computation.51 | async-start | bytes 3932160 | tf_op jit(solution)/shard_map/reduce_scatter | solution.py:230
  1789.6 475.0 %reduce-scatter.39.cloned.1.call-start = ((), (), s32[]{:S(2)}) async-start(), calls=%async_computation.43 | async-start | bytes 3932160 | tf_op jit(solution)/shard_map/reduce_scatter | solution.py:230
  1797.4 507.2 %reduce-scatter.43.cloned.1.call-start = ((), (), s32[]{:S(2)}) async-start(), calls=%async_computation.47 | async-start | bytes 3932160 | tf_op jit(solution)/shard_map/reduce_scatter | solution.py:230
  1810.8 493.8 %copy-start.73 = (f32[1,1024]{1,0:T(1,128)S(1)}, f32[1,1024]{1,0:T(1,128)}, u32[]{:S(2)}) copy-start(f32[1,1024]{1,0:T(1,128)} %copy-done.72) | copy-start | bytes 12292
  1810.8 493.8 %copy-start.75 = (f32[640]{0:T(1024)S(1)}, f32[640]{0:T(1024)}, u32[]{:S(2)}) copy-start(f32[640]{0:T(1024)} %copy-done.74) | copy-start | bytes 7684
  1810.8 493.8 %copy-start.77 = (f32[640]{0:T(1024)S(1)}, f32[640]{0:T(1024)}, u32[]{:S(2)}) copy-start(f32[640]{0:T(1024)} %copy-done.76) | copy-start | bytes 7684
  1810.8 493.8 %copy-start.79 = (f32[640]{0:T(1024)S(1)}, f32[640]{0:T(1024)}, u32[]{:S(2)}) copy-start(f32[640]{0:T(1024)} %copy-done.78) | copy-start | bytes 7684
  (188 other events, 3285.7 us)
Sparse Core Ops, SparseCore 0:
  10.2 48.2 all-gather.21
  60.5 37.3 all-gather.19
  100.1 37.8 all-gather.23
  139.4 38.0 all-gather.31
  178.8 38.9 all-gather.35
  220.6 65.7 reduce-scatter.24
  288.7 65.7 reduce-scatter.28
  356.8 65.7 reduce-scatter.32
  424.7 50.3 all-gather.27
  476.5 37.5 all-gather.37
  516.3 50.3 all-gather.29
  568.1 37.5 all-gather.33
  607.7 38.9 all-gather.25
  648.9 65.7 reduce-scatter.34
  716.9 65.7 reduce-scatter.30
  785.4 65.7 reduce-scatter.26
  871.7 38.9 all-gather.47
  912.1 38.9 all-gather.43
  952.7 38.9 all-gather.39
  993.9 65.7 reduce-scatter.44
  1062.6 65.7 reduce-scatter.40
  1130.7 65.7 reduce-scatter.36
  1222.7 38.9 all-gather.49
  1263.1 38.9 all-gather.41
  1303.7 38.9 all-gather.45
  1346.4 72.7 reduce-scatter.70
  1422.9 71.8 reduce-scatter.66
  1498.7 71.8 reduce-scatter.68
  1575.1 71.7 reduce-scatter.64
  1650.6 71.7 reduce-scatter.62
  1726.3 71.9 reduce-scatter.60
  1802.0 56.7 reduce-scatter.56
  1862.2 56.5 reduce-scatter.54
  1922.4 56.6 reduce-scatter.58
  1982.9 65.4 reduce-scatter.52
  2052.0 65.1 reduce-scatter.48
  2120.9 65.1 reduce-scatter.50
  2188.4 36.4 reduce-scatter.46
  2227.0 37.6 reduce-scatter.38
  2266.9 37.6 reduce-scatter.42
where the time goes:
time: 2380 us; the launch traced here: 2370 us
  waiting for transfers between devices  1220 us (51%)
  matrix products  752 us (32%)
  other arithmetic  266 us (11%)
  local copies, waits for them, and re-layouts  57.4 us (2%)
  blocking collectives  54.8 us (2%)
    reduce_scatter x3, waiting for transfers between devices, scatter_grads(): lax.psum_scatter(grad_tuple[0].astype(jnp.bfloat16), 'fsdp', scatter_dime...  205 us
    reduce_scatter x3, waiting for transfers between devices, on_device(): lax.psum_scatter(contract_cols(grad_up, full_up), 'tp', scatter_dimension...  179 us
    reduce_scatter x3, waiting for transfers between devices, on_device(): lax.psum_scatter(jnp.dot(hidden, full_down, preferred_element_type=jnp.fl...  177 us
    reduce_scatter x3, waiting for transfers between devices, scatter_grads(): lax.psum_scatter(grad_tuple[1].astype(jnp.bfloat16), 'fsdp', scatter_dime...  164 us
    convert_element_type x6, other arithmetic, attention_backward(): grad_scores = (prob_rows * (grad_probs - row_dot)).astype(jnp.bfloat16)  127 us
    dot_general x6, matrix products, attention_backward(): jnp.einsum('hqd,hkd->hqk', grad_blk, val_all, preferred_element_type=jnp....  120 us
    reduce_scatter x3, waiting for transfers between devices, on_device(): lax.psum_scatter(contract_cols(grad_qkv, qkv_matrix).astype(jnp.bfloat16)...  117 us
    dot_general x12, matrix products, contract_cols(): lax.dot_general(left, right, (((1,), (1,)), ((), ())), preferred_element_...  103 us
  transfers between devices with their start and end apart: 40, of which 27 were waited for; matrix products, arithmetic and copies ran while one was open for 40% of the time, Pallas kernels for 0%

commit v1 on v0

v1 whole, which is shorter than its diff:
```python
import math

import jax
import jax.numpy as jnp
from jax import lax
from jax.experimental import pallas as pl
from jax.experimental.pallas import tpu as pltpu
from jax.sharding import PartitionSpec as P

HEAD_DIM = 64
norm_eps = 1e-05
masked_value = -1e30
f32 = jnp.float32
bf16 = jnp.bfloat16
exp2_scale = math.log2(math.e) / math.sqrt(HEAD_DIM)
grad_scale = 1.0 / math.sqrt(HEAD_DIM)


def dot_nn(a, b):
    return lax.dot_general(a, b, (((1,), (0,)), ((), ())), preferred_element_type=f32)


def dot_nt(a, b):
    return lax.dot_general(a, b, (((1,), (1,)), ((), ())), preferred_element_type=f32)


def dot_tn(a, b):
    return lax.dot_general(a, b, (((0,), (0,)), ((), ())), preferred_element_type=f32)


def split_heads(x):
    lane = lax.broadcasted_iota(jnp.int32, x.shape, 1)
    zero = jnp.zeros_like(x)
    return jnp.where(lane < HEAD_DIM, x, zero), jnp.where(lane >= HEAD_DIM, x, zero)


def block_rows(tree_len):
    return 256 if tree_len % 256 == 0 else 128


def attention_forward_kernel(q_ref, k_ref, v_ref, col_ref, row_ref, o_ref, lse_ref, bias):
    tree_len = q_ref.shape[0]
    rows = block_rows(tree_len)

    @pl.when(pl.program_id(0) == 0)
    def _():
        for start in range(0, tree_len, rows):
            stop = start + rows
            key_seg = row_ref[0:1, :stop]
            ok = col_ref[start:stop, 0:1] == key_seg
            ok = ok | (col_ref[start:stop, 1:2] == key_seg)
            ok = ok | (col_ref[start:stop, 2:3] == key_seg)
            i = lax.broadcasted_iota(jnp.int32, (rows, stop), 0) + start
            j = lax.broadcasted_iota(jnp.int32, (rows, stop), 1)
            bias[start:stop, :stop] = jnp.where(ok & (j <= i), 0.0, masked_value).astype(f32)

    for start in range(0, tree_len, rows):
        stop = start + rows
        queries = split_heads(q_ref[start:stop, :])
        outs = []
        for h in range(2):
            scores = dot_nt(queries[h], k_ref[:stop, :]) + bias[start:stop, :stop]
            top = jnp.max(scores, axis=1, keepdims=True)
            weights = jnp.exp2((scores - top) * exp2_scale)
            total = jnp.sum(weights, axis=1, keepdims=True)
            outs.append(dot_nn(weights.astype(bf16), v_ref[:stop, :]) / total)
            lse = jnp.broadcast_to(top * exp2_scale + jnp.log2(total), (rows, 128))
            lse_ref[0, h : h + 1, start:stop] = jnp.transpose(lse)[0:1, :]
        lane = lax.broadcasted_iota(jnp.int32, (rows, 128), 1)
        o_ref[start:stop, :] = jnp.where(lane < HEAD_DIM, outs[0], outs[1]).astype(bf16)


def attention_forward(qkv, cols, rows):
    tree_len, width = qkv.shape
    pairs = width // 384
    tile = (tree_len, 128)
    return pl.pallas_call(
        attention_forward_kernel,
        name="attention_forward",
        out_shape=(
            jax.ShapeDtypeStruct((tree_len, width // 3), bf16),
            jax.ShapeDtypeStruct((pairs, 8, tree_len), f32),
        ),
        grid=(pairs,),
        in_specs=[
            pl.BlockSpec(tile, lambda p: (0, p)),
            pl.BlockSpec(tile, lambda p: (0, pairs + p)),
            pl.BlockSpec(tile, lambda p: (0, 2 * pairs + p)),
            pl.BlockSpec(cols.shape, lambda p: (0, 0)),
            pl.BlockSpec(rows.shape, lambda p: (0, 0)),
        ],
        out_specs=(
            pl.BlockSpec(tile, lambda p: (0, p)),
            pl.BlockSpec((1, 8, tree_len), lambda p: (p, 0, 0)),
        ),
        scratch_shapes=[pltpu.VMEM((tree_len, tree_len), f32)],
        compiler_params=pltpu.CompilerParams(vmem_limit_bytes=40 << 20),
        cost_estimate=pl.CostEstimate(
            flops=int(0.6 * 2 * pairs * 4 * tree_len * tree_len * 256),
            bytes_accessed=tree_len * width * 3,
            transcendentals=pairs * tree_len * tree_len,
        ),
    )(qkv, qkv, qkv, cols, rows)


def attention_backward_kernel(
    q_ref, k_ref, v_ref, do_ref, o_ref, lse_ref, col_ref, row_ref, dx_ref, bias, split_k, dk, dv
):
    tree_len = q_ref.shape[0]
    rows = block_rows(tree_len)
    pair = pl.program_id(0)
    pairs = pl.num_programs(0)

    @pl.when(pair == 0)
    def _():
        for start in range(0, tree_len, rows):
            stop = start + rows
            key_seg = col_ref[:stop, 0:1]
            ok = row_ref[0:1, start:stop] == key_seg
            ok = ok | (row_ref[1:2, start:stop] == key_seg)
            ok = ok | (row_ref[2:3, start:stop] == key_seg)
            j = lax.broadcasted_iota(jnp.int32, (stop, rows), 0)
            i = lax.broadcasted_iota(jnp.int32, (stop, rows), 1) + start
            bias[:stop, start:stop] = jnp.where(ok & (j <= i), 0.0, masked_value).astype(f32)

    split_k[0], split_k[1] = split_heads(k_ref[...])
    dk[...] = jnp.zeros_like(dk)
    dv[...] = jnp.zeros_like(dv)
    sub = lax.broadcasted_iota(jnp.int32, (8, 128), 0)
    lane = lax.broadcasted_iota(jnp.int32, (8, 128), 1)
    own = jnp.where(lane // HEAD_DIM == sub, 1.0, 0.0).astype(f32)
    for start in range(0, tree_len, rows):
        stop = start + rows
        queries = split_heads(q_ref[start:stop, :])
        grads = split_heads(do_ref[start:stop, :])
        product = do_ref[start:stop, :].astype(f32) * o_ref[start:stop, :].astype(f32)
        row_dot = lax.dot_general(
            own,
            product,
            (((1,), (1,)), ((), ())),
            precision=lax.Precision.HIGHEST,
            preferred_element_type=f32,
        )
        probs_low = []
        grad_scores = []
        for h in range(2):
            shift = bias[:stop, start:stop] - lse_ref[0, h : h + 1, start:stop]
            probs = jnp.exp2(dot_nt(k_ref[:stop, :], queries[h]) * exp2_scale + shift)
            grad_probs = dot_nt(v_ref[:stop, :], grads[h])
            probs_low.append(probs.astype(bf16))
            grad_scores.append((probs * (grad_probs - row_dot[h : h + 1, :])).astype(bf16))
        dv[:stop, :] += dot_nn(jnp.concatenate(probs_low, 1), jnp.concatenate(grads, 0))
        dk[:stop, :] += dot_nn(jnp.concatenate(grad_scores, 1), jnp.concatenate(queries, 0))
        dq = dot_tn(grad_scores[0], split_k[0, :stop, :])
        dq = dq + dot_tn(grad_scores[1], split_k[1, :stop, :])
        dq = (dq.astype(bf16).astype(f32) * grad_scale).astype(bf16)
        dx_ref[start:stop, pl.ds(pl.multiple_of(pair * 128, 128), 128)] = dq
    dx_ref[:, pl.ds(pl.multiple_of((pairs + pair) * 128, 128), 128)] = (
        dk[...] * grad_scale
    ).astype(bf16)
    dx_ref[:, pl.ds(pl.multiple_of((2 * pairs + pair) * 128, 128), 128)] = dv[...].astype(bf16)


def attention_backward(qkv, grad, out, lse, cols, rows):
    tree_len, width = qkv.shape
    pairs = width // 384
    tile = (tree_len, 128)
    return pl.pallas_call(
        attention_backward_kernel,
        name="attention_backward",
        out_shape=jax.ShapeDtypeStruct((tree_len, width), bf16),
        grid=(pairs,),
        in_specs=[
            pl.BlockSpec(tile, lambda p: (0, p)),
            pl.BlockSpec(tile, lambda p: (0, pairs + p)),
            pl.BlockSpec(tile, lambda p: (0, 2 * pairs + p)),
            pl.BlockSpec(tile, lambda p: (0, p)),
            pl.BlockSpec(tile, lambda p: (0, p)),
            pl.BlockSpec((1, 8, tree_len), lambda p: (p, 0, 0)),
            pl.BlockSpec(cols.shape, lambda p: (0, 0)),
            pl.BlockSpec(rows.shape, lambda p: (0, 0)),
        ],
        out_specs=pl.BlockSpec((tree_len, width), lambda p: (0, 0)),
        scratch_shapes=[
            pltpu.VMEM((tree_len, tree_len), f32),
            pltpu.VMEM((2, tree_len, 128), bf16),
            pltpu.VMEM(tile, f32),
            pltpu.VMEM(tile, f32),
        ],
        compiler_params=pltpu.CompilerParams(vmem_limit_bytes=40 << 20),
        cost_estimate=pl.CostEstimate(
            flops=int(0.6 * 5 * pairs * 4 * tree_len * tree_len * 256),
            bytes_accessed=tree_len * width * 6,
            transcendentals=pairs * tree_len * tree_len,
        ),
    )(qkv, qkv, qkv, grad, out, lse, cols, rows)


def norm_parts(values):
    centered = values - jnp.mean(values, axis=-1, keepdims=True)
    scale = lax.rsqrt(jnp.mean(centered * centered, axis=-1, keepdims=True) + norm_eps)
    return centered * scale, scale


def norm_forward(values, gain, shift):
    return norm_parts(values)[0] * gain + shift


def norm_backward(values, gain, grad):
    xhat, scale = norm_parts(values)
    h = grad * gain
    inner = h - jnp.mean(h, axis=-1, keepdims=True)
    inner = inner - xhat * jnp.mean(h * xhat, axis=-1, keepdims=True)
    return scale * inner, jnp.stack([jnp.sum(grad * xhat, axis=0), jnp.sum(grad, axis=0)])


def gelu_tanh(values):
    return jax.nn.gelu(values, approximate=True)


def pick(pieces, position):
    chosen = pieces[0]
    for number in range(1, len(pieces)):
        chosen = jnp.where(position == number, pieces[number], chosen)
    return chosen


def swap_tp(pieces):
    count = len(pieces)
    here = lax.axis_index("tp")
    arrived = [pick(pieces, here)]
    for step in range(1, count):
        pairs = [(s, (s + step) % count) for s in range(count)]
        sent = pick(pieces, (here + step) % count)
        low = sent.astype(bf16) if sent.dtype == f32 else sent
        arrived.append(lax.ppermute(low, "tp", pairs).astype(sent.dtype))
    return [pick(arrived, (here - s) % count) for s in range(count)]


def sum_everywhere(values):
    for axis in ("tp", "fsdp"):
        count = lax.axis_size(axis)
        if count & (count - 1):
            values = lax.psum(values, axis)
            continue
        step = 1
        while step < count:
            values = values + lax.ppermute(values, axis, [(s, s ^ step) for s in range(count)])
            step *= 2
    return values


def gather_weight(shard):
    return lax.all_gather(shard, ("tp", "fsdp"), axis=0, tiled=True)


def scatter_grad(parts):
    whole = jnp.concatenate([part.astype(bf16) for part in parts], axis=0)
    return lax.psum_scatter(whole, ("tp", "fsdp"), scatter_dimension=0, tiled=True).astype(f32)


def segment_tables(segments, parents):
    labels = jnp.arange(parents.shape[0], dtype=jnp.int32)
    up = lambda seg: jnp.sum(jnp.where(seg[:, None] == labels, parents, 0), axis=1)
    parent = up(segments)
    table = jnp.stack([segments, parent, up(parent)])
    return jnp.pad(table.T, ((0, 0), (0, 5))), jnp.pad(table, ((0, 5), (0, 0)))


def on_device(
    tokens, segments, parents, norm_gains, norm_biases, w_qkv, w_out, w_up, w_down, cotangent
):
    tp = lax.axis_size("tp")
    here = lax.axis_index("tp")
    micro = tokens.shape[0]
    own_rows = tokens.shape[2]
    width = tokens.shape[3]
    tree_len = own_rows * tp
    head_width = w_out.shape[0]
    whole = micro // tp
    shared = list(range(whole * tp, micro))
    halves = range(tp)

    def tree_rows(values):
        rows = []
        for n in range(whole):
            rows += swap_tp([values[n * tp + s, 0] for s in halves])
        return rows, [values[m, 0] for m in shared]

    def rows_back(values):
        back = [None] * micro
        for n in range(whole):
            tree = values[n * tree_len : (n + 1) * tree_len]
            parts = swap_tp([tree[s * own_rows : (s + 1) * own_rows] for s in halves])
            for s in halves:
                back[n * tp + s] = parts[s]
        for number, m in enumerate(shared):
            start = whole * tree_len + number * own_rows
            back[m] = values[start : start + own_rows]
        return back

    weight = lambda gathered: [gathered[t * width : (t + 1) * width] for t in halves]
    full_qkv = weight(gather_weight(w_qkv.reshape(w_qkv.shape[0], -1)))
    full_out = weight(gather_weight(w_out.T))
    full_up = weight(gather_weight(w_up))
    full_down = weight(gather_weight(w_down.T))

    seg_all = jnp.concatenate(swap_tp([segments[:, 0]] * tp), axis=1)
    whole_tokens, share_tokens = tree_rows(tokens)
    whole_cot, share_cot = tree_rows(cotangent)
    whole_tables = []
    for n in range(whole):
        seg = pick([seg_all[n * tp + s] for s in halves], here)
        par = pick([parents[n * tp + s, 0] for s in halves], here)
        whole_tables.append(segment_tables(seg, par))
    share_tables = [segment_tables(seg_all[m], parents[m, 0]) for m in shared]

    share_count = len(shared)
    x = jnp.concatenate(whole_tokens + share_tokens, axis=0).astype(f32)
    split = whole * tree_len

    normed = norm_forward(x, norm_gains[0], norm_biases[0]).astype(bf16)
    share_qkv = [dot_nn(normed[split:], w).astype(bf16) for w in full_qkv]
    whole_qkv = [dot_nn(normed[:split], w).astype(bf16) for w in full_qkv] if whole else []
    share_calls = []
    for n in range(share_count):
        cut = slice(n * own_rows, (n + 1) * own_rows)
        share_calls.append(jnp.concatenate(swap_tp([part[cut] for part in share_qkv]), axis=0))
    whole_out = [[] for _ in halves]
    saved = {}
    for n in range(whole):
        for t in halves:
            qkv = whole_qkv[t][n * tree_len : (n + 1) * tree_len]
            out, lse = attention_forward(qkv, *whole_tables[n])
            saved[n, t] = (qkv, out, lse)
            whole_out[t].append(out)
    share_out = [[] for _ in halves]
    for n in range(share_count):
        out, lse = attention_forward(share_calls[n], *share_tables[n])
        saved[n] = (share_calls[n], out, lse)
        parts = swap_tp([out[s * own_rows : (s + 1) * own_rows] for s in halves])
        for t in halves:
            share_out[t].append(parts[t])
    attended = [jnp.concatenate(whole_out[t] + share_out[t], axis=0) for t in halves]
    branch_a = sum(dot_nt(attended[t], full_out[t]) for t in halves)
    residual = x + norm_forward(branch_a, norm_gains[1], norm_biases[1])

    normed_f = norm_forward(residual, norm_gains[2], norm_biases[2]).astype(bf16)
    up_low = []
    hidden = []
    for t in halves:
        up = dot_nn(normed_f, full_up[t])
        hidden.append(gelu_tanh(up).astype(bf16))
        up_low.append(up.astype(bf16))
    branch_f = sum(dot_nt(hidden[t], full_down[t]) for t in halves)
    out = (residual + norm_forward(branch_f, norm_gains[3], norm_biases[3])).astype(bf16)
    out_rows = jnp.stack(rows_back(out))[:, None]

    grad_out = jnp.concatenate(whole_cot + share_cot, axis=0).astype(f32)
    grad_branch_f, sums_3 = norm_backward(branch_f, norm_gains[3], grad_out)
    grad_branch_f = grad_branch_f.astype(bf16)
    grad_down = scatter_grad([dot_tn(grad_branch_f, hidden[t]) for t in halves])
    grad_up = []
    for t in halves:
        pull = jax.vjp(gelu_tanh, up_low[t].astype(f32))[1]
        grad_up.append(pull(dot_nn(grad_branch_f, full_down[t]))[0].astype(bf16))
    grad_w_up = scatter_grad([dot_tn(normed_f, grad_up[t]) for t in halves])
    grad_normed_f = sum(dot_nt(grad_up[t], full_up[t]) for t in halves)
    grad_part, sums_2 = norm_backward(residual, norm_gains[2], grad_normed_f)
    grad_residual = grad_out + grad_part

    grad_branch_a, sums_1 = norm_backward(branch_a, norm_gains[1], grad_residual)
    grad_branch_a = grad_branch_a.astype(bf16)
    share_grad = [dot_nn(grad_branch_a[split:], w).astype(bf16) for w in full_out]
    share_do = []
    for n in range(share_count):
        cut = slice(n * own_rows, (n + 1) * own_rows)
        share_do.append(jnp.concatenate(swap_tp([part[cut] for part in share_grad]), axis=0))
    grad_w_out = scatter_grad([dot_tn(grad_branch_a, attended[t]) for t in halves])
    whole_grad = [dot_nn(grad_branch_a[:split], w).astype(bf16) for w in full_out] if whole else []
    grad_qkv = [[] for _ in halves]
    share_parts = [[] for _ in halves]
    for n in range(share_count):
        qkv, att, lse = saved[n]
        dx = attention_backward(qkv, share_do[n], att, lse, *share_tables[n])
        parts = swap_tp([dx[s * own_rows : (s + 1) * own_rows] for s in halves])
        for t in halves:
            share_parts[t].append(parts[t])
    for n in range(whole):
        for t in halves:
            qkv, att, lse = saved[n, t]
            do = whole_grad[t][n * tree_len : (n + 1) * tree_len]
            grad_qkv[t].append(attention_backward(qkv, do, att, lse, *whole_tables[n]))
    grad_qkv = [jnp.concatenate(grad_qkv[t] + share_parts[t], axis=0) for t in halves]
    grad_w_qkv = scatter_grad([dot_tn(normed, grad_qkv[t]) for t in halves])
    grad_normed = sum(dot_nt(grad_qkv[t], full_qkv[t]) for t in halves)
    grad_part, sums_0 = norm_backward(x, norm_gains[0], grad_normed)
    grad_x = grad_residual + grad_part
    input_rows = jnp.stack(rows_back(grad_x))[:, None]
    early = sum_everywhere(jnp.stack([sums_1, sums_2, sums_3]))
    late = sum_everywhere(sums_0[None])
    sums = jnp.concatenate([late, early], axis=0)
    return (
        out_rows,
        input_rows,
        grad_w_qkv.reshape(w_qkv.shape),
        grad_w_out.T,
        grad_w_up,
        grad_down.T,
        sums[:, 0],
        sums[:, 1],
    )


def solution(mesh):
    in_specs = (
        P(None, "fsdp", "tp", None),
        P(None, "fsdp", "tp"),
        P(None, "fsdp", None),
        P(),
        P(),
        P("fsdp", None, "tp"),
        P("tp", "fsdp"),
        P("fsdp", "tp"),
        P("tp", "fsdp"),
        P(None, "fsdp", "tp", None),
    )
    out_specs = (
        P(None, "fsdp", "tp", None),
        P(None, "fsdp", "tp", None),
        P("fsdp", None, "tp"),
        P("tp", "fsdp"),
        P("fsdp", "tp"),
        P("tp", "fsdp"),
        P(),
        P(),
    )
    return jax.shard_map(
        on_device, mesh=mesh, in_specs=in_specs, out_specs=out_specs, check_vma=False
    )
```

time: 2380 us -> 1050 us (0.44)
  waiting for transfers between devices: 1220 us -> 410 us
  matrix products: 752 us -> 285 us
  other arithmetic: 266 us -> 106 us
  Pallas kernels: 0 us -> 145 us
  blocking collectives: 54.8 us -> 0 us
  starting transfers between devices: 3.9 us -> 29.9 us
    reduce_scatter x24 -> x4, waiting for transfers between devices: 928 us -> 232 us  [scatter_grad(): lax.psum_scatter(whole, ('tp', 'fsdp'), scatter_dimension=0, tiled=True)]
    dot_general x66 -> x28, matrix products: 662 us -> 285 us  [the longest x12 106 us: dot_nn(): lax.dot_general(a, b, (((1,), (0,)), ((), ())), preferred_element_type=f32)]
    all_gather x16 -> x4, waiting for transfers between devices: 288 us -> 70.6 us  [gather_weight(): return lax.all_gather(shard, ('tp', 'fsdp'), axis=0, tiled=True)]
    pallas_call x0 -> x6, Pallas kernels: none -> 145 us  [the longest x3 79.9 us: attention_backward(): pl.pallas_call(attention_backward_kernel, name='attention_backward', out_...]
    convert_element_type x14 -> x6, other arithmetic: 146 us -> 16.7 us  [the longest x1 6.19 us: on_device(): grad_branch_f = grad_branch_f.astype(bf16)]
    ppermute x0 -> x19, waiting for transfers between devices: none -> 107 us  [the longest x9 81.9 us: swap_tp(): arrived.append(lax.ppermute(low, 'tp', pairs).astype(sent.dtype))]
    sub x6 -> x0, matrix products: 90.1 us -> none  [attention_forward(): exp_rows = jnp.exp(masked - top_row)]
    reduce_sum x36 -> x11, other arithmetic: 80.2 us -> 24.9 us  [the longest x2 14.5 us: norm_backward(): jnp.sum(grad * xhat, axis=0)]
  transfers between devices with their start and end apart: 40 -> 27, of which waited for: 27 -> 15; matrix products, arithmetic and copies ran while one was open for 40% -> 27% of each run, Pallas kernels for 0% -> 14%
where the time goes in v1:
time: 1050 us; the launch traced here: 1040 us
  waiting for transfers between devices  410 us (39%)
  matrix products  285 us (27%)
  Pallas kernels  145 us (14%)
  other arithmetic  106 us (10%)
  local copies, waits for them, and re-layouts  52.4 us (5%)
  starting transfers between devices  29.9 us (3%)
  between operations  16 us (2%)
    reduce_scatter x4, waiting for transfers between devices, scatter_grad(): lax.psum_scatter(whole, ('tp', 'fsdp'), scatter_dimension=0, tiled=True)  232 us
    dot_general x12, matrix products, dot_nn(): lax.dot_general(a, b, (((1,), (0,)), ((), ())), preferred_element_type=f32)  106 us
    dot_general x8, matrix products, dot_nt(): lax.dot_general(a, b, (((1,), (1,)), ((), ())), preferred_element_type=f32)  105 us
    ppermute x9, waiting for transfers between devices, swap_tp(): arrived.append(lax.ppermute(low, 'tp', pairs).astype(sent.dtype))  81.9 us
    pallas_call x3, Pallas kernels, attention_backward(): pl.pallas_call(attention_backward_kernel, name='attention_backward', out_...  79.9 us
    dot_general x8, matrix products, dot_tn(): lax.dot_general(a, b, (((0,), (0,)), ((), ())), preferred_element_type=f32)  75.2 us
    all_gather x4, waiting for transfers between devices, gather_weight(): return lax.all_gather(shard, ('tp', 'fsdp'), axis=0, tiled=True)  70.6 us
    pallas_call x3, Pallas kernels, attention_forward(): pl.pallas_call(attention_forward_kernel, name='attention_forward', out_sh...  64.6 us
  transfers between devices with their start and end apart: 27, of which 15 were waited for; matrix products, arithmetic and copies ran while one was open for 27% of the time, Pallas kernels for 14%

profile of v1, /device:TPU:0, one launch (start us, length us, event | category | flops | bytes accessed | tf_op | source)
XLA Modules:
  0.0 1044.9 jit_solution(5026032605426909232)
XLA Ops:
  14.1 4.0 fusion.125
  40.9 19.8 %collective-permute-done = bf16[640,1024]{0,1:T(8,128)(2,1)} collective-permute-done((bf16[640,1024]{0,1:T(8,128)(2,1)}, bf16[640,1024]{0,1:T(8,128)(2,1)}, u32[]{:S(2)}, u32[]{:S(2)}) %collective-permute-start) | collective-permute-done | bytes 1310752 | tf_op jit(solution)/shard_map/ppermute | solution.py:236
  67.6 31.5 %collective-permute-done.5 = bf16[640,1024]{0,1:T(8,128)(2,1)} collective-permute-done((bf16[640,1024]{0,1:T(8,128)(2,1)}, bf16[640,1024]{0,1:T(8,128)(2,1)}, u32[]{:S(2)}, u32[]{:S(2)}) %collective-permute-start.5) | collective-permute-done | bytes 1310752 | tf_op jit(solution)/shard_map/ppermute | solution.py:236
  102.3 4.7 convolution_convert_fusion.6
  111.5 4.6 convolution_convert_fusion.q_ref.k_ref.v_ref
  116.1 21.5 %attention_forward.5 = (bf16[1280,512]{1,0:T(8,128)(2,1)S(1)}, f32[4,8,1280]{2,1,0:T(8,128)S(1)}) custom-call(bf16[1280,1536]{1,0:T(8,128)(2,1)S(1)} %convolution_convert_fusion.q_ref.k_ref.v_ref, bf16[1280,1536]{1,0:T(8,128)(2,1)S(1)} %convolution_convert_fusion.q_ref.k_ref.v_ref, bf16[1280,1536]{1,0:T(8,128)(2,1)S(1)} %convolution_convert_fusion.q_ref.k_ref.v_ref, ...), custom_call_target="tpu_custom_call" | custom-call | flops 8053063680 | bytes 5898240 | tf_op jit(solution)/shard_map/attention_forward/pallas_call | solution.py:77
  137.7 6.9 convolution_convert_fusion.1.q_ref.k_ref.v_ref
  144.6 16.5 %collective-permute-done.2 = bf16[640,1536]{1,0:T(8,128)(2,1)S(1)} collective-permute-done((bf16[640,1536]{1,0:T(8,128)(2,1)}, bf16[640,1536]{1,0:T(8,128)(2,1)S(1)}, u32[]{:S(2)}, u32[]{:S(2)}) %collective-permute-start.2) | collective-permute-done | bytes 1966112 | tf_op jit(solution)/shard_map/ppermute | solution.py:236
  161.7 21.7 %attention_forward.4 = (bf16[1280,512]{1,0:T(8,128)(2,1)S(1)}, f32[4,8,1280]{2,1,0:T(8,128)S(1)}) custom-call(bf16[1280,1536]{1,0:T(8,128)(2,1)S(1)} %pad_maximum_fusion.6.q_ref.k_ref.v_ref, bf16[1280,1536]{1,0:T(8,128)(2,1)S(1)} %pad_maximum_fusion.6.q_ref.k_ref.v_ref, bf16[1280,1536]{1,0:T(8,128)(2,1)S(1)} %pad_maximum_fusion.6.q_ref.k_ref.v_ref, ...), custom_call_target="tpu_custom_call" | custom-call | flops 8053063680 | bytes 5898240 | tf_op jit(solution)/shard_map/attention_forward/pallas_call | solution.py:77
  184.5 21.4 %attention_forward.3 = (bf16[1280,512]{1,0:T(8,128)(2,1)S(1)}, f32[4,8,1280]{2,1,0:T(8,128)S(1)}) custom-call(bf16[1280,1536]{1,0:T(8,128)(2,1)S(1)} %convolution_convert_fusion.1.q_ref.k_ref.v_ref, bf16[1280,1536]{1,0:T(8,128)(2,1)S(1)} %convolution_convert_fusion.1.q_ref.k_ref.v_ref, bf16[1280,1536]{1,0:T(8,128)(2,1)S(1)} %convolution_convert_fusion.1.q_ref.k_ref.v_ref, ...), custom_call_target="tpu_custom_call" | custom-call | flops 8053063680 | bytes 5898240 | tf_op jit(solution)/shard_map/attention_forward/pallas_call | solution.py:77
  208.1 3.9 fusion.91
  228.0 18.8 %all-gather.9.cloned.1.call-done = bf16[2048,2048]{1,0:T(8,128)(2,1)} async-done(((bf16[64,2048]{1,0:T(8,128)(2,1)}), bf16[2048,2048]{1,0:T(8,128)(2,1)}) %all-gather.9.cloned.1.call-update) | async-done | bytes 8388624 | tf_op jit(solution)/shard_map/all_gather | solution.py:254
  246.8 14.8 %fusion.67 = f32[1920,2048]{1,0:T(8,128)} fusion(bf16[1920,1024]{0,1:T(8,128)(2,1)} %add_convert_fusion.1, bf16[2048,2048]{1,0:T(8,128)(2,1)} %all-gather.9.cloned.1.call-done), kind=kOutput, calls=%fused_computation.118 | convolution fusion | flops 8053063680 | bytes 23855104 | tf_op jit(solution)/shard_map/dot_general | solution.py:20
  261.7 11.8 %fusion.77 = f32[1920,2048]{1,0:T(8,128)} fusion(bf16[1920,1024]{0,1:T(8,128)(2,1)S(1)} %copy-done.53, bf16[2048,2048]{1,0:T(8,128)(2,1)S(1)} %copy-done.94), kind=kOutput, calls=%fused_computation.126 | convolution fusion | flops 8053063680 | bytes 23855104 | tf_op jit(solution)/shard_map/dot_general | solution.py:20
  273.5 51.8 %all-gather.11.cloned.1.call-done = bf16[2048,2048]{1,0:T(8,128)(2,1)} async-done(((bf16[64,2048]{1,0:T(8,128)(2,1)}), bf16[2048,2048]{1,0:T(8,128)(2,1)}) %all-gather.11.cloned.1.call-update) | async-done | bytes 8388624 | tf_op jit(solution)/shard_map/all_gather | solution.py:254
  325.3 15.7 %fusion.71 = f32[1920,1024]{0,1:T(8,128)} fusion(bf16[2048,2048]{1,0:T(8,128)(2,1)} %all-gather.11.cloned.1.call-done, f32[1920,2048]{1,0:T(8,128)} %fusion.77), kind=kOutput, calls=%fused_computation.122 | convolution fusion | flops 8088453120 | bytes 27787264 | tf_op jit(solution)/shard_map/dot_general | solution.py:24
  341.0 17.3 %fusion.129 = (f32[1920]{0:T(1024)S(1)}, f32[1920,1024]{0,1:T(8,128)}) fusion(f32[1920,1024]{0,1:T(8,128)} %fusion.71, bf16[2048,2048]{1,0:T(8,128)(2,1)} %all-gather.11.cloned.1.call-done, f32[1920,2048]{1,0:T(8,128)} %fusion.67), kind=kOutput, calls=%fused_computation.265 | convolution fusion | flops 8092383232 | bytes 35659264 | tf_op jit(solution)/shard_map/dot_general | solution.py:24
  358.3 4.2 multiply_reduce_fusion.4
  363.7 4.3 fusion.55
  368.1 6.2 fusion.53
  374.3 24.9 %fusion.4 = bf16[1920,2048]{1,0:T(8,128)(2,1)} fusion(f32[1920,2048]{1,0:T(8,128)} %fusion.67, bf16[1920,1024]{0,1:T(8,128)(2,1)} %get-tuple-element.69, bf16[2048,2048]{1,0:T(8,128)(2,1)} %all-gather.11.cloned.1.call-done), kind=kOutput, calls=%fused_computation.14 | convolution fusion | flops 8139571200 | bytes 31719424 | tf_op jit(solution)/shard_map/dot_general | solution.py:20
  399.2 23.6 %fusion.7 = bf16[1920,2048]{1,0:T(8,128)(2,1)} fusion(f32[1920,2048]{1,0:T(8,128)} %fusion.77, bf16[1920,1024]{0,1:T(8,128)(2,1)S(1)} %copy-done.48, bf16[2048,2048]{1,0:T(8,128)(2,1)} %all-gather.11.cloned.1.call-done), kind=kOutput, calls=%fused_computation.17 | convolution fusion | flops 8139571200 | bytes 31719424 | tf_op jit(solution)/shard_map/dot_general | solution.py:20
  422.7 14.6 %fusion.75 = f32[1920,1024]{0,1:T(8,128)} fusion(bf16[1920,2048]{1,0:T(8,128)(2,1)} %fusion.7, bf16[2048,2048]{1,0:T(8,128)(2,1)} %all-gather.9.cloned.1.call-done), kind=kOutput, calls=%fused_computation.124 | convolution fusion | flops 8053063680 | bytes 19922944 | tf_op jit(solution)/shard_map/dot_general | solution.py:24
  437.4 20.7 %multiply_reduce_fusion = (f32[1024]{0:T(1024)}, f32[1920]{0:T(1024)S(1)}, f32[1920]{0:T(1024)S(1)}, f32[1024]{0:T(1024)}, f32[1920,1024]{0,1:T(8,128)}) fusion(f32[1920,1024]{0,1:T(8,128)} %copy-done.25, f32[1920]{0:T(1024)S(1)} %copy-done.73, f32[1920]{0:T(1024)S(1)} %copy-done.70, f32[1024]{0:T(1024)S(1)} %bitcast.119, f32[1920,1024]{0,1:T(8,128)} %fusion.75, ...), kind=kOutput, calls=%fused_computation.76 | convolution fusion | flops 8072718336 | bytes 35694592 | tf_op jit(solution)/shard_map/dot_general | solution.py:24
  458.2 10.2 multiply_reduce_fusion.1
  486.6 26.4 %attention_backward.5 = bf16[1280,1536]{1,0:T(8,128)(2,1)S(1)} custom-call(bf16[1280,1536]{1,0:T(8,128)(2,1)S(1)} %copy-done.15, bf16[1280,1536]{1,0:T(8,128)(2,1)S(1)} %copy-done.15, bf16[1280,1536]{1,0:T(8,128)(2,1)S(1)} %copy-done.15, bf16[1280,512]{1,0:T(8,128)(2,1)S(1)} %convolution_convert_fusion.8.do_ref, bf16[1280,512]{1,0:T(8,128)(2,1)S(1)} %copy-done.11, ...), custom_call_target="tpu_custom_call" | custom-call | flops 20132659200 | bytes 11796480 | tf_op jit(solution)/shard_map/attention_backward/pallas_call | solution.py:168
  513.3 26.6 %attention_backward.4 = bf16[1280,1536]{1,0:T(8,128)(2,1)S(1)} custom-call(bf16[1280,1536]{1,0:T(8,128)(2,1)S(1)} %copy-done.3, bf16[1280,1536]{1,0:T(8,128)(2,1)S(1)} %copy-done.3, bf16[1280,1536]{1,0:T(8,128)(2,1)S(1)} %copy-done.3, bf16[1280,512]{1,0:T(8,128)(2,1)S(1)} %pad_maximum_fusion.19.do_ref, bf16[1280,512]{1,0:T(8,128)(2,1)S(1)} %copy-done.1, ...), custom_call_target="tpu_custom_call" | custom-call | flops 20132659200 | bytes 11796480 | tf_op jit(solution)/shard_map/attention_backward/pallas_call | solution.py:168
  540.8 3.9 convolution_convert_fusion.9.do_ref
  544.8 26.8 %attention_backward.3 = bf16[1280,1536]{1,0:T(8,128)(2,1)S(1)} custom-call(bf16[1280,1536]{1,0:T(8,128)(2,1)S(1)} %copy-done.13, bf16[1280,1536]{1,0:T(8,128)(2,1)S(1)} %copy-done.13, bf16[1280,1536]{1,0:T(8,128)(2,1)S(1)} %copy-done.13, bf16[1280,512]{1,0:T(8,128)(2,1)S(1)} %convolution_convert_fusion.9.do_ref, bf16[1280,512]{1,0:T(8,128)(2,1)S(1)} %copy-done.5, ...), custom_call_target="tpu_custom_call" | custom-call | flops 20132659200 | bytes 11796480 | tf_op jit(solution)/shard_map/attention_backward/pallas_call | solution.py:168
  571.6 13.3 %collective-permute-done.7 = bf16[640,1536]{1,0:T(8,128)(2,1)S(1)} collective-permute-done((bf16[640,1536]{1,0:T(8,128)(2,1)S(1)}, bf16[640,1536]{1,0:T(8,128)(2,1)S(1)}, u32[]{:S(2)}, u32[]{:S(2)}) %collective-permute-start.7) | collective-permute-done | bytes 1966112 | tf_op jit(solution)/shard_map/ppermute | solution.py:236
  585.3 6.9 fusion.59
  592.2 7.1 fusion.60
  602.4 15.2 %convolution_convert_fusion.2 = bf16[1024,2048]{1,0:T(8,128)(2,1)} fusion(bf16[1920,1024]{0,1:T(8,128)(2,1)} %get-tuple-element.69, f32[1920,2048]{1,0:T(8,128)} %fusion.67), kind=kOutput, calls=%fused_computation.108 | convolution fusion | flops 8090550272 | bytes 23855104 | tf_op jit(solution)/shard_map/dot_general | solution.py:28
  617.6 14.0 %convolution_convert_fusion.3 = bf16[1024,2048]{1,0:T(8,128)(2,1)} fusion(bf16[1920,1024]{0,1:T(8,128)(2,1)S(1)} %copy-done.49, f32[1920,2048]{1,0:T(8,128)} %fusion.77), kind=kOutput, calls=%fused_computation.109 | convolution fusion | flops 8090550272 | bytes 23855104 | tf_op jit(solution)/shard_map/dot_general | solution.py:28
  631.6 8.7 pad_maximum_fusion.1
  640.4 14.8 %convolution_convert_fusion.5 = bf16[1024,2048]{1,0:T(8,128)(2,1)} fusion(bf16[1920,1024]{0,1:T(8,128)(2,1)} %add_convert_fusion.1, bf16[1920,2048]{1,0:T(8,128)(2,1)} %fusion.7), kind=kOutput, calls=%fused_computation.111 | convolution fusion | flops 8055160832 | bytes 15990784 | tf_op jit(solution)/shard_map/dot_general | solution.py:28
  655.2 12.6 %convolution_convert_fusion.4 = bf16[1024,2048]{1,0:T(8,128)(2,1)} fusion(bf16[1920,1024]{0,1:T(8,128)(2,1)S(1)} %copy-done.54, bf16[1920,2048]{1,0:T(8,128)(2,1)} %fusion.4), kind=kOutput, calls=%fused_computation.110 | convolution fusion | flops 8055160832 | bytes 15990784 | tf_op jit(solution)/shard_map/dot_general | solution.py:28
  667.9 8.9 pad_maximum_fusion
  683.4 12.5 %fusion.57 = f32[1920,1024]{0,1:T(8,128)} fusion(bf16[640,1536]{1,0:T(8,128)(2,1)} %copy-done.59, bf16[1280,1536]{1,0:T(8,128)(2,1)} %copy-done.16, bf16[2048,1536]{1,0:T(8,128)(2,1)} %all-gather.5.cloned.1.call-done), kind=kOutput, calls=%fused_computation.104 | convolution fusion | flops 6051594240 | bytes 16908288 | tf_op jit(solution)/shard_map/dot_general | solution.py:24
  696.0 17.6 %fusion.49 = (f32[1024]{0:T(1024)}, f32[1920]{0:T(1024)}, f32[1920]{0:T(1024)}, f32[1024]{0:T(1024)}, f32[1920,1024]{0,1:T(8,128)}) fusion(f32[1920]{0:T(1024)} %copy-done.71, f32[1920]{0:T(1024)S(1)} %copy-done.66, bf16[640,1024]{0,1:T(8,128)(2,1)S(1)} %bitcast.99, bf16[640,1024]{0,1:T(8,128)(2,1)S(1)} %copy-done.36, bf16[640,1024]{0,1:T(8,128)(2,1)S(1)} %copy-done.33, ...), kind=kOutput, calls=%fused_computation.68 | convolution fusion | flops 6083045376 | bytes 28748288 | tf_op jit(solution)/shard_map/dot_general | solution.py:24
  715.0 7.1 fusion.48
  739.2 14.6 %collective-permute-done.9 = f32[1,2,1024]{2,0,1:T(1,128)S(1)} collective-permute-done((f32[1,2,1024]{2,0,1:T(1,128)S(1)}, f32[1,2,1024]{2,0,1:T(1,128)S(1)}, u32[]{:S(2)}, u32[]{:S(2)}) %collective-permute-start.9) | collective-permute-done | bytes 8224 | tf_op jit(solution)/shard_map/ppermute | solution.py:248
  755.0 9.8 collective-permute-start.11
  775.9 6.3 copy.74
  782.8 3.9 fusion.79
  790.2 9.1 copy.75
  802.6 84.0 %reduce-scatter.11.cloned.1.call-done = bf16[64,2048]{1,0:T(8,128)(2,1)} async-done(((bf16[2048,2048]{1,0:T(8,128)(2,1)}), bf16[64,2048]{1,0:T(8,128)(2,1)}) %reduce-scatter.11.cloned.1.call-update) | async-done | bytes 262160 | tf_op jit(solution)/shard_map/reduce_scatter | solution.py:259
  888.4 147.6 %reduce-scatter.9.cloned.1.call-done = bf16[64,2048]{1,0:T(8,128)(2,1)} async-done(((bf16[2048,2048]{1,0:T(8,128)(2,1)}), bf16[64,2048]{1,0:T(8,128)(2,1)}) %reduce-scatter.9.cloned.1.call-update) | async-done | bytes 262160 | tf_op jit(solution)/shard_map/reduce_scatter | solution.py:259
  (358 shorter events, 135.6 us)
Async XLA Ops:
  7.2 95.1 %all-gather.5.cloned.1.call-start = ((), (), s32[]{:S(2)}) async-start(), calls=%async_computation.4 | async-start | bytes 6488064 | tf_op jit(solution)/shard_map/all_gather | solution.py:254
  8.9 199.2 %all-gather.7.cloned.1.call-start = ((), (), s32[]{:S(2)}) async-start(), calls=%async_computation.5 | async-start | bytes 2162688 | tf_op jit(solution)/shard_map/all_gather | solution.py:254
  9.6 237.2 %all-gather.9.cloned.1.call-start = ((), (), s32[]{:S(2)}) async-start(), calls=%async_computation.6 | async-start | bytes 8650752 | tf_op jit(solution)/shard_map/all_gather | solution.py:254
  10.3 314.9 %all-gather.11.cloned.1.call-start = ((), (), s32[]{:S(2)}) async-start(), calls=%async_computation.7 | async-start | bytes 8650752 | tf_op jit(solution)/shard_map/all_gather | solution.py:254
  11.1 26.7 %collective-permute-start.1 = (s32[3,640]{1,0:T(4,128)S(1)}, s32[3,640]{1,0:T(4,128)S(1)}, u32[]{:S(2)}, u32[]{:S(2)}) collective-permute-start(s32[3,640]{1,0:T(4,128)S(1)} %bitcast.129), channel_id=1, source_target_pairs={{0,1},{1,0},{2,3},{3,2},{4,5},{5,4},{6,7},{7,6},{8,9},{9,8},{10,11... | collective-permute-start | bytes 23048 | tf_op jit(solution)/shard_map/ppermute | solution.py:236
  22.2 38.5 %collective-permute-start = (bf16[640,1024]{0,1:T(8,128)(2,1)}, bf16[640,1024]{0,1:T(8,128)(2,1)}, u32[]{:S(2)}, u32[]{:S(2)}) collective-permute-start(bf16[640,1024]{0,1:T(8,128)(2,1)} %select_bitcast_fusion.3), channel_id=1, source_target_pairs={{0,1},{1,0},{2,3},{3,2},{4,5},{5,4},{6,7},{7,6},{8,9},{9,8},{10,11... | collective-permute-start | bytes 3932168 | tf_op jit(solution)/shard_map/ppermute | solution.py:236
  31.5 67.6 %collective-permute-start.5 = (bf16[640,1024]{0,1:T(8,128)(2,1)}, bf16[640,1024]{0,1:T(8,128)(2,1)}, u32[]{:S(2)}, u32[]{:S(2)}) collective-permute-start(bf16[640,1024]{0,1:T(8,128)(2,1)} %select_bitcast_fusion), channel_id=1, source_target_pairs={{0,1},{1,0},{2,3},{3,2},{4,5},{5,4},{6,7},{7,6},{8,9},{9,8},{10,11... | collective-permute-start | bytes 3932168 | tf_op jit(solution)/shard_map/ppermute | solution.py:236
  31.6 767.7 %reduce-scatter.7.cloned.1.call-start = ((), (), s32[]{:S(2)}) async-start(), calls=%async_computation.9 | async-start | bytes 2162688 | tf_op jit(solution)/shard_map/reduce_scatter | solution.py:259
  32.5 32.1 %copy-start.76 = (f32[1,1024]{1,0:T(1,128)}, f32[1,1024]{1,0:T(1,128)S(1)}, u32[]{:S(2)}) copy-start(f32[1,1024]{1,0:T(1,128)S(1)} %get-tuple-element.101) | copy-start | bytes 12292
  32.5 182.8 %copy-start.74 = (f32[1,1024]{1,0:T(1,128)}, f32[1,1024]{1,0:T(1,128)S(1)}, u32[]{:S(2)}) copy-start(f32[1,1024]{1,0:T(1,128)S(1)} %get-tuple-element.100) | copy-start | bytes 12292
  32.5 190.4 %copy-start.79 = (f32[1,1024]{1,0:T(1,128)}, f32[1,1024]{1,0:T(1,128)S(1)}, u32[]{:S(2)}) copy-start(f32[1,1024]{1,0:T(1,128)S(1)} %get-tuple-element.102) | copy-start | bytes 12292
  34.8 29.7 %copy-start.28 = (bf16[1,1,640,1024]{2,3,1,0:T(8,128)(2,1)}, bf16[1,1,640,1024]{2,3,1,0:T(8,128)(2,1)S(1)}, u32[]{:S(2)}) copy-start(bf16[1,1,640,1024]{2,3,1,0:T(8,128)(2,1)S(1)} %copy.84) | copy-start | bytes 3932164
  38.3 123.4 %copy-start.8 = (s32[8,1280]{1,0:T(8,128)}, s32[8,1280]{1,0:T(8,128)S(1)}, u32[]{:S(2)}) copy-start(s32[8,1280]{1,0:T(8,128)S(1)} %pad.17.row_ref) | copy-start | bytes 122884
  38.7 123.1 %copy-start.6 = (s32[1280,8]{1,0:T(8,128)}, s32[1280,8]{1,0:T(8,128)S(1)}, u32[]{:S(2)}) copy-start(s32[1280,8]{1,0:T(8,128)S(1)} %pad.16.clone.col_ref) | copy-start | bytes 122884
  63.4 35.7 %copy-start.43 = (bf16[1,1,640,1024]{2,3,1,0:T(8,128)(2,1)S(1)}, bf16[1,1,640,1024]{2,3,1,0:T(8,128)(2,1)}, u32[]{:S(2)}) copy-start(bf16[1,1,640,1024]{2,3,1,0:T(8,128)(2,1)} %copy-done.42) | copy-start | bytes 3932164
  63.4 35.7 %copy-start.45 = (bf16[1,1,640,1024]{2,3,1,0:T(8,128)(2,1)S(1)}, bf16[1,1,640,1024]{2,3,1,0:T(8,128)(2,1)}, u32[]{:S(2)}) copy-start(bf16[1,1,640,1024]{2,3,1,0:T(8,128)(2,1)} %copy-done.44) | copy-start | bytes 3932164
  63.4 38.8 %copy-start.65 = (f32[1920]{0:T(1024)}, f32[1920]{0:T(1024)S(1)}, u32[]{:S(2)}) copy-start(f32[1920]{0:T(1024)S(1)} %broadcast_multiply_fusion.11) | copy-start | bytes 23044
  64.5 37.7 %copy-start.71 = (f32[1920]{0:T(1024)}, f32[1920]{0:T(1024)S(1)}, u32[]{:S(2)}) copy-start(f32[1920]{0:T(1024)S(1)} %add_rsqrt_fusion.3) | copy-start | bytes 23044
  111.2 49.9 %collective-permute-start.2 = (bf16[640,1536]{1,0:T(8,128)(2,1)}, bf16[640,1536]{1,0:T(8,128)(2,1)S(1)}, u32[]{:S(2)}, u32[]{:S(2)}) collective-permute-start(bf16[640,1536]{1,0:T(8,128)(2,1)} %get-tuple-element.113), channel_id=1, source_target_pairs={{0,1},{1,0},{2,3},{3,2},{4,5},{5,4},{6,7},{7,6},{8,9},{9,8},{10,11... | collective-permute-start | bytes 5898248 | tf_op jit(solution)/shard_map/ppermute | solution.py:236
  137.7 70.4 %copy-start.10 = (bf16[1280,512]{1,0:T(8,128)(2,1)}, bf16[1280,512]{1,0:T(8,128)(2,1)S(1)}, u32[]{:S(2)}) copy-start(bf16[1280,512]{1,0:T(8,128)(2,1)S(1)} %get-tuple-element.16.o_ref) | copy-start | bytes 3932164
  144.6 39.8 %copy-start.12 = (bf16[1280,1536]{1,0:T(8,128)(2,1)}, bf16[1280,1536]{1,0:T(8,128)(2,1)S(1)}, u32[]{:S(2)}) copy-start(bf16[1280,1536]{1,0:T(8,128)(2,1)S(1)} %convolution_convert_fusion.1.q_ref.k_ref.v_ref) | copy-start | bytes 11796484
  184.1 22.7 %collective-permute-start.3 = (bf16[640,512]{1,0:T(8,128)(2,1)S(1)}, bf16[640,512]{1,0:T(8,128)(2,1)S(1)}, u32[]{:S(2)}, u32[]{:S(2)}) collective-permute-start(bf16[640,512]{1,0:T(8,128)(2,1)S(1)} %broadcast_select_fusion.17), channel_id=1, source_target_pairs={{0,1},{1,0},{2,3},{3,2},{4,5},{5,4},{6,7},{7,6},{8,9},{9,8},{10,11... | collective-permute-start | bytes 1966088 | tf_op jit(solution)/shard_map/ppermute | solution.py:236
  222.9 38.8 %copy-start.72 = (f32[1920]{0:T(1024)}, f32[1920]{0:T(1024)S(1)}, u32[]{:S(2)}) copy-start(f32[1920]{0:T(1024)S(1)} %add_rsqrt_fusion.1) | copy-start | bytes 23044
  422.7 35.4 %slice-start = ((s8[7864320]{0:T(1024)(128)(4,1)}), s8[4194304]{0:T(1024)(128)(4,1)S(1)}, s32[]{:S(2)}) async-start(s8[7864320]{0:T(1024)(128)(4,1)} %bitcast.91), calls=%async_computation.12 | async-start | bytes 8388608
  478.0 322.8 %reduce-scatter.5.cloned.1.call-start = ((), (), s32[]{:S(2)}) async-start(), calls=%async_computation.8 | async-start | bytes 6488064 | tf_op jit(solution)/shard_map/reduce_scatter | solution.py:259
  483.4 29.6 %collective-permute-start.6 = (bf16[640,512]{1,0:T(8,128)(2,1)S(1)}, bf16[640,512]{1,0:T(8,128)(2,1)S(1)}, u32[]{:S(2)}, u32[]{:S(2)}) collective-permute-start(bf16[640,512]{1,0:T(8,128)(2,1)S(1)} %get-tuple-element.120), channel_id=1, source_target_pairs={{0,1},{1,0},{2,3},{3,2},{4,5},{5,4},{6,7},{7,6},{8,9},{9,8},{10,11... | collective-permute-start | bytes 1966088 | tf_op jit(solution)/shard_map/ppermute | solution.py:236
  486.5 26.7 %copy-start.1 = (bf16[1280,512]{1,0:T(8,128)(2,1)S(1)}, bf16[1280,512]{1,0:T(8,128)(2,1)}, u32[]{:S(2)}) copy-start(bf16[1280,512]{1,0:T(8,128)(2,1)} %copy-done) | copy-start | bytes 3932164
  486.5 26.7 %copy-start.3 = (bf16[1280,1536]{1,0:T(8,128)(2,1)S(1)}, bf16[1280,1536]{1,0:T(8,128)(2,1)}, u32[]{:S(2)}) copy-start(bf16[1280,1536]{1,0:T(8,128)(2,1)} %copy-done.2) | copy-start | bytes 11796484
  486.5 26.7 %copy-start.7 = (s32[1280,8]{1,0:T(8,128)S(1)}, s32[1280,8]{1,0:T(8,128)}, u32[]{:S(2)}) copy-start(s32[1280,8]{1,0:T(8,128)} %copy-done.6) | copy-start | bytes 122884
  486.5 26.7 %copy-start.9 = (s32[8,1280]{1,0:T(8,128)S(1)}, s32[8,1280]{1,0:T(8,128)}, u32[]{:S(2)}) copy-start(s32[8,1280]{1,0:T(8,128)} %copy-done.8) | copy-start | bytes 122884
  513.0 26.9 %copy-start.16 = (bf16[1280,1536]{1,0:T(8,128)(2,1)}, bf16[1280,1536]{1,0:T(8,128)(2,1)S(1)}, u32[]{:S(2)}) copy-start(bf16[1280,1536]{1,0:T(8,128)(2,1)S(1)} %attention_backward.5) | copy-start | bytes 11796484
  540.1 44.8 %collective-permute-start.7 = (bf16[640,1536]{1,0:T(8,128)(2,1)S(1)}, bf16[640,1536]{1,0:T(8,128)(2,1)S(1)}, u32[]{:S(2)}, u32[]{:S(2)}) collective-permute-start(bf16[640,1536]{1,0:T(8,128)(2,1)S(1)} %broadcast_select_fusion.4), channel_id=1, source_target_pairs={{0,1},{1,0},{2,3},{3,2},{4,5},{5,4},{6,7},{7,6},{8,9},{9,8},{10,11... | collective-permute-start | bytes 5898248 | tf_op jit(solution)/shard_map/ppermute | solution.py:236
  602.3 284.3 %reduce-scatter.11.cloned.1.call-start = ((), (), s32[]{:S(2)}) async-start(), calls=%async_computation.11 | async-start | bytes 8650752 | tf_op jit(solution)/shard_map/reduce_scatter | solution.py:259
  640.3 395.6 %reduce-scatter.9.cloned.1.call-start = ((), (), s32[]{:S(2)}) async-start(), calls=%async_computation.10 | async-start | bytes 8650752 | tf_op jit(solution)/shard_map/reduce_scatter | solution.py:259
  677.6 5.0 collective-permute-start.14
  681.7 85.9 %collective-permute-start.4 = (bf16[640,1024]{0,1:T(8,128)(2,1)}, bf16[640,1024]{0,1:T(8,128)(2,1)}, u32[]{:S(2)}, u32[]{:S(2)}) collective-permute-start(bf16[640,1024]{0,1:T(8,128)(2,1)} %broadcast_select_fusion.11), channel_id=1, source_target_pairs={{0,1},{1,0},{2,3},{3,2},{4,5},{5,4},{6,7},{7,6},{8,9},{9,8},{10,11... | collective-permute-start | bytes 3932168 | tf_op jit(solution)/shard_map/ppermute | solution.py:236
  683.3 40.1 %collective-permute-start.15 = (f32[3,2,1024]{2,0,1:T(4,128)}, f32[3,2,1024]{2,0,1:T(4,128)}, u32[]{:S(2)}, u32[]{:S(2)}) collective-permute-start(f32[3,2,1024]{2,0,1:T(4,128)} %fusion.116), channel_id=1, source_target_pairs={{0,2},{2,0},{4,6},{6,4},{8,10},{10,8},{12,14},{14,12},{16,18},{18,... | collective-permute-start | bytes 73736 | tf_op jit(solution)/shard_map/ppermute | solution.py:248
  722.1 47.2 %copy-start.37 = (f32[1920,1024]{0,1:T(8,128)}, f32[1920,1024]{0,1:T(8,128)S(1)}, u32[]{:S(2)}) copy-start(f32[1920,1024]{0,1:T(8,128)S(1)} %fusion.48) | copy-start | bytes 23592964
  722.1 45.5 %copy-start.38 = (bf16[1920,1024]{0,1:T(8,128)(2,1)S(1)}, bf16[1920,1024]{0,1:T(8,128)(2,1)}, u32[]{:S(2)}) copy-start(bf16[1920,1024]{0,1:T(8,128)(2,1)} %get-tuple-element.70) | copy-start | bytes 11796484
  722.4 60.4 %collective-permute-start.8 = (bf16[640,1024]{0,1:T(8,128)(2,1)S(1)}, bf16[640,1024]{0,1:T(8,128)(2,1)S(1)}, u32[]{:S(2)}, u32[]{:S(2)}) collective-permute-start(bf16[640,1024]{0,1:T(8,128)(2,1)S(1)} %select_convert_fusion), channel_id=1, source_target_pairs={{0,1},{1,0},{2,3},{3,2},{4,5},{5,4},{6,7},{7,6},{8,9},{9,8},{10,11... | collective-permute-start | bytes 3932168 | tf_op jit(solution)/shard_map/ppermute | solution.py:236
  726.9 6.0 collective-permute-start.16
  732.9 4.0 collective-permute-start.17
  733.0 20.7 %collective-permute-start.9 = (f32[1,2,1024]{2,0,1:T(1,128)S(1)}, f32[1,2,1024]{2,0,1:T(1,128)S(1)}, u32[]{:S(2)}, u32[]{:S(2)}) collective-permute-start(f32[1,2,1024]{2,0,1:T(1,128)S(1)} %broadcast_in_dim.27), channel_id=1, source_target_pairs={{0,1},{1,0},{2,3},{3,2},{4,5},{5,4},{6,7},{7,6},{8,9},{9,8},{10,11... | collective-permute-start | bytes 24584 | tf_op jit(solution)/shard_map/ppermute | solution.py:248
  736.9 27.9 %collective-permute-start.18 = (f32[3,2,1024]{2,0,1:T(4,128)S(1)}, f32[3,2,1024]{2,0,1:T(4,128)S(1)}, u32[]{:S(2)}, u32[]{:S(2)}) collective-permute-start(f32[3,2,1024]{2,0,1:T(4,128)S(1)} %add.262), channel_id=1, source_target_pairs={{0,16},{2,18},{4,20},{6,22},{8,24},{10,26},{12,28},{14,30},{16,0},... | collective-permute-start | bytes 73736 | tf_op jit(solution)/shard_map/ppermute | solution.py:248
  753.7 1.3 collective-permute-start.10
  755.0 12.5 %collective-permute-start.11 = (f32[1,2,1024]{2,0,1:T(1,128)S(1)}, f32[1,2,1024]{2,0,1:T(1,128)S(1)}, u32[]{:S(2)}, u32[]{:S(2)}) collective-permute-start(f32[1,2,1024]{2,0,1:T(1,128)S(1)} %add.255), channel_id=1, source_target_pairs={{0,4},{2,6},{4,0},{6,2},{8,12},{10,14},{12,8},{14,10},{16,20},{18,... | collective-permute-start | bytes 24584 | tf_op jit(solution)/shard_map/ppermute | solution.py:248
  767.5 3.7 collective-permute-start.12
  771.2 10.9 %collective-permute-start.13 = (f32[1,2,1024]{2,0,1:T(1,128)S(1)}, f32[1,2,1024]{2,0,1:T(1,128)S(1)}, u32[]{:S(2)}, u32[]{:S(2)}) collective-permute-start(f32[1,2,1024]{2,0,1:T(1,128)S(1)} %add.257), channel_id=1, source_target_pairs={{0,16},{2,18},{4,20},{6,22},{8,24},{10,26},{12,28},{14,30},{16,0},... | collective-permute-start | bytes 24584 | tf_op jit(solution)/shard_map/ppermute | solution.py:248
  (79 other events, 753.3 us)
Sparse Core Ops, SparseCore 0:
  11.4 88.6 all-gather.4
  103.1 58.7 all-gather.6
  164.7 82.0 all-gather.8
  249.5 75.6 all-gather.10
  478.1 138.4 reduce-scatter.6
  622.1 112.3 reduce-scatter.4
  736.8 149.7 reduce-scatter.10
  888.9 147.0 reduce-scatter.8

commit v2 on v1

--- a/solution.py
+++ b/solution.py
@@ -218,6 +218,87 @@
     return jax.nn.gelu(values, approximate=True)
 
 
+def width_orders():
+    count = lax.axis_size("z")
+    z, y, core = (lax.axis_index(name) for name in ("z", "y", "core"))
+    place = jnp.arange(4 * count, dtype=jnp.int32)
+    inward = ((z ^ (place % count)) * 2 + (y ^ (place // count % 2))) * 2
+    inward = inward + (core ^ (place // (2 * count)))
+    outward = ((core ^ (place % 2)) * 2 + (y ^ (place // 2 % 2))) * count
+    outward = outward + (z ^ (place // 4))
+    return inward, outward
+
+
+def arrange_small(values, source):
+    blocks = values.reshape(values.shape[0], 1, source.shape[0], -1)
+    hit = source[:, None] == jnp.arange(source.shape[0], dtype=jnp.int32)
+    return jnp.sum(jnp.where(hit[None, :, :, None], blocks, 0.0), axis=2).reshape(values.shape)
+
+
+def arrange_kernel(source, first_at, second_at, use_second, first_ref, second_ref, out_ref):
+    rows, width = out_ref.shape
+    block = width // source.shape[0]
+    per = 128 // block
+    lane = lax.broadcasted_iota(jnp.int32, (rows, 128), 1)
+
+    def fill(ref):
+        for tile in range(width // 128):
+            made = None
+            for part in range(per):
+                at = source[tile * per + part]
+                start = pl.multiple_of(lax.div(at, per) * 128, 128)
+                values = ref[:, pl.ds(start, 128)].astype(f32)
+                turn = lax.rem(part - lax.rem(at, per) + per, per) * block
+                values = pltpu.roll(values, turn, 1)
+                made = values if part == 0 else jnp.where(lane >= part * block, values, made)
+            out_ref[:, tile * 128 : (tile + 1) * 128] = made.astype(out_ref.dtype)
+
+    second = use_second[pl.program_id(0)]
+
+    @pl.when(second == 0)
+    def _():
+        fill(first_ref)
+
+    @pl.when(second != 0)
+    def _():
+        fill(second_ref)
+
+
+def arrange(first, second, source, plan, rows, out_type):
+    width = first.shape[1]
+    first_at, second_at, use_second = (jnp.stack(list(column)).astype(jnp.int32) for column in zip(*plan))
+    return pl.pallas_call(
+        arrange_kernel,
+        name="arrange",
+        out_shape=jax.ShapeDtypeStruct((len(plan) * rows, width), out_type),
+        grid_spec=pltpu.PrefetchScalarGridSpec(
+            num_scalar_prefetch=4,
+            grid=(len(plan),),
+            in_specs=[
+                pl.BlockSpec((rows, width), lambda i, s, a, b, u: (a[i], 0)),
+                pl.BlockSpec((rows, width), lambda i, s, a, b, u: (b[i], 0)),
+            ],
+            out_specs=pl.BlockSpec((rows, width), lambda i, s, a, b, u: (i, 0)),
+        ),
+        cost_estimate=pl.CostEstimate(
+            flops=len(plan) * rows * width * 8,
+            bytes_accessed=len(plan) * rows * width * 8,
+            transcendentals=0,
+        ),
+    )(source, first_at, second_at, use_second, first, second)
+
+
+def send(values, axes, distance):
+    count = 1
+    for axis in (axes,) if isinstance(axes, str) else axes:
+        count *= lax.axis_size(axis)
+    return lax.ppermute(values, axes, [(s, s ^ distance) for s in range(count)])
+
+
+def after(values, *others):
+    return lax.optimization_barrier((values,) + others)[0]
+
+
 def pick(pieces, position):
     chosen = pieces[0]
     for number in range(1, len(pieces)):
@@ -225,38 +306,68 @@
     return chosen
 
 
-def swap_tp(pieces):
-    count = len(pieces)
+def exchange_tp(pieces):
+    return pieces[:1] + [send(pieces[k], "tp", k) for k in range(1, len(pieces))]
+
+
+def in_place_order(pieces):
     here = lax.axis_index("tp")
-    arrived = [pick(pieces, here)]
-    for step in range(1, count):
-        pairs = [(s, (s + step) % count) for s in range(count)]
-        sent = pick(pieces, (here + step) % count)
-        low = sent.astype(bf16) if sent.dtype == f32 else sent
-        arrived.append(lax.ppermute(low, "tp", pairs).astype(sent.dtype))
-    return [pick(arrived, (here - s) % count) for s in range(count)]
+    return jnp.concatenate([pick(pieces, here ^ s) for s in range(len(pieces))], axis=0)
 
 
 def sum_everywhere(values):
-    for axis in ("tp", "fsdp"):
-        count = lax.axis_size(axis)
-        if count & (count - 1):
-            values = lax.psum(values, axis)
-            continue
-        step = 1
-        while step < count:
-            values = values + lax.ppermute(values, axis, [(s, s ^ step) for s in range(count)])
-            step *= 2
+    for axes in (("y", "tp"), ("z",), ("core",)):
+        count = 1
+        for axis in axes:
+            count *= lax.axis_size(axis)
+        values = sum([send(values, axes, k) for k in range(1, count)], values)
     return values
 
 
-def gather_weight(shard):
-    return lax.all_gather(shard, ("tp", "fsdp"), axis=0, tiled=True)
+def gather_z(shard):
+    count = lax.axis_size("z")
+    return jnp.concatenate([shard] + [send(shard, "z", k) for k in range(1, count)], axis=0)
+
+
+def gather_plane(block):
+    count = lax.axis_size("tp")
+    places = [(k // 2, k % 2) for k in range(1, 2 * count)]
+    return [block] + [send(block, ("y", "tp"), y * count + t) for t, y in places]
+
+
+def gather_core(blocks):
+    other = [send(block, "core", 1) for block in blocks]
+    halves = range(len(blocks) // 2)
+    pair = lambda pieces, t: pieces[2 * t : 2 * t + 2]
+    return [jnp.concatenate(pair(blocks, t) + pair(other, t), axis=0) for t in halves]
+
+
+def scatter_core(part):
+    half = part.shape[0] // 2
+    came = send(part[half:], "core", 1)
+    return (part[:half].astype(f32) + came.astype(f32)).astype(bf16)
+
+
+def scatter_plane(parts):
+    half = parts[0].shape[0] // 2
+    total = parts[0][:half].astype(f32)
+    for k in range(2 * len(parts) - 1, 0, -1):
+        piece = parts[k // 2][k % 2 * half : (k % 2 + 1) * half]
+        total = total + send(piece, ("y", "tp"), k % 2 * len(parts) + k // 2).astype(f32)
+    return total.astype(bf16)
+
+
+def scatter_z(part):
+    count = lax.axis_size("z")
+    rows = part.shape[0] // count
+    total = part[:rows].astype(f32)
+    for k in range(1, count):
+        total = total + send(part[k * rows : (k + 1) * rows], "z", k).astype(f32)
+    return total
 
 
 def scatter_grad(parts):
-    whole = jnp.concatenate([part.astype(bf16) for part in parts], axis=0)
-    return lax.psum_scatter(whole, ("tp", "fsdp"), scatter_dimension=0, tiled=True).astype(f32)
+    return scatter_z(scatter_plane([scatter_core(part.astype(bf16)) for part in parts]))
 
 
 def segment_tables(segments, parents):
@@ -276,38 +387,65 @@
     own_rows = tokens.shape[2]
     width = tokens.shape[3]
     tree_len = own_rows * tp
-    head_width = w_out.shape[0]
     whole = micro // tp
     shared = list(range(whole * tp, micro))
+    share_count = len(shared)
     halves = range(tp)
+    inward, outward = width_orders()
+    split = whole * tree_len
+
+    zero = jnp.int32(0)
+    in_plan = []
+    for n in range(whole):
+        for s in halves:
+            far = here ^ s
+            in_plan.append((n * tp + here, n * (tp - 1) + jnp.maximum(far - 1, 0), far != 0))
+    in_plan += [(zero + m, zero, zero != 0) for m in shared]
+    out_plan = []
+    for n in range(whole):
+        for s in halves:
+            far = here ^ s
+            out_plan.append((n * tp + here, n * (tp - 1) + jnp.maximum(far - 1, 0), far != 0))
+    out_plan += [(zero + m, zero, zero != 0) for m in shared]
 
     def tree_rows(values):
-        rows = []
+        flat = values.reshape(micro * own_rows, width)
+        came = []
         for n in range(whole):
-            rows += swap_tp([values[n * tp + s, 0] for s in halves])
-        return rows, [values[m, 0] for m in shared]
-
-    def rows_back(values):
-        back = [None] * micro
+            for k in range(1, tp):
+                start = (n * tp + (here ^ k)) * own_rows
+                came.append(send(lax.dynamic_slice_in_dim(flat, start, own_rows), "tp", k))
+        came = jnp.concatenate(came, axis=0) if came else flat
+        return arrange(flat, came, inward, in_plan, own_rows, bf16)
+
+    def rows_back(values, out_type):
+        came = []
         for n in range(whole):
-            tree = values[n * tree_len : (n + 1) * tree_len]
-            parts = swap_tp([tree[s * own_rows : (s + 1) * own_rows] for s in halves])
-            for s in halves:
-                back[n * tp + s] = parts[s]
-        for number, m in enumerate(shared):
-            start = whole * tree_len + number * own_rows
-            back[m] = values[start : start + own_rows]
-        return back
-
-    weight = lambda gathered: [gathered[t * width : (t + 1) * width] for t in halves]
-    full_qkv = weight(gather_weight(w_qkv.reshape(w_qkv.shape[0], -1)))
-    full_out = weight(gather_weight(w_out.T))
-    full_up = weight(gather_weight(w_up))
-    full_down = weight(gather_weight(w_down.T))
-
-    seg_all = jnp.concatenate(swap_tp([segments[:, 0]] * tp), axis=1)
-    whole_tokens, share_tokens = tree_rows(tokens)
-    whole_cot, share_cot = tree_rows(cotangent)
+            for k in range(1, tp):
+                start = (n * tp + (here ^ k)) * own_rows
+                piece = lax.dynamic_slice_in_dim(values, start, own_rows).astype(bf16)
+                came.append(send(piece, "tp", k))
+        came = jnp.concatenate(came, axis=0) if came else values
+        back = arrange(values, came, outward, out_plan, own_rows, out_type)
+        return back.reshape(micro, 1, own_rows, width)
+
+    qkv_z = gather_z(w_qkv.reshape(w_qkv.shape[0], -1))
+    qkv_plane = gather_plane(qkv_z)
+    full_qkv = gather_core(qkv_plane)
+    out_z = gather_z(after(w_out.T, qkv_z))
+    up_z = gather_z(after(w_up, qkv_z))
+    out_plane = gather_plane(after(out_z, qkv_plane[1]))
+    up_plane = gather_plane(after(up_z, qkv_plane[1]))
+    down_z = gather_z(after(w_down.T, qkv_plane[1]))
+    full_out = gather_core(out_plane)
+    full_up = gather_core(up_plane)
+    full_down = gather_core(gather_plane(after(down_z, up_plane[1])))
+
+    seg_came = exchange_tp([segments[:, 0]] * tp)
+    seg_all = jnp.concatenate([pick(seg_came, here ^ s) for s in halves], axis=1)
+    gains = arrange_small(norm_gains, inward)
+    biases = arrange_small(norm_biases, inward)
+    x = tree_rows(tokens).astype(f32)
     whole_tables = []
     for n in range(whole):
         seg = pick([seg_all[n * tp + s] for s in halves], here)
@@ -315,17 +453,16 @@
         whole_tables.append(segment_tables(seg, par))
     share_tables = [segment_tables(seg_all[m], parents[m, 0]) for m in shared]
 
-    share_count = len(shared)
-    x = jnp.concatenate(whole_tokens + share_tokens, axis=0).astype(f32)
-    split = whole * tree_len
-
-    normed = norm_forward(x, norm_gains[0], norm_biases[0]).astype(bf16)
+    def share_rows(values, k):
+        return lax.dynamic_slice_in_dim(values, (here ^ k) * own_rows, own_rows)
+
+    normed = norm_forward(x, gains[0], biases[0]).astype(bf16)
     share_qkv = [dot_nn(normed[split:], w).astype(bf16) for w in full_qkv]
     whole_qkv = [dot_nn(normed[:split], w).astype(bf16) for w in full_qkv] if whole else []
     share_calls = []
     for n in range(share_count):
         cut = slice(n * own_rows, (n + 1) * own_rows)
-        share_calls.append(jnp.concatenate(swap_tp([part[cut] for part in share_qkv]), axis=0))
+        share_calls.append(in_place_order(exchange_tp([part[cut] for part in share_qkv])))
     whole_out = [[] for _ in halves]
     saved = {}
     for n in range(whole):
@@ -338,14 +475,14 @@
     for n in range(share_count):
         out, lse = attention_forward(share_calls[n], *share_tables[n])
         saved[n] = (share_calls[n], out, lse)
-        parts = swap_tp([out[s * own_rows : (s + 1) * own_rows] for s in halves])
+        parts = exchange_tp([share_rows(out, k) for k in halves])
         for t in halves:
             share_out[t].append(parts[t])
     attended = [jnp.concatenate(whole_out[t] + share_out[t], axis=0) for t in halves]
     branch_a = sum(dot_nt(attended[t], full_out[t]) for t in halves)
-    residual = x + norm_forward(branch_a, norm_gains[1], norm_biases[1])
-
-    normed_f = norm_forward(residual, norm_gains[2], norm_biases[2]).astype(bf16)
+    residual = x + norm_forward(branch_a, gains[1], biases[1])
+
+    normed_f = norm_forward(residual, gains[2], biases[2]).astype(bf16)
     up_low = []
     hidden = []
     for t in halves:
@@ -353,11 +490,11 @@
         hidden.append(gelu_tanh(up).astype(bf16))
         up_low.append(up.astype(bf16))
     branch_f = sum(dot_nt(hidden[t], full_down[t]) for t in halves)
-    out = (residual + norm_forward(branch_f, norm_gains[3], norm_biases[3])).astype(bf16)
-    out_rows = jnp.stack(rows_back(out))[:, None]
-
-    grad_out = jnp.concatenate(whole_cot + share_cot, axis=0).astype(f32)
-    grad_branch_f, sums_3 = norm_backward(branch_f, norm_gains[3], grad_out)
+    out = (residual + norm_forward(branch_f, gains[3], biases[3])).astype(bf16)
+    out_rows = rows_back(out, bf16)
+
+    grad_out = tree_rows(after(cotangent, full_qkv[0])).astype(f32)
+    grad_branch_f, sums_3 = norm_backward(branch_f, gains[3], grad_out)
     grad_branch_f = grad_branch_f.astype(bf16)
     grad_down = scatter_grad([dot_tn(grad_branch_f, hidden[t]) for t in halves])
     grad_up = []
@@ -366,16 +503,16 @@
         grad_up.append(pull(dot_nn(grad_branch_f, full_down[t]))[0].astype(bf16))
     grad_w_up = scatter_grad([dot_tn(normed_f, grad_up[t]) for t in halves])
     grad_normed_f = sum(dot_nt(grad_up[t], full_up[t]) for t in halves)
-    grad_part, sums_2 = norm_backward(residual, norm_gains[2], grad_normed_f)
+    grad_part, sums_2 = norm_backward(residual, gains[2], grad_normed_f)
     grad_residual = grad_out + grad_part
 
-    grad_branch_a, sums_1 = norm_backward(branch_a, norm_gains[1], grad_residual)
+    grad_branch_a, sums_1 = norm_backward(branch_a, gains[1], grad_residual)
     grad_branch_a = grad_branch_a.astype(bf16)
     share_grad = [dot_nn(grad_branch_a[split:], w).astype(bf16) for w in full_out]
     share_do = []
     for n in range(share_count):
         cut = slice(n * own_rows, (n + 1) * own_rows)
-        share_do.append(jnp.concatenate(swap_tp([part[cut] for part in share_grad]), axis=0))
+        share_do.append(in_place_order(exchange_tp([part[cut] for part in share_grad])))
     grad_w_out = scatter_grad([dot_tn(grad_branch_a, attended[t]) for t in halves])
     whole_grad = [dot_nn(grad_branch_a[:split], w).astype(bf16) for w in full_out] if whole else []
     grad_qkv = [[] for _ in halves]
@@ -383,7 +520,7 @@
     for n in range(share_count):
         qkv, att, lse = saved[n]
         dx = attention_backward(qkv, share_do[n], att, lse, *share_tables[n])
-        parts = swap_tp([dx[s * own_rows : (s + 1) * own_rows] for s in halves])
+        parts = exchange_tp([share_rows(dx, k) for k in halves])
         for t in halves:
             share_parts[t].append(parts[t])
     for n in range(whole):
@@ -394,12 +531,11 @@
     grad_qkv = [jnp.concatenate(grad_qkv[t] + share_parts[t], axis=0) for t in halves]
     grad_w_qkv = scatter_grad([dot_tn(normed, grad_qkv[t]) for t in halves])
     grad_normed = sum(dot_nt(grad_qkv[t], full_qkv[t]) for t in halves)
-    grad_part, sums_0 = norm_backward(x, norm_gains[0], grad_normed)
-    grad_x = grad_residual + grad_part
-    input_rows = jnp.stack(rows_back(grad_x))[:, None]
-    early = sum_everywhere(jnp.stack([sums_1, sums_2, sums_3]))
-    late = sum_everywhere(sums_0[None])
-    sums = jnp.concatenate([late, early], axis=0)
+    grad_part, sums_0 = norm_backward(x, gains[0], grad_normed)
+    input_rows = rows_back(grad_residual + grad_part, f32)
+    early = sum_everywhere(arrange_small(jnp.concatenate([sums_1, sums_2, sums_3]), outward))
+    late = sum_everywhere(arrange_small(sums_0, outward))
+    sums = jnp.concatenate([late, early], axis=0).reshape(4, 2, width)
     return (
         out_rows,
         input_rows,
@@ -413,28 +549,31 @@
 
 
 def solution(mesh):
+    groups, tp = mesh.devices.shape
+    fine = jax.sharding.Mesh(mesh.devices.reshape(groups // 4, 2, 2, tp), ("z", "y", "core", "tp"))
+    fsdp = ("z", "y", "core")
     in_specs = (
-        P(None, "fsdp", "tp", None),
-        P(None, "fsdp", "tp"),
-        P(None, "fsdp", None),
+        P(None, fsdp, "tp", None),
+        P(None, fsdp, "tp"),
+        P(None, fsdp, None),
         P(),
         P(),
-        P("fsdp", None, "tp"),
-        P("tp", "fsdp"),
-        P("fsdp", "tp"),
-        P("tp", "fsdp"),
-        P(None, "fsdp", "tp", None),
+        P(fsdp, None, "tp"),
+        P("tp", fsdp),
+        P(fsdp, "tp"),
+        P("tp", fsdp),
+        P(None, fsdp, "tp", None),
     )
     out_specs = (
-        P(None, "fsdp", "tp", None),
-        P(None, "fsdp", "tp", None),
-        P("fsdp", None, "tp"),
-        P("tp", "fsdp"),
-        P("fsdp", "tp"),
-        P("tp", "fsdp"),
+        P(None, fsdp, "tp", None),
+        P(None, fsdp, "tp", None),
+        P(fsdp, None, "tp"),
+        P("tp", fsdp),
+        P(fsdp, "tp"),
+        P("tp", fsdp),
         P(),
         P(),
     )
     return jax.shard_map(
-        on_device, mesh=mesh, in_specs=in_specs, out_specs=out_specs, check_vma=False
+        on_device, mesh=fine, in_specs=in_specs, out_specs=out_specs, check_vma=False
     )

time: 1050 us -> 976 us (0.930)
  waiting for transfers between devices: 410 us -> 265 us
  starting transfers between devices: 29.9 us -> 91.3 us
  local copies, waits for them, and re-layouts: 52.4 us -> 87.8 us
  Pallas kernels: 145 us -> 178 us
  matrix products: 285 us -> 257 us
  other arithmetic: 106 us -> 88.7 us
  between operations: 16 us -> 2.87 us
    reduce_scatter x4 -> x0, waiting for transfers between devices: 232 us -> none  [scatter_grad(): lax.psum_scatter(whole, ('tp', 'fsdp'), scatter_dimension=0, tiled=True)]
    ppermute x19 -> x95, waiting for transfers between devices: 107 us -> 265 us  [send(): return lax.ppermute(values, axes, [(s, s ^ distance) for s in range(count)])]
    all_gather x4 -> x0, waiting for transfers between devices: 70.6 us -> none  [gather_weight(): return lax.all_gather(shard, ('tp', 'fsdp'), axis=0, tiled=True)]
    ppermute x19 -> x95, starting transfers between devices: 29.2 us -> 91.3 us  [send(): return lax.ppermute(values, axes, [(s, s ^ distance) for s in range(count)])]
    pallas_call x0 -> x4, Pallas kernels: none -> 33.2 us  [arrange(): pl.pallas_call(arrange_kernel, name='arrange', out_shape=jax.ShapeDtypeSt...]
    concatenate x6, other arithmetic: 22.5 us -> 4.48 us  [the longest x3 4.13 us: gather_z(): jnp.concatenate([shard] + [send(shard, 'z', k) for k in range(1, count)],...]
    dot_general x12, matrix products: 106 us -> 89.5 us  [dot_nn(): lax.dot_general(a, b, (((1,), (0,)), ((), ())), preferred_element_type=f32)]
    dot_general x8, matrix products: 105 us -> 90.4 us  [dot_nt(): lax.dot_general(a, b, (((1,), (1,)), ((), ())), preferred_element_type=f32)]
  transfers between devices with their start and end apart: 27 -> 95, of which waited for: 15 -> 26; matrix products, arithmetic and copies ran while one was open for 27% -> 20% of each run, Pallas kernels for 14% -> 18%
where the time goes in v2:
time: 976 us; the launch traced here: 971 us
  waiting for transfers between devices  265 us (27%)
  matrix products  257 us (26%)
  Pallas kernels  178 us (18%)
  starting transfers between devices  91.3 us (9%)
  other arithmetic  88.7 us (9%)
  local copies, waits for them, and re-layouts  87.8 us (9%)
    ppermute x95, waiting for transfers between devices, send(): return lax.ppermute(values, axes, [(s, s ^ distance) for s in range(count)])  265 us
    ppermute x95, starting transfers between devices, send(): return lax.ppermute(values, axes, [(s, s ^ distance) for s in range(count)])  91.3 us
    dot_general x8, matrix products, dot_nt(): lax.dot_general(a, b, (((1,), (1,)), ((), ())), preferred_element_type=f32)  90.4 us
    dot_general x12, matrix products, dot_nn(): lax.dot_general(a, b, (((1,), (0,)), ((), ())), preferred_element_type=f32)  89.5 us
    pallas_call x3, Pallas kernels, attention_backward(): pl.pallas_call(attention_backward_kernel, name='attention_backward', out_...  80.2 us
    dot_general x8, matrix products, dot_tn(): lax.dot_general(a, b, (((0,), (0,)), ((), ())), preferred_element_type=f32)  76.8 us
    pallas_call x3, Pallas kernels, attention_forward(): pl.pallas_call(attention_forward_kernel, name='attention_forward', out_sh...  64.7 us
    unnamed x276, local copies, waits for them, and re-layouts  45.3 us
  transfers between devices with their start and end apart: 95, of which 26 were waited for; matrix products, arithmetic and copies ran while one was open for 20% of the time, Pallas kernels for 18%

profile of v2, /device:TPU:0, one launch (start us, length us, event | category | flops | bytes accessed | tf_op | source)
XLA Modules:
  0.0 970.7 jit_solution(12457628059756424186)
XLA Ops:
  1.7 5.1 collective-permute-start.3
  44.4 12.4 %collective-permute-done.25 = bf16[64,2048]{1,0:T(8,128)(2,1)} collective-permute-done((bf16[64,2048]{1,0:T(8,128)(2,1)S(1)}, bf16[64,2048]{1,0:T(8,128)(2,1)}, u32[]{:S(2)}, u32[]{:S(2)}) %collective-permute-start.25) | collective-permute-done | bytes 262176 | tf_op jit(solution)/shard_map/ppermute | solution.py:295
  67.1 40.3 %collective-permute-done.9 = bf16[256,1536]{1,0:T(8,128)(2,1)S(1)} collective-permute-done((bf16[256,1536]{1,0:T(8,128)(2,1)}, bf16[256,1536]{1,0:T(8,128)(2,1)S(1)}, u32[]{:S(2)}, u32[]{:S(2)}) %collective-permute-start.9) | collective-permute-done | bytes 786464 | tf_op jit(solution)/shard_map/ppermute | solution.py:295
  121.8 10.5 %collective-permute-done.31 = bf16[64,2048]{1,0:T(8,128)(2,1)S(1)} collective-permute-done((bf16[64,2048]{1,0:T(8,128)(2,1)S(1)}, bf16[64,2048]{1,0:T(8,128)(2,1)S(1)}, u32[]{:S(2)}, u32[]{:S(2)}) %collective-permute-start.31) | collective-permute-done | bytes 262176 | tf_op jit(solution)/shard_map/ppermute | solution.py:295
  134.0 7.6 arrange.4
  162.4 4.4 convolution_convert_fusion.1.q_ref.k_ref.v_ref
  167.7 4.4 convolution_convert_fusion.q_ref.k_ref.v_ref
  172.1 21.8 %attention_forward.5 = (bf16[1280,512]{1,0:T(8,128)(2,1)S(1)}, f32[4,8,1280]{2,1,0:T(8,128)S(1)}) custom-call(bf16[1280,1536]{1,0:T(8,128)(2,1)S(1)} %convolution_convert_fusion.q_ref.k_ref.v_ref, bf16[1280,1536]{1,0:T(8,128)(2,1)S(1)} %convolution_convert_fusion.q_ref.k_ref.v_ref, bf16[1280,1536]{1,0:T(8,128)(2,1)S(1)} %convolution_convert_fusion.q_ref.k_ref.v_ref, ...), custom_call_target="tpu_custom_call" | custom-call | flops 8053063680 | bytes 5898240 | tf_op jit(solution)/shard_map/attention_forward/pallas_call | solution.py:77
  193.9 21.5 %attention_forward.3 = (bf16[1280,512]{1,0:T(8,128)(2,1)S(1)}, f32[4,8,1280]{2,1,0:T(8,128)S(1)}) custom-call(bf16[1280,1536]{1,0:T(8,128)(2,1)S(1)} %convolution_convert_fusion.1.q_ref.k_ref.v_ref, bf16[1280,1536]{1,0:T(8,128)(2,1)S(1)} %convolution_convert_fusion.1.q_ref.k_ref.v_ref, bf16[1280,1536]{1,0:T(8,128)(2,1)S(1)} %convolution_convert_fusion.1.q_ref.k_ref.v_ref, ...), custom_call_target="tpu_custom_call" | custom-call | flops 8053063680 | bytes 5898240 | tf_op jit(solution)/shard_map/attention_forward/pallas_call | solution.py:77
  233.0 13.2 %collective-permute-done.41 = bf16[256,2048]{1,0:T(8,128)(2,1)} collective-permute-done((bf16[256,2048]{1,0:T(8,128)(2,1)}, bf16[256,2048]{1,0:T(8,128)(2,1)}, u32[]{:S(2)}, u32[]{:S(2)}) %collective-permute-start.41) | collective-permute-done | bytes 1048608 | tf_op jit(solution)/shard_map/ppermute | solution.py:295
  247.4 7.3 arrange.6
  254.7 14.0 %collective-permute-done.40 = bf16[256,2048]{1,0:T(8,128)(2,1)} collective-permute-done((bf16[256,2048]{1,0:T(8,128)(2,1)}, bf16[256,2048]{1,0:T(8,128)(2,1)}, u32[]{:S(2)}, u32[]{:S(2)}) %collective-permute-start.40) | collective-permute-done | bytes 1048608 | tf_op jit(solution)/shard_map/ppermute | solution.py:295
  280.7 29.2 %collective-permute-done.12 = bf16[640,1536]{1,0:T(8,128)(2,1)} collective-permute-done((bf16[640,1536]{1,0:T(8,128)(2,1)}, bf16[640,1536]{1,0:T(8,128)(2,1)}, u32[]{:S(2)}, u32[]{:S(2)}) %collective-permute-start.12) | collective-permute-done | bytes 1966112 | tf_op jit(solution)/shard_map/ppermute | solution.py:295
  311.9 21.5 %attention_forward.4 = (bf16[1280,512]{1,0:T(8,128)(2,1)S(1)}, f32[4,8,1280]{2,1,0:T(8,128)S(1)}) custom-call(bf16[1280,1536]{1,0:T(8,128)(2,1)S(1)} %pad_maximum_fusion.2.q_ref.k_ref.v_ref, bf16[1280,1536]{1,0:T(8,128)(2,1)S(1)} %pad_maximum_fusion.2.q_ref.k_ref.v_ref, bf16[1280,1536]{1,0:T(8,128)(2,1)S(1)} %pad_maximum_fusion.2.q_ref.k_ref.v_ref, ...), custom_call_target="tpu_custom_call" | custom-call | flops 8053063680 | bytes 5898240 | tf_op jit(solution)/shard_map/attention_forward/pallas_call | solution.py:77
  338.0 11.5 %collective-permute-done.19 = bf16[640,512]{1,0:T(8,128)(2,1)S(1)} collective-permute-done((bf16[640,512]{1,0:T(8,128)(2,1)S(1)}, bf16[640,512]{1,0:T(8,128)(2,1)S(1)}, u32[]{:S(2)}, u32[]{:S(2)}) %collective-permute-start.19) | collective-permute-done | bytes 655392 | tf_op jit(solution)/shard_map/ppermute | solution.py:295
  365.7 11.0 %fusion.115 = f32[1920,2048]{1,0:T(8,128)} fusion(bf16[1920,1024]{1,0:T(8,128)(2,1)S(1)} %add_convert_fusion.1, bf16[1024,2048]{1,0:T(8,128)(2,1)S(1)} %constant_dynamic-update-slice_fusion.33), kind=kOutput, calls=%fused_computation.315 | convolution fusion | flops 8053063680 | bytes 23855104 | tf_op jit(solution)/shard_map/dot_general | solution.py:20
  376.7 13.7 %fusion.114 = f32[1920,2048]{1,0:T(8,128)} fusion(bf16[1920,1024]{1,0:T(8,128)(2,1)S(1)} %add_convert_fusion.1, bf16[1024,2048]{1,0:T(8,128)(2,1)} %constant_dynamic-update-slice_fusion.25), kind=kOutput, calls=%fused_computation.314 | convolution fusion | flops 8053063680 | bytes 23855104 | tf_op jit(solution)/shard_map/dot_general | solution.py:20
  390.4 14.9 %fusion.95 = f32[1920,1024]{1,0:T(8,128)} fusion(bf16[1024,2048]{1,0:T(8,128)(2,1)S(1)} %copy-done.67, f32[1920,2048]{1,0:T(8,128)} %fusion.115), kind=kOutput, calls=%fused_computation.296 | convolution fusion | flops 8088453120 | bytes 27787264 | tf_op jit(solution)/shard_map/dot_general | solution.py:24
  405.3 18.2 %fusion.112 = (f32[1920]{0:T(1024)S(1)}, f32[1920,1024]{1,0:T(8,128)}) fusion(f32[1920,1024]{1,0:T(8,128)} %fusion.95, bf16[1024,2048]{1,0:T(8,128)(2,1)} %constant_dynamic-update-slice_fusion.29, f32[1920,2048]{1,0:T(8,128)} %fusion.114), kind=kOutput, calls=%fused_computation.312 | convolution fusion | flops 8092383232 | bytes 35659264 | tf_op jit(solution)/shard_map/dot_general | solution.py:24
  429.0 6.6 fusion.55
  435.6 4.7 fusion.53
  440.4 20.8 %fusion.7 = bf16[1920,2048]{1,0:T(8,128)(2,1)} fusion(f32[1920,2048]{1,0:T(8,128)} %fusion.114, bf16[1920,1024]{1,0:T(8,128)(2,1)S(1)} %get-tuple-element.83, bf16[1024,2048]{1,0:T(8,128)(2,1)S(1)} %copy-done.61), kind=kOutput, calls=%fused_computation.17 | convolution fusion | flops 8139571200 | bytes 31719424 | tf_op jit(solution)/shard_map/dot_general | solution.py:20
  461.2 14.8 %convolution_convert_fusion.3 = bf16[1024,2048]{1,0:T(8,128)(2,1)} fusion(bf16[1920,1024]{1,0:T(8,128)(2,1)S(1)} %get-tuple-element.83, f32[1920,2048]{1,0:T(8,128)} %fusion.114), kind=kOutput, calls=%fused_computation.106 | convolution fusion | flops 8090550272 | bytes 23855104 | tf_op jit(solution)/shard_map/dot_general | solution.py:28
  476.1 20.8 %fusion.4 = bf16[1920,2048]{1,0:T(8,128)(2,1)} fusion(f32[1920,2048]{1,0:T(8,128)} %fusion.115, bf16[1920,1024]{1,0:T(8,128)(2,1)S(1)} %get-tuple-element.83, bf16[1024,2048]{1,0:T(8,128)(2,1)S(1)} %copy-done.68), kind=kOutput, calls=%fused_computation.14 | convolution fusion | flops 8139571200 | bytes 31719424 | tf_op jit(solution)/shard_map/dot_general | solution.py:20
  496.9 14.9 %convolution_convert_fusion.2 = bf16[1024,2048]{1,0:T(8,128)(2,1)} fusion(bf16[1920,1024]{1,0:T(8,128)(2,1)S(1)} %get-tuple-element.83, f32[1920,2048]{1,0:T(8,128)} %fusion.115), kind=kOutput, calls=%fused_computation.105 | convolution fusion | flops 8090550272 | bytes 23855104 | tf_op jit(solution)/shard_map/dot_general | solution.py:28
  511.8 10.6 %fusion.116 = f32[1920,1024]{1,0:T(8,128)} fusion(bf16[1920,2048]{1,0:T(8,128)(2,1)S(1)} %copy-done.115, bf16[1024,2048]{1,0:T(8,128)(2,1)S(1)} %copy-done.65), kind=kOutput, calls=%fused_computation.316 | convolution fusion | flops 8053063680 | bytes 19922944 | tf_op jit(solution)/shard_map/dot_general | solution.py:24
  522.4 11.1 %convolution_convert_fusion.4 = bf16[1024,2048]{1,0:T(8,128)(2,1)} fusion(bf16[1920,1024]{1,0:T(8,128)(2,1)S(1)} %copy-done.40, bf16[1920,2048]{1,0:T(8,128)(2,1)S(1)} %copy-done.115), kind=kOutput, calls=%fused_computation.107 | convolution fusion | flops 8055160832 | bytes 15990784 | tf_op jit(solution)/shard_map/dot_general | solution.py:28
  533.6 14.1 %convolution_convert_fusion.5 = bf16[1024,2048]{1,0:T(8,128)(2,1)} fusion(bf16[1920,1024]{1,0:T(8,128)(2,1)} %copy-done.39, bf16[1920,2048]{1,0:T(8,128)(2,1)} %fusion.7), kind=kOutput, calls=%fused_computation.108 | convolution fusion | flops 8055160832 | bytes 15990784 | tf_op jit(solution)/shard_map/dot_general | solution.py:28
  547.8 17.7 %multiply_reduce_fusion = (f32[1024]{0:T(1024)S(1)}, f32[1920]{0:T(1024)S(1)}, f32[1920]{0:T(1024)S(1)}, f32[1024]{0:T(1024)S(1)}, f32[1920,1024]{1,0:T(8,128)}) fusion(f32[1920,1024]{1,0:T(8,128)} %copy-done.15, f32[1920]{0:T(1024)S(1)} %copy-done.86, f32[1920]{0:T(1024)S(1)} %copy-done.82, f32[1024]{0:T(1024)S(1)} %copy-done.100, ...), kind=kOutput, calls=%fused_computation.73 | convolution fusion | flops 8072718336 | bytes 35694592 | tf_op jit(solution)/shard_map/dot_general | solution.py:24
  565.6 15.1 %multiply_reduce_fusion.1 = (f32[1024]{0:T(1024)S(1)}, f32[1920]{0:T(1024)S(1)}, f32[1920]{0:T(1024)S(1)}, f32[1024]{0:T(1024)S(1)}, f32[1920,1024]{1,0:T(8,128)}) fusion(f32[1920,1024]{1,0:T(8,128)} %copy-done.14, f32[1920]{0:T(1024)S(1)} %copy-done.80, f32[1920]{0:T(1024)S(1)} %copy-done.72, f32[1024]{0:T(1024)S(1)} %copy-done.95, ...), kind=kLoop, calls=%fused_computation.74 | loop fusion | flops 35383552 | bytes 35467264 | tf_op jit(solution)/shard_map/reduce_sum | solution.py:214
  584.8 7.0 multiply_convert_fusion
  603.3 26.7 %attention_backward.3 = bf16[1280,1536]{1,0:T(8,128)(2,1)S(1)} custom-call(bf16[1280,1536]{1,0:T(8,128)(2,1)S(1)} %copy-done.7, bf16[1280,1536]{1,0:T(8,128)(2,1)S(1)} %copy-done.7, bf16[1280,1536]{1,0:T(8,128)(2,1)S(1)} %copy-done.7, bf16[1280,512]{1,0:T(8,128)(2,1)S(1)} %convolution_convert_fusion.9.do_ref, bf16[1280,512]{1,0:T(8,128)(2,1)S(1)} %get-tuple-element.21.o_ref, ...), custom_call_target="tpu_custom_call" | custom-call | flops 20132659200 | bytes 11796480 | tf_op jit(solution)/shard_map/attention_backward/pallas_call | solution.py:168
  630.0 26.9 %attention_backward.5 = bf16[1280,1536]{1,0:T(8,128)(2,1)S(1)} custom-call(bf16[1280,1536]{1,0:T(8,128)(2,1)S(1)} %copy-done.9, bf16[1280,1536]{1,0:T(8,128)(2,1)S(1)} %copy-done.9, bf16[1280,1536]{1,0:T(8,128)(2,1)S(1)} %copy-done.9, bf16[1280,512]{1,0:T(8,128)(2,1)S(1)} %convolution_convert_fusion.8.do_ref, bf16[1280,512]{1,0:T(8,128)(2,1)S(1)} %copy-done.3, ...), custom_call_target="tpu_custom_call" | custom-call | flops 20132659200 | bytes 11796480 | tf_op jit(solution)/shard_map/attention_backward/pallas_call | solution.py:168
  676.4 14.1 %collective-permute-done.46 = bf16[640,512]{1,0:T(8,128)(2,1)S(1)} collective-permute-done((bf16[640,512]{1,0:T(8,128)(2,1)S(1)}, bf16[640,512]{1,0:T(8,128)(2,1)S(1)}, u32[]{:S(2)}, u32[]{:S(2)}) %collective-permute-start.46) | collective-permute-done | bytes 655392 | tf_op jit(solution)/shard_map/ppermute | solution.py:295
  691.1 26.6 %attention_backward.4 = bf16[1280,1536]{1,0:T(8,128)(2,1)S(1)} custom-call(bf16[1280,1536]{1,0:T(8,128)(2,1)S(1)} %copy-done.1, bf16[1280,1536]{1,0:T(8,128)(2,1)S(1)} %copy-done.1, bf16[1280,1536]{1,0:T(8,128)(2,1)S(1)} %copy-done.1, bf16[1280,512]{1,0:T(8,128)(2,1)S(1)} %pad_maximum_fusion.12.do_ref, bf16[1280,512]{1,0:T(8,128)(2,1)S(1)} %copy-done.5, ...), custom_call_target="tpu_custom_call" | custom-call | flops 20132659200 | bytes 11796480 | tf_op jit(solution)/shard_map/attention_backward/pallas_call | solution.py:168
  726.5 7.1 fusion.59
  736.7 7.5 arrange.5
  765.6 16.0 %collective-permute-done.47 = bf16[640,1536]{1,0:T(8,128)(2,1)} collective-permute-done((bf16[640,1536]{1,0:T(8,128)(2,1)}, bf16[640,1536]{1,0:T(8,128)(2,1)}, u32[]{:S(2)}, u32[]{:S(2)}) %collective-permute-start.47) | collective-permute-done | bytes 1966112 | tf_op jit(solution)/shard_map/ppermute | solution.py:295
  781.6 8.8 fusion.57
  790.4 15.4 %fusion.49 = (f32[1024]{0:T(1024)}, f32[1920]{0:T(1024)}, f32[1920]{0:T(1024)S(1)}, f32[1024]{0:T(1024)S(1)}, f32[1920,1024]{1,0:T(8,128)}) fusion(bf16[1920,1024]{1,0:T(8,128)(2,1)S(1)} %copy-done.18, f32[1920]{0:T(1024)S(1)} %copy-done.84, f32[1920]{0:T(1024)S(1)} %copy-done.78, f32[1024]{0:T(1024)S(1)} %copy-done.97, f32[1920,1024]{1,0:T(8,128)} %fusion.57, ...), kind=kOutput, calls=%fused_computation.66 | convolution fusion | flops 6073214976 | bytes 28747776 | tf_op jit(solution)/shard_map/dot_general | solution.py:24
  810.4 10.1 %fusion.60 = bf16[1024,1536]{1,0:T(8,128)(2,1)S(1)} fusion(bf16[1920,1024]{1,0:T(8,128)(2,1)} %copy-done.35, bf16[640,1536]{1,0:T(8,128)(2,1)} %collective-permute-done.47, bf16[1280,1536]{1,0:T(8,128)(2,1)} %copy-done.10), kind=kOutput, calls=%fused_computation.104 | convolution fusion | flops 6053167104 | bytes 12976128 | tf_op jit(solution)/shard_map/dot_general | solution.py:28
  827.3 7.5 fusion.48.first_ref
  850.0 33.7 %collective-permute-done.69 = bf16[256,2048]{1,0:T(8,128)(2,1)} collective-permute-done((bf16[256,2048]{1,0:T(8,128)(2,1)}, bf16[256,2048]{1,0:T(8,128)(2,1)}, u32[]{:S(2)}, u32[]{:S(2)}) %collective-permute-start.69) | collective-permute-done | bytes 1048608 | tf_op jit(solution)/shard_map/ppermute | solution.py:295
  898.3 7.2 collective-permute-done.79
  906.5 6.0 collective-permute-done.53
  916.4 15.3 %collective-permute-done.52 = bf16[256,1536]{1,0:T(8,128)(2,1)S(1)} collective-permute-done((bf16[256,1536]{1,0:T(8,128)(2,1)S(1)}, bf16[256,1536]{1,0:T(8,128)(2,1)S(1)}, u32[]{:S(2)}, u32[]{:S(2)}) %collective-permute-start.52) | collective-permute-done | bytes 786464 | tf_op jit(solution)/shard_map/ppermute | solution.py:295
  937.3 19.4 %collective-permute-done.48.second_ref = bf16[640,1024]{1,0:T(8,128)(2,1)S(1)} collective-permute-done((bf16[640,1024]{1,0:T(8,128)(2,1)S(1)}, bf16[640,1024]{1,0:T(8,128)(2,1)S(1)}, u32[]{:S(2)}, u32[]{:S(2)}) %collective-permute-start.48) | collective-permute-done | bytes 1310752 | tf_op jit(solution)/shard_map/ppermute | solution.py:295
  957.8 10.8 %arrange.7 = f32[1920,1024]{1,0:T(8,128)} custom-call(s32[16]{0:T(128)} %copy-done.112, s32[3]{0:T(128)} %get-tuple-element.147.first_at, s32[3]{0:T(128)} %get-tuple-element.148.second_at, s32[3]{0:T(128)} %add_convert_fusion.14.use_second, f32[1920,1024]{1,0:T(8,128)} %copy-done.22, bf16[640,1024]{1,0:T(8,128)(2,1)} %copy-done.51), custom_call_target="tpu_custom_call" | custom-call | flops 15728640 | bytes 15728640 | tf_op jit(solution)/shard_map/arrange/pallas_call | solution.py:270
  (603 shorter events, 268.0 us)
Async XLA Ops:
  29.3 31.5 %collective-permute-start.4 = (bf16[256,1536]{1,0:T(8,128)(2,1)}, bf16[256,1536]{1,0:T(8,128)(2,1)S(1)}, u32[]{:S(2)}, u32[]{:S(2)}) collective-permute-start(bf16[256,1536]{1,0:T(8,128)(2,1)} %get-tuple-element.114), channel_id=1, source_target_pairs={{0,4},{1,5},{4,0},{5,1},{2,6},{3,7},{6,2},{7,3},{8,12},{9,13},{12,... | collective-permute-start | bytes 2359304 | tf_op jit(solution)/shard_map/ppermute | solution.py:295
  39.6 25.5 %collective-permute-start.8 = (bf16[256,1536]{1,0:T(8,128)(2,1)}, bf16[256,1536]{1,0:T(8,128)(2,1)S(1)}, u32[]{:S(2)}, u32[]{:S(2)}) collective-permute-start(bf16[256,1536]{1,0:T(8,128)(2,1)} %get-tuple-element.114), channel_id=1, source_target_pairs={{0,1},{1,0},{4,5},{5,4},{2,3},{3,2},{6,7},{7,6},{8,9},{9,8},{12,13... | collective-permute-start | bytes 2359304 | tf_op jit(solution)/shard_map/ppermute | solution.py:295
  43.8 90.1 %collective-permute-start = (bf16[640,1024]{1,0:T(8,128)(2,1)}, bf16[640,1024]{1,0:T(8,128)(2,1)}, u32[]{:S(2)}, u32[]{:S(2)}) collective-permute-start(bf16[640,1024]{1,0:T(8,128)(2,1)} %constant_dynamic-slice_fusion.6), channel_id=1, source_target_pairs={{0,1},{1,0},{2,3},{3,2},{4,5},{5,4},{6,7},{7,6},{8,9},{9,8},{10,11... | collective-permute-start | bytes 3932168 | tf_op jit(solution)/shard_map/ppermute | solution.py:295
  56.7 50.6 %collective-permute-start.9 = (bf16[256,1536]{1,0:T(8,128)(2,1)}, bf16[256,1536]{1,0:T(8,128)(2,1)S(1)}, u32[]{:S(2)}, u32[]{:S(2)}) collective-permute-start(bf16[256,1536]{1,0:T(8,128)(2,1)} %get-tuple-element.114), channel_id=1, source_target_pairs={{0,5},{1,4},{4,1},{5,0},{2,7},{3,6},{6,3},{7,2},{8,13},{9,12},{12,... | collective-permute-start | bytes 2359304 | tf_op jit(solution)/shard_map/ppermute | solution.py:295
  60.8 53.4 %collective-permute-start.21 = (bf16[256,512]{1,0:T(8,128)(2,1)S(1)}, bf16[256,512]{1,0:T(8,128)(2,1)S(1)}, u32[]{:S(2)}, u32[]{:S(2)}) collective-permute-start(bf16[256,512]{1,0:T(8,128)(2,1)S(1)} %pad_maximum_fusion.17), channel_id=1, source_target_pairs={{0,5},{1,4},{4,1},{5,0},{2,7},{3,6},{6,3},{7,2},{8,13},{9,12},{12,... | collective-permute-start | bytes 786440 | tf_op jit(solution)/shard_map/ppermute | solution.py:295
  65.1 45.4 %collective-permute-start.20 = (bf16[256,512]{1,0:T(8,128)(2,1)S(1)}, bf16[256,512]{1,0:T(8,128)(2,1)}, u32[]{:S(2)}, u32[]{:S(2)}) collective-permute-start(bf16[256,512]{1,0:T(8,128)(2,1)S(1)} %pad_maximum_fusion.17), channel_id=1, source_target_pairs={{0,1},{1,0},{4,5},{5,4},{2,3},{3,2},{6,7},{7,6},{8,9},{9,8},{12,13... | collective-permute-start | bytes 786440 | tf_op jit(solution)/shard_map/ppermute | solution.py:295
  66.1 52.4 %collective-permute-start.17 = (bf16[256,512]{1,0:T(8,128)(2,1)S(1)}, bf16[256,512]{1,0:T(8,128)(2,1)S(1)}, u32[]{:S(2)}, u32[]{:S(2)}) collective-permute-start(bf16[256,512]{1,0:T(8,128)(2,1)S(1)} %pad_maximum_fusion.17), channel_id=1, source_target_pairs={{0,2},{2,0},{1,3},{3,1},{4,6},{6,4},{5,7},{7,5},{8,10},{10,8},{9,1... | collective-permute-start | bytes 786440 | tf_op jit(solution)/shard_map/ppermute | solution.py:295
  118.5 103.5 %collective-permute-start.37 = (bf16[256,2048]{1,0:T(8,128)(2,1)}, bf16[256,2048]{1,0:T(8,128)(2,1)}, u32[]{:S(2)}, u32[]{:S(2)}) collective-permute-start(bf16[256,2048]{1,0:T(8,128)(2,1)} %pad_maximum_fusion.15), channel_id=1, source_target_pairs={{0,5},{1,4},{4,1},{5,0},{2,7},{3,6},{6,3},{7,2},{8,13},{9,12},{12,... | collective-permute-start | bytes 3145736 | tf_op jit(solution)/shard_map/ppermute | solution.py:295
  121.7 32.8 %collective-permute-start.6 = (bf16[256,1536]{1,0:T(8,128)(2,1)S(1)}, bf16[256,1536]{1,0:T(8,128)(2,1)}, u32[]{:S(2)}, u32[]{:S(2)}) collective-permute-start(bf16[256,1536]{1,0:T(8,128)(2,1)S(1)} %collective-permute-done.4), channel_id=1, source_target_pairs={{0,2},{2,0},{1,3},{3,1},{4,6},{6,4},{5,7},{7,5},{8,10},{10,8},{9,1... | collective-permute-start | bytes 2359304 | tf_op jit(solution)/shard_map/ppermute | solution.py:295
  147.9 77.5 %collective-permute-start.36 = (bf16[256,2048]{1,0:T(8,128)(2,1)}, bf16[256,2048]{1,0:T(8,128)(2,1)}, u32[]{:S(2)}, u32[]{:S(2)}) collective-permute-start(bf16[256,2048]{1,0:T(8,128)(2,1)} %pad_maximum_fusion.15), channel_id=1, source_target_pairs={{0,1},{1,0},{4,5},{5,4},{2,3},{3,2},{6,7},{7,6},{8,9},{9,8},{12,13... | collective-permute-start | bytes 3145736 | tf_op jit(solution)/shard_map/ppermute | solution.py:295
  150.8 77.6 %collective-permute-start.28 = (bf16[256,2048]{1,0:T(8,128)(2,1)}, bf16[256,2048]{1,0:T(8,128)(2,1)S(1)}, u32[]{:S(2)}, u32[]{:S(2)}) collective-permute-start(bf16[256,2048]{1,0:T(8,128)(2,1)} %pad_maximum_fusion.15), channel_id=1, source_target_pairs={{0,2},{2,0},{1,3},{3,1},{4,6},{6,4},{5,7},{7,5},{8,10},{10,8},{9,1... | collective-permute-start | bytes 3145736 | tf_op jit(solution)/shard_map/ppermute | solution.py:295
  152.7 66.3 %collective-permute-start.27 = (bf16[256,2048]{1,0:T(8,128)(2,1)}, bf16[256,2048]{1,0:T(8,128)(2,1)S(1)}, u32[]{:S(2)}, u32[]{:S(2)}) collective-permute-start(bf16[256,2048]{1,0:T(8,128)(2,1)} %pad_maximum_fusion.15), channel_id=1, source_target_pairs={{0,4},{1,5},{4,0},{5,1},{2,6},{3,7},{6,2},{7,3},{8,12},{9,13},{12,... | collective-permute-start | bytes 3145736 | tf_op jit(solution)/shard_map/ppermute | solution.py:295
  166.8 63.0 %collective-permute-start.45 = (bf16[640,1024]{1,0:T(8,128)(2,1)S(1)}, bf16[640,1024]{1,0:T(8,128)(2,1)}, u32[]{:S(2)}, u32[]{:S(2)}) collective-permute-start(bf16[640,1024]{1,0:T(8,128)(2,1)S(1)} %constant_dynamic-slice_fusion.2), channel_id=1, source_target_pairs={{0,1},{1,0},{2,3},{3,2},{4,5},{5,4},{6,7},{7,6},{8,9},{9,8},{10,11... | collective-permute-start | bytes 3932168 | tf_op jit(solution)/shard_map/ppermute | solution.py:295
  219.0 27.3 %collective-permute-start.41 = (bf16[256,2048]{1,0:T(8,128)(2,1)}, bf16[256,2048]{1,0:T(8,128)(2,1)}, u32[]{:S(2)}, u32[]{:S(2)}) collective-permute-start(bf16[256,2048]{1,0:T(8,128)(2,1)} %pad_maximum_fusion.16), channel_id=1, source_target_pairs={{0,5},{1,4},{4,1},{5,0},{2,7},{3,6},{6,3},{7,2},{8,13},{9,12},{12,... | collective-permute-start | bytes 3145736 | tf_op jit(solution)/shard_map/ppermute | solution.py:295
  222.0 46.7 %collective-permute-start.40 = (bf16[256,2048]{1,0:T(8,128)(2,1)}, bf16[256,2048]{1,0:T(8,128)(2,1)}, u32[]{:S(2)}, u32[]{:S(2)}) collective-permute-start(bf16[256,2048]{1,0:T(8,128)(2,1)} %pad_maximum_fusion.16), channel_id=1, source_target_pairs={{0,1},{1,0},{4,5},{5,4},{2,3},{3,2},{6,7},{7,6},{8,9},{9,8},{12,13... | collective-permute-start | bytes 3145736 | tf_op jit(solution)/shard_map/ppermute | solution.py:295
  225.4 44.6 %collective-permute-start.33 = (bf16[256,2048]{1,0:T(8,128)(2,1)}, bf16[256,2048]{1,0:T(8,128)(2,1)}, u32[]{:S(2)}, u32[]{:S(2)}) collective-permute-start(bf16[256,2048]{1,0:T(8,128)(2,1)} %pad_maximum_fusion.16), channel_id=1, source_target_pairs={{0,4},{1,5},{4,0},{5,1},{2,6},{3,7},{6,2},{7,3},{8,12},{9,13},{12,... | collective-permute-start | bytes 3145736 | tf_op jit(solution)/shard_map/ppermute | solution.py:295
  228.4 46.6 %collective-permute-start.34 = (bf16[256,2048]{1,0:T(8,128)(2,1)}, bf16[256,2048]{1,0:T(8,128)(2,1)}, u32[]{:S(2)}, u32[]{:S(2)}) collective-permute-start(bf16[256,2048]{1,0:T(8,128)(2,1)} %pad_maximum_fusion.16), channel_id=1, source_target_pairs={{0,2},{2,0},{1,3},{3,1},{4,6},{6,4},{5,7},{7,5},{8,10},{10,8},{9,1... | collective-permute-start | bytes 3145736 | tf_op jit(solution)/shard_map/ppermute | solution.py:295
  231.8 78.1 %collective-permute-start.12 = (bf16[640,1536]{1,0:T(8,128)(2,1)}, bf16[640,1536]{1,0:T(8,128)(2,1)}, u32[]{:S(2)}, u32[]{:S(2)}) collective-permute-start(bf16[640,1536]{1,0:T(8,128)(2,1)} %convolution_convert_fusion.7), channel_id=1, source_target_pairs={{0,1},{1,0},{2,3},{3,2},{4,5},{5,4},{6,7},{7,6},{8,9},{9,8},{10,11... | collective-permute-start | bytes 5898248 | tf_op jit(solution)/shard_map/ppermute | solution.py:295
  246.2 31.2 %collective-permute-start.38 = (bf16[256,2048]{1,0:T(8,128)(2,1)}, bf16[256,2048]{1,0:T(8,128)(2,1)}, u32[]{:S(2)}, u32[]{:S(2)}) collective-permute-start(bf16[256,2048]{1,0:T(8,128)(2,1)} %collective-permute-done.36), channel_id=1, source_target_pairs={{0,2},{2,0},{1,3},{3,1},{4,6},{6,4},{5,7},{7,5},{8,10},{10,8},{9,1... | collective-permute-start | bytes 3145736 | tf_op jit(solution)/shard_map/ppermute | solution.py:295
  275.0 60.8 %collective-permute-start.43 = (bf16[256,2048]{1,0:T(8,128)(2,1)}, bf16[256,2048]{1,0:T(8,128)(2,1)S(1)}, u32[]{:S(2)}, u32[]{:S(2)}) collective-permute-start(bf16[256,2048]{1,0:T(8,128)(2,1)} %collective-permute-done.41), channel_id=1, source_target_pairs={{0,2},{2,0},{1,3},{3,1},{4,6},{6,4},{5,7},{7,5},{8,10},{10,8},{9,1... | collective-permute-start | bytes 3145736 | tf_op jit(solution)/shard_map/ppermute | solution.py:295
  277.4 57.2 %collective-permute-start.42 = (bf16[256,2048]{1,0:T(8,128)(2,1)}, bf16[256,2048]{1,0:T(8,128)(2,1)S(1)}, u32[]{:S(2)}, u32[]{:S(2)}) collective-permute-start(bf16[256,2048]{1,0:T(8,128)(2,1)} %collective-permute-done.40), channel_id=1, source_target_pairs={{0,2},{2,0},{1,3},{3,1},{4,6},{6,4},{5,7},{7,5},{8,10},{10,8},{9,1... | collective-permute-start | bytes 3145736 | tf_op jit(solution)/shard_map/ppermute | solution.py:295
  279.2 57.6 %collective-permute-start.35 = (bf16[256,2048]{1,0:T(8,128)(2,1)}, bf16[256,2048]{1,0:T(8,128)(2,1)S(1)}, u32[]{:S(2)}, u32[]{:S(2)}) collective-permute-start(bf16[256,2048]{1,0:T(8,128)(2,1)} %collective-permute-done.33), channel_id=1, source_target_pairs={{0,2},{2,0},{1,3},{3,1},{4,6},{6,4},{5,7},{7,5},{8,10},{10,8},{9,1... | collective-permute-start | bytes 3145736 | tf_op jit(solution)/shard_map/ppermute | solution.py:295
  581.3 75.6 %collective-permute-start.90 = (f32[6,1024]{1,0:T(8,128)S(1)}, f32[6,1024]{1,0:T(8,128)S(1)}, u32[]{:S(2)}, u32[]{:S(2)}) collective-permute-start(f32[6,1024]{1,0:T(8,128)S(1)} %reshape.312), channel_id=1, source_target_pairs={{0,5},{1,4},{4,1},{5,0},{2,7},{3,6},{6,3},{7,2},{8,13},{9,12},{12,... | collective-permute-start | bytes 73736 | tf_op jit(solution)/shard_map/ppermute | solution.py:295
  582.6 74.4 %collective-permute-start.89 = (f32[6,1024]{1,0:T(8,128)S(1)}, f32[6,1024]{1,0:T(8,128)S(1)}, u32[]{:S(2)}, u32[]{:S(2)}) collective-permute-start(f32[6,1024]{1,0:T(8,128)S(1)} %reshape.312), channel_id=1, source_target_pairs={{0,4},{1,5},{4,0},{5,1},{2,6},{3,7},{6,2},{7,3},{8,12},{9,13},{12,... | collective-permute-start | bytes 73736 | tf_op jit(solution)/shard_map/ppermute | solution.py:295
  583.7 73.2 %collective-permute-start.88 = (f32[6,1024]{1,0:T(8,128)S(1)}, f32[6,1024]{1,0:T(8,128)S(1)}, u32[]{:S(2)}, u32[]{:S(2)}) collective-permute-start(f32[6,1024]{1,0:T(8,128)S(1)} %reshape.312), channel_id=1, source_target_pairs={{0,1},{1,0},{4,5},{5,4},{2,3},{3,2},{6,7},{7,6},{8,9},{9,8},{12,13... | collective-permute-start | bytes 73736 | tf_op jit(solution)/shard_map/ppermute | solution.py:295
  600.6 135.0 %collective-permute-start.44 = (bf16[640,1024]{1,0:T(8,128)(2,1)S(1)}, bf16[640,1024]{1,0:T(8,128)(2,1)}, u32[]{:S(2)}, u32[]{:S(2)}) collective-permute-start(bf16[640,1024]{1,0:T(8,128)(2,1)S(1)} %constant_dynamic-slice_fusion.3), channel_id=1, source_target_pairs={{0,1},{1,0},{2,3},{3,2},{4,5},{5,4},{6,7},{7,6},{8,9},{9,8},{10,11... | collective-permute-start | bytes 3932168 | tf_op jit(solution)/shard_map/ppermute | solution.py:295
  603.2 141.0 %collective-permute-start.73 = (bf16[512,2048]{1,0:T(8,128)(2,1)}, bf16[512,2048]{1,0:T(8,128)(2,1)}, u32[]{:S(2)}, u32[]{:S(2)}) collective-permute-start(bf16[512,2048]{1,0:T(8,128)(2,1)} %slice.337), channel_id=1, source_target_pairs={{0,2},{2,0},{1,3},{3,1},{4,6},{6,4},{5,7},{7,5},{8,10},{10,8},{9,1... | collective-permute-start | bytes 6291464 | tf_op jit(solution)/shard_map/ppermute | solution.py:295
  674.3 43.3 %collective-permute-start.59 = (bf16[256,512]{1,0:T(8,128)(2,1)S(1)}, bf16[256,512]{1,0:T(8,128)(2,1)S(1)}, u32[]{:S(2)}, u32[]{:S(2)}) collective-permute-start(bf16[256,512]{1,0:T(8,128)(2,1)S(1)} %get-tuple-element.108), channel_id=1, source_target_pairs={{0,5},{1,4},{4,1},{5,0},{2,7},{3,6},{6,3},{7,2},{8,13},{9,12},{12,... | collective-permute-start | bytes 786440 | tf_op jit(solution)/shard_map/ppermute | solution.py:295
  675.0 42.8 %collective-permute-start.60 = (bf16[256,512]{1,0:T(8,128)(2,1)S(1)}, bf16[256,512]{1,0:T(8,128)(2,1)S(1)}, u32[]{:S(2)}, u32[]{:S(2)}) collective-permute-start(bf16[256,512]{1,0:T(8,128)(2,1)S(1)} %get-tuple-element.109), channel_id=1, source_target_pairs={{0,1},{1,0},{4,5},{5,4},{2,3},{3,2},{6,7},{7,6},{8,9},{9,8},{12,13... | collective-permute-start | bytes 786440 | tf_op jit(solution)/shard_map/ppermute | solution.py:295
  690.5 27.2 %collective-permute-start.61 = (bf16[256,512]{1,0:T(8,128)(2,1)S(1)}, bf16[256,512]{1,0:T(8,128)(2,1)S(1)}, u32[]{:S(2)}, u32[]{:S(2)}) collective-permute-start(bf16[256,512]{1,0:T(8,128)(2,1)S(1)} %slice.319), channel_id=1, source_target_pairs={{0,4},{1,5},{4,0},{5,1},{2,6},{3,7},{6,2},{7,3},{8,12},{9,13},{12,... | collective-permute-start | bytes 786440 | tf_op jit(solution)/shard_map/ppermute | solution.py:295
  717.7 31.1 %collective-permute-start.74 = (bf16[512,2048]{1,0:T(8,128)(2,1)}, bf16[512,2048]{1,0:T(8,128)(2,1)}, u32[]{:S(2)}, u32[]{:S(2)}) collective-permute-start(bf16[512,2048]{1,0:T(8,128)(2,1)} %slice.340), channel_id=1, source_target_pairs={{0,2},{2,0},{1,3},{3,1},{4,6},{6,4},{5,7},{7,5},{8,10},{10,8},{9,1... | collective-permute-start | bytes 6291464 | tf_op jit(solution)/shard_map/ppermute | solution.py:295
  722.5 32.2 %collective-permute-start.65 = (bf16[512,2048]{1,0:T(8,128)(2,1)}, bf16[512,2048]{1,0:T(8,128)(2,1)}, u32[]{:S(2)}, u32[]{:S(2)}) collective-permute-start(bf16[512,2048]{1,0:T(8,128)(2,1)} %slice.325), channel_id=1, source_target_pairs={{0,2},{2,0},{1,3},{3,1},{4,6},{6,4},{5,7},{7,5},{8,10},{10,8},{9,1... | collective-permute-start | bytes 6291464 | tf_op jit(solution)/shard_map/ppermute | solution.py:295
  734.9 24.3 %collective-permute-start.66 = (bf16[512,2048]{1,0:T(8,128)(2,1)}, bf16[512,2048]{1,0:T(8,128)(2,1)}, u32[]{:S(2)}, u32[]{:S(2)}) collective-permute-start(bf16[512,2048]{1,0:T(8,128)(2,1)} %slice.328), channel_id=1, source_target_pairs={{0,2},{2,0},{1,3},{3,1},{4,6},{6,4},{5,7},{7,5},{8,10},{10,8},{9,1... | collective-permute-start | bytes 6291464 | tf_op jit(solution)/shard_map/ppermute | solution.py:295
  735.6 46.0 %collective-permute-start.47 = (bf16[640,1536]{1,0:T(8,128)(2,1)}, bf16[640,1536]{1,0:T(8,128)(2,1)}, u32[]{:S(2)}, u32[]{:S(2)}) collective-permute-start(bf16[640,1536]{1,0:T(8,128)(2,1)} %get-tuple-element.86), channel_id=1, source_target_pairs={{0,1},{1,0},{2,3},{3,2},{4,5},{5,4},{6,7},{7,6},{8,9},{9,8},{10,11... | collective-permute-start | bytes 5898248 | tf_op jit(solution)/shard_map/ppermute | solution.py:295
  748.8 94.1 %collective-permute-start.77 = (bf16[256,2048]{1,0:T(8,128)(2,1)}, bf16[256,2048]{1,0:T(8,128)(2,1)}, u32[]{:S(2)}, u32[]{:S(2)}) collective-permute-start(bf16[256,2048]{1,0:T(8,128)(2,1)} %slice.343), channel_id=1, source_target_pairs={{0,4},{1,5},{4,0},{5,1},{2,6},{3,7},{6,2},{7,3},{8,12},{9,13},{12,... | collective-permute-start | bytes 3145736 | tf_op jit(solution)/shard_map/ppermute | solution.py:295
  754.7 89.5 %collective-permute-start.75 = (bf16[256,2048]{1,0:T(8,128)(2,1)}, bf16[256,2048]{1,0:T(8,128)(2,1)}, u32[]{:S(2)}, u32[]{:S(2)}) collective-permute-start(bf16[256,2048]{1,0:T(8,128)(2,1)} %get-tuple-element.89), channel_id=1, source_target_pairs={{0,5},{1,4},{4,1},{5,0},{2,7},{3,6},{6,3},{7,2},{8,13},{9,12},{12,... | collective-permute-start | bytes 3145736 | tf_op jit(solution)/shard_map/ppermute | solution.py:295
  820.6 26.4 %collective-permute-start.76 = (bf16[256,2048]{1,0:T(8,128)(2,1)}, bf16[256,2048]{1,0:T(8,128)(2,1)}, u32[]{:S(2)}, u32[]{:S(2)}) collective-permute-start(bf16[256,2048]{1,0:T(8,128)(2,1)} %get-tuple-element.90), channel_id=1, source_target_pairs={{0,1},{1,0},{4,5},{5,4},{2,3},{3,2},{6,7},{7,6},{8,9},{9,8},{12,13... | collective-permute-start | bytes 3145736 | tf_op jit(solution)/shard_map/ppermute | solution.py:295
  834.8 48.9 %collective-permute-start.69 = (bf16[256,2048]{1,0:T(8,128)(2,1)}, bf16[256,2048]{1,0:T(8,128)(2,1)}, u32[]{:S(2)}, u32[]{:S(2)}) collective-permute-start(bf16[256,2048]{1,0:T(8,128)(2,1)} %slice.331), channel_id=1, source_target_pairs={{0,4},{1,5},{4,0},{5,1},{2,6},{3,7},{6,2},{7,3},{8,12},{9,13},{12,... | collective-permute-start | bytes 3145736 | tf_op jit(solution)/shard_map/ppermute | solution.py:295
  839.4 46.3 %collective-permute-start.67 = (bf16[256,2048]{1,0:T(8,128)(2,1)}, bf16[256,2048]{1,0:T(8,128)(2,1)}, u32[]{:S(2)}, u32[]{:S(2)}) collective-permute-start(bf16[256,2048]{1,0:T(8,128)(2,1)} %get-tuple-element.91), channel_id=1, source_target_pairs={{0,5},{1,4},{4,1},{5,0},{2,7},{3,6},{6,3},{7,2},{8,13},{9,12},{12,... | collective-permute-start | bytes 3145736 | tf_op jit(solution)/shard_map/ppermute | solution.py:295
  842.9 46.4 %collective-permute-start.68 = (bf16[256,2048]{1,0:T(8,128)(2,1)}, bf16[256,2048]{1,0:T(8,128)(2,1)S(1)}, u32[]{:S(2)}, u32[]{:S(2)}) collective-permute-start(bf16[256,2048]{1,0:T(8,128)(2,1)} %get-tuple-element.92), channel_id=1, source_target_pairs={{0,1},{1,0},{4,5},{5,4},{2,3},{3,2},{6,7},{7,6},{8,9},{9,8},{12,13... | collective-permute-start | bytes 3145736 | tf_op jit(solution)/shard_map/ppermute | solution.py:295
  844.2 68.2 %collective-permute-start.53 = (bf16[256,1536]{1,0:T(8,128)(2,1)}, bf16[256,1536]{1,0:T(8,128)(2,1)S(1)}, u32[]{:S(2)}, u32[]{:S(2)}) collective-permute-start(bf16[256,1536]{1,0:T(8,128)(2,1)} %slice.307), channel_id=1, source_target_pairs={{0,4},{1,5},{4,0},{5,1},{2,6},{3,7},{6,2},{7,3},{8,12},{9,13},{12,... | collective-permute-start | bytes 2359304 | tf_op jit(solution)/shard_map/ppermute | solution.py:295
  847.0 45.6 %collective-permute-start.50 = (bf16[512,1536]{1,0:T(8,128)(2,1)}, bf16[512,1536]{1,0:T(8,128)(2,1)S(1)}, u32[]{:S(2)}, u32[]{:S(2)}) collective-permute-start(bf16[512,1536]{1,0:T(8,128)(2,1)} %slice.304), channel_id=1, source_target_pairs={{0,2},{2,0},{1,3},{3,1},{4,6},{6,4},{5,7},{7,5},{8,10},{10,8},{9,1... | collective-permute-start | bytes 4718600 | tf_op jit(solution)/shard_map/ppermute | solution.py:295
  895.7 36.0 %collective-permute-start.52 = (bf16[256,1536]{1,0:T(8,128)(2,1)S(1)}, bf16[256,1536]{1,0:T(8,128)(2,1)S(1)}, u32[]{:S(2)}, u32[]{:S(2)}) collective-permute-start(bf16[256,1536]{1,0:T(8,128)(2,1)S(1)} %get-tuple-element.94), channel_id=1, source_target_pairs={{0,1},{1,0},{4,5},{5,4},{2,3},{3,2},{6,7},{7,6},{8,9},{9,8},{12,13... | collective-permute-start | bytes 2359304 | tf_op jit(solution)/shard_map/ppermute | solution.py:295
  897.5 59.2 %collective-permute-start.48 = (bf16[640,1024]{1,0:T(8,128)(2,1)S(1)}, bf16[640,1024]{1,0:T(8,128)(2,1)S(1)}, u32[]{:S(2)}, u32[]{:S(2)}) collective-permute-start(bf16[640,1024]{1,0:T(8,128)(2,1)S(1)} %dynamic-slice_convert_fusion), channel_id=1, source_target_pairs={{0,1},{1,0},{2,3},{3,2},{4,5},{5,4},{6,7},{7,6},{8,9},{9,8},{10,11... | collective-permute-start | bytes 3932168 | tf_op jit(solution)/shard_map/ppermute | solution.py:295
  905.5 28.4 %collective-permute-start.70 = (bf16[64,2048]{1,0:T(8,128)(2,1)S(1)}, bf16[64,2048]{1,0:T(8,128)(2,1)S(1)}, u32[]{:S(2)}, u32[]{:S(2)}) collective-permute-start(bf16[64,2048]{1,0:T(8,128)(2,1)S(1)} %get-tuple-element.102), channel_id=1, source_target_pairs={{0,8},{8,0},{16,24},{24,16},{1,9},{9,1},{17,25},{25,17},{2,10},{10... | collective-permute-start | bytes 786440 | tf_op jit(solution)/shard_map/ppermute | solution.py:295
  932.9 35.7 %collective-permute-start.54 = (bf16[64,1536]{1,0:T(8,128)(2,1)}, bf16[64,1536]{1,0:T(8,128)(2,1)}, u32[]{:S(2)}, u32[]{:S(2)}) collective-permute-start(bf16[64,1536]{1,0:T(8,128)(2,1)} %get-tuple-element.105), channel_id=1, source_target_pairs={{0,8},{8,0},{16,24},{24,16},{1,9},{9,1},{17,25},{25,17},{2,10},{10... | collective-permute-start | bytes 589832 | tf_op jit(solution)/shard_map/ppermute | solution.py:295
  933.9 34.7 %collective-permute-start.56 = (bf16[64,1536]{1,0:T(8,128)(2,1)}, bf16[64,1536]{1,0:T(8,128)(2,1)}, u32[]{:S(2)}, u32[]{:S(2)}) collective-permute-start(bf16[64,1536]{1,0:T(8,128)(2,1)} %get-tuple-element.106), channel_id=1, source_target_pairs={{0,24},{8,16},{16,8},{24,0},{1,25},{9,17},{17,9},{25,1},{2,26},{10... | collective-permute-start | bytes 589832 | tf_op jit(solution)/shard_map/ppermute | solution.py:295
  936.2 32.4 %collective-permute-start.55 = (bf16[64,1536]{1,0:T(8,128)(2,1)}, bf16[64,1536]{1,0:T(8,128)(2,1)}, u32[]{:S(2)}, u32[]{:S(2)}) collective-permute-start(bf16[64,1536]{1,0:T(8,128)(2,1)} %get-tuple-element.107), channel_id=1, source_target_pairs={{0,16},{8,24},{16,0},{24,8},{1,17},{9,25},{17,1},{25,9},{2,18},{10... | collective-permute-start | bytes 589832 | tf_op jit(solution)/shard_map/ppermute | solution.py:295
  (166 other events, 2410.1 us)

commit v3 on v2

--- a/solution.py
+++ b/solution.py
@@ -1,3 +1,4 @@
+import functools
 import math
 
 import jax
@@ -14,6 +15,8 @@
 bf16 = jnp.bfloat16
 exp2_scale = math.log2(math.e) / math.sqrt(HEAD_DIM)
 grad_scale = 1.0 / math.sqrt(HEAD_DIM)
+gelu_scale = math.sqrt(2.0 / math.pi)
+gelu_cubic = 0.044715
 
 
 def dot_nn(a, b):
@@ -214,8 +217,171 @@
     return scale * inner, jnp.stack([jnp.sum(grad * xhat, axis=0), jnp.sum(grad, axis=0)])
 
 
-def gelu_tanh(values):
-    return jax.nn.gelu(values, approximate=True)
+def gelu_and_slope(values):
+    square = values * values
+    bent = jnp.tanh(gelu_scale * values * (1.0 + gelu_cubic * square))
+    half = 0.5 + 0.5 * bent
+    slope = half + 2.0 * gelu_scale * values * half * (1.0 - half) * (1.0 + 3.0 * gelu_cubic * square)
+    return values * half, slope
+
+
+def gather_kernel(chunks, weights, extra, *refs):
+    shards, refs = refs[: weights + extra], refs[weights + extra :]
+    tp = lax.axis_size("tp")
+    depth = lax.axis_size("z")
+    outs, refs = refs[: weights * tp + extra], refs[weights * tp + extra :]
+    send_sems, recv_sems, local_sems = refs
+    z, y, core, x = (lax.axis_index(name) for name in ("z", "y", "core", "tp"))
+
+    barrier = pltpu.get_barrier_semaphore()
+    partners = [{"z": z ^ k} for k in range(1, depth)] + [{"tp": x ^ k} for k in range(1, tp)]
+    partners += [{"y": y ^ 1}, {"core": core ^ 1}]
+    for partner in partners:
+        pl.semaphore_signal(barrier, inc=1, device_id=partner, device_id_type=pl.DeviceIdType.MESH)
+    pl.semaphore_wait(barrier, len(partners))
+
+    first = (0, depth // 2)
+    second = (depth // 2, depth - depth // 2)
+    started = []
+
+    def copy(source, target, partner):
+        slot = len(started)
+        made = pltpu.make_async_remote_copy(
+            src_ref=source,
+            dst_ref=target,
+            send_sem=send_sems.at[slot],
+            recv_sem=recv_sems.at[slot],
+            device_id=partner,
+            device_id_type=pl.DeviceIdType.MESH,
+        )
+        made.start()
+        started.append(made)
+        return made
+
+    def part(number, t, c, j, span):
+        weight, low, rows = chunks[number]
+        start = (2 * c + j) * depth + span[0]
+        return outs[weight * tp + t].at[pl.ds(start, span[1]), pl.ds(low, rows)]
+
+    def along_z(number):
+        weight, low, rows = chunks[number]
+        own = shards[weight].at[pl.ds(low, rows)]
+        keep = pltpu.make_async_copy(
+            own, outs[weight * tp].at[0, pl.ds(low, rows)], local_sems.at[number]
+        )
+        keep.start()
+        sent = [
+            copy(own, outs[weight * tp].at[k, pl.ds(low, rows)], {"z": z ^ k})
+            for k in range(1, depth)
+        ]
+        return keep, sent
+
+    crossed = []
+
+    def to_core(number, t, j, span):
+        made = copy(part(number, t, 0, j, span), part(number, t, 1, j, span), {"core": core ^ 1})
+        crossed.append(made)
+
+    def plane_start(number, keep, sent):
+        keep.wait()
+        for k in range(1, depth // 2):
+            sent[k - 1].wait_recv()
+        over_x = [
+            copy(part(number, 0, 0, 0, first), part(number, k, 0, 0, first), {"tp": x ^ k})
+            for k in range(1, tp)
+        ]
+        for k in range(max(depth // 2, 1), depth):
+            sent[k - 1].wait_recv()
+        over_y = copy(part(number, 0, 0, 0, second), part(number, 0, 0, 1, second), {"y": y ^ 1})
+        made = copy(part(number, 0, 0, 0, first), part(number, 0, 0, 1, first), {"y": y ^ 1})
+        last = [(made, 0, 1, first)]
+        for k in range(1, tp):
+            made = copy(part(number, 0, 0, 0, second), part(number, k, 0, 0, second), {"tp": x ^ k})
+            last.append((made, k, 0, second))
+        to_core(number, 0, 0, first)
+        to_core(number, 0, 0, second)
+        return over_x, over_y, last
+
+    def plane_turn(number, over_x, over_y, last):
+        for k in range(1, tp):
+            over_x[k - 1].wait_recv()
+            made = copy(part(number, k, 0, 0, first), part(number, k, 0, 1, first), {"y": y ^ 1})
+            last.append((made, k, 1, first))
+            to_core(number, k, 0, first)
+        over_y.wait_recv()
+        for k in range(1, tp):
+            made = copy(part(number, 0, 0, 1, second), part(number, k, 0, 1, second), {"tp": x ^ k})
+            last.append((made, k, 1, second))
+        to_core(number, 0, 1, second)
+        return last
+
+    def plane_end(number, last):
+        for made, t, j, span in last:
+            made.wait_recv()
+            to_core(number, t, j, span)
+
+    count = len(chunks)
+    state = {0: along_z(0)}
+    columns = []
+    for step in range(count + 2):
+        if step < count:
+            state[step] = plane_start(step, *state[step])
+            if step + 1 < count:
+                state[step + 1] = along_z(step + 1)
+            else:
+                for number in range(extra):
+                    own, made = shards[weights + number], outs[weights * tp + number]
+                    keep = pltpu.make_async_copy(own, made.at[0], local_sems.at[count + number])
+                    keep.start()
+                    columns.append(keep)
+                    columns += [copy(own, made.at[k], {"z": z ^ k}) for k in range(1, depth)]
+        if 0 <= step - 1 < count:
+            state[step - 1] = plane_turn(step - 1, *state[step - 1])
+        if 0 <= step - 2 < count:
+            plane_end(step - 2, state[step - 2])
+    for made in crossed:
+        made.wait_recv()
+    for number, made in enumerate(columns):
+        if number % depth:
+            made.wait_recv()
+        else:
+            made.wait()
+    for made in started:
+        made.wait_send()
+
+
+def gather_weights(shards, pieces, extra=()):
+    tp = lax.axis_size("tp")
+    depth = lax.axis_size("z")
+    chunks = []
+    for number, (shard, split) in enumerate(zip(shards, pieces)):
+        rows = shard.shape[0] // split
+        chunks += [(number, piece * rows, rows) for piece in range(split)]
+    copies = len(chunks) * (depth + 1 + 4 * (tp - 1) + 4 * tp) + len(extra) * (depth - 1)
+    shapes = [
+        jax.ShapeDtypeStruct((4 * depth,) + shard.shape, shard.dtype)
+        for shard in shards
+        for _ in range(tp)
+    ]
+    shapes += [jax.ShapeDtypeStruct((depth,) + shard.shape, shard.dtype) for shard in extra]
+    sent = sum(shape.size for shape in shapes) * 2
+    whole = pl.pallas_call(
+        functools.partial(gather_kernel, chunks, len(shards), len(extra)),
+        name="gather_weights",
+        out_shape=shapes,
+        in_specs=[pl.BlockSpec(memory_space=pltpu.VMEM)] * (len(shards) + len(extra)),
+        out_specs=[pl.BlockSpec(memory_space=pl.ANY)] * len(shapes),
+        scratch_shapes=[
+            pltpu.SemaphoreType.DMA((copies,)),
+            pltpu.SemaphoreType.DMA((copies,)),
+            pltpu.SemaphoreType.DMA((len(chunks) + len(extra),)),
+        ],
+        compiler_params=pltpu.CompilerParams(collective_id=0, has_side_effects=True),
+        cost_estimate=pl.CostEstimate(flops=0, bytes_accessed=2 * sent, transcendentals=0),
+    )(*shards, *extra)
+    made = [array.reshape(-1, array.shape[2]) for array in whole]
+    gathered = [made[number * tp : (number + 1) * tp] for number in range(len(shards))]
+    return gathered, made[len(shards) * tp :]
 
 
 def width_orders():
@@ -266,7 +432,11 @@
 
 def arrange(first, second, source, plan, rows, out_type):
     width = first.shape[1]
-    first_at, second_at, use_second = (jnp.stack(list(column)).astype(jnp.int32) for column in zip(*plan))
+    cuts = 4 if rows % 64 == 0 else 1
+    rows //= cuts
+    plan = [(a * cuts + cut, b * cuts + cut, u) for a, b, u in plan for cut in range(cuts)]
+    columns = [jnp.stack(list(column)).astype(jnp.int32) for column in zip(*plan)]
+    first_at, second_at, use_second = columns
     return pl.pallas_call(
         arrange_kernel,
         name="arrange",
@@ -324,11 +494,6 @@
     return values
 
 
-def gather_z(shard):
-    count = lax.axis_size("z")
-    return jnp.concatenate([shard] + [send(shard, "z", k) for k in range(1, count)], axis=0)
-
-
 def gather_plane(block):
     count = lax.axis_size("tp")
     places = [(k // 2, k % 2) for k in range(1, 2 * count)]
@@ -336,10 +501,16 @@
 
 
 def gather_core(blocks):
-    other = [send(block, "core", 1) for block in blocks]
-    halves = range(len(blocks) // 2)
-    pair = lambda pieces, t: pieces[2 * t : 2 * t + 2]
-    return [jnp.concatenate(pair(blocks, t) + pair(other, t), axis=0) for t in halves]
+    return list(blocks), [send(block, "core", 1) for block in blocks]
+
+
+def assemble(blocks, columns):
+    own, other = blocks
+    made = []
+    for t in range(len(own) // 2):
+        pair = own[2 * t : 2 * t + 2] + other[2 * t : 2 * t + 2]
+        made.append(jnp.concatenate([block[:, columns] for block in pair], axis=0))
+    return jnp.concatenate(made, axis=1)
 
 
 def scatter_core(part):
@@ -348,26 +519,30 @@
     return (part[:half].astype(f32) + came.astype(f32)).astype(bf16)
 
 
-def scatter_plane(parts):
-    half = parts[0].shape[0] // 2
-    total = parts[0][:half].astype(f32)
-    for k in range(2 * len(parts) - 1, 0, -1):
-        piece = parts[k // 2][k % 2 * half : (k % 2 + 1) * half]
-        total = total + send(piece, ("y", "tp"), k % 2 * len(parts) + k // 2).astype(f32)
-    return total.astype(bf16)
+def scatter_plane(part):
+    tp = lax.axis_size("tp")
+    rows, columns = part.shape[0] // 2, part.shape[1] // tp
+    straight, across = [part[:rows, :columns]], []
+    for t in range(tp):
+        for y in range(2):
+            if t or y:
+                piece = part[y * rows : (y + 1) * rows, t * columns : (t + 1) * columns]
+                came = send(piece, ("y", "tp"), y * tp + t)
+                (across if t and y else straight).append(came)
+    return straight, across
+
+
+def total(pieces):
+    return sum([piece.astype(f32) for piece in pieces[1:]], pieces[0].astype(f32)).astype(bf16)
 
 
 def scatter_z(part):
     count = lax.axis_size("z")
     rows = part.shape[0] // count
-    total = part[:rows].astype(f32)
+    made = part[:rows].astype(f32)
     for k in range(1, count):
-        total = total + send(part[k * rows : (k + 1) * rows], "z", k).astype(f32)
-    return total
-
-
-def scatter_grad(parts):
-    return scatter_z(scatter_plane([scatter_core(part.astype(bf16)) for part in parts]))
+        made = made + send(part[k * rows : (k + 1) * rows], "z", k).astype(f32)
+    return made
 
 
 def segment_tables(segments, parents):
@@ -429,17 +604,10 @@
         back = arrange(values, came, outward, out_plan, own_rows, out_type)
         return back.reshape(micro, 1, own_rows, width)
 
-    qkv_z = gather_z(w_qkv.reshape(w_qkv.shape[0], -1))
-    qkv_plane = gather_plane(qkv_z)
-    full_qkv = gather_core(qkv_plane)
-    out_z = gather_z(after(w_out.T, qkv_z))
-    up_z = gather_z(after(w_up, qkv_z))
-    out_plane = gather_plane(after(out_z, qkv_plane[1]))
-    up_plane = gather_plane(after(up_z, qkv_plane[1]))
-    down_z = gather_z(after(w_down.T, qkv_plane[1]))
-    full_out = gather_core(out_plane)
-    full_up = gather_core(up_plane)
-    full_down = gather_core(gather_plane(after(down_z, up_plane[1])))
+    head_width = w_out.shape[0]
+    shard_qkv = w_qkv.reshape(w_qkv.shape[0], -1)
+    shard_mid = jnp.concatenate([w_out.T, w_up], axis=1)
+    (full_qkv,), (mid_z, down_z) = gather_weights([shard_qkv], [4], [shard_mid, w_down.T])
 
     seg_came = exchange_tp([segments[:, 0]] * tp)
     seg_all = jnp.concatenate([pick(seg_came, here ^ s) for s in halves], axis=1)
@@ -464,85 +632,107 @@
         cut = slice(n * own_rows, (n + 1) * own_rows)
         share_calls.append(in_place_order(exchange_tp([part[cut] for part in share_qkv])))
     whole_out = [[] for _ in halves]
+    share_out = [[] for _ in halves]
     saved = {}
+    share_made = []
+    mid_plane = gather_plane(mid_z)
     for n in range(whole):
         for t in halves:
             qkv = whole_qkv[t][n * tree_len : (n + 1) * tree_len]
             out, lse = attention_forward(qkv, *whole_tables[n])
             saved[n, t] = (qkv, out, lse)
             whole_out[t].append(out)
-    share_out = [[] for _ in halves]
+    share_calls = [after(call, *mid_plane[1:], *whole_out[0]) for call in share_calls]
+    mid_core = gather_core(mid_plane)
+    down_plane = gather_plane(after(down_z, mid_plane[1]))
     for n in range(share_count):
         out, lse = attention_forward(share_calls[n], *share_tables[n])
         saved[n] = (share_calls[n], out, lse)
         parts = exchange_tp([share_rows(out, k) for k in halves])
         for t in halves:
             share_out[t].append(parts[t])
+    full_out = assemble(mid_core, slice(0, head_width))
+    full_up = assemble(mid_core, slice(head_width, None))
+    full_down = assemble(gather_core(down_plane), slice(None))
     attended = [jnp.concatenate(whole_out[t] + share_out[t], axis=0) for t in halves]
-    branch_a = sum(dot_nt(attended[t], full_out[t]) for t in halves)
+    attended = jnp.concatenate(attended, axis=1)
+    branch_a = dot_nt(attended, full_out)
     residual = x + norm_forward(branch_a, gains[1], biases[1])
 
     normed_f = norm_forward(residual, gains[2], biases[2]).astype(bf16)
-    up_low = []
-    hidden = []
-    for t in halves:
-        up = dot_nn(normed_f, full_up[t])
-        hidden.append(gelu_tanh(up).astype(bf16))
-        up_low.append(up.astype(bf16))
-    branch_f = sum(dot_nt(hidden[t], full_down[t]) for t in halves)
+    hidden, slope = gelu_and_slope(dot_nn(normed_f, full_up))
+    hidden, slope = lax.optimization_barrier((hidden.astype(bf16), slope.astype(bf16)))
+    branch_f = dot_nt(hidden, full_down)
     out = (residual + norm_forward(branch_f, gains[3], biases[3])).astype(bf16)
     out_rows = rows_back(out, bf16)
 
     grad_out = tree_rows(after(cotangent, full_qkv[0])).astype(f32)
     grad_branch_f, sums_3 = norm_backward(branch_f, gains[3], grad_out)
     grad_branch_f = grad_branch_f.astype(bf16)
-    grad_down = scatter_grad([dot_tn(grad_branch_f, hidden[t]) for t in halves])
-    grad_up = []
-    for t in halves:
-        pull = jax.vjp(gelu_tanh, up_low[t].astype(f32))[1]
-        grad_up.append(pull(dot_nn(grad_branch_f, full_down[t]))[0].astype(bf16))
-    grad_w_up = scatter_grad([dot_tn(normed_f, grad_up[t]) for t in halves])
-    grad_normed_f = sum(dot_nt(grad_up[t], full_up[t]) for t in halves)
+    core_down = scatter_core(dot_tn(grad_branch_f, hidden).astype(bf16))
+    grad_up = (dot_nn(grad_branch_f, full_down) * slope.astype(f32)).astype(bf16)
+    grad_up = after(grad_up, core_down)
+    straight_down, across_down = scatter_plane(core_down)
+    dw_up = dot_tn(normed_f, grad_up).astype(bf16)
+    core_up = scatter_core(dw_up)
+    grad_normed_f = dot_nt(after(grad_up, dw_up, *straight_down), full_up)
     grad_part, sums_2 = norm_backward(residual, gains[2], grad_normed_f)
     grad_residual = grad_out + grad_part
 
     grad_branch_a, sums_1 = norm_backward(branch_a, gains[1], grad_residual)
-    grad_branch_a = grad_branch_a.astype(bf16)
-    share_grad = [dot_nn(grad_branch_a[split:], w).astype(bf16) for w in full_out]
+    grad_branch_a = after(grad_branch_a.astype(bf16), core_up, *across_down)
+    z_down = scatter_z(total(straight_down + across_down))
+    straight_up, across_up = scatter_plane(core_up)
+    grad_attended = dot_nn(grad_branch_a, full_out).astype(bf16)
+    share_grad = [grad_attended[split:, t * head_width : (t + 1) * head_width] for t in halves]
     share_do = []
     for n in range(share_count):
         cut = slice(n * own_rows, (n + 1) * own_rows)
         share_do.append(in_place_order(exchange_tp([part[cut] for part in share_grad])))
-    grad_w_out = scatter_grad([dot_tn(grad_branch_a, attended[t]) for t in halves])
-    whole_grad = [dot_nn(grad_branch_a[:split], w).astype(bf16) for w in full_out] if whole else []
+    core_out = scatter_core(dot_tn(grad_branch_a, attended).astype(bf16))
     grad_qkv = [[] for _ in halves]
     share_parts = [[] for _ in halves]
+
+    def whole_backward(t, *others):
+        for n in range(whole):
+            qkv, att, lse = saved[n, t]
+            do = grad_attended[n * tree_len : (n + 1) * tree_len, t * head_width : (t + 1) * head_width]
+            made = attention_backward(qkv, after(do, *others), att, lse, *whole_tables[n])
+            grad_qkv[t].append(made)
+        return grad_qkv[t]
+
+    made = []
+    for t in range(1, tp):
+        made += whole_backward(t)
     for n in range(share_count):
         qkv, att, lse = saved[n]
-        dx = attention_backward(qkv, share_do[n], att, lse, *share_tables[n])
+        do = after(share_do[n], z_down, *made)
+        dx = attention_backward(qkv, do, att, lse, *share_tables[n])
+        made = [dx]
         parts = exchange_tp([share_rows(dx, k) for k in halves])
         for t in halves:
             share_parts[t].append(parts[t])
-    for n in range(whole):
-        for t in halves:
-            qkv, att, lse = saved[n, t]
-            do = whole_grad[t][n * tree_len : (n + 1) * tree_len]
-            grad_qkv[t].append(attention_backward(qkv, do, att, lse, *whole_tables[n]))
-    grad_qkv = [jnp.concatenate(grad_qkv[t] + share_parts[t], axis=0) for t in halves]
-    grad_w_qkv = scatter_grad([dot_tn(normed, grad_qkv[t]) for t in halves])
+    made = whole_backward(0, core_out, *straight_up, *made)
+    straight_out, across_out = scatter_plane(core_out)
+    ready = [*across_up, *straight_out, *across_out, *made]
+    grad_qkv = [after(jnp.concatenate(grad_qkv[t] + share_parts[t], axis=0), *ready) for t in halves]
+    z_up = scatter_z(total(straight_up + across_up))
+    z_out = scatter_z(total(straight_out + across_out))
+    core_qkv = [scatter_core(dot_tn(normed, grad_qkv[t]).astype(bf16)) for t in reversed(halves)]
+    straight_qkv, across_qkv = scatter_plane(jnp.concatenate(core_qkv[::-1], axis=1))
+    z_qkv = scatter_z(total(straight_qkv + across_qkv))
     grad_normed = sum(dot_nt(grad_qkv[t], full_qkv[t]) for t in halves)
     grad_part, sums_0 = norm_backward(x, gains[0], grad_normed)
     input_rows = rows_back(grad_residual + grad_part, f32)
-    early = sum_everywhere(arrange_small(jnp.concatenate([sums_1, sums_2, sums_3]), outward))
-    late = sum_everywhere(arrange_small(sums_0, outward))
-    sums = jnp.concatenate([late, early], axis=0).reshape(4, 2, width)
+    sums = jnp.concatenate([sums_0, sums_1, sums_2, sums_3])
+    sums = sum_everywhere(arrange_small(sums, outward)).reshape(4, 2, width)
     return (
         out_rows,
         input_rows,
-        grad_w_qkv.reshape(w_qkv.shape),
-        grad_w_out.T,
-        grad_w_up,
-        grad_down.T,
+        z_qkv.reshape(w_qkv.shape),
+        z_out.T,
+        z_up,
+        z_down.T,
         sums[:, 0],
         sums[:, 1],
     )

time: 976 us -> 993 us (1.017)
  waiting for transfers between devices: 265 us -> 139 us
  Pallas kernels: 178 us -> 267 us
  matrix products: 257 us -> 293 us
  starting transfers between devices: 91.3 us -> 67.6 us
  other arithmetic: 88.7 us -> 111 us
  local copies, waits for them, and re-layouts: 87.8 us -> 107 us
    ppermute x95 -> x59, waiting for transfers between devices: 265 us -> 139 us  [send(): return lax.ppermute(values, axes, [(s, s ^ distance) for s in range(count)])]
    pallas_call x0 -> x1, Pallas kernels: none -> 76.1 us  [gather_weights(): pl.pallas_call(functools.partial(gather_kernel, chunks, len(shards), len(...]
    slice x12 -> x27, local copies, waits for them, and re-layouts: 7.33 us -> 33.9 us  [the longest x16 25.7 us: assemble(): made.append(jnp.concatenate([block[:, columns] for block in pair], axis=0))]
    ppermute x95 -> x59, starting transfers between devices: 91.3 us -> 67.6 us  [send(): return lax.ppermute(values, axes, [(s, s ^ distance) for s in range(count)])]
    unnamed x276 -> x224, local copies, waits for them, and re-layouts: 45.3 us -> 21.7 us
    dot_general x0 -> x2, local copies, waits for them, and re-layouts: none -> 18.2 us  [dot_nt(): lax.dot_general(a, b, (((1,), (1,)), ((), ())), preferred_element_type=f32)]
    pallas_call x4, Pallas kernels: 33.2 us -> 46.6 us  [arrange(): pl.pallas_call(arrange_kernel, name='arrange', out_shape=jax.ShapeDtypeSt...]
    dot_general x8 -> x5, matrix products: 76.8 us -> 90 us  [dot_tn(): lax.dot_general(a, b, (((0,), (0,)), ((), ())), preferred_element_type=f32)]
  transfers between devices with their start and end apart: 95 -> 59, of which waited for: 26 -> 13; matrix products, arithmetic and copies ran while one was open for 20% -> 36% of each run, Pallas kernels for 18% -> 19%
where the time goes in v3:
time: 993 us; the launch traced here: 987 us
  matrix products  293 us (30%)
  Pallas kernels  267 us (27%)
  waiting for transfers between devices  139 us (14%)
  other arithmetic  111 us (11%)
  local copies, waits for them, and re-layouts  107 us (11%)
  starting transfers between devices  67.6 us (7%)
    ppermute x59, waiting for transfers between devices, send(): return lax.ppermute(values, axes, [(s, s ^ distance) for s in range(count)])  139 us
    dot_general x5, matrix products, dot_nt(): lax.dot_general(a, b, (((1,), (1,)), ((), ())), preferred_element_type=f32)  103 us
    dot_general x7, matrix products, dot_nn(): lax.dot_general(a, b, (((1,), (0,)), ((), ())), preferred_element_type=f32)  99.5 us
    dot_general x5, matrix products, dot_tn(): lax.dot_general(a, b, (((0,), (0,)), ((), ())), preferred_element_type=f32)  90 us
    pallas_call x3, Pallas kernels, attention_backward(): pl.pallas_call(attention_backward_kernel, name='attention_backward', out_...  80.1 us
    pallas_call x1, Pallas kernels, gather_weights(): pl.pallas_call(functools.partial(gather_kernel, chunks, len(shards), len(...  76.1 us
    ppermute x59, starting transfers between devices, send(): return lax.ppermute(values, axes, [(s, s ^ distance) for s in range(count)])  67.6 us
    pallas_call x3, Pallas kernels, attention_forward(): pl.pallas_call(attention_forward_kernel, name='attention_forward', out_sh...  64.7 us
  transfers between devices with their start and end apart: 59, of which 13 were waited for; matrix products, arithmetic and copies ran while one was open for 36% of the time, Pallas kernels for 19%

profile of v3, /device:TPU:0, one launch (start us, length us, event | category | flops | bytes accessed | tf_op | source)
XLA Modules:
  0.0 986.9 jit_solution(3006308892220278183)
XLA Ops:
  4.0 76.1 %gather_weights.1 = (bf16[16,64,1536]{2,1,0:T(8,128)(2,1)}, bf16[16,64,1536]{2,1,0:T(8,128)(2,1)}, bf16[4,64,2560]{2,1,0:T(8,128)(2,1)}, bf16[4,64,2048]{2,1,0:T(8,128)(2,1)}) custom-call(bf16[64,1536]{1,0:T(8,128)(2,1)} %bitcast.90, bf16[64,2560]{1,0:T(8,128)(2,1)} %pad_maximum_fusion.4.refs_1_, bf16[64,2048]{1,0:T(8,128)(2,1)} %bitcast.93), custom_call_target="tpu_custom_call" | custom-call | bytes 17301504 | tf_op jit(solution)/shard_map/gather_weights/pallas_call | solution.py:368
  102.3 62.8 %collective-permute-done.1 = s32[3,640]{1,0:T(4,128)S(1)} collective-permute-done((s32[3,640]{1,0:T(4,128)S(1)}, s32[3,640]{1,0:T(4,128)S(1)}, u32[]{:S(2)}, u32[]{:S(2)}) %collective-permute-start.1) | collective-permute-done | bytes 7712 | tf_op jit(solution)/shard_map/ppermute | solution.py:465
  168.1 11.2 %arrange.4 = bf16[1920,1024]{1,0:T(8,128)(2,1)} custom-call(s32[16]{0:T(128)} %copy-done.95, s32[12]{0:T(128)} %stack.50.first_at, s32[12]{0:T(128)} %stack.59.second_at, s32[12]{0:T(128)} %convert_element_type.225.use_second, bf16[1920,1024]{1,0:T(8,128)(2,1)} %bitcast.83, bf16[640,1024]{1,0:T(8,128)(2,1)} %copy-done.43), custom_call_target="tpu_custom_call" | custom-call | flops 15728640 | bytes 15728640 | tf_op jit(solution)/shard_map/arrange/pallas_call | solution.py:440
  210.7 5.8 convolution_convert_fusion.1.q_ref.k_ref.v_ref
  216.5 10.9 %arrange.6 = bf16[1920,1024]{1,0:T(8,128)(2,1)} custom-call(s32[16]{0:T(128)} %copy-done.95, s32[12]{0:T(128)} %stack.50.first_at, s32[12]{0:T(128)} %stack.59.second_at, s32[12]{0:T(128)} %convert_element_type.225.use_second, bf16[1920,1024]{1,0:T(8,128)(2,1)} %bitcast.85, bf16[640,1024]{1,0:T(8,128)(2,1)} %collective-permute-done.19.second_ref), custom_call_target="tpu_custom_call" | custom-call | flops 15728640 | bytes 15728640 | tf_op jit(solution)/shard_map/arrange/pallas_call | solution.py:440
  227.4 4.6 convolution_convert_fusion.7
  232.1 21.6 %attention_forward.3 = (bf16[1280,512]{1,0:T(8,128)(2,1)S(1)}, f32[4,8,1280]{2,1,0:T(8,128)S(1)}) custom-call(bf16[1280,1536]{1,0:T(8,128)(2,1)S(1)} %copy-done.8, bf16[1280,1536]{1,0:T(8,128)(2,1)S(1)} %copy-done.8, bf16[1280,1536]{1,0:T(8,128)(2,1)S(1)} %copy-done.8, s32[1280,8]{1,0:T(8,128)S(1)} %pad.14.clone.col_ref, s32[8,1280]{1,0:T(8,128)S(1)} %pad.15.row_ref), custom_call_target="tpu_custom_call" | custom-call | flops 8053063680 | bytes 5898240 | tf_op jit(solution)/shard_map/attention_forward/pallas_call | solution.py:80
  253.7 4.4 convolution_convert_fusion.q_ref.k_ref.v_ref
  258.1 26.8 %collective-permute-done.2 = bf16[640,1536]{1,0:T(8,128)(2,1)} collective-permute-done((bf16[640,1536]{1,0:T(8,128)(2,1)}, bf16[640,1536]{1,0:T(8,128)(2,1)}, u32[]{:S(2)}, u32[]{:S(2)}) %collective-permute-start.2) | collective-permute-done | bytes 1966112 | tf_op jit(solution)/shard_map/ppermute | solution.py:465
  287.6 21.7 %attention_forward.4 = (bf16[1280,512]{1,0:T(8,128)(2,1)S(1)}, f32[4,8,1280]{2,1,0:T(8,128)S(1)}) custom-call(bf16[1280,1536]{1,0:T(8,128)(2,1)S(1)} %pad_maximum_fusion.2.q_ref.k_ref.v_ref, bf16[1280,1536]{1,0:T(8,128)(2,1)S(1)} %pad_maximum_fusion.2.q_ref.k_ref.v_ref, bf16[1280,1536]{1,0:T(8,128)(2,1)S(1)} %pad_maximum_fusion.2.q_ref.k_ref.v_ref, ...), custom_call_target="tpu_custom_call" | custom-call | flops 8053063680 | bytes 5898240 | tf_op jit(solution)/shard_map/attention_forward/pallas_call | solution.py:80
  312.3 21.4 %attention_forward.5 = (bf16[1280,512]{1,0:T(8,128)(2,1)S(1)}, f32[4,8,1280]{2,1,0:T(8,128)S(1)}) custom-call(bf16[1280,1536]{1,0:T(8,128)(2,1)S(1)} %convolution_convert_fusion.q_ref.k_ref.v_ref, bf16[1280,1536]{1,0:T(8,128)(2,1)S(1)} %convolution_convert_fusion.q_ref.k_ref.v_ref, bf16[1280,1536]{1,0:T(8,128)(2,1)S(1)} %convolution_convert_fusion.q_ref.k_ref.v_ref, ...), custom_call_target="tpu_custom_call" | custom-call | flops 8053063680 | bytes 5898240 | tf_op jit(solution)/shard_map/attention_forward/pallas_call | solution.py:80
  341.0 7.8 fusion.66
  348.8 9.1 copy.46
  357.9 4.3 multiply_reduce_fusion.6
  363.4 4.7 fusion.51
  374.2 42.9 %add_convert_fusion = (bf16[1920,4096]{1,0:T(8,128)(2,1)}, bf16[1920,4096]{1,0:T(8,128)(2,1)}) fusion(bf16[256,2048]{1,0:T(8,128)(2,1)} %slice.357, bf16[256,2048]{1,0:T(8,128)(2,1)} %slice.356, bf16[256,2048]{1,0:T(8,128)(2,1)} %slice.355, bf16[256,2048]{1,0:T(8,128)(2,1)} %slice.354, bf16[256,2048]{1,0:T(8,128)(2,1)} %slice.353, ...), kind=kOutput, calls=%fused_computation.1 | convolution fusion | flops 16314793984 | bytes 43778048 | tf_op jit(solution)/shard_map/dot_general | solution.py:23
  417.2 35.8 %fusion.67 = (f32[1920]{0:T(1024)S(1)}, f32[1920,1024]{0,1:T(8,128)}) fusion(bf16[1920,4096]{1,0:T(8,128)(2,1)} %get-tuple-element.37, bf16[256,2048]{1,0:T(8,128)(2,1)} %collective-permute-done.17, bf16[256,2048]{1,0:T(8,128)(2,1)} %collective-permute-done.16, bf16[256,2048]{1,0:T(8,128)(2,1)} %collective-permute-done.15, ...), kind=kOutput, calls=%fused_computation.207 | convolution fusion | flops 16175200256 | bytes 31989248 | tf_op jit(solution)/shard_map/dot_general | solution.py:27
  453.0 9.1 copy.47
  462.1 4.3 multiply_reduce_fusion.4
  467.5 9.1 fusion.21
  476.6 29.5 %convolution_convert_fusion.3 = bf16[1024,4096]{1,0:T(8,128)(2,1)} fusion(bf16[1920,4096]{1,0:T(8,128)(2,1)} %get-tuple-element.37, bf16[1920,1024]{1,0:T(8,128)(2,1)} %arrange.6, f32[1920,1024]{1,0:T(8,128)} %copy.47, f32[1920]{0:T(1024)S(1)} %broadcast_multiply_fusion.6, f32[1920]{0:T(1024)S(1)} %broadcast_multiply_fusion.7, f32[1024]{0:T(1024)S(1)} %copy-done.87, ...), kind=kOutput, calls=%fused_computation.50 | convolution fusion | flops 16128016384 | bytes 35948544 | tf_op jit(solution)/shard_map/dot_general | solution.py:31
  506.2 7.4 fusion.90
  519.6 27.4 %multiply_convert_fusion = bf16[1920,4096]{1,0:T(8,128)(2,1)} fusion(bf16[1920,4096]{1,0:T(8,128)(2,1)} %get-tuple-element.41, bf16[256,2048]{1,0:T(8,128)(2,1)} %collective-permute-done.17, bf16[256,2048]{1,0:T(8,128)(2,1)} %collective-permute-done.16, bf16[256,2048]{1,0:T(8,128)(2,1)} %collective-permute-done.15, ...), kind=kOutput, calls=%fused_computation | convolution fusion | flops 16196829184 | bytes 43778048 | tf_op jit(solution)/shard_map/dot_general | solution.py:23
  551.6 10.9 %arrange.5 = bf16[1920,1024]{1,0:T(8,128)(2,1)} custom-call(s32[16]{0:T(128)} %copy-done.94, s32[12]{0:T(128)} %stack.50.first_at, s32[12]{0:T(128)} %stack.59.second_at, s32[12]{0:T(128)} %convert_element_type.225.use_second, bf16[1920,1024]{1,0:T(8,128)(2,1)} %get-tuple-element.103.first_ref, bf16[640,1024]{1,0:T(8,128)(2,1)} %copy-done.44), custom_call_target="tpu_custom_call" | custom-call | flops 15728640 | bytes 15728640 | tf_op jit(solution)/shard_map/arrange/pallas_call | solution.py:440
  562.6 5.0 add_convert_fusion.2
  570.0 25.6 %convolution_convert_fusion.2 = bf16[1024,4096]{1,0:T(8,128)(2,1)S(1)} fusion(bf16[1920,4096]{1,0:T(8,128)(2,1)} %multiply_convert_fusion, f32[1920,1024]{1,0:T(8,128)} %copy-done.17, f32[1024]{0:T(1024)S(1)} %copy-done.92, f32[1024]{0:T(1024)S(1)} %copy-done.89, f32[1920]{0:T(1024)S(1)} %copy-done.81, f32[1920]{0:T(1024)S(1)} %copy-done.77), kind=kOutput, calls=%fused_computation.49 | convolution fusion | flops 16120152064 | bytes 32005120 | tf_op jit(solution)/shard_map/dot_general | solution.py:31
  602.9 34.6 %multiply_reduce_fusion = (f32[1024]{0:T(1024)S(1)}, f32[1920]{0:T(1024)S(1)}, f32[1920]{0:T(1024)S(1)}, f32[1024]{0:T(1024)S(1)}, f32[1920,1024]{1,0:T(8,128)}) fusion(f32[1920,1024]{1,0:T(8,128)} %copy-done.17, f32[1920]{0:T(1024)S(1)} %copy-done.81, f32[1920]{0:T(1024)S(1)} %copy-done.77, f32[1024]{0:T(1024)S(1)} %copy-done.89, ...), kind=kOutput, calls=%fused_computation.37 | convolution fusion | flops 16190924800 | bytes 39888896 | tf_op jit(solution)/shard_map/dot_general | solution.py:27
  641.5 6.2 collective-permute-start.29
  650.1 11.8 %multiply_reduce_fusion.1 = (f32[1024]{0:T(1024)S(1)}, f32[1920]{0:T(1024)S(1)}, f32[1920]{0:T(1024)S(1)}, f32[1024]{0:T(1024)S(1)}, f32[1920,1024]{1,0:T(8,128)S(1)}) fusion(f32[1920,1024]{1,0:T(8,128)} %copy.46, f32[1920]{0:T(1024)S(1)} %copy-done.75, f32[1920]{0:T(1024)S(1)} %copy-done.71, f32[1024]{0:T(1024)S(1)} %copy-done.84, ...), kind=kLoop, calls=%fused_computation.38 | loop fusion | flops 35383552 | bytes 35467264 | tf_op jit(solution)/shard_map/reduce_sum | solution.py:217
  662.0 4.4 multiply_convert_fusion.2
  671.5 5.0 add_convert_fusion.1
  676.6 10.9 %convolution_convert_fusion.6 = bf16[1920,1024]{1,0:T(8,128)(2,1)S(1)} fusion(bf16[1920,1024]{1,0:T(8,128)(2,1)S(1)} %copy-done.37, bf16[256,512]{1,0:T(8,128)(2,1)S(1)} %copy-done.67, bf16[256,512]{1,0:T(8,128)(2,1)S(1)} %copy-done.65, bf16[256,512]{1,0:T(8,128)(2,1)S(1)} %copy-done.59, bf16[256,512]{1,0:T(8,128)(2,1)S(1)} %copy-done.57, ...), kind=kOutput, calls=%fused_computation.64 | convolution fusion | flops 4045275136 | bytes 9961472 | tf_op jit(solution)/shard_map/dot_general | solution.py:23
  693.2 17.1 %convolution_convert_fusion.9 = bf16[1024,1024]{1,0:T(8,128)(2,1)S(1)} fusion(bf16[1920,1024]{1,0:T(8,128)(2,1)S(1)} %copy-done.38, bf16[640,512]{1,0:T(8,128)(2,1)S(1)} %copy-done.101, bf16[1280,512]{1,0:T(8,128)(2,1)S(1)} %copy-done.15, bf16[640,512]{1,0:T(8,128)(2,1)S(1)} %copy-done.50, bf16[1280,512]{1,0:T(8,128)(2,1)S(1)} %copy-done.13), kind=kOutput, calls=%fused_computation.78 | convolution fusion | flops 4043309056 | bytes 9961472 | tf_op jit(solution)/shard_map/dot_general | solution.py:31
  715.4 26.8 %attention_backward.3 = bf16[1280,1536]{1,0:T(8,128)(2,1)S(1)} custom-call(bf16[1280,1536]{1,0:T(8,128)(2,1)S(1)} %copy-done.11, bf16[1280,1536]{1,0:T(8,128)(2,1)S(1)} %copy-done.11, bf16[1280,1536]{1,0:T(8,128)(2,1)S(1)} %copy-done.11, bf16[1280,512]{1,0:T(8,128)(2,1)S(1)} %get-tuple-element.115.do_ref, bf16[1280,512]{1,0:T(8,128)(2,1)S(1)} %copy-done.15, ...), custom_call_target="tpu_custom_call" | custom-call | flops 20132659200 | bytes 11796480 | tf_op jit(solution)/shard_map/attention_backward/pallas_call | solution.py:171
  743.7 26.6 %attention_backward.4 = bf16[1280,1536]{1,0:T(8,128)(2,1)S(1)} custom-call(bf16[1280,1536]{1,0:T(8,128)(2,1)S(1)} %copy-done.1, bf16[1280,1536]{1,0:T(8,128)(2,1)S(1)} %copy-done.1, bf16[1280,1536]{1,0:T(8,128)(2,1)S(1)} %copy-done.1, bf16[1280,512]{1,0:T(8,128)(2,1)S(1)} %pad_maximum_fusion.3.do_ref, bf16[1280,512]{1,0:T(8,128)(2,1)S(1)} %copy-done.3, ...), custom_call_target="tpu_custom_call" | custom-call | flops 20132659200 | bytes 11796480 | tf_op jit(solution)/shard_map/attention_backward/pallas_call | solution.py:171
  783.8 5.0 collective-permute-start.49
  788.8 26.6 %attention_backward.5 = bf16[1280,1536]{1,0:T(8,128)(2,1)S(1)} custom-call(bf16[1280,1536]{1,0:T(8,128)(2,1)S(1)} %copy-done.9, bf16[1280,1536]{1,0:T(8,128)(2,1)S(1)} %copy-done.9, bf16[1280,1536]{1,0:T(8,128)(2,1)S(1)} %copy-done.9, bf16[1280,512]{1,0:T(8,128)(2,1)S(1)} %get-tuple-element.48.do_ref, bf16[1280,512]{1,0:T(8,128)(2,1)S(1)} %copy-done.13, ...), custom_call_target="tpu_custom_call" | custom-call | flops 20132659200 | bytes 11796480 | tf_op jit(solution)/shard_map/attention_backward/pallas_call | solution.py:171
  818.5 5.1 collective-permute-done.34
  827.6 10.4 %convolution_convert_fusion.5 = bf16[1024,1536]{1,0:T(8,128)(2,1)S(1)} fusion(bf16[1920,1024]{1,0:T(8,128)(2,1)} %copy-done.33, bf16[1920,1536]{1,0:T(8,128)(2,1)} %pad_maximum_fusion), kind=kOutput, calls=%fused_computation.63 | convolution fusion | flops 6041370624 | bytes 12976128 | tf_op jit(solution)/shard_map/dot_general | solution.py:31
  843.5 4.5 pad_maximum_fusion.1
  848.0 10.7 %fusion.68 = f32[1920,1024]{1,0:T(8,128)} fusion(bf16[1920,1536]{1,0:T(8,128)(2,1)} %pad_maximum_fusion.1, bf16[1024,1536]{1,0:T(8,128)(2,1)S(1)} %bitcast.105), kind=kOutput, calls=%fused_computation.208 | convolution fusion | flops 6039797760 | bytes 16908288 | tf_op jit(solution)/shard_map/dot_general | solution.py:27
  858.8 7.4 convolution_convert_fusion.4
  866.2 14.4 %fusion.15 = (f32[1024]{0:T(1024)S(1)}, f32[1920]{0:T(1024)}, f32[1920]{0:T(1024)}, f32[1024]{0:T(1024)}, f32[1920,1024]{1,0:T(8,128)}) fusion(bf16[1920,1024]{1,0:T(8,128)(2,1)S(1)} %copy-done.19, f32[1920]{0:T(1024)S(1)} %copy-done.79, f32[1920]{0:T(1024)S(1)} %copy-done.73, f32[1024]{0:T(1024)S(1)} %copy-done.86, f32[1920,1024]{1,0:T(8,128)} %fusion.68, ...), kind=kOutput, calls=%fused_computation.30 | convolution fusion | flops 6061418496 | bytes 28747776 | tf_op jit(solution)/shard_map/dot_general | solution.py:27
  895.7 5.0 collective-permute-start.46
  912.6 5.3 fusion.14.first_ref
  931.5 16.4 %collective-permute-done.42 = bf16[256,1536]{1,0:T(8,128)(2,1)} collective-permute-done((bf16[256,1536]{1,0:T(8,128)(2,1)S(1)}, bf16[256,1536]{1,0:T(8,128)(2,1)}, u32[]{:S(2)}, u32[]{:S(2)}) %collective-permute-start.42) | collective-permute-done | bytes 786464 | tf_op jit(solution)/shard_map/ppermute | solution.py:465
  955.6 16.4 %collective-permute-done.37.second_ref = bf16[640,1024]{1,0:T(8,128)(2,1)} collective-permute-done((bf16[640,1024]{1,0:T(8,128)(2,1)}, bf16[640,1024]{1,0:T(8,128)(2,1)}, u32[]{:S(2)}, u32[]{:S(2)}) %collective-permute-start.37) | collective-permute-done | bytes 1310752 | tf_op jit(solution)/shard_map/ppermute | solution.py:465
  972.1 13.5 %arrange.7 = f32[1920,1024]{1,0:T(8,128)} custom-call(s32[16]{0:T(128)} %copy-done.94, s32[12]{0:T(128)} %stack.50.first_at, s32[12]{0:T(128)} %stack.59.second_at, s32[12]{0:T(128)} %convert_element_type.225.use_second, f32[1920,1024]{1,0:T(8,128)} %copy-done.24, bf16[640,1024]{1,0:T(8,128)(2,1)} %collective-permute-done.37.second_ref), custom_call_target="tpu_custom_call" | custom-call | flops 15728640 | bytes 15728640 | tf_op jit(solution)/shard_map/arrange/pallas_call | solution.py:440
  (468 shorter events, 199.4 us)
Async XLA Ops:
  80.1 105.4 %collective-permute-start.3 = (bf16[256,2560]{1,0:T(8,128)(2,1)}, bf16[256,2560]{1,0:T(8,128)(2,1)}, u32[]{:S(2)}, u32[]{:S(2)}) collective-permute-start(bf16[256,2560]{1,0:T(8,128)(2,1)} %bitcast.21), channel_id=1, source_target_pairs={{0,4},{1,5},{4,0},{5,1},{2,6},{3,7},{6,2},{7,3},{8,12},{9,13},{12,... | collective-permute-start | bytes 3932168 | tf_op jit(solution)/shard_map/ppermute | solution.py:465
  81.7 107.8 %collective-permute-start.4 = (bf16[256,2560]{1,0:T(8,128)(2,1)}, bf16[256,2560]{1,0:T(8,128)(2,1)}, u32[]{:S(2)}, u32[]{:S(2)}) collective-permute-start(bf16[256,2560]{1,0:T(8,128)(2,1)} %bitcast.21), channel_id=1, source_target_pairs={{0,1},{1,0},{4,5},{5,4},{2,3},{3,2},{6,7},{7,6},{8,9},{9,8},{12,13... | collective-permute-start | bytes 3932168 | tf_op jit(solution)/shard_map/ppermute | solution.py:465
  83.4 111.1 %collective-permute-start.5 = (bf16[256,2560]{1,0:T(8,128)(2,1)}, bf16[256,2560]{1,0:T(8,128)(2,1)}, u32[]{:S(2)}, u32[]{:S(2)}) collective-permute-start(bf16[256,2560]{1,0:T(8,128)(2,1)} %bitcast.21), channel_id=1, source_target_pairs={{0,5},{1,4},{4,1},{5,0},{2,7},{3,6},{6,3},{7,2},{8,13},{9,12},{12,... | collective-permute-start | bytes 3932168 | tf_op jit(solution)/shard_map/ppermute | solution.py:465
  86.1 80.2 %collective-permute-start = (bf16[640,1024]{1,0:T(8,128)(2,1)}, bf16[640,1024]{1,0:T(8,128)(2,1)S(1)}, u32[]{:S(2)}, u32[]{:S(2)}) collective-permute-start(bf16[640,1024]{1,0:T(8,128)(2,1)} %constant_dynamic-slice_fusion.6), channel_id=1, source_target_pairs={{0,1},{1,0},{2,3},{3,2},{4,5},{5,4},{6,7},{7,6},{8,9},{9,8},{10,11... | collective-permute-start | bytes 3932168 | tf_op jit(solution)/shard_map/ppermute | solution.py:465
  88.3 76.9 %collective-permute-start.1 = (s32[3,640]{1,0:T(4,128)S(1)}, s32[3,640]{1,0:T(4,128)S(1)}, u32[]{:S(2)}, u32[]{:S(2)}) collective-permute-start(s32[3,640]{1,0:T(4,128)S(1)} %bitcast.99), channel_id=1, source_target_pairs={{0,1},{1,0},{2,3},{3,2},{4,5},{5,4},{6,7},{7,6},{8,9},{9,8},{10,11... | collective-permute-start | bytes 23048 | tf_op jit(solution)/shard_map/ppermute | solution.py:465
  165.1 40.6 %collective-permute-start.7 = (bf16[256,2560]{1,0:T(8,128)(2,1)}, bf16[256,2560]{1,0:T(8,128)(2,1)}, u32[]{:S(2)}, u32[]{:S(2)}) collective-permute-start(bf16[256,2560]{1,0:T(8,128)(2,1)} %bitcast.21), channel_id=1, source_target_pairs={{0,2},{2,0},{1,3},{3,1},{4,6},{6,4},{5,7},{7,5},{8,10},{10,8},{9,1... | collective-permute-start | bytes 3932168 | tf_op jit(solution)/shard_map/ppermute | solution.py:465
  166.3 50.2 %collective-permute-start.19 = (bf16[640,1024]{1,0:T(8,128)(2,1)}, bf16[640,1024]{1,0:T(8,128)(2,1)}, u32[]{:S(2)}, u32[]{:S(2)}) collective-permute-start(bf16[640,1024]{1,0:T(8,128)(2,1)} %constant_dynamic-slice_fusion.2), channel_id=1, source_target_pairs={{0,1},{1,0},{2,3},{3,2},{4,5},{5,4},{6,7},{7,6},{8,9},{9,8},{10,11... | collective-permute-start | bytes 3932168 | tf_op jit(solution)/shard_map/ppermute | solution.py:465
  185.5 153.2 %collective-permute-start.11 = (bf16[256,2048]{1,0:T(8,128)(2,1)}, bf16[256,2048]{1,0:T(8,128)(2,1)}, u32[]{:S(2)}, u32[]{:S(2)}) collective-permute-start(bf16[256,2048]{1,0:T(8,128)(2,1)} %bitcast.24), channel_id=1, source_target_pairs={{0,4},{1,5},{4,0},{5,1},{2,6},{3,7},{6,2},{7,3},{8,12},{9,13},{12,... | collective-permute-start | bytes 3145736 | tf_op jit(solution)/shard_map/ppermute | solution.py:465
  189.5 149.2 %collective-permute-start.14 = (bf16[256,2048]{1,0:T(8,128)(2,1)}, bf16[256,2048]{1,0:T(8,128)(2,1)}, u32[]{:S(2)}, u32[]{:S(2)}) collective-permute-start(bf16[256,2048]{1,0:T(8,128)(2,1)} %bitcast.24), channel_id=1, source_target_pairs={{0,1},{1,0},{4,5},{5,4},{2,3},{3,2},{6,7},{7,6},{8,9},{9,8},{12,13... | collective-permute-start | bytes 3145736 | tf_op jit(solution)/shard_map/ppermute | solution.py:465
  194.5 144.7 %collective-permute-start.15 = (bf16[256,2048]{1,0:T(8,128)(2,1)}, bf16[256,2048]{1,0:T(8,128)(2,1)}, u32[]{:S(2)}, u32[]{:S(2)}) collective-permute-start(bf16[256,2048]{1,0:T(8,128)(2,1)} %bitcast.24), channel_id=1, source_target_pairs={{0,5},{1,4},{4,1},{5,0},{2,7},{3,6},{6,3},{7,2},{8,13},{9,12},{12,... | collective-permute-start | bytes 3145736 | tf_op jit(solution)/shard_map/ppermute | solution.py:465
  205.7 79.2 %collective-permute-start.2 = (bf16[640,1536]{1,0:T(8,128)(2,1)}, bf16[640,1536]{1,0:T(8,128)(2,1)}, u32[]{:S(2)}, u32[]{:S(2)}) collective-permute-start(bf16[640,1536]{1,0:T(8,128)(2,1)} %convolution_convert_fusion.8), channel_id=1, source_target_pairs={{0,1},{1,0},{2,3},{3,2},{4,5},{5,4},{6,7},{7,6},{8,9},{9,8},{10,11... | collective-permute-start | bytes 5898248 | tf_op jit(solution)/shard_map/ppermute | solution.py:465
  216.5 70.6 %collective-permute-start.8 = (bf16[256,2560]{1,0:T(8,128)(2,1)}, bf16[256,2560]{1,0:T(8,128)(2,1)}, u32[]{:S(2)}, u32[]{:S(2)}) collective-permute-start(bf16[256,2560]{1,0:T(8,128)(2,1)} %collective-permute-done.3), channel_id=1, source_target_pairs={{0,2},{2,0},{1,3},{3,1},{4,6},{6,4},{5,7},{7,5},{8,10},{10,8},{9,1... | collective-permute-start | bytes 3932168 | tf_op jit(solution)/shard_map/ppermute | solution.py:465
  285.0 25.6 %collective-permute-start.9 = (bf16[256,2560]{1,0:T(8,128)(2,1)}, bf16[256,2560]{1,0:T(8,128)(2,1)S(1)}, u32[]{:S(2)}, u32[]{:S(2)}) collective-permute-start(bf16[256,2560]{1,0:T(8,128)(2,1)} %collective-permute-done.4), channel_id=1, source_target_pairs={{0,2},{2,0},{1,3},{3,1},{4,6},{6,4},{5,7},{7,5},{8,10},{10,8},{9,1... | collective-permute-start | bytes 3932168 | tf_op jit(solution)/shard_map/ppermute | solution.py:465
  287.1 52.2 %collective-permute-start.10 = (bf16[256,2560]{1,0:T(8,128)(2,1)}, bf16[256,2560]{1,0:T(8,128)(2,1)S(1)}, u32[]{:S(2)}, u32[]{:S(2)}) collective-permute-start(bf16[256,2560]{1,0:T(8,128)(2,1)} %collective-permute-done.5), channel_id=1, source_target_pairs={{0,2},{2,0},{1,3},{3,1},{4,6},{6,4},{5,7},{7,5},{8,10},{10,8},{9,1... | collective-permute-start | bytes 3932168 | tf_op jit(solution)/shard_map/ppermute | solution.py:465
  310.6 30.4 %collective-permute-start.6 = (bf16[640,512]{1,0:T(8,128)(2,1)S(1)}, bf16[640,512]{1,0:T(8,128)(2,1)S(1)}, u32[]{:S(2)}, u32[]{:S(2)}) collective-permute-start(bf16[640,512]{1,0:T(8,128)(2,1)S(1)} %get-tuple-element.121), channel_id=1, source_target_pairs={{0,1},{1,0},{2,3},{3,2},{4,5},{5,4},{6,7},{7,6},{8,9},{9,8},{10,11... | collective-permute-start | bytes 1966088 | tf_op jit(solution)/shard_map/ppermute | solution.py:465
  338.7 78.5 %collective-permute-start.12 = (bf16[256,2048]{1,0:T(8,128)(2,1)}, bf16[256,2048]{1,0:T(8,128)(2,1)}, u32[]{:S(2)}, u32[]{:S(2)}) collective-permute-start(bf16[256,2048]{1,0:T(8,128)(2,1)} %bitcast.24), channel_id=1, source_target_pairs={{0,2},{2,0},{1,3},{3,1},{4,6},{6,4},{5,7},{7,5},{8,10},{10,8},{9,1... | collective-permute-start | bytes 3145736 | tf_op jit(solution)/shard_map/ppermute | solution.py:465
  338.7 78.5 %collective-permute-start.13 = (bf16[256,2048]{1,0:T(8,128)(2,1)}, bf16[256,2048]{1,0:T(8,128)(2,1)}, u32[]{:S(2)}, u32[]{:S(2)}) collective-permute-start(bf16[256,2048]{1,0:T(8,128)(2,1)} %collective-permute-done.11), channel_id=1, source_target_pairs={{0,2},{2,0},{1,3},{3,1},{4,6},{6,4},{5,7},{7,5},{8,10},{10,8},{9,1... | collective-permute-start | bytes 3145736 | tf_op jit(solution)/shard_map/ppermute | solution.py:465
  339.2 78.0 %collective-permute-start.16 = (bf16[256,2048]{1,0:T(8,128)(2,1)}, bf16[256,2048]{1,0:T(8,128)(2,1)}, u32[]{:S(2)}, u32[]{:S(2)}) collective-permute-start(bf16[256,2048]{1,0:T(8,128)(2,1)} %collective-permute-done.14), channel_id=1, source_target_pairs={{0,2},{2,0},{1,3},{3,1},{4,6},{6,4},{5,7},{7,5},{8,10},{10,8},{9,1... | collective-permute-start | bytes 3145736 | tf_op jit(solution)/shard_map/ppermute | solution.py:465
  339.3 77.9 %collective-permute-start.17 = (bf16[256,2048]{1,0:T(8,128)(2,1)}, bf16[256,2048]{1,0:T(8,128)(2,1)}, u32[]{:S(2)}, u32[]{:S(2)}) collective-permute-start(bf16[256,2048]{1,0:T(8,128)(2,1)} %collective-permute-done.15), channel_id=1, source_target_pairs={{0,2},{2,0},{1,3},{3,1},{4,6},{6,4},{5,7},{7,5},{8,10},{10,8},{9,1... | collective-permute-start | bytes 3145736 | tf_op jit(solution)/shard_map/ppermute | solution.py:465
  516.7 45.9 %collective-permute-start.20 = (bf16[512,4096]{1,0:T(8,128)(2,1)}, bf16[512,4096]{1,0:T(8,128)(2,1)}, u32[]{:S(2)}, u32[]{:S(2)}) collective-permute-start(bf16[512,4096]{1,0:T(8,128)(2,1)} %slice.361), channel_id=1, source_target_pairs={{0,2},{2,0},{1,3},{3,1},{4,6},{6,4},{5,7},{7,5},{8,10},{10,8},{9,1... | collective-permute-start | bytes 12582920 | tf_op jit(solution)/shard_map/ppermute | solution.py:465
  519.2 31.3 %collective-permute-start.18 = (bf16[640,1024]{1,0:T(8,128)(2,1)}, bf16[640,1024]{1,0:T(8,128)(2,1)S(1)}, u32[]{:S(2)}, u32[]{:S(2)}) collective-permute-start(bf16[640,1024]{1,0:T(8,128)(2,1)} %constant_dynamic-slice_fusion.3), channel_id=1, source_target_pairs={{0,1},{1,0},{2,3},{3,2},{4,5},{5,4},{6,7},{7,6},{8,9},{9,8},{10,11... | collective-permute-start | bytes 3932168 | tf_op jit(solution)/shard_map/ppermute | solution.py:465
  569.2 33.7 %collective-permute-start.21 = (bf16[256,2048]{1,0:T(8,128)(2,1)S(1)}, bf16[256,2048]{1,0:T(8,128)(2,1)S(1)}, u32[]{:S(2)}, u32[]{:S(2)}) collective-permute-start(bf16[256,2048]{1,0:T(8,128)(2,1)S(1)} %get-tuple-element.111), channel_id=1, source_target_pairs={{0,4},{1,5},{4,0},{5,1},{2,6},{3,7},{6,2},{7,3},{8,12},{9,13},{12,... | collective-permute-start | bytes 3145736 | tf_op jit(solution)/shard_map/ppermute | solution.py:465
  569.5 33.3 %collective-permute-start.22 = (bf16[256,2048]{1,0:T(8,128)(2,1)S(1)}, bf16[256,2048]{1,0:T(8,128)(2,1)}, u32[]{:S(2)}, u32[]{:S(2)}) collective-permute-start(bf16[256,2048]{1,0:T(8,128)(2,1)S(1)} %get-tuple-element.110), channel_id=1, source_target_pairs={{0,1},{1,0},{4,5},{5,4},{2,3},{3,2},{6,7},{7,6},{8,9},{9,8},{12,13... | collective-permute-start | bytes 3145736 | tf_op jit(solution)/shard_map/ppermute | solution.py:465
  600.1 71.4 %collective-permute-start.23 = (bf16[512,4096]{1,0:T(8,128)(2,1)}, bf16[512,4096]{1,0:T(8,128)(2,1)}, u32[]{:S(2)}, u32[]{:S(2)}) collective-permute-start(bf16[512,4096]{1,0:T(8,128)(2,1)} %slice.366), channel_id=1, source_target_pairs={{0,2},{2,0},{1,3},{3,1},{4,6},{6,4},{5,7},{7,5},{8,10},{10,8},{9,1... | collective-permute-start | bytes 12582920 | tf_op jit(solution)/shard_map/ppermute | solution.py:465
  600.1 37.4 %collective-permute-start.24 = (bf16[256,2048]{1,0:T(8,128)(2,1)}, bf16[256,2048]{1,0:T(8,128)(2,1)}, u32[]{:S(2)}, u32[]{:S(2)}) collective-permute-start(bf16[256,2048]{1,0:T(8,128)(2,1)} %get-tuple-element.109), channel_id=1, source_target_pairs={{0,5},{1,4},{4,1},{5,0},{2,7},{3,6},{6,3},{7,2},{8,13},{9,12},{12,... | collective-permute-start | bytes 3145736 | tf_op jit(solution)/shard_map/ppermute | solution.py:465
  641.5 27.6 %collective-permute-start.29 = (bf16[64,2048]{1,0:T(8,128)(2,1)}, bf16[64,2048]{1,0:T(8,128)(2,1)}, u32[]{:S(2)}, u32[]{:S(2)}) collective-permute-start(bf16[64,2048]{1,0:T(8,128)(2,1)} %get-tuple-element.129), channel_id=1, source_target_pairs={{0,8},{8,0},{16,24},{24,16},{1,9},{9,1},{17,25},{25,17},{2,10},{10... | collective-permute-start | bytes 786440 | tf_op jit(solution)/shard_map/ppermute | solution.py:465
  647.7 21.6 %collective-permute-start.30 = (bf16[64,2048]{1,0:T(8,128)(2,1)}, bf16[64,2048]{1,0:T(8,128)(2,1)}, u32[]{:S(2)}, u32[]{:S(2)}) collective-permute-start(bf16[64,2048]{1,0:T(8,128)(2,1)} %get-tuple-element.131), channel_id=1, source_target_pairs={{0,16},{8,24},{16,0},{24,8},{1,17},{9,25},{17,1},{25,9},{2,18},{10... | collective-permute-start | bytes 786440 | tf_op jit(solution)/shard_map/ppermute | solution.py:465
  711.5 62.3 %collective-permute-start.25 = (bf16[512,1024]{1,0:T(8,128)(2,1)}, bf16[512,1024]{1,0:T(8,128)(2,1)}, u32[]{:S(2)}, u32[]{:S(2)}) collective-permute-start(bf16[512,1024]{1,0:T(8,128)(2,1)} %slice.370), channel_id=1, source_target_pairs={{0,2},{2,0},{1,3},{3,1},{4,6},{6,4},{5,7},{7,5},{8,10},{10,8},{9,1... | collective-permute-start | bytes 3145736 | tf_op jit(solution)/shard_map/ppermute | solution.py:465
  711.5 30.7 %collective-permute-start.28 = (bf16[640,512]{1,0:T(8,128)(2,1)S(1)}, bf16[640,512]{1,0:T(8,128)(2,1)}, u32[]{:S(2)}, u32[]{:S(2)}) collective-permute-start(bf16[640,512]{1,0:T(8,128)(2,1)S(1)} %slice.374), channel_id=1, source_target_pairs={{0,1},{1,0},{2,3},{3,2},{4,5},{5,4},{6,7},{7,6},{8,9},{9,8},{10,11... | collective-permute-start | bytes 1966088 | tf_op jit(solution)/shard_map/ppermute | solution.py:465
  711.8 63.6 %collective-permute-start.26 = (bf16[256,2048]{1,0:T(8,128)(2,1)}, bf16[256,2048]{1,0:T(8,128)(2,1)S(1)}, u32[]{:S(2)}, u32[]{:S(2)}) collective-permute-start(bf16[256,2048]{1,0:T(8,128)(2,1)} %get-tuple-element.108), channel_id=1, source_target_pairs={{0,4},{1,5},{4,0},{5,1},{2,6},{3,7},{6,2},{7,3},{8,12},{9,13},{12,... | collective-permute-start | bytes 3145736 | tf_op jit(solution)/shard_map/ppermute | solution.py:465
  712.3 63.1 %collective-permute-start.27 = (bf16[256,2048]{1,0:T(8,128)(2,1)}, bf16[256,2048]{1,0:T(8,128)(2,1)}, u32[]{:S(2)}, u32[]{:S(2)}) collective-permute-start(bf16[256,2048]{1,0:T(8,128)(2,1)} %get-tuple-element.106), channel_id=1, source_target_pairs={{0,1},{1,0},{4,5},{5,4},{2,3},{3,2},{6,7},{7,6},{8,9},{9,8},{12,13... | collective-permute-start | bytes 3145736 | tf_op jit(solution)/shard_map/ppermute | solution.py:465
  713.9 66.0 %collective-permute-start.32 = (bf16[256,2048]{1,0:T(8,128)(2,1)}, bf16[256,2048]{1,0:T(8,128)(2,1)}, u32[]{:S(2)}, u32[]{:S(2)}) collective-permute-start(bf16[256,2048]{1,0:T(8,128)(2,1)} %get-tuple-element.107), channel_id=1, source_target_pairs={{0,5},{1,4},{4,1},{5,0},{2,7},{3,6},{6,3},{7,2},{8,13},{9,12},{12,... | collective-permute-start | bytes 3145736 | tf_op jit(solution)/shard_map/ppermute | solution.py:465
  772.1 71.4 %collective-permute-start.36 = (bf16[640,1536]{1,0:T(8,128)(2,1)}, bf16[640,1536]{1,0:T(8,128)(2,1)}, u32[]{:S(2)}, u32[]{:S(2)}) collective-permute-start(bf16[640,1536]{1,0:T(8,128)(2,1)} %get-tuple-element.113), channel_id=1, source_target_pairs={{0,1},{1,0},{2,3},{3,2},{4,5},{5,4},{6,7},{7,6},{8,9},{9,8},{10,11... | collective-permute-start | bytes 5898248 | tf_op jit(solution)/shard_map/ppermute | solution.py:465
  776.4 42.1 %collective-permute-start.33 = (bf16[256,512]{1,0:T(8,128)(2,1)}, bf16[256,512]{1,0:T(8,128)(2,1)S(1)}, u32[]{:S(2)}, u32[]{:S(2)}) collective-permute-start(bf16[256,512]{1,0:T(8,128)(2,1)} %get-tuple-element.127), channel_id=1, source_target_pairs={{0,4},{1,5},{4,0},{5,1},{2,6},{3,7},{6,2},{7,3},{8,12},{9,13},{12,... | collective-permute-start | bytes 786440 | tf_op jit(solution)/shard_map/ppermute | solution.py:465
  776.8 46.8 %collective-permute-start.34 = (bf16[256,512]{1,0:T(8,128)(2,1)}, bf16[256,512]{1,0:T(8,128)(2,1)S(1)}, u32[]{:S(2)}, u32[]{:S(2)}) collective-permute-start(bf16[256,512]{1,0:T(8,128)(2,1)} %get-tuple-element.126), channel_id=1, source_target_pairs={{0,1},{1,0},{4,5},{5,4},{2,3},{3,2},{6,7},{7,6},{8,9},{9,8},{12,13... | collective-permute-start | bytes 786440 | tf_op jit(solution)/shard_map/ppermute | solution.py:465
  777.7 49.9 %collective-permute-start.35 = (bf16[256,512]{1,0:T(8,128)(2,1)}, bf16[256,512]{1,0:T(8,128)(2,1)S(1)}, u32[]{:S(2)}, u32[]{:S(2)}) collective-permute-start(bf16[256,512]{1,0:T(8,128)(2,1)} %get-tuple-element.125), channel_id=1, source_target_pairs={{0,5},{1,4},{4,1},{5,0},{2,7},{3,6},{6,3},{7,2},{8,13},{9,12},{12,... | collective-permute-start | bytes 786440 | tf_op jit(solution)/shard_map/ppermute | solution.py:465
  783.8 57.7 %collective-permute-start.49 = (bf16[64,2048]{1,0:T(8,128)(2,1)}, bf16[64,2048]{1,0:T(8,128)(2,1)}, u32[]{:S(2)}, u32[]{:S(2)}) collective-permute-start(bf16[64,2048]{1,0:T(8,128)(2,1)} %get-tuple-element.122), channel_id=1, source_target_pairs={{0,8},{8,0},{16,24},{24,16},{1,9},{9,1},{17,25},{25,17},{2,10},{10... | collective-permute-start | bytes 786440 | tf_op jit(solution)/shard_map/ppermute | solution.py:465
  818.5 23.0 %collective-permute-start.50 = (bf16[64,2048]{1,0:T(8,128)(2,1)S(1)}, bf16[64,2048]{1,0:T(8,128)(2,1)S(1)}, u32[]{:S(2)}, u32[]{:S(2)}) collective-permute-start(bf16[64,2048]{1,0:T(8,128)(2,1)S(1)} %copy-done.69), channel_id=1, source_target_pairs={{0,16},{8,24},{16,0},{24,8},{1,17},{9,25},{17,1},{25,9},{2,18},{10... | collective-permute-start | bytes 786440 | tf_op jit(solution)/shard_map/ppermute | solution.py:465
  839.4 64.5 %collective-permute-start.38 = (bf16[512,1536]{1,0:T(8,128)(2,1)}, bf16[512,1536]{1,0:T(8,128)(2,1)}, u32[]{:S(2)}, u32[]{:S(2)}) collective-permute-start(bf16[512,1536]{1,0:T(8,128)(2,1)} %slice.387), channel_id=1, source_target_pairs={{0,2},{2,0},{1,3},{3,1},{4,6},{6,4},{5,7},{7,5},{8,10},{10,8},{9,1... | collective-permute-start | bytes 4718600 | tf_op jit(solution)/shard_map/ppermute | solution.py:465
  884.6 22.9 %collective-permute-start.40 = (bf16[512,1536]{1,0:T(8,128)(2,1)}, bf16[512,1536]{1,0:T(8,128)(2,1)S(1)}, u32[]{:S(2)}, u32[]{:S(2)}) collective-permute-start(bf16[512,1536]{1,0:T(8,128)(2,1)} %slice.391), channel_id=1, source_target_pairs={{0,2},{2,0},{1,3},{3,1},{4,6},{6,4},{5,7},{7,5},{8,10},{10,8},{9,1... | collective-permute-start | bytes 4718600 | tf_op jit(solution)/shard_map/ppermute | solution.py:465
  895.7 22.2 %collective-permute-start.46 = (bf16[64,512]{1,0:T(8,128)(2,1)}, bf16[64,512]{1,0:T(8,128)(2,1)S(1)}, u32[]{:S(2)}, u32[]{:S(2)}) collective-permute-start(bf16[64,512]{1,0:T(8,128)(2,1)} %get-tuple-element.135), channel_id=1, source_target_pairs={{0,8},{8,0},{16,24},{24,16},{1,9},{9,1},{17,25},{25,17},{2,10},{10... | collective-permute-start | bytes 196616 | tf_op jit(solution)/shard_map/ppermute | solution.py:465
  907.1 24.4 %collective-permute-start.39 = (bf16[256,1536]{1,0:T(8,128)(2,1)}, bf16[256,1536]{1,0:T(8,128)(2,1)}, u32[]{:S(2)}, u32[]{:S(2)}) collective-permute-start(bf16[256,1536]{1,0:T(8,128)(2,1)} %slice.389), channel_id=1, source_target_pairs={{0,4},{1,5},{4,0},{5,1},{2,6},{3,7},{6,2},{7,3},{8,12},{9,13},{12,... | collective-permute-start | bytes 2359304 | tf_op jit(solution)/shard_map/ppermute | solution.py:465
  909.4 22.1 %collective-permute-start.41 = (bf16[256,1536]{1,0:T(8,128)(2,1)S(1)}, bf16[256,1536]{1,0:T(8,128)(2,1)}, u32[]{:S(2)}, u32[]{:S(2)}) collective-permute-start(bf16[256,1536]{1,0:T(8,128)(2,1)S(1)} %get-tuple-element.118), channel_id=1, source_target_pairs={{0,1},{1,0},{4,5},{5,4},{2,3},{3,2},{6,7},{7,6},{8,9},{9,8},{12,13... | collective-permute-start | bytes 2359304 | tf_op jit(solution)/shard_map/ppermute | solution.py:465
  909.9 38.0 %collective-permute-start.42 = (bf16[256,1536]{1,0:T(8,128)(2,1)S(1)}, bf16[256,1536]{1,0:T(8,128)(2,1)}, u32[]{:S(2)}, u32[]{:S(2)}) collective-permute-start(bf16[256,1536]{1,0:T(8,128)(2,1)S(1)} %get-tuple-element.119), channel_id=1, source_target_pairs={{0,5},{1,4},{4,1},{5,0},{2,7},{3,6},{6,3},{7,2},{8,13},{9,12},{12,... | collective-permute-start | bytes 2359304 | tf_op jit(solution)/shard_map/ppermute | solution.py:465
  928.1 44.0 %collective-permute-start.37 = (bf16[640,1024]{1,0:T(8,128)(2,1)}, bf16[640,1024]{1,0:T(8,128)(2,1)}, u32[]{:S(2)}, u32[]{:S(2)}) collective-permute-start(bf16[640,1024]{1,0:T(8,128)(2,1)} %dynamic-slice_convert_fusion), channel_id=1, source_target_pairs={{0,1},{1,0},{2,3},{3,2},{4,5},{5,4},{6,7},{7,6},{8,9},{9,8},{10,11... | collective-permute-start | bytes 3932168 | tf_op jit(solution)/shard_map/ppermute | solution.py:465
  949.9 35.6 %collective-permute-start.43 = (bf16[64,1536]{1,0:T(8,128)(2,1)S(1)}, bf16[64,1536]{1,0:T(8,128)(2,1)S(1)}, u32[]{:S(2)}, u32[]{:S(2)}) collective-permute-start(bf16[64,1536]{1,0:T(8,128)(2,1)S(1)} %get-tuple-element.132), channel_id=1, source_target_pairs={{0,8},{8,0},{16,24},{24,16},{1,9},{9,1},{17,25},{25,17},{2,10},{10... | collective-permute-start | bytes 589832 | tf_op jit(solution)/shard_map/ppermute | solution.py:465
  950.0 35.6 %collective-permute-start.44 = (bf16[64,1536]{1,0:T(8,128)(2,1)S(1)}, bf16[64,1536]{1,0:T(8,128)(2,1)S(1)}, u32[]{:S(2)}, u32[]{:S(2)}) collective-permute-start(bf16[64,1536]{1,0:T(8,128)(2,1)S(1)} %get-tuple-element.134), channel_id=1, source_target_pairs={{0,16},{8,24},{16,0},{24,8},{1,17},{9,25},{17,1},{25,9},{2,18},{10... | collective-permute-start | bytes 589832 | tf_op jit(solution)/shard_map/ppermute | solution.py:465
  951.0 34.6 %collective-permute-start.45 = (bf16[64,1536]{1,0:T(8,128)(2,1)S(1)}, bf16[64,1536]{1,0:T(8,128)(2,1)S(1)}, u32[]{:S(2)}, u32[]{:S(2)}) collective-permute-start(bf16[64,1536]{1,0:T(8,128)(2,1)S(1)} %get-tuple-element.133), channel_id=1, source_target_pairs={{0,24},{8,16},{16,8},{24,0},{1,25},{9,17},{17,9},{25,1},{2,26},{10... | collective-permute-start | bytes 589832 | tf_op jit(solution)/shard_map/ppermute | solution.py:465
  (117 other events, 3939.8 us)

commit v4 on v3

v4 whole, which is shorter than its diff:
```python
import functools
import math

import jax
import jax.numpy as jnp
from jax import lax
from jax.experimental import pallas as pl
from jax.experimental.pallas import tpu as pltpu
from jax.sharding import PartitionSpec as P

HEAD_DIM = 64
norm_eps = 1e-05
masked_value = -1e30
f32 = jnp.float32
bf16 = jnp.bfloat16
exp2_scale = math.log2(math.e) / math.sqrt(HEAD_DIM)
grad_scale = 1.0 / math.sqrt(HEAD_DIM)
gelu_scale = math.sqrt(2.0 / math.pi)
gelu_cubic = 0.044715


def dot_nn(a, b):
    return lax.dot_general(a, b, (((1,), (0,)), ((), ())), preferred_element_type=f32)


def dot_nt(a, b):
    return lax.dot_general(a, b, (((1,), (1,)), ((), ())), preferred_element_type=f32)


def dot_tn(a, b):
    return lax.dot_general(a, b, (((0,), (0,)), ((), ())), preferred_element_type=f32)


def split_heads(x):
    lane = lax.broadcasted_iota(jnp.int32, x.shape, 1)
    zero = jnp.zeros_like(x)
    return jnp.where(lane < HEAD_DIM, x, zero), jnp.where(lane >= HEAD_DIM, x, zero)


def block_rows(tree_len):
    return 256 if tree_len % 256 == 0 else 128


def attention_forward_kernel(q_ref, k_ref, v_ref, col_ref, row_ref, o_ref, lse_ref, bias):
    tree_len = q_ref.shape[0]
    rows = block_rows(tree_len)

    @pl.when(pl.program_id(0) == 0)
    def _():
        for start in range(0, tree_len, rows):
            stop = start + rows
            key_seg = row_ref[0:1, :stop]
            ok = col_ref[start:stop, 0:1] == key_seg
            ok = ok | (col_ref[start:stop, 1:2] == key_seg)
            ok = ok | (col_ref[start:stop, 2:3] == key_seg)
            i = lax.broadcasted_iota(jnp.int32, (rows, stop), 0) + start
            j = lax.broadcasted_iota(jnp.int32, (rows, stop), 1)
            bias[start:stop, :stop] = jnp.where(ok & (j <= i), 0.0, masked_value).astype(f32)

    for start in range(0, tree_len, rows):
        stop = start + rows
        queries = split_heads(q_ref[start:stop, :])
        outs = []
        for h in range(2):
            scores = dot_nt(queries[h], k_ref[:stop, :]) + bias[start:stop, :stop]
            top = jnp.max(scores, axis=1, keepdims=True)
            weights = jnp.exp2((scores - top) * exp2_scale)
            total = jnp.sum(weights, axis=1, keepdims=True)
            outs.append(dot_nn(weights.astype(bf16), v_ref[:stop, :]) / total)
            lse = jnp.broadcast_to(top * exp2_scale + jnp.log2(total), (rows, 128))
            lse_ref[0, h : h + 1, start:stop] = jnp.transpose(lse)[0:1, :]
        lane = lax.broadcasted_iota(jnp.int32, (rows, 128), 1)
        o_ref[start:stop, :] = jnp.where(lane < HEAD_DIM, outs[0], outs[1]).astype(bf16)


def attention_forward(qkv, cols, rows):
    tree_len, width = qkv.shape
    pairs = width // 384
    tile = (tree_len, 128)
    return pl.pallas_call(
        attention_forward_kernel,
        name="attention_forward",
        out_shape=(
            jax.ShapeDtypeStruct((tree_len, width // 3), bf16),
            jax.ShapeDtypeStruct((pairs, 8, tree_len), f32),
        ),
        grid=(pairs,),
        in_specs=[
            pl.BlockSpec(tile, lambda p: (0, p)),
            pl.BlockSpec(tile, lambda p: (0, pairs + p)),
            pl.BlockSpec(tile, lambda p: (0, 2 * pairs + p)),
            pl.BlockSpec(cols.shape, lambda p: (0, 0)),
            pl.BlockSpec(rows.shape, lambda p: (0, 0)),
        ],
        out_specs=(
            pl.BlockSpec(tile, lambda p: (0, p)),
            pl.BlockSpec((1, 8, tree_len), lambda p: (p, 0, 0)),
        ),
        scratch_shapes=[pltpu.VMEM((tree_len, tree_len), f32)],
        compiler_params=pltpu.CompilerParams(vmem_limit_bytes=40 << 20),
        cost_estimate=pl.CostEstimate(
            flops=int(0.6 * 2 * pairs * 4 * tree_len * tree_len * 256),
            bytes_accessed=tree_len * width * 3,
            transcendentals=pairs * tree_len * tree_len,
        ),
    )(qkv, qkv, qkv, cols, rows)


def attention_backward_kernel(
    q_ref, k_ref, v_ref, do_ref, o_ref, lse_ref, col_ref, row_ref, dx_ref, bias, split_k, dk, dv
):
    tree_len = q_ref.shape[0]
    rows = block_rows(tree_len)
    pair = pl.program_id(0)
    pairs = pl.num_programs(0)

    @pl.when(pair == 0)
    def _():
        for start in range(0, tree_len, rows):
            stop = start + rows
            key_seg = col_ref[:stop, 0:1]
            ok = row_ref[0:1, start:stop] == key_seg
            ok = ok | (row_ref[1:2, start:stop] == key_seg)
            ok = ok | (row_ref[2:3, start:stop] == key_seg)
            j = lax.broadcasted_iota(jnp.int32, (stop, rows), 0)
            i = lax.broadcasted_iota(jnp.int32, (stop, rows), 1) + start
            bias[:stop, start:stop] = jnp.where(ok & (j <= i), 0.0, masked_value).astype(f32)

    split_k[0], split_k[1] = split_heads(k_ref[...])
    dk[...] = jnp.zeros_like(dk)
    dv[...] = jnp.zeros_like(dv)
    sub = lax.broadcasted_iota(jnp.int32, (8, 128), 0)
    lane = lax.broadcasted_iota(jnp.int32, (8, 128), 1)
    own = jnp.where(lane // HEAD_DIM == sub, 1.0, 0.0).astype(f32)
    for start in range(0, tree_len, rows):
        stop = start + rows
        queries = split_heads(q_ref[start:stop, :])
        grads = split_heads(do_ref[start:stop, :])
        product = do_ref[start:stop, :].astype(f32) * o_ref[start:stop, :].astype(f32)
        row_dot = lax.dot_general(
            own,
            product,
            (((1,), (1,)), ((), ())),
            precision=lax.Precision.HIGHEST,
            preferred_element_type=f32,
        )
        probs_low = []
        grad_scores = []
        for h in range(2):
            shift = bias[:stop, start:stop] - lse_ref[0, h : h + 1, start:stop]
            probs = jnp.exp2(dot_nt(k_ref[:stop, :], queries[h]) * exp2_scale + shift)
            grad_probs = dot_nt(v_ref[:stop, :], grads[h])
            probs_low.append(probs.astype(bf16))
            grad_scores.append((probs * (grad_probs - row_dot[h : h + 1, :])).astype(bf16))
        dv[:stop, :] += dot_nn(jnp.concatenate(probs_low, 1), jnp.concatenate(grads, 0))
        dk[:stop, :] += dot_nn(jnp.concatenate(grad_scores, 1), jnp.concatenate(queries, 0))
        dq = dot_tn(grad_scores[0], split_k[0, :stop, :])
        dq = dq + dot_tn(grad_scores[1], split_k[1, :stop, :])
        dq = (dq.astype(bf16).astype(f32) * grad_scale).astype(bf16)
        dx_ref[start:stop, pl.ds(pl.multiple_of(pair * 128, 128), 128)] = dq
    dx_ref[:, pl.ds(pl.multiple_of((pairs + pair) * 128, 128), 128)] = (
        dk[...] * grad_scale
    ).astype(bf16)
    dx_ref[:, pl.ds(pl.multiple_of((2 * pairs + pair) * 128, 128), 128)] = dv[...].astype(bf16)


def attention_backward(qkv, grad, out, lse, cols, rows):
    tree_len, width = qkv.shape
    pairs = width // 384
    tile = (tree_len, 128)
    return pl.pallas_call(
        attention_backward_kernel,
        name="attention_backward",
        out_shape=jax.ShapeDtypeStruct((tree_len, width), bf16),
        grid=(pairs,),
        in_specs=[
            pl.BlockSpec(tile, lambda p: (0, p)),
            pl.BlockSpec(tile, lambda p: (0, pairs + p)),
            pl.BlockSpec(tile, lambda p: (0, 2 * pairs + p)),
            pl.BlockSpec(tile, lambda p: (0, p)),
            pl.BlockSpec(tile, lambda p: (0, p)),
            pl.BlockSpec((1, 8, tree_len), lambda p: (p, 0, 0)),
            pl.BlockSpec(cols.shape, lambda p: (0, 0)),
            pl.BlockSpec(rows.shape, lambda p: (0, 0)),
        ],
        out_specs=pl.BlockSpec((tree_len, width), lambda p: (0, 0)),
        scratch_shapes=[
            pltpu.VMEM((tree_len, tree_len), f32),
            pltpu.VMEM((2, tree_len, 128), bf16),
            pltpu.VMEM(tile, f32),
            pltpu.VMEM(tile, f32),
        ],
        compiler_params=pltpu.CompilerParams(vmem_limit_bytes=40 << 20),
        cost_estimate=pl.CostEstimate(
            flops=int(0.6 * 5 * pairs * 4 * tree_len * tree_len * 256),
            bytes_accessed=tree_len * width * 6,
            transcendentals=pairs * tree_len * tree_len,
        ),
    )(qkv, qkv, qkv, grad, out, lse, cols, rows)


def norm_parts(values):
    centered = values - jnp.mean(values, axis=-1, keepdims=True)
    scale = lax.rsqrt(jnp.mean(centered * centered, axis=-1, keepdims=True) + norm_eps)
    return centered * scale, scale


def norm_forward(values, gain, shift):
    return norm_parts(values)[0] * gain + shift


def norm_backward(values, gain, grad):
    xhat, scale = norm_parts(values)
    h = grad * gain
    inner = h - jnp.mean(h, axis=-1, keepdims=True)
    inner = inner - xhat * jnp.mean(h * xhat, axis=-1, keepdims=True)
    return scale * inner, jnp.stack([jnp.sum(grad * xhat, axis=0), jnp.sum(grad, axis=0)])


def gelu_and_slope(values):
    square = values * values
    bent = jnp.tanh(gelu_scale * values * (1.0 + gelu_cubic * square))
    half = 0.5 + 0.5 * bent
    slope = half + 2.0 * gelu_scale * values * half * (1.0 - half) * (1.0 + 3.0 * gelu_cubic * square)
    return values * half, slope


def apart(position, distance):
    bit = 1
    while bit <= distance:
        if distance & bit:
            position = position + bit - 2 * bit * (position // bit % 2)
        bit *= 2
    return position


def gather_kernel(chunks, weights, moved, *refs):
    shards, refs = refs[:weights], refs[weights:]
    tokens, segments, refs = refs[0], refs[1], refs[2:]
    tp = lax.axis_size("tp")
    depth = lax.axis_size("z")
    outs, refs = refs[: weights * tp], refs[weights * tp :]
    segments_out, refs = refs[0], refs[1:]
    tokens_out, refs = (refs[0], refs[1:]) if moved else (None, refs)
    send_sems, recv_sems, local_sems = refs
    z, y, core, x = (lax.axis_index(name) for name in ("z", "y", "core", "tp"))

    barrier = pltpu.get_barrier_semaphore()
    partners = [{"z": apart(z, k)} for k in range(1, depth)]
    partners += [{"tp": apart(x, k)} for k in range(1, tp)]
    partners += [{"y": 1 - y}, {"core": 1 - core}]
    for partner in partners:
        pl.semaphore_signal(barrier, inc=1, device_id=partner, device_id_type=pl.DeviceIdType.MESH)
    pl.semaphore_wait(barrier, len(partners))

    half = depth // 2
    first = pl.ds(z // half * half, half)
    second = pl.ds(half - z // half * half, half)
    started = []

    def copy(source, target, partner):
        slot = len(started)
        made = pltpu.make_async_remote_copy(
            src_ref=source,
            dst_ref=target,
            send_sem=send_sems.at[slot],
            recv_sem=recv_sems.at[slot],
            device_id=partner,
            device_id_type=pl.DeviceIdType.MESH,
        )
        made.start()
        started.append(made)
        return made

    crossed = []
    for k in range(1, tp):
        partner = {"tp": apart(x, k)}
        crossed.append(copy(segments, segments_out.at[k - 1], partner))
        for n in range(moved):
            source = tokens.at[n * tp + apart(x, k)]
            crossed.append(copy(source, tokens_out.at[n * (tp - 1) + k - 1], partner))

    def part(number, t, at_y, span):
        weight, low, rows = chunks[number]
        return outs[weight * tp + t].at[span, at_y, core, pl.ds(low, rows)]

    def along_z(number):
        weight, low, rows = chunks[number]
        own = shards[weight].at[pl.ds(low, rows)]
        target = outs[weight * tp].at[z, y, core, pl.ds(low, rows)]
        keep = pltpu.make_async_copy(own, target, local_sems.at[number])
        keep.start()
        return keep, [copy(own, target, {"z": apart(z, k)}) for k in range(1, depth)]

    def over(number, t, target_t, at_y, span, partner):
        return copy(part(number, t, at_y, span), part(number, target_t, at_y, span), partner)

    def to_core(number, t, at_y, span):
        crossed.append(over(number, t, t, at_y, span, {"core": 1 - core}))

    def plane_start(number, keep, sent):
        keep.wait()
        for k in range(1, half):
            sent[k - 1].wait_recv()
        over_x = [over(number, 0, k, y, first, {"tp": apart(x, k)}) for k in range(1, tp)]
        for k in range(half, depth):
            sent[k - 1].wait_recv()
        over_y = over(number, 0, 0, y, second, {"y": 1 - y})
        last = [(over(number, 0, 0, y, first, {"y": 1 - y}), 0, 1 - y, first)]
        for k in range(1, tp):
            made = over(number, 0, k, y, second, {"tp": apart(x, k)})
            last.append((made, k, y, second))
        to_core(number, 0, y, first)
        to_core(number, 0, y, second)
        return over_x, over_y, last

    def plane_turn(number, over_x, over_y, last):
        for k in range(1, tp):
            over_x[k - 1].wait_recv()
            made = over(number, k, k, y, first, {"y": 1 - y})
            last.append((made, k, 1 - y, first))
            to_core(number, k, y, first)
        over_y.wait_recv()
        for k in range(1, tp):
            made = over(number, 0, k, 1 - y, second, {"tp": apart(x, k)})
            last.append((made, k, 1 - y, second))
        to_core(number, 0, 1 - y, second)
        return last

    def plane_end(number, last):
        for made, t, at_y, span in last:
            made.wait_recv()
            to_core(number, t, at_y, span)

    count = len(chunks)
    state = {0: along_z(0)}
    for step in range(count + 2):
        if step < count:
            state[step] = plane_start(step, *state[step])
            if step + 1 < count:
                state[step + 1] = along_z(step + 1)
        if 0 <= step - 1 < count:
            state[step - 1] = plane_turn(step - 1, *state[step - 1])
        if 0 <= step - 2 < count:
            plane_end(step - 2, state[step - 2])
    for made in crossed:
        made.wait_recv()
    for made in started:
        made.wait_send()


def gather_weights(shards, pieces, tokens, segments):
    tp = lax.axis_size("tp")
    depth = lax.axis_size("z")
    moved = tokens.shape[0] // tp
    chunks = []
    for number, (shard, split) in enumerate(zip(shards, pieces)):
        rows = shard.shape[0] // split
        chunks += [(number, piece * rows, rows) for piece in range(split)]
    copies = len(chunks) * (depth + 1 + 4 * (tp - 1) + 4 * tp)
    copies += (moved + 1) * (tp - 1)
    shapes = [
        jax.ShapeDtypeStruct((depth, 2, 2) + shard.shape, shard.dtype)
        for shard in shards
        for _ in range(tp)
    ]
    sent = sum(shape.size for shape in shapes) * 2
    shapes += [jax.ShapeDtypeStruct((tp - 1,) + segments.shape, segments.dtype)]
    if moved:
        shapes += [jax.ShapeDtypeStruct((moved * (tp - 1),) + tokens.shape[1:], tokens.dtype)]
    inside = pl.BlockSpec(memory_space=pltpu.VMEM)
    outside = pl.BlockSpec(memory_space=pl.ANY)
    made = pl.pallas_call(
        functools.partial(gather_kernel, chunks, len(shards), moved),
        name="gather_weights",
        out_shape=shapes,
        in_specs=[inside] * len(shards) + [outside, inside],
        out_specs=[outside] * len(shapes),
        scratch_shapes=[
            pltpu.SemaphoreType.DMA((copies,)),
            pltpu.SemaphoreType.DMA((copies,)),
            pltpu.SemaphoreType.DMA((len(chunks),)),
        ],
        compiler_params=pltpu.CompilerParams(collective_id=0, has_side_effects=True),
        cost_estimate=pl.CostEstimate(flops=0, bytes_accessed=2 * sent, transcendentals=0),
    )(*shards, tokens, segments)
    count = len(shards) * tp
    full = [array.reshape(-1, array.shape[-1]) for array in made[:count]]
    full = [full[number * tp : (number + 1) * tp] for number in range(len(shards))]
    crossed = made[count:]
    came = [crossed[1][number] for number in range(moved * (tp - 1))] if moved else []
    return full, [crossed[0][k] for k in range(tp - 1)], came


def send(values, axes, distance):
    count = 1
    for axis in (axes,) if isinstance(axes, str) else axes:
        count *= lax.axis_size(axis)
    return lax.ppermute(values, axes, [(s, s ^ distance) for s in range(count)])


def after(values, *others):
    return lax.optimization_barrier((values,) + others)[0]


def pick(pieces, position):
    chosen = pieces[0]
    for number in range(1, len(pieces)):
        chosen = jnp.where(position == number, pieces[number], chosen)
    return chosen


def exchange_tp(pieces):
    return pieces[:1] + [send(pieces[k], "tp", k) for k in range(1, len(pieces))]


def in_place_order(pieces):
    here = lax.axis_index("tp")
    return jnp.concatenate([pick(pieces, here ^ s) for s in range(len(pieces))], axis=0)


def sum_everywhere(values):
    for axes in (("y", "tp"), ("z",), ("core",)):
        count = 1
        for axis in axes:
            count *= lax.axis_size(axis)
        values = sum([send(values, axes, k) for k in range(1, count)], values)
    return values


def block_at(values, axis, index):
    return lax.dynamic_index_in_dim(values, index, axis, keepdims=False)


def scatter_core(part):
    depth, core = lax.axis_size("z"), lax.axis_index("core")
    blocks = part.reshape(depth, 2, 2, -1, part.shape[1])
    came = send(block_at(blocks, 2, 1 - core), "core", 1)
    return (block_at(blocks, 2, core).astype(f32) + came.astype(f32)).astype(bf16)


def scatter_plane(parts):
    y = lax.axis_index("y")
    straight, across = [block_at(parts[0], 1, y)], []
    for t in range(len(parts)):
        for j in range(2):
            if t or j:
                came = send(block_at(parts[t], 1, y ^ j), ("y", "tp"), j * len(parts) + t)
                (across if t and j else straight).append(came)
    return straight, across


def total(pieces):
    return sum([piece.astype(f32) for piece in pieces[1:]], pieces[0].astype(f32)).astype(bf16)


def scatter_z(part):
    z = lax.axis_index("z")
    made = block_at(part, 0, z).astype(f32)
    for k in range(1, part.shape[0]):
        made = made + send(block_at(part, 0, z ^ k), "z", k).astype(f32)
    return made


def segment_tables(segments, parents):
    labels = jnp.arange(parents.shape[0], dtype=jnp.int32)
    up = lambda seg: jnp.sum(jnp.where(seg[:, None] == labels, parents, 0), axis=1)
    parent = up(segments)
    table = jnp.stack([segments, parent, up(parent)])
    return jnp.pad(table.T, ((0, 0), (0, 5))), jnp.pad(table, ((0, 5), (0, 0)))


def on_device(
    tokens, segments, parents, norm_gains, norm_biases, w_qkv, w_out, w_up, w_down, cotangent
):
    tp = lax.axis_size("tp")
    here = lax.axis_index("tp")
    micro = tokens.shape[0]
    own_rows = tokens.shape[2]
    width = tokens.shape[3]
    head_width = w_out.shape[0]
    tree_len = own_rows * tp
    whole = micro // tp
    shared = list(range(whole * tp, micro))
    share_count = len(shared)
    halves = range(tp)
    split = whole * tree_len

    def outgoing(values):
        return [block_at(values, 0, n * tp + (here ^ k)) for n in range(whole) for k in range(1, tp)]

    def tree_rows(values, came):
        rows = []
        for n in range(whole):
            near = [block_at(values, 0, n * tp + here)]
            rows.append(in_place_order(near + came[n * (tp - 1) : (n + 1) * (tp - 1)]))
        return lax.optimization_barrier(jnp.concatenate(rows + [values[m] for m in shared], axis=0))

    def rows_back(values):
        trees = values.reshape(micro, own_rows, width)
        back = []
        for n in range(whole):
            pieces = [block_at(trees, 0, n * tp + here)]
            for k in range(1, tp):
                low = block_at(trees, 0, n * tp + (here ^ k)).astype(bf16)
                pieces.append(send(low, "tp", k).astype(values.dtype))
            back += [pick(pieces, here ^ s) for s in halves]
        return jnp.stack(back + [trees[m] for m in shared])[:, None]

    def share_rows(values, k):
        return lax.dynamic_slice_in_dim(values, (here ^ k) * own_rows, own_rows)

    shard_qkv = w_qkv.reshape(w_qkv.shape[0], -1)
    (full_qkv, full_out, full_up, full_down), seg_came, tokens_came = gather_weights(
        [shard_qkv, w_out.T, w_up, w_down.T], [4, 1, 4, 4], tokens[:, 0], segments[:, 0]
    )
    seg_came = [segments[:, 0]] + seg_came
    seg_all = jnp.concatenate([pick(seg_came, here ^ s) for s in halves], axis=1)
    x = tree_rows(tokens[:, 0], tokens_came).astype(f32)
    whole_tables = []
    for n in range(whole):
        seg = pick([seg_all[n * tp + s] for s in halves], here)
        par = pick([parents[n * tp + s, 0] for s in halves], here)
        whole_tables.append(segment_tables(seg, par))
    share_tables = [segment_tables(seg_all[m], parents[m, 0]) for m in shared]

    normed = norm_forward(x, norm_gains[0], norm_biases[0]).astype(bf16)
    share_qkv = [dot_nn(normed[split:], w).astype(bf16) for w in full_qkv]
    whole_qkv = [dot_nn(normed[:split], w).astype(bf16) for w in full_qkv] if whole else []
    share_calls = []
    for n in range(share_count):
        cut = slice(n * own_rows, (n + 1) * own_rows)
        share_calls.append(in_place_order(exchange_tp([part[cut] for part in share_qkv])))
    whole_out = [[] for _ in halves]
    share_out = [[] for _ in halves]
    saved = {}
    for n in range(whole):
        for t in halves:
            qkv = whole_qkv[t][n * tree_len : (n + 1) * tree_len]
            out, lse = attention_forward(qkv, *whole_tables[n])
            saved[n, t] = (qkv, out, lse)
            whole_out[t].append(out)
    share_calls = [after(call, *whole_out[0]) for call in share_calls]
    for n in range(share_count):
        out, lse = attention_forward(share_calls[n], *share_tables[n])
        saved[n] = (share_calls[n], out, lse)
        parts = exchange_tp([share_rows(out, k) for k in halves])
        for t in halves:
            share_out[t].append(parts[t])
    attended = [jnp.concatenate(whole_out[t] + share_out[t], axis=0) for t in halves]
    cotangent = after(cotangent[:, 0], *attended)
    cotangent_came = [send(piece, "tp", n % (tp - 1) + 1) for n, piece in enumerate(outgoing(cotangent))]
    branch_a = sum(dot_nt(attended[t], full_out[t]) for t in halves)
    residual = x + norm_forward(branch_a, norm_gains[1], norm_biases[1])

    normed_f = norm_forward(residual, norm_gains[2], norm_biases[2]).astype(bf16)
    hidden = []
    slope = []
    for t in halves:
        values, bent = gelu_and_slope(dot_nn(normed_f, full_up[t]))
        values, bent = lax.optimization_barrier((values.astype(bf16), bent.astype(bf16)))
        hidden.append(values)
        slope.append(bent)
    branch_f = sum(dot_nt(hidden[t], full_down[t]) for t in halves)
    out = (residual + norm_forward(branch_f, norm_gains[3], norm_biases[3])).astype(bf16)
    out_rows = rows_back(out)

    grad_out = tree_rows(cotangent, cotangent_came).astype(f32)
    grad_branch_f, sums_3 = norm_backward(branch_f, norm_gains[3], grad_out)
    grad_branch_f = grad_branch_f.astype(bf16)
    core_down = [scatter_core(dot_tn(grad_branch_f, hidden[t]).astype(bf16)) for t in halves]
    grad_up = [
        (dot_nn(grad_branch_f, full_down[t]) * slope[t].astype(f32)).astype(bf16) for t in halves
    ]
    grad_up = [after(values, *core_down) for values in grad_up]
    straight_down, across_down = scatter_plane(core_down)
    dw_up = [dot_tn(normed_f, grad_up[t]).astype(bf16) for t in halves]
    core_up = [scatter_core(part) for part in dw_up]
    ready = [*dw_up, *straight_down]
    grad_normed_f = sum(dot_nt(after(grad_up[t], *ready), full_up[t]) for t in halves)
    grad_part, sums_2 = norm_backward(residual, norm_gains[2], grad_normed_f)
    grad_residual = grad_out + grad_part

    grad_branch_a, sums_1 = norm_backward(branch_a, norm_gains[1], grad_residual)
    grad_branch_a = after(grad_branch_a.astype(bf16), *core_up, *across_down)
    z_down = scatter_z(total(straight_down + across_down))
    straight_up, across_up = scatter_plane(core_up)
    share_grad = [dot_nn(grad_branch_a[split:], w).astype(bf16) for w in full_out]
    whole_grad = [dot_nn(grad_branch_a[:split], w).astype(bf16) for w in full_out] if whole else []
    share_do = []
    for n in range(share_count):
        cut = slice(n * own_rows, (n + 1) * own_rows)
        share_do.append(in_place_order(exchange_tp([part[cut] for part in share_grad])))
    core_out = [scatter_core(dot_tn(grad_branch_a, part).astype(bf16)) for part in attended]
    grad_qkv = [[] for _ in halves]
    share_parts = [[] for _ in halves]

    def whole_backward(t, *others):
        for n in range(whole):
            qkv, att, lse = saved[n, t]
            do = whole_grad[t][n * tree_len : (n + 1) * tree_len]
            made = attention_backward(qkv, after(do, *others), att, lse, *whole_tables[n])
            grad_qkv[t].append(made)
        return grad_qkv[t]

    made = []
    for t in range(1, tp):
        made += whole_backward(t)
    for n in range(share_count):
        qkv, att, lse = saved[n]
        do = after(share_do[n], z_down, *made)
        dx = attention_backward(qkv, do, att, lse, *share_tables[n])
        made = [dx]
        parts = exchange_tp([share_rows(dx, k) for k in halves])
        for t in halves:
            share_parts[t].append(parts[t])
    made = whole_backward(0, *core_out, *straight_up, *made)
    straight_out, across_out = scatter_plane(core_out)
    ready = [*across_up, *straight_out, *across_out, *made]
    grad_qkv = [after(jnp.concatenate(grad_qkv[t] + share_parts[t], axis=0), *ready) for t in halves]
    z_up = scatter_z(total(straight_up + across_up))
    z_out = scatter_z(total(straight_out + across_out))
    dw_qkv = [dot_tn(normed, grad_qkv[t]).astype(bf16) for t in halves]
    straight_qkv, across_qkv = scatter_plane([scatter_core(part) for part in dw_qkv])
    z_qkv = scatter_z(total(straight_qkv + across_qkv))
    grad_normed = sum(dot_nt(after(grad_qkv[t], *dw_qkv), full_qkv[t]) for t in halves)
    grad_part, sums_0 = norm_backward(x, norm_gains[0], grad_normed)
    input_rows = rows_back(grad_residual + grad_part)
    sums = jnp.concatenate([sums_0, sums_1, sums_2, sums_3])
    sums = sum_everywhere(sums).reshape(4, 2, width)
    return (
        out_rows,
        input_rows,
        z_qkv.reshape(w_qkv.shape),
        z_out.T,
        z_up,
        z_down.T,
        sums[:, 0],
        sums[:, 1],
    )


def solution(mesh):
    groups, tp = mesh.devices.shape
    fine = jax.sharding.Mesh(mesh.devices.reshape(groups // 4, 2, 2, tp), ("z", "y", "core", "tp"))
    fsdp = ("z", "y", "core")
    in_specs = (
        P(None, fsdp, "tp", None),
        P(None, fsdp, "tp"),
        P(None, fsdp, None),
        P(),
        P(),
        P(fsdp, None, "tp"),
        P("tp", fsdp),
        P(fsdp, "tp"),
        P("tp", fsdp),
        P(None, fsdp, "tp", None),
    )
    out_specs = (
        P(None, fsdp, "tp", None),
        P(None, fsdp, "tp", None),
        P(fsdp, None, "tp"),
        P("tp", fsdp),
        P(fsdp, "tp"),
        P("tp", fsdp),
        P(),
        P(),
    )
    return jax.shard_map(
        on_device, mesh=fine, in_specs=in_specs, out_specs=out_specs, check_vma=False
    )
```

time: 993 us -> 911 us (0.917)
  local copies, waits for them, and re-layouts: 107 us -> 45.2 us
  matrix products: 293 us -> 254 us
  waiting for transfers between devices: 139 us -> 166 us
  other arithmetic: 111 us -> 87.8 us
  Pallas kernels: 267 us -> 288 us
    slice x33 -> x4, local copies, waits for them, and re-layouts: 42.3 us -> 2.6 us  [the longest x2 1.39 us: rows_back(): return jnp.stack(back + [trees[m] for m in shared])[:, None]]
    ppermute x59 -> x46, waiting for transfers between devices: 139 us -> 166 us  [send(): return lax.ppermute(values, axes, [(s, s ^ distance) for s in range(count)])]
    pallas_call x5 -> x1, Pallas kernels: 123 us -> 143 us  [gather_weights(): pl.pallas_call(functools.partial(gather_kernel, chunks, len(shards), move...]
    dot_general x5 -> x8, matrix products: 90 us -> 70.1 us  [dot_tn(): lax.dot_general(a, b, (((0,), (0,)), ((), ())), preferred_element_type=f32)]
    dot_general x2 -> x0, local copies, waits for them, and re-layouts: 18.2 us -> none  [dot_nt(): lax.dot_general(a, b, (((1,), (1,)), ((), ())), preferred_element_type=f32)]
    squeeze x0 -> x22, local copies, waits for them, and re-layouts: none -> 16.9 us  [the longest x21 15.5 us: block_at(): return lax.dynamic_index_in_dim(values, index, axis, keepdims=False)]
    dot_general x5 -> x8, matrix products: 103 us -> 90.2 us  [dot_nt(): lax.dot_general(a, b, (((1,), (1,)), ((), ())), preferred_element_type=f32)]
    ppermute x59 -> x46, starting transfers between devices: 67.6 us -> 59 us  [send(): return lax.ppermute(values, axes, [(s, s ^ distance) for s in range(count)])]
  transfers between devices with their start and end apart: 59 -> 46, of which waited for: 13 -> 17; matrix products, arithmetic and copies ran while one was open for 36% -> 26% of each run, Pallas kernels for 19% -> 14%
where the time goes in v4:
time: 911 us; the launch traced here: 903 us
  Pallas kernels  288 us (32%)
  matrix products  254 us (28%)
  waiting for transfers between devices  166 us (18%)
  other arithmetic  87.8 us (10%)
  starting transfers between devices  59 us (6%)
  local copies, waits for them, and re-layouts  45.2 us (5%)
    ppermute x46, waiting for transfers between devices, send(): return lax.ppermute(values, axes, [(s, s ^ distance) for s in range(count)])  166 us
    pallas_call x1, Pallas kernels, gather_weights(): pl.pallas_call(functools.partial(gather_kernel, chunks, len(shards), move...  143 us
    dot_general x12, matrix products, dot_nn(): lax.dot_general(a, b, (((1,), (0,)), ((), ())), preferred_element_type=f32)  93.5 us
    dot_general x8, matrix products, dot_nt(): lax.dot_general(a, b, (((1,), (1,)), ((), ())), preferred_element_type=f32)  90.2 us
    pallas_call x3, Pallas kernels, attention_backward(): pl.pallas_call(attention_backward_kernel, name='attention_backward', out_...  80.1 us
    dot_general x8, matrix products, dot_tn(): lax.dot_general(a, b, (((0,), (0,)), ((), ())), preferred_element_type=f32)  70.1 us
    pallas_call x3, Pallas kernels, attention_forward(): pl.pallas_call(attention_forward_kernel, name='attention_forward', out_sh...  64.7 us
    ppermute x46, starting transfers between devices, send(): return lax.ppermute(values, axes, [(s, s ^ distance) for s in range(count)])  59 us
  transfers between devices with their start and end apart: 46, of which 17 were waited for; matrix products, arithmetic and copies ran while one was open for 26% of the time, Pallas kernels for 14%

profile of v4, /device:TPU:0, one launch (start us, length us, event | category | flops | bytes accessed | tf_op | source)
XLA Modules:
  0.0 902.6 jit_solution(12698399957974758932)
XLA Ops:
  5.0 143.2 %gather_weights.1 = (bf16[4,2,2,64,1536]{4,3,2,1,0:T(8,128)(2,1)}, bf16[4,2,2,64,1536]{4,3,2,1,0:T(8,128)(2,1)}, bf16[4,2,2,64,512]{4,3,2,1,0:T(8,128)(2,1)}, bf...) custom-call(bf16[64,1536]{1,0:T(8,128)(2,1)} %bitcast.312, ...), custom_call_target="tpu_custom_call" | custom-call | bytes 50331648 | tf_op jit(solution)/shard_map/gather_weights/pallas_call | solution.py:373
  159.6 5.7 convolution_convert_fusion.1.q_ref.k_ref.v_ref
  168.1 21.5 %attention_forward.3 = (bf16[1280,512]{1,0:T(8,128)(2,1)S(1)}, f32[4,8,1280]{2,1,0:T(8,128)S(1)}) custom-call(bf16[1280,1536]{1,0:T(8,128)(2,1)S(1)} %copy-done.8, bf16[1280,1536]{1,0:T(8,128)(2,1)S(1)} %copy-done.8, bf16[1280,1536]{1,0:T(8,128)(2,1)S(1)} %copy-done.8, s32[1280,8]{1,0:T(8,128)S(1)} %pad.14.clone.col_ref, s32[8,1280]{1,0:T(8,128)S(1)} %pad.15.row_ref), custom_call_target="tpu_custom_call" | custom-call | flops 8053063680 | bytes 5898240 | tf_op jit(solution)/shard_map/attention_forward/pallas_call | solution.py:80
  190.1 6.9 convolution_convert_fusion.q_ref.k_ref.v_ref
  197.0 21.7 %attention_forward.5 = (bf16[1280,512]{1,0:T(8,128)(2,1)S(1)}, f32[4,8,1280]{2,1,0:T(8,128)S(1)}) custom-call(bf16[1280,1536]{1,0:T(8,128)(2,1)S(1)} %convolution_convert_fusion.q_ref.k_ref.v_ref, bf16[1280,1536]{1,0:T(8,128)(2,1)S(1)} %convolution_convert_fusion.q_ref.k_ref.v_ref, bf16[1280,1536]{1,0:T(8,128)(2,1)S(1)} %convolution_convert_fusion.q_ref.k_ref.v_ref, ...), custom_call_target="tpu_custom_call" | custom-call | flops 8053063680 | bytes 5898240 | tf_op jit(solution)/shard_map/attention_forward/pallas_call | solution.py:80
  218.8 4.6 broadcast_select_fusion.1
  223.7 21.5 %attention_forward.4 = (bf16[1280,512]{1,0:T(8,128)(2,1)S(1)}, f32[4,8,1280]{2,1,0:T(8,128)S(1)}) custom-call(bf16[1280,1536]{1,0:T(8,128)(2,1)S(1)} %pad_maximum_fusion.3.q_ref.k_ref.v_ref, bf16[1280,1536]{1,0:T(8,128)(2,1)S(1)} %pad_maximum_fusion.3.q_ref.k_ref.v_ref, bf16[1280,1536]{1,0:T(8,128)(2,1)S(1)} %pad_maximum_fusion.3.q_ref.k_ref.v_ref, ...), custom_call_target="tpu_custom_call" | custom-call | flops 8053063680 | bytes 5898240 | tf_op jit(solution)/shard_map/attention_forward/pallas_call | solution.py:80
  249.4 13.1 %collective-permute-done.1 = bf16[640,512]{1,0:T(8,128)(2,1)S(1)} collective-permute-done((bf16[640,512]{1,0:T(8,128)(2,1)S(1)}, bf16[640,512]{1,0:T(8,128)(2,1)S(1)}, u32[]{:S(2)}, u32[]{:S(2)}) %collective-permute-start.1) | collective-permute-done | bytes 655392 | tf_op jit(solution)/shard_map/ppermute | solution.py:399
  266.1 3.9 copy-done.15
  279.6 18.2 %add_convert_fusion = (bf16[1920,2048]{1,0:T(8,128)(2,1)}, bf16[1920,2048]{1,0:T(8,128)(2,1)}) fusion(bf16[1920,1024]{1,0:T(8,128)(2,1)S(1)} %add_convert_fusion.3, bf16[1024,2048]{1,0:T(8,128)(2,1)S(1)} %bitcast.346), kind=kOutput, calls=%fused_computation.2 | convolution fusion | flops 8123842560 | bytes 23855104 | tf_op jit(solution)/shard_map/dot_general | solution.py:23
  297.8 20.4 %add_convert_fusion.1 = (bf16[1920,2048]{1,0:T(8,128)(2,1)}, bf16[1920,2048]{1,0:T(8,128)(2,1)}) fusion(bf16[1920,1024]{1,0:T(8,128)(2,1)S(1)} %add_convert_fusion.3, bf16[1024,2048]{1,0:T(8,128)(2,1)} %bitcast.344), kind=kOutput, calls=%fused_computation.5 | convolution fusion | flops 8123842560 | bytes 23855104 | tf_op jit(solution)/shard_map/dot_general | solution.py:23
  320.4 13.0 %fusion.67 = f32[1920,1024]{1,0:T(8,128)} fusion(bf16[1920,2048]{1,0:T(8,128)(2,1)} %get-tuple-element.52, bf16[1024,2048]{1,0:T(8,128)(2,1)S(1)} %bitcast.349), kind=kOutput, calls=%fused_computation.244 | convolution fusion | flops 8053063680 | bytes 19922944 | tf_op jit(solution)/shard_map/dot_general | solution.py:27
  333.4 18.3 %fusion.66 = (f32[1920]{0:T(1024)S(1)}, f32[1920,1024]{1,0:T(8,128)S(1)}) fusion(f32[1920,1024]{1,0:T(8,128)} %fusion.67, bf16[1920,2048]{1,0:T(8,128)(2,1)} %get-tuple-element.55, bf16[1024,2048]{1,0:T(8,128)(2,1)} %bitcast.350), kind=kOutput, calls=%fused_computation.243 | convolution fusion | flops 8056993792 | bytes 27794944 | tf_op jit(solution)/shard_map/dot_general | solution.py:27
  355.3 4.8 fusion.21
  360.1 4.8 fusion.19
  365.0 13.0 %convolution_convert_fusion.6 = bf16[1024,2048]{1,0:T(8,128)(2,1)S(1)} fusion(bf16[1920,1024]{1,0:T(8,128)(2,1)S(1)} %get-tuple-element.133, bf16[1920,2048]{1,0:T(8,128)(2,1)} %get-tuple-element.55), kind=kOutput, calls=%fused_computation.76 | convolution fusion | flops 8055160832 | bytes 15990784 | tf_op jit(solution)/shard_map/dot_general | solution.py:31
  378.0 11.6 %convolution_convert_fusion.7 = bf16[1024,2048]{1,0:T(8,128)(2,1)S(1)} fusion(bf16[1920,1024]{1,0:T(8,128)(2,1)S(1)} %get-tuple-element.133, bf16[1920,2048]{1,0:T(8,128)(2,1)} %get-tuple-element.52), kind=kOutput, calls=%fused_computation.77 | convolution fusion | flops 8055160832 | bytes 15990784 | tf_op jit(solution)/shard_map/dot_general | solution.py:31
  393.3 13.7 %multiply_convert_fusion = bf16[1920,2048]{1,0:T(8,128)(2,1)} fusion(bf16[1920,2048]{1,0:T(8,128)(2,1)} %get-tuple-element.60, bf16[1920,1024]{1,0:T(8,128)(2,1)S(1)} %copy-done.35, bf16[1024,2048]{1,0:T(8,128)(2,1)} %bitcast.351), kind=kOutput, calls=%fused_computation | convolution fusion | flops 8064860160 | bytes 23855104 | tf_op jit(solution)/shard_map/dot_general | solution.py:23
  409.4 13.2 %multiply_convert_fusion.1 = bf16[1920,2048]{1,0:T(8,128)(2,1)} fusion(bf16[1920,2048]{1,0:T(8,128)(2,1)} %get-tuple-element.58, bf16[1920,1024]{1,0:T(8,128)(2,1)S(1)} %copy-done.35, bf16[1024,2048]{1,0:T(8,128)(2,1)} %bitcast.348), kind=kOutput, calls=%fused_computation.1 | convolution fusion | flops 8064860160 | bytes 23855104 | tf_op jit(solution)/shard_map/dot_general | solution.py:23
  427.1 11.7 %convolution_convert_fusion.4 = bf16[1024,2048]{1,0:T(8,128)(2,1)S(1)} fusion(bf16[1920,1024]{1,0:T(8,128)(2,1)S(1)} %copy-done.39, bf16[1920,2048]{1,0:T(8,128)(2,1)} %multiply_convert_fusion), kind=kOutput, calls=%fused_computation.74 | convolution fusion | flops 8055160832 | bytes 15990784 | tf_op jit(solution)/shard_map/dot_general | solution.py:31
  444.9 10.0 %convolution_convert_fusion.5 = bf16[1024,2048]{1,0:T(8,128)(2,1)S(1)} fusion(bf16[1920,1024]{1,0:T(8,128)(2,1)S(1)} %copy-done.39, bf16[1920,2048]{1,0:T(8,128)(2,1)S(1)} %bitcast.362), kind=kOutput, calls=%fused_computation.75 | convolution fusion | flops 8055160832 | bytes 15990784 | tf_op jit(solution)/shard_map/dot_general | solution.py:31
  458.5 9.9 %collective-permute-done.10 = bf16[4,64,2048]{2,1,0:T(8,128)(2,1)S(1)} collective-permute-done((bf16[4,64,2048]{2,1,0:T(8,128)(2,1)S(1)}, bf16[4,64,2048]{2,1,0:T(8,128)(2,1)S(1)}, u32[]{:S(2)}, u32[]{:S(2)}) %collective-permute-start.10) | collective-permute-done | bytes 1048608 | tf_op jit(solution)/shard_map/ppermute | solution.py:399
  468.4 21.7 %collective-permute-done.7 = bf16[4,64,2048]{2,1,0:T(8,128)(2,1)S(1)} collective-permute-done((bf16[4,64,2048]{2,1,0:T(8,128)(2,1)S(1)}, bf16[4,64,2048]{2,1,0:T(8,128)(2,1)S(1)}, u32[]{:S(2)}, u32[]{:S(2)}) %collective-permute-start.7) | collective-permute-done | bytes 1048608 | tf_op jit(solution)/shard_map/ppermute | solution.py:399
  490.9 11.1 %fusion.68 = f32[1920,1024]{1,0:T(8,128)} fusion(bf16[1920,2048]{1,0:T(8,128)(2,1)S(1)} %bitcast.364, bf16[1024,2048]{1,0:T(8,128)(2,1)S(1)} %bitcast.347), kind=kOutput, calls=%fused_computation.245 | convolution fusion | flops 8053063680 | bytes 19922944 | tf_op jit(solution)/shard_map/dot_general | solution.py:27
  502.1 21.2 %multiply_reduce_fusion = (f32[1024]{0:T(1024)}, f32[1920]{0:T(1024)S(1)}, f32[1920]{0:T(1024)S(1)}, f32[1024]{0:T(1024)}, f32[1920,1024]{1,0:T(8,128)}) fusion(f32[1920,1024]{1,0:T(8,128)} %copy-done.13, f32[1920]{0:T(1024)S(1)} %copy-done.60, f32[1920]{0:T(1024)S(1)} %copy-done.56, f32[1024]{0:T(1024)S(1)} %bitcast.328, f32[1920,1024]{1,0:T(8,128)} %fusion.68, ...), kind=kOutput, calls=%fused_computation.38 | convolution fusion | flops 8072718336 | bytes 35694592 | tf_op jit(solution)/shard_map/dot_general | solution.py:27
  523.3 13.1 %multiply_reduce_fusion.1 = (f32[1024]{0:T(1024)}, f32[1920]{0:T(1024)S(1)}, f32[1920]{0:T(1024)S(1)}, f32[1024]{0:T(1024)}, f32[1920,1024]{1,0:T(8,128)S(1)}) fusion(f32[1920,1024]{1,0:T(8,128)} %copy-done.12, f32[1920]{0:T(1024)S(1)} %copy-done.54, f32[1920]{0:T(1024)S(1)} %copy-done.50, f32[1024]{0:T(1024)S(1)} %bitcast.319, ...), kind=kLoop, calls=%fused_computation.39 | loop fusion | flops 35383552 | bytes 35467264 | tf_op jit(solution)/shard_map/reduce_sum | solution.py:217
  541.0 4.0 multiply_convert_fusion.4
  545.0 4.2 collective-permute-done.16
  549.1 9.4 %collective-permute-done.17 = bf16[64,2048]{1,0:T(8,128)(2,1)S(1)} collective-permute-done((bf16[64,2048]{1,0:T(8,128)(2,1)S(1)}, bf16[64,2048]{1,0:T(8,128)(2,1)S(1)}, u32[]{:S(2)}, u32[]{:S(2)}) %collective-permute-start.17) | collective-permute-done | bytes 262176 | tf_op jit(solution)/shard_map/ppermute | solution.py:399
  580.9 26.6 %attention_backward.3 = bf16[1280,1536]{1,0:T(8,128)(2,1)S(1)} custom-call(bf16[1280,1536]{1,0:T(8,128)(2,1)S(1)} %copy-done.11, bf16[1280,1536]{1,0:T(8,128)(2,1)S(1)} %copy-done.11, bf16[1280,1536]{1,0:T(8,128)(2,1)S(1)} %copy-done.11, bf16[1280,512]{1,0:T(8,128)(2,1)S(1)} %convolution_convert_fusion.10.do_ref, bf16[1280,512]{1,0:T(8,128)(2,1)S(1)} %copy-done.5, ...), custom_call_target="tpu_custom_call" | custom-call | flops 20132659200 | bytes 11796480 | tf_op jit(solution)/shard_map/attention_backward/pallas_call | solution.py:171
  616.0 26.9 %attention_backward.4 = bf16[1280,1536]{1,0:T(8,128)(2,1)S(1)} custom-call(bf16[1280,1536]{1,0:T(8,128)(2,1)S(1)} %copy-done.1, bf16[1280,1536]{1,0:T(8,128)(2,1)S(1)} %copy-done.1, bf16[1280,1536]{1,0:T(8,128)(2,1)S(1)} %copy-done.1, bf16[1280,512]{1,0:T(8,128)(2,1)S(1)} %pad_maximum_fusion.6.do_ref, bf16[1280,512]{1,0:T(8,128)(2,1)S(1)} %copy-done.3, ...), custom_call_target="tpu_custom_call" | custom-call | flops 20132659200 | bytes 11796480 | tf_op jit(solution)/shard_map/attention_backward/pallas_call | solution.py:171
  648.1 19.0 %collective-permute-done.20 = bf16[4,64,512]{2,1,0:T(8,128)(2,1)S(1)} collective-permute-done((bf16[4,64,512]{2,1,0:T(8,128)(2,1)S(1)}, bf16[4,64,512]{2,1,0:T(8,128)(2,1)S(1)}, u32[]{:S(2)}, u32[]{:S(2)}) %collective-permute-start.20) | collective-permute-done | bytes 262176 | tf_op jit(solution)/shard_map/ppermute | solution.py:399
  670.9 26.6 %attention_backward.5 = bf16[1280,1536]{1,0:T(8,128)(2,1)S(1)} custom-call(bf16[1280,1536]{1,0:T(8,128)(2,1)S(1)} %copy-done.9, bf16[1280,1536]{1,0:T(8,128)(2,1)S(1)} %copy-done.9, bf16[1280,1536]{1,0:T(8,128)(2,1)S(1)} %copy-done.9, bf16[1280,512]{1,0:T(8,128)(2,1)S(1)} %convolution_convert_fusion.11.do_ref, bf16[1280,512]{1,0:T(8,128)(2,1)S(1)} %copy-done.7, ...), custom_call_target="tpu_custom_call" | custom-call | flops 20132659200 | bytes 11796480 | tf_op jit(solution)/shard_map/attention_backward/pallas_call | solution.py:171
  697.5 4.6 pad_maximum_fusion
  702.1 9.1 %convolution_convert_fusion.3 = bf16[1024,1536]{1,0:T(8,128)(2,1)S(1)} fusion(bf16[1920,1024]{1,0:T(8,128)(2,1)S(1)} %copy-done.37, bf16[1920,1536]{1,0:T(8,128)(2,1)} %pad_maximum_fusion), kind=kOutput, calls=%fused_computation.73 | convolution fusion | flops 6041370624 | bytes 12976128 | tf_op jit(solution)/shard_map/dot_general | solution.py:31
  714.8 7.0 collective-permute-start.33
  736.5 13.9 %collective-permute-done.37 = bf16[64,2048]{1,0:T(8,128)(2,1)S(1)} collective-permute-done((bf16[64,2048]{1,0:T(8,128)(2,1)S(1)}, bf16[64,2048]{1,0:T(8,128)(2,1)S(1)}, u32[]{:S(2)}, u32[]{:S(2)}) %collective-permute-start.37) | collective-permute-done | bytes 262176 | tf_op jit(solution)/shard_map/ppermute | solution.py:399
  754.4 4.7 collective-permute-done.23
  761.1 10.0 %convolution_convert_fusion.2 = bf16[1024,1536]{1,0:T(8,128)(2,1)} fusion(bf16[1920,1024]{1,0:T(8,128)(2,1)} %copy-done.36, bf16[1920,1536]{1,0:T(8,128)(2,1)S(1)} %pad_maximum_fusion.1), kind=kOutput, calls=%fused_computation.72 | convolution fusion | flops 6041370624 | bytes 12976128 | tf_op jit(solution)/shard_map/dot_general | solution.py:31
  771.2 9.1 %fusion.69 = f32[1920,1024]{1,0:T(8,128)} fusion(bf16[1920,1536]{1,0:T(8,128)(2,1)S(1)} %bitcast.289, bf16[1024,1536]{1,0:T(8,128)(2,1)S(1)} %bitcast.357), kind=kOutput, calls=%fused_computation.246 | convolution fusion | flops 6039797760 | bytes 16908288 | tf_op jit(solution)/shard_map/dot_general | solution.py:27
  780.4 12.8 %fusion.15 = (f32[1024]{0:T(1024)S(1)}, f32[1920]{0:T(1024)S(1)}, f32[1920]{0:T(1024)S(1)}, f32[1024]{0:T(1024)S(1)}, f32[1920,1024]{1,0:T(8,128)}) fusion(bf16[1920,1024]{1,0:T(8,128)(2,1)S(1)} %copy-done.16, f32[1920]{0:T(1024)S(1)} %copy-done.58, f32[1920]{0:T(1024)S(1)} %copy-done.52, f32[1024]{0:T(1024)S(1)} %bitcast.323, f32[1920,1024]{1,0:T(8,128)} %fusion.69, ...), kind=kOutput, calls=%fused_computation.30 | convolution fusion | flops 6061418496 | bytes 28747776 | tf_op jit(solution)/shard_map/dot_general | solution.py:27
  798.5 8.4 fusion.14
  806.9 7.2 collective-permute-start.42
  825.3 24.5 %collective-permute-done.24 = bf16[640,1024]{1,0:T(8,128)(2,1)} collective-permute-done((bf16[640,1024]{1,0:T(8,128)(2,1)}, bf16[640,1024]{1,0:T(8,128)(2,1)}, u32[]{:S(2)}, u32[]{:S(2)}) %collective-permute-start.24) | collective-permute-done | bytes 1310752 | tf_op jit(solution)/shard_map/ppermute | solution.py:399
  852.9 13.6 %collective-permute-done.28 = bf16[4,64,1536]{2,1,0:T(8,128)(2,1)S(1)} collective-permute-done((bf16[4,64,1536]{2,1,0:T(8,128)(2,1)}, bf16[4,64,1536]{2,1,0:T(8,128)(2,1)S(1)}, u32[]{:S(2)}, u32[]{:S(2)}) %collective-permute-start.28) | collective-permute-done | bytes 786464 | tf_op jit(solution)/shard_map/ppermute | solution.py:399
  866.5 15.7 %collective-permute-done.29 = bf16[4,64,1536]{2,1,0:T(8,128)(2,1)} collective-permute-done((bf16[4,64,1536]{2,1,0:T(8,128)(2,1)}, bf16[4,64,1536]{2,1,0:T(8,128)(2,1)}, u32[]{:S(2)}, u32[]{:S(2)}) %collective-permute-start.29) | collective-permute-done | bytes 786464 | tf_op jit(solution)/shard_map/ppermute | solution.py:399
  888.6 3.7 maximum_bitcast_fusion
  893.5 7.8 collective-permute-done.31
  (399 shorter events, 159.0 us)
Async XLA Ops:
  153.1 113.0 %copy-start.61 = (f32[1,1024]{1,0:T(1,128)}, f32[1,1024]{1,0:T(1,128)S(1)}, u32[]{:S(2)}) copy-start(f32[1,1024]{1,0:T(1,128)S(1)} %get-tuple-element.180) | copy-start | bytes 12292
  153.1 121.3 %copy-start.66 = (f32[1,1024]{1,0:T(1,128)}, f32[1,1024]{1,0:T(1,128)S(1)}, u32[]{:S(2)}) copy-start(f32[1,1024]{1,0:T(1,128)S(1)} %get-tuple-element.182) | copy-start | bytes 12292
  158.9 59.8 %collective-permute-start = (bf16[640,1536]{1,0:T(8,128)(2,1)}, bf16[640,1536]{1,0:T(8,128)(2,1)}, u32[]{:S(2)}, u32[]{:S(2)}) collective-permute-start(bf16[640,1536]{1,0:T(8,128)(2,1)} %convolution_convert_fusion.9), channel_id=1, source_target_pairs={{0,1},{1,0},{2,3},{3,2},{4,5},{5,4},{6,7},{7,6},{8,9},{9,8},{10,11... | collective-permute-start | bytes 5898248 | tf_op jit(solution)/shard_map/ppermute | solution.py:399
  245.3 17.1 %collective-permute-start.1 = (bf16[640,512]{1,0:T(8,128)(2,1)S(1)}, bf16[640,512]{1,0:T(8,128)(2,1)S(1)}, u32[]{:S(2)}, u32[]{:S(2)}) collective-permute-start(bf16[640,512]{1,0:T(8,128)(2,1)S(1)} %get-tuple-element.157), channel_id=1, source_target_pairs={{0,1},{1,0},{2,3},{3,2},{4,5},{5,4},{6,7},{7,6},{8,9},{9,8},{10,11... | collective-permute-start | bytes 1966088 | tf_op jit(solution)/shard_map/ppermute | solution.py:399
  318.5 34.2 %collective-permute-start.3 = (bf16[640,1024]{1,0:T(8,128)(2,1)S(1)}, bf16[640,1024]{1,0:T(8,128)(2,1)}, u32[]{:S(2)}, u32[]{:S(2)}) collective-permute-start(bf16[640,1024]{1,0:T(8,128)(2,1)S(1)} %get-tuple-element.143), channel_id=1, source_target_pairs={{0,1},{1,0},{2,3},{3,2},{4,5},{5,4},{6,7},{7,6},{8,9},{9,8},{10,11... | collective-permute-start | bytes 3932168 | tf_op jit(solution)/shard_map/ppermute | solution.py:399
  391.2 31.4 %collective-permute-start.5 = (bf16[4,2,64,2048]{3,2,1,0:T(8,128)(2,1)}, bf16[4,2,64,2048]{3,2,1,0:T(8,128)(2,1)}, u32[]{:S(2)}, u32[]{:S(2)}) collective-permute-start(bf16[4,2,64,2048]{3,2,1,0:T(8,128)(2,1)} %dynamic-slice_bitcast_fusion.2), channel_id=1, source_target_pairs={{0,2},{2,0},{1,3},{3,1},{4,6},{6,4},{5,7},{7,5},{8,10},{10,8},{9,1... | collective-permute-start | bytes 6291464 | tf_op jit(solution)/shard_map/ppermute | solution.py:399
  392.8 32.2 %collective-permute-start.4 = (bf16[4,2,64,2048]{3,2,1,0:T(8,128)(2,1)}, bf16[4,2,64,2048]{3,2,1,0:T(8,128)(2,1)S(1)}, u32[]{:S(2)}, u32[]{:S(2)}) collective-permute-start(bf16[4,2,64,2048]{3,2,1,0:T(8,128)(2,1)} %dynamic-slice_bitcast_fusion.3), channel_id=1, source_target_pairs={{0,2},{2,0},{1,3},{3,1},{4,6},{6,4},{5,7},{7,5},{8,10},{10,8},{9,1... | collective-permute-start | bytes 6291464 | tf_op jit(solution)/shard_map/ppermute | solution.py:399
  440.6 118.8 %collective-permute-start.9 = (bf16[4,2,64,2048]{3,2,1,0:T(8,128)(2,1)}, bf16[4,2,64,2048]{3,2,1,0:T(8,128)(2,1)}, u32[]{:S(2)}, u32[]{:S(2)}) collective-permute-start(bf16[4,2,64,2048]{3,2,1,0:T(8,128)(2,1)} %dynamic-slice_bitcast_fusion), channel_id=1, source_target_pairs={{0,2},{2,0},{1,3},{3,1},{4,6},{6,4},{5,7},{7,5},{8,10},{10,8},{9,1... | collective-permute-start | bytes 6291464 | tf_op jit(solution)/shard_map/ppermute | solution.py:399
  441.4 27.0 %collective-permute-start.10 = (bf16[4,64,2048]{2,1,0:T(8,128)(2,1)S(1)}, bf16[4,64,2048]{2,1,0:T(8,128)(2,1)S(1)}, u32[]{:S(2)}, u32[]{:S(2)}) collective-permute-start(bf16[4,64,2048]{2,1,0:T(8,128)(2,1)S(1)} %get-tuple-element.152), channel_id=1, source_target_pairs={{0,5},{1,4},{4,1},{5,0},{2,7},{3,6},{6,3},{7,2},{8,13},{9,12},{12,... | collective-permute-start | bytes 3145736 | tf_op jit(solution)/shard_map/ppermute | solution.py:399
  443.9 46.2 %collective-permute-start.7 = (bf16[4,64,2048]{2,1,0:T(8,128)(2,1)S(1)}, bf16[4,64,2048]{2,1,0:T(8,128)(2,1)S(1)}, u32[]{:S(2)}, u32[]{:S(2)}) collective-permute-start(bf16[4,64,2048]{2,1,0:T(8,128)(2,1)S(1)} %get-tuple-element.151), channel_id=1, source_target_pairs={{0,1},{1,0},{4,5},{5,4},{2,3},{3,2},{6,7},{7,6},{8,9},{9,8},{12,13... | collective-permute-start | bytes 3145736 | tf_op jit(solution)/shard_map/ppermute | solution.py:399
  444.4 45.7 %collective-permute-start.6 = (bf16[4,64,2048]{2,1,0:T(8,128)(2,1)S(1)}, bf16[4,64,2048]{2,1,0:T(8,128)(2,1)S(1)}, u32[]{:S(2)}, u32[]{:S(2)}) collective-permute-start(bf16[4,64,2048]{2,1,0:T(8,128)(2,1)S(1)} %dynamic-slice_bitcast_fusion.13), channel_id=1, source_target_pairs={{0,4},{1,5},{4,0},{5,1},{2,6},{3,7},{6,2},{7,3},{8,12},{9,13},{12,... | collective-permute-start | bytes 3145736 | tf_op jit(solution)/shard_map/ppermute | solution.py:399
  458.5 103.4 %collective-permute-start.8 = (bf16[4,2,64,2048]{3,2,1,0:T(8,128)(2,1)}, bf16[4,2,64,2048]{3,2,1,0:T(8,128)(2,1)}, u32[]{:S(2)}, u32[]{:S(2)}) collective-permute-start(bf16[4,2,64,2048]{3,2,1,0:T(8,128)(2,1)} %dynamic-slice_bitcast_fusion.1), channel_id=1, source_target_pairs={{0,2},{2,0},{1,3},{3,1},{4,6},{6,4},{5,7},{7,5},{8,10},{10,8},{9,1... | collective-permute-start | bytes 6291464 | tf_op jit(solution)/shard_map/ppermute | solution.py:399
  536.6 12.6 %collective-permute-start.16 = (bf16[64,2048]{1,0:T(8,128)(2,1)S(1)}, bf16[64,2048]{1,0:T(8,128)(2,1)S(1)}, u32[]{:S(2)}, u32[]{:S(2)}) collective-permute-start(bf16[64,2048]{1,0:T(8,128)(2,1)S(1)} %get-tuple-element.162), channel_id=1, source_target_pairs={{0,8},{8,0},{16,24},{24,16},{1,9},{9,1},{17,25},{25,17},{2,10},{10... | collective-permute-start | bytes 786440 | tf_op jit(solution)/shard_map/ppermute | solution.py:399
  537.2 21.3 %collective-permute-start.17 = (bf16[64,2048]{1,0:T(8,128)(2,1)S(1)}, bf16[64,2048]{1,0:T(8,128)(2,1)S(1)}, u32[]{:S(2)}, u32[]{:S(2)}) collective-permute-start(bf16[64,2048]{1,0:T(8,128)(2,1)S(1)} %get-tuple-element.164), channel_id=1, source_target_pairs={{0,16},{8,24},{16,0},{24,8},{1,17},{9,25},{17,1},{25,9},{2,18},{10... | collective-permute-start | bytes 786440 | tf_op jit(solution)/shard_map/ppermute | solution.py:399
  538.7 19.8 %collective-permute-start.18 = (bf16[64,2048]{1,0:T(8,128)(2,1)S(1)}, bf16[64,2048]{1,0:T(8,128)(2,1)S(1)}, u32[]{:S(2)}, u32[]{:S(2)}) collective-permute-start(bf16[64,2048]{1,0:T(8,128)(2,1)S(1)} %get-tuple-element.163), channel_id=1, source_target_pairs={{0,24},{8,16},{16,8},{24,0},{1,25},{9,17},{17,9},{25,1},{2,26},{10... | collective-permute-start | bytes 786440 | tf_op jit(solution)/shard_map/ppermute | solution.py:399
  575.7 37.7 %collective-permute-start.15 = (bf16[640,512]{1,0:T(8,128)(2,1)}, bf16[640,512]{1,0:T(8,128)(2,1)S(1)}, u32[]{:S(2)}, u32[]{:S(2)}) collective-permute-start(bf16[640,512]{1,0:T(8,128)(2,1)} %convolution_convert_fusion.15), channel_id=1, source_target_pairs={{0,1},{1,0},{2,3},{3,2},{4,5},{5,4},{6,7},{7,6},{8,9},{9,8},{10,11... | collective-permute-start | bytes 1966088 | tf_op jit(solution)/shard_map/ppermute | solution.py:399
  577.3 33.7 %collective-permute-start.12 = (bf16[4,2,64,512]{3,2,1,0:T(8,128)(2,1)S(1)}, bf16[4,2,64,512]{3,2,1,0:T(8,128)(2,1)S(1)}, u32[]{:S(2)}, u32[]{:S(2)}) collective-permute-start(bf16[4,2,64,512]{3,2,1,0:T(8,128)(2,1)S(1)} %dynamic-slice_bitcast_fusion.18), channel_id=1, source_target_pairs={{0,2},{2,0},{1,3},{3,1},{4,6},{6,4},{5,7},{7,5},{8,10},{10,8},{9,1... | collective-permute-start | bytes 1572872 | tf_op jit(solution)/shard_map/ppermute | solution.py:399
  577.5 34.4 %collective-permute-start.11 = (bf16[4,2,64,512]{3,2,1,0:T(8,128)(2,1)S(1)}, bf16[4,2,64,512]{3,2,1,0:T(8,128)(2,1)S(1)}, u32[]{:S(2)}, u32[]{:S(2)}) collective-permute-start(bf16[4,2,64,512]{3,2,1,0:T(8,128)(2,1)S(1)} %dynamic-slice_bitcast_fusion.19), channel_id=1, source_target_pairs={{0,2},{2,0},{1,3},{3,1},{4,6},{6,4},{5,7},{7,5},{8,10},{10,8},{9,1... | collective-permute-start | bytes 1572872 | tf_op jit(solution)/shard_map/ppermute | solution.py:399
  578.0 89.3 %collective-permute-start.14 = (bf16[4,64,2048]{2,1,0:T(8,128)(2,1)}, bf16[4,64,2048]{2,1,0:T(8,128)(2,1)}, u32[]{:S(2)}, u32[]{:S(2)}) collective-permute-start(bf16[4,64,2048]{2,1,0:T(8,128)(2,1)} %get-tuple-element.149), channel_id=1, source_target_pairs={{0,1},{1,0},{4,5},{5,4},{2,3},{3,2},{6,7},{7,6},{8,9},{9,8},{12,13... | collective-permute-start | bytes 3145736 | tf_op jit(solution)/shard_map/ppermute | solution.py:399
  578.6 88.7 %collective-permute-start.19 = (bf16[4,64,2048]{2,1,0:T(8,128)(2,1)S(1)}, bf16[4,64,2048]{2,1,0:T(8,128)(2,1)}, u32[]{:S(2)}, u32[]{:S(2)}) collective-permute-start(bf16[4,64,2048]{2,1,0:T(8,128)(2,1)S(1)} %get-tuple-element.150), channel_id=1, source_target_pairs={{0,5},{1,4},{4,1},{5,0},{2,7},{3,6},{6,3},{7,2},{8,13},{9,12},{12,... | collective-permute-start | bytes 3145736 | tf_op jit(solution)/shard_map/ppermute | solution.py:399
  611.1 56.2 %collective-permute-start.13 = (bf16[4,64,2048]{2,1,0:T(8,128)(2,1)}, bf16[4,64,2048]{2,1,0:T(8,128)(2,1)}, u32[]{:S(2)}, u32[]{:S(2)}) collective-permute-start(bf16[4,64,2048]{2,1,0:T(8,128)(2,1)} %dynamic-slice_bitcast_fusion.9), channel_id=1, source_target_pairs={{0,4},{1,5},{4,0},{5,1},{2,6},{3,7},{6,2},{7,3},{8,12},{9,13},{12,... | collective-permute-start | bytes 3145736 | tf_op jit(solution)/shard_map/ppermute | solution.py:399
  611.9 31.0 %collective-permute-start.21 = (bf16[4,64,512]{2,1,0:T(8,128)(2,1)S(1)}, bf16[4,64,512]{2,1,0:T(8,128)(2,1)S(1)}, u32[]{:S(2)}, u32[]{:S(2)}) collective-permute-start(bf16[4,64,512]{2,1,0:T(8,128)(2,1)S(1)} %get-tuple-element.168), channel_id=1, source_target_pairs={{0,1},{1,0},{4,5},{5,4},{2,3},{3,2},{6,7},{7,6},{8,9},{9,8},{12,13... | collective-permute-start | bytes 786440 | tf_op jit(solution)/shard_map/ppermute | solution.py:399
  613.4 33.2 %collective-permute-start.22 = (bf16[4,64,512]{2,1,0:T(8,128)(2,1)S(1)}, bf16[4,64,512]{2,1,0:T(8,128)(2,1)S(1)}, u32[]{:S(2)}, u32[]{:S(2)}) collective-permute-start(bf16[4,64,512]{2,1,0:T(8,128)(2,1)S(1)} %get-tuple-element.169), channel_id=1, source_target_pairs={{0,5},{1,4},{4,1},{5,0},{2,7},{3,6},{6,3},{7,2},{8,13},{9,12},{12,... | collective-permute-start | bytes 786440 | tf_op jit(solution)/shard_map/ppermute | solution.py:399
  642.9 24.2 %collective-permute-start.20 = (bf16[4,64,512]{2,1,0:T(8,128)(2,1)S(1)}, bf16[4,64,512]{2,1,0:T(8,128)(2,1)S(1)}, u32[]{:S(2)}, u32[]{:S(2)}) collective-permute-start(bf16[4,64,512]{2,1,0:T(8,128)(2,1)S(1)} %copy-done.48), channel_id=1, source_target_pairs={{0,4},{1,5},{4,0},{5,1},{2,6},{3,7},{6,2},{7,3},{8,12},{9,13},{12,... | collective-permute-start | bytes 786440 | tf_op jit(solution)/shard_map/ppermute | solution.py:399
  646.6 65.1 %collective-permute-start.2 = (bf16[640,1024]{1,0:T(8,128)(2,1)}, bf16[640,1024]{1,0:T(8,128)(2,1)}, u32[]{:S(2)}, u32[]{:S(2)}) collective-permute-start(bf16[640,1024]{1,0:T(8,128)(2,1)} %dynamic-slice_bitcast_fusion.6), channel_id=1, source_target_pairs={{0,1},{1,0},{2,3},{3,2},{4,5},{5,4},{6,7},{7,6},{8,9},{9,8},{10,11... | collective-permute-start | bytes 3932168 | tf_op jit(solution)/shard_map/ppermute | solution.py:399
  711.6 39.7 %collective-permute-start.25 = (bf16[4,2,64,1536]{3,2,0,1:T(8,128)(2,1)S(1)}, bf16[4,2,64,1536]{3,2,0,1:T(8,128)(2,1)S(1)}, u32[]{:S(2)}, u32[]{:S(2)}) collective-permute-start(bf16[4,2,64,1536]{3,2,0,1:T(8,128)(2,1)S(1)} %bitcast.303), channel_id=1, source_target_pairs={{0,2},{2,0},{1,3},{3,1},{4,6},{6,4},{5,7},{7,5},{8,10},{10,8},{9,1... | collective-permute-start | bytes 4718600 | tf_op jit(solution)/shard_map/ppermute | solution.py:399
  713.8 45.3 %collective-permute-start.23 = (bf16[640,1536]{1,0:T(8,128)(2,1)S(1)}, bf16[640,1536]{1,0:T(8,128)(2,1)}, u32[]{:S(2)}, u32[]{:S(2)}) collective-permute-start(bf16[640,1536]{1,0:T(8,128)(2,1)S(1)} %copy-done.43), channel_id=1, source_target_pairs={{0,1},{1,0},{2,3},{3,2},{4,5},{5,4},{6,7},{7,6},{8,9},{9,8},{10,11... | collective-permute-start | bytes 5898248 | tf_op jit(solution)/shard_map/ppermute | solution.py:399
  714.8 9.5 %collective-permute-start.33 = (bf16[64,512]{1,0:T(8,128)(2,1)S(1)}, bf16[64,512]{1,0:T(8,128)(2,1)S(1)}, u32[]{:S(2)}, u32[]{:S(2)}) collective-permute-start(bf16[64,512]{1,0:T(8,128)(2,1)S(1)} %get-tuple-element.170), channel_id=1, source_target_pairs={{0,8},{8,0},{16,24},{24,16},{1,9},{9,1},{17,25},{25,17},{2,10},{10... | collective-permute-start | bytes 196616 | tf_op jit(solution)/shard_map/ppermute | solution.py:399
  721.9 8.0 collective-permute-start.34
  721.9 7.9 collective-permute-start.35
  724.4 12.1 %collective-permute-start.36 = (bf16[64,2048]{1,0:T(8,128)(2,1)S(1)}, bf16[64,2048]{1,0:T(8,128)(2,1)S(1)}, u32[]{:S(2)}, u32[]{:S(2)}) collective-permute-start(bf16[64,2048]{1,0:T(8,128)(2,1)S(1)} %get-tuple-element.159), channel_id=1, source_target_pairs={{0,8},{8,0},{16,24},{24,16},{1,9},{9,1},{17,25},{25,17},{2,10},{10... | collective-permute-start | bytes 786440 | tf_op jit(solution)/shard_map/ppermute | solution.py:399
  729.8 20.5 %collective-permute-start.37 = (bf16[64,2048]{1,0:T(8,128)(2,1)S(1)}, bf16[64,2048]{1,0:T(8,128)(2,1)S(1)}, u32[]{:S(2)}, u32[]{:S(2)}) collective-permute-start(bf16[64,2048]{1,0:T(8,128)(2,1)S(1)} %get-tuple-element.161), channel_id=1, source_target_pairs={{0,16},{8,24},{16,0},{24,8},{1,17},{9,25},{17,1},{25,9},{2,18},{10... | collective-permute-start | bytes 786440 | tf_op jit(solution)/shard_map/ppermute | solution.py:399
  729.8 20.5 %collective-permute-start.38 = (bf16[64,2048]{1,0:T(8,128)(2,1)S(1)}, bf16[64,2048]{1,0:T(8,128)(2,1)S(1)}, u32[]{:S(2)}, u32[]{:S(2)}) collective-permute-start(bf16[64,2048]{1,0:T(8,128)(2,1)S(1)} %get-tuple-element.160), channel_id=1, source_target_pairs={{0,24},{8,16},{16,8},{24,0},{1,25},{9,17},{17,9},{25,1},{2,26},{10... | collective-permute-start | bytes 786440 | tf_op jit(solution)/shard_map/ppermute | solution.py:399
  753.8 99.1 %collective-permute-start.26 = (bf16[4,64,1536]{2,1,0:T(8,128)(2,1)}, bf16[4,64,1536]{2,1,0:T(8,128)(2,1)}, u32[]{:S(2)}, u32[]{:S(2)}) collective-permute-start(bf16[4,64,1536]{2,1,0:T(8,128)(2,1)} %dynamic-slice_bitcast_fusion.17), channel_id=1, source_target_pairs={{0,4},{1,5},{4,0},{5,1},{2,6},{3,7},{6,2},{7,3},{8,12},{9,13},{12,... | collective-permute-start | bytes 2359304 | tf_op jit(solution)/shard_map/ppermute | solution.py:399
  793.3 13.6 %collective-permute-start.39 = (f32[8,1024]{1,0:T(8,128)S(1)}, f32[8,1024]{1,0:T(8,128)S(1)}, u32[]{:S(2)}, u32[]{:S(2)}) collective-permute-start(f32[8,1024]{1,0:T(8,128)S(1)} %concatenate.39), channel_id=1, source_target_pairs={{0,1},{1,0},{4,5},{5,4},{2,3},{3,2},{6,7},{7,6},{8,9},{9,8},{12,13... | collective-permute-start | bytes 98312 | tf_op jit(solution)/shard_map/ppermute | solution.py:399
  794.4 12.5 %collective-permute-start.40 = (f32[8,1024]{1,0:T(8,128)S(1)}, f32[8,1024]{1,0:T(8,128)S(1)}, u32[]{:S(2)}, u32[]{:S(2)}) collective-permute-start(f32[8,1024]{1,0:T(8,128)S(1)} %concatenate.39), channel_id=1, source_target_pairs={{0,4},{1,5},{4,0},{5,1},{2,6},{3,7},{6,2},{7,3},{8,12},{9,13},{12,... | collective-permute-start | bytes 98312 | tf_op jit(solution)/shard_map/ppermute | solution.py:399
  794.8 12.1 %collective-permute-start.41 = (f32[8,1024]{1,0:T(8,128)S(1)}, f32[8,1024]{1,0:T(8,128)S(1)}, u32[]{:S(2)}, u32[]{:S(2)}) collective-permute-start(f32[8,1024]{1,0:T(8,128)S(1)} %concatenate.39), channel_id=1, source_target_pairs={{0,5},{1,4},{4,1},{5,0},{2,7},{3,6},{6,3},{7,2},{8,13},{9,12},{12,... | collective-permute-start | bytes 98312 | tf_op jit(solution)/shard_map/ppermute | solution.py:399
  798.4 21.7 %collective-permute-start.27 = (bf16[4,2,64,1536]{3,2,1,0:T(8,128)(2,1)S(1)}, bf16[4,2,64,1536]{3,2,1,0:T(8,128)(2,1)S(1)}, u32[]{:S(2)}, u32[]{:S(2)}) collective-permute-start(bf16[4,2,64,1536]{3,2,1,0:T(8,128)(2,1)S(1)} %dynamic-slice_bitcast_fusion.4), channel_id=1, source_target_pairs={{0,2},{2,0},{1,3},{3,1},{4,6},{6,4},{5,7},{7,5},{8,10},{10,8},{9,1... | collective-permute-start | bytes 4718600 | tf_op jit(solution)/shard_map/ppermute | solution.py:399
  806.9 10.9 %collective-permute-start.42 = (f32[8,1024]{1,0:T(8,128)S(1)}, f32[8,1024]{1,0:T(8,128)S(1)}, u32[]{:S(2)}, u32[]{:S(2)}) collective-permute-start(f32[8,1024]{1,0:T(8,128)S(1)} %add_add_fusion.1), channel_id=1, source_target_pairs={{0,8},{8,0},{16,24},{24,16},{1,9},{9,1},{17,25},{25,17},{2,10},{10... | collective-permute-start | bytes 98312 | tf_op jit(solution)/shard_map/ppermute | solution.py:399
  814.1 5.9 collective-permute-start.43
  814.3 5.7 collective-permute-start.44
  817.8 32.0 %collective-permute-start.24 = (bf16[640,1024]{1,0:T(8,128)(2,1)}, bf16[640,1024]{1,0:T(8,128)(2,1)}, u32[]{:S(2)}, u32[]{:S(2)}) collective-permute-start(bf16[640,1024]{1,0:T(8,128)(2,1)} %fusion.37), channel_id=1, source_target_pairs={{0,1},{1,0},{2,3},{3,2},{4,5},{5,4},{6,7},{7,6},{8,9},{9,8},{10,11... | collective-permute-start | bytes 3932168 | tf_op jit(solution)/shard_map/ppermute | solution.py:399
  820.0 3.9 collective-permute-start.45
  821.9 44.7 %collective-permute-start.28 = (bf16[4,64,1536]{2,1,0:T(8,128)(2,1)}, bf16[4,64,1536]{2,1,0:T(8,128)(2,1)S(1)}, u32[]{:S(2)}, u32[]{:S(2)}) collective-permute-start(bf16[4,64,1536]{2,1,0:T(8,128)(2,1)} %get-tuple-element.153), channel_id=1, source_target_pairs={{0,1},{1,0},{4,5},{5,4},{2,3},{3,2},{6,7},{7,6},{8,9},{9,8},{12,13... | collective-permute-start | bytes 2359304 | tf_op jit(solution)/shard_map/ppermute | solution.py:399
  822.7 59.6 %collective-permute-start.29 = (bf16[4,64,1536]{2,1,0:T(8,128)(2,1)}, bf16[4,64,1536]{2,1,0:T(8,128)(2,1)}, u32[]{:S(2)}, u32[]{:S(2)}) collective-permute-start(bf16[4,64,1536]{2,1,0:T(8,128)(2,1)} %get-tuple-element.154), channel_id=1, source_target_pairs={{0,5},{1,4},{4,1},{5,0},{2,7},{3,6},{6,3},{7,2},{8,13},{9,12},{12,... | collective-permute-start | bytes 2359304 | tf_op jit(solution)/shard_map/ppermute | solution.py:399
  884.1 9.4 %collective-permute-start.30 = (bf16[64,1536]{1,0:T(8,128)(2,1)S(1)}, bf16[64,1536]{1,0:T(8,128)(2,1)S(1)}, u32[]{:S(2)}, u32[]{:S(2)}) collective-permute-start(bf16[64,1536]{1,0:T(8,128)(2,1)S(1)} %get-tuple-element.165), channel_id=1, source_target_pairs={{0,8},{8,0},{16,24},{24,16},{1,9},{9,1},{17,25},{25,17},{2,10},{10... | collective-permute-start | bytes 589832 | tf_op jit(solution)/shard_map/ppermute | solution.py:399
  884.9 16.3 %collective-permute-start.31 = (bf16[64,1536]{1,0:T(8,128)(2,1)S(1)}, bf16[64,1536]{1,0:T(8,128)(2,1)S(1)}, u32[]{:S(2)}, u32[]{:S(2)}) collective-permute-start(bf16[64,1536]{1,0:T(8,128)(2,1)S(1)} %get-tuple-element.167), channel_id=1, source_target_pairs={{0,16},{8,24},{16,0},{24,8},{1,17},{9,25},{17,1},{25,9},{2,18},{10... | collective-permute-start | bytes 589832 | tf_op jit(solution)/shard_map/ppermute | solution.py:399
  886.1 15.1 %collective-permute-start.32 = (bf16[64,1536]{1,0:T(8,128)(2,1)S(1)}, bf16[64,1536]{1,0:T(8,128)(2,1)S(1)}, u32[]{:S(2)}, u32[]{:S(2)}) collective-permute-start(bf16[64,1536]{1,0:T(8,128)(2,1)S(1)} %get-tuple-element.166), channel_id=1, source_target_pairs={{0,24},{8,16},{16,8},{24,0},{1,25},{9,17},{17,9},{25,1},{2,26},{10... | collective-permute-start | bytes 589832 | tf_op jit(solution)/shard_map/ppermute | solution.py:399
  (96 other events, 1279.5 us)

commit v5 on v4

--- a/solution.py
+++ b/solution.py
@@ -234,15 +234,13 @@
     return position
 
 
-def gather_kernel(chunks, weights, moved, *refs):
+def gather_kernel(chunks, weights, *refs):
     shards, refs = refs[:weights], refs[weights:]
     tokens, segments, refs = refs[0], refs[1], refs[2:]
     tp = lax.axis_size("tp")
     depth = lax.axis_size("z")
     outs, refs = refs[: weights * tp], refs[weights * tp :]
-    segments_out, refs = refs[0], refs[1:]
-    tokens_out, refs = (refs[0], refs[1:]) if moved else (None, refs)
-    send_sems, recv_sems, local_sems = refs
+    segments_out, tokens_out, send_sems, recv_sems, local_sems = refs
     z, y, core, x = (lax.axis_index(name) for name in ("z", "y", "core", "tp"))
 
     barrier = pltpu.get_barrier_semaphore()
@@ -276,9 +274,12 @@
     for k in range(1, tp):
         partner = {"tp": apart(x, k)}
         crossed.append(copy(segments, segments_out.at[k - 1], partner))
-        for n in range(moved):
-            source = tokens.at[n * tp + apart(x, k)]
-            crossed.append(copy(source, tokens_out.at[n * (tp - 1) + k - 1], partner))
+        micro = tokens.shape[0]
+        sources = [n * tp + apart(x, k) for n in range(micro // tp)]
+        sources += range(micro // tp * tp, micro)
+        for n, source in enumerate(sources):
+            target = tokens_out.at[n * (tp - 1) + k - 1]
+            crossed.append(copy(tokens.at[source], target, partner))
 
     def part(number, t, at_y, span):
         weight, low, rows = chunks[number]
@@ -352,7 +353,7 @@
 def gather_weights(shards, pieces, tokens, segments):
     tp = lax.axis_size("tp")
     depth = lax.axis_size("z")
-    moved = tokens.shape[0] // tp
+    moved = tokens.shape[0] // tp + tokens.shape[0] % tp
     chunks = []
     for number, (shard, split) in enumerate(zip(shards, pieces)):
         rows = shard.shape[0] // split
@@ -366,12 +367,11 @@
     ]
     sent = sum(shape.size for shape in shapes) * 2
     shapes += [jax.ShapeDtypeStruct((tp - 1,) + segments.shape, segments.dtype)]
-    if moved:
-        shapes += [jax.ShapeDtypeStruct((moved * (tp - 1),) + tokens.shape[1:], tokens.dtype)]
+    shapes += [jax.ShapeDtypeStruct((moved * (tp - 1),) + tokens.shape[1:], tokens.dtype)]
     inside = pl.BlockSpec(memory_space=pltpu.VMEM)
     outside = pl.BlockSpec(memory_space=pl.ANY)
     made = pl.pallas_call(
-        functools.partial(gather_kernel, chunks, len(shards), moved),
+        functools.partial(gather_kernel, chunks, len(shards)),
         name="gather_weights",
         out_shape=shapes,
         in_specs=[inside] * len(shards) + [outside, inside],
@@ -388,7 +388,7 @@
     full = [array.reshape(-1, array.shape[-1]) for array in made[:count]]
     full = [full[number * tp : (number + 1) * tp] for number in range(len(shards))]
     crossed = made[count:]
-    came = [crossed[1][number] for number in range(moved * (tp - 1))] if moved else []
+    came = [crossed[1][number] for number in range(moved * (tp - 1))]
     return full, [crossed[0][k] for k in range(tp - 1)], came
 
 
@@ -489,12 +489,12 @@
     def outgoing(values):
         return [block_at(values, 0, n * tp + (here ^ k)) for n in range(whole) for k in range(1, tp)]
 
-    def tree_rows(values, came):
+    def whole_trees(values, came):
         rows = []
         for n in range(whole):
             near = [block_at(values, 0, n * tp + here)]
             rows.append(in_place_order(near + came[n * (tp - 1) : (n + 1) * (tp - 1)]))
-        return lax.optimization_barrier(jnp.concatenate(rows + [values[m] for m in shared], axis=0))
+        return rows
 
     def rows_back(values):
         trees = values.reshape(micro, own_rows, width)
@@ -511,12 +511,21 @@
         return lax.dynamic_slice_in_dim(values, (here ^ k) * own_rows, own_rows)
 
     shard_qkv = w_qkv.reshape(w_qkv.shape[0], -1)
-    (full_qkv, full_out, full_up, full_down), seg_came, tokens_came = gather_weights(
-        [shard_qkv, w_out.T, w_up, w_down.T], [4, 1, 4, 4], tokens[:, 0], segments[:, 0]
+    (full_qkv, full_out, full_up), seg_came, tokens_came = gather_weights(
+        [shard_qkv, w_out.T, w_up], [4, 1, 4], tokens[:, 0], segments[:, 0]
     )
+    down = lax.all_gather(
+        after(w_down.T, full_qkv[0]), ("tp", "z", "y", "core"), axis=0, tiled=True
+    ).reshape(tp, width, -1)
+    full_down = [pick([down[s] for s in halves], here ^ t) for t in halves]
     seg_came = [segments[:, 0]] + seg_came
     seg_all = jnp.concatenate([pick(seg_came, here ^ s) for s in halves], axis=1)
-    x = tree_rows(tokens[:, 0], tokens_came).astype(f32)
+    all_rows = whole_trees(tokens[:, 0], tokens_came)
+    for n, m in enumerate(shared):
+        start = (whole + n) * (tp - 1)
+        all_rows.append(in_place_order([tokens[m, 0]] + tokens_came[start : start + tp - 1]))
+    all_rows = lax.optimization_barrier(jnp.concatenate(all_rows, axis=0))
+    x = jnp.concatenate([all_rows[:split]] + [tokens[m, 0] for m in shared], axis=0).astype(f32)
     whole_tables = []
     for n in range(whole):
         seg = pick([seg_all[n * tp + s] for s in halves], here)
@@ -524,29 +533,28 @@
         whole_tables.append(segment_tables(seg, par))
     share_tables = [segment_tables(seg_all[m], parents[m, 0]) for m in shared]
 
-    normed = norm_forward(x, norm_gains[0], norm_biases[0]).astype(bf16)
-    share_qkv = [dot_nn(normed[split:], w).astype(bf16) for w in full_qkv]
-    whole_qkv = [dot_nn(normed[:split], w).astype(bf16) for w in full_qkv] if whole else []
-    share_calls = []
-    for n in range(share_count):
-        cut = slice(n * own_rows, (n + 1) * own_rows)
-        share_calls.append(in_place_order(exchange_tp([part[cut] for part in share_qkv])))
+    normed = norm_forward(all_rows.astype(f32), norm_gains[0], norm_biases[0]).astype(bf16)
+    normed_shared = normed[split:]
+    normed_whole = normed[:split]
+    shared_qkv = dot_nn(normed_shared, full_qkv[0]).astype(bf16)
+    whole_qkv = [dot_nn(normed_whole, w).astype(bf16) for w in full_qkv] if whole else []
     whole_out = [[] for _ in halves]
     share_out = [[] for _ in halves]
     saved = {}
+    for n in range(share_count):
+        qkv = shared_qkv[n * tree_len : (n + 1) * tree_len]
+        out, lse = attention_forward(qkv, *share_tables[n])
+        saved[n] = (qkv, out, lse)
+        parts = exchange_tp([share_rows(out, k) for k in halves])
+        for t in halves:
+            share_out[t].append(parts[t])
+    first = [saved[n][1] for n in range(share_count)]
     for n in range(whole):
         for t in halves:
-            qkv = whole_qkv[t][n * tree_len : (n + 1) * tree_len]
+            qkv = after(whole_qkv[t][n * tree_len : (n + 1) * tree_len], *first)
             out, lse = attention_forward(qkv, *whole_tables[n])
             saved[n, t] = (qkv, out, lse)
             whole_out[t].append(out)
-    share_calls = [after(call, *whole_out[0]) for call in share_calls]
-    for n in range(share_count):
-        out, lse = attention_forward(share_calls[n], *share_tables[n])
-        saved[n] = (share_calls[n], out, lse)
-        parts = exchange_tp([share_rows(out, k) for k in halves])
-        for t in halves:
-            share_out[t].append(parts[t])
     attended = [jnp.concatenate(whole_out[t] + share_out[t], axis=0) for t in halves]
     cotangent = after(cotangent[:, 0], *attended)
     cotangent_came = [send(piece, "tp", n % (tp - 1) + 1) for n, piece in enumerate(outgoing(cotangent))]
@@ -565,7 +573,8 @@
     out = (residual + norm_forward(branch_f, norm_gains[3], norm_biases[3])).astype(bf16)
     out_rows = rows_back(out)
 
-    grad_out = tree_rows(cotangent, cotangent_came).astype(f32)
+    grad_out = whole_trees(cotangent, cotangent_came) + [cotangent[m] for m in shared]
+    grad_out = lax.optimization_barrier(jnp.concatenate(grad_out, axis=0)).astype(f32)
     grad_branch_f, sums_3 = norm_backward(branch_f, norm_gains[3], grad_out)
     grad_branch_f = grad_branch_f.astype(bf16)
     core_down = [scatter_core(dot_tn(grad_branch_f, hidden[t]).astype(bf16)) for t in halves]
@@ -593,7 +602,6 @@
         share_do.append(in_place_order(exchange_tp([part[cut] for part in share_grad])))
     core_out = [scatter_core(dot_tn(grad_branch_a, part).astype(bf16)) for part in attended]
     grad_qkv = [[] for _ in halves]
-    share_parts = [[] for _ in halves]
 
     def whole_backward(t, *others):
         for n in range(whole):
@@ -604,26 +612,43 @@
         return grad_qkv[t]
 
     made = []
+    dw_qkv = [None] * tp
     for t in range(1, tp):
         made += whole_backward(t)
+        if whole:
+            dw_qkv[t] = dot_tn(normed_whole, jnp.concatenate(grad_qkv[t], axis=0)).astype(bf16)
+        else:
+            dw_qkv[t] = jnp.zeros(full_qkv[t].shape, bf16)
+    core_qkv = [None] + [scatter_core(part) for part in dw_qkv[1:]]
+    grad_shared = []
+    own_part = []
     for n in range(share_count):
         qkv, att, lse = saved[n]
-        do = after(share_do[n], z_down, *made)
+        do = after(share_do[n], *made)
         dx = attention_backward(qkv, do, att, lse, *share_tables[n])
         made = [dx]
-        parts = exchange_tp([share_rows(dx, k) for k in halves])
-        for t in halves:
-            share_parts[t].append(parts[t])
-    made = whole_backward(0, *core_out, *straight_up, *made)
+        grad_shared.append(dx)
+    whole_backward(0, *core_out, *straight_up, *core_qkv[1:], *made)
+    for n in range(share_count):
+        part = dot_nt(grad_shared[n], full_qkv[0])
+        pieces = exchange_tp([share_rows(part, 0)] + [share_rows(part, k).astype(bf16) for k in halves[1:]])
+        own_part.append(sum([piece.astype(f32) for piece in pieces[1:]], pieces[0]))
     straight_out, across_out = scatter_plane(core_out)
-    ready = [*across_up, *straight_out, *across_out, *made]
-    grad_qkv = [after(jnp.concatenate(grad_qkv[t] + share_parts[t], axis=0), *ready) for t in halves]
+    ready = [*across_up, *straight_out, *across_out, z_down]
+    owned = after(jnp.concatenate(grad_qkv[0] + grad_shared, axis=0), *ready)
     z_up = scatter_z(total(straight_up + across_up))
     z_out = scatter_z(total(straight_out + across_out))
-    dw_qkv = [dot_tn(normed, grad_qkv[t]).astype(bf16) for t in halves]
-    straight_qkv, across_qkv = scatter_plane([scatter_core(part) for part in dw_qkv])
+    dw_qkv[0] = dot_tn(normed, owned).astype(bf16)
+    core_qkv[0] = scatter_core(dw_qkv[0])
+    straight_qkv, across_qkv = scatter_plane(core_qkv)
     z_qkv = scatter_z(total(straight_qkv + across_qkv))
-    grad_normed = sum(dot_nt(after(grad_qkv[t], *dw_qkv), full_qkv[t]) for t in halves)
+    ready = [dw_qkv[0], *across_qkv]
+    grad_normed = list(own_part)
+    if whole:
+        trees = [after(jnp.concatenate(grad_qkv[t], axis=0), *ready) for t in halves]
+        trees[1:] = [after(rows, core_qkv[0]) for rows in trees[1:]]
+        grad_normed = [sum(dot_nt(trees[t], full_qkv[t]) for t in halves)] + grad_normed
+    grad_normed = jnp.concatenate(grad_normed, axis=0)
     grad_part, sums_0 = norm_backward(x, norm_gains[0], grad_normed)
     input_rows = rows_back(grad_residual + grad_part)
     sums = jnp.concatenate([sums_0, sums_1, sums_2, sums_3])

time: 911 us -> 924 us (1.014)
  other arithmetic: 87.8 us -> 126 us
  waiting for transfers between devices: 166 us -> 138 us
  between operations: 2.99 us -> 16.2 us
  starting transfers between devices: 59 us -> 48.4 us
    ppermute x46 -> x45, waiting for transfers between devices: 166 us -> 138 us  [send(): return lax.ppermute(values, axes, [(s, s ^ distance) for s in range(count)])]
    concatenate x4 -> x3, other arithmetic: 7.64 us -> 22.5 us  [the longest x1 13.4 us: on_device(): all_rows = lax.optimization_barrier(jnp.concatenate(all_rows, axis=0))]
    ppermute x46 -> x45, starting transfers between devices: 59 us -> 48.3 us  [send(): return lax.ppermute(values, axes, [(s, s ^ distance) for s in range(count)])]
    dot_general x12 -> x11, matrix products: 93.5 us -> 102 us  [dot_nn(): lax.dot_general(a, b, (((1,), (0,)), ((), ())), preferred_element_type=f32)]
    reduce_sum x2 -> x3, other arithmetic: 18 us -> 23.1 us  [norm_backward(): jnp.sum(grad * xhat, axis=0)]
    unnamed x202 -> x228, local copies, waits for them, and re-layouts: 19.2 us -> 20.2 us
    dot_general x8 -> x9, matrix products: 90.2 us -> 89.3 us  [dot_nt(): lax.dot_general(a, b, (((1,), (1,)), ((), ())), preferred_element_type=f32)]
  transfers between devices with their start and end apart: 46 -> 46, of which waited for: 17 -> 12; matrix products, arithmetic and copies ran while one was open for 26% -> 32% of each run, Pallas kernels for 14% -> 13%
where the time goes in v5:
time: 924 us; the launch traced here: 920 us
  Pallas kernels  281 us (30%)
  matrix products  261 us (28%)
  waiting for transfers between devices  138 us (15%)
  other arithmetic  126 us (14%)
  local copies, waits for them, and re-layouts  49.1 us (5%)
  starting transfers between devices  48.4 us (5%)
  between operations  16.2 us (2%)
    ppermute x45, waiting for transfers between devices, send(): return lax.ppermute(values, axes, [(s, s ^ distance) for s in range(count)])  138 us
    pallas_call x1, Pallas kernels, gather_weights(): pl.pallas_call(functools.partial(gather_kernel, chunks, len(shards)), nam...  136 us
    dot_general x11, matrix products, dot_nn(): lax.dot_general(a, b, (((1,), (0,)), ((), ())), preferred_element_type=f32)  102 us
    dot_general x9, matrix products, dot_nt(): lax.dot_general(a, b, (((1,), (1,)), ((), ())), preferred_element_type=f32)  89.3 us
    pallas_call x3, Pallas kernels, attention_backward(): pl.pallas_call(attention_backward_kernel, name='attention_backward', out_...  80.1 us
    dot_general x8, matrix products, dot_tn(): lax.dot_general(a, b, (((0,), (0,)), ((), ())), preferred_element_type=f32)  69.7 us
    pallas_call x3, Pallas kernels, attention_forward(): pl.pallas_call(attention_forward_kernel, name='attention_forward', out_sh...  64.7 us
    ppermute x45, starting transfers between devices, send(): return lax.ppermute(values, axes, [(s, s ^ distance) for s in range(count)])  48.3 us
  transfers between devices with their start and end apart: 46, of which 12 were waited for; matrix products, arithmetic and copies ran while one was open for 32% of the time, Pallas kernels for 13%

profile of v5, /device:TPU:0, one launch (start us, length us, event | category | flops | bytes accessed | tf_op | source)
XLA Modules:
  0.0 920.0 jit_solution(4314234461922518031)
XLA Ops:
  10.1 136.3 %gather_weights.1 = (bf16[4,2,2,64,1536]{4,3,2,1,0:T(8,128)(2,1)}, bf16[4,2,2,64,1536]{4,3,2,1,0:T(8,128)(2,1)}, bf16[4,2,2,64,512]{4,3,2,1,0:T(8,128)(2,1)}, bf...) custom-call(bf16[64,1536]{1,0:T(8,128)(2,1)} %bitcast.317, ...), custom_call_target="tpu_custom_call" | custom-call | bytes 33554432 | tf_op jit(solution)/shard_map/gather_weights/pallas_call | solution.py:373
  149.3 13.4 %pad_maximum_fusion.2 = bf16[2560,1024]{1,0:T(8,128)(2,1)S(1)} fusion(bf16[640,1024]{1,0:T(8,128)(2,1)S(1)} %get-tuple-element.138, bf16[640,1024]{1,0:T(8,128)(2,1)S(1)} %get-tuple-element.139, bf16[640,1024]{1,0:T(8,128)(2,1)S(1)} %get-tuple-element.137, bf16[640,1024]{1,0:T(8,128)(2,1)S(1)} %get-tuple-element.136), kind=kLoop, calls=%fused_computation.64 | loop fusion | flops 20971520 | bytes 10485760 | tf_op jit(solution)/shard_map/concatenate | solution.py:527
  167.1 4.6 fusion.8
  174.0 5.7 convolution_convert_fusion.1.q_ref.k_ref.v_ref
  181.8 21.8 %attention_forward.3 = (bf16[1280,512]{1,0:T(8,128)(2,1)S(1)}, f32[4,8,1280]{2,1,0:T(8,128)S(1)}) custom-call(bf16[1280,1536]{1,0:T(8,128)(2,1)S(1)} %copy-done.15, bf16[1280,1536]{1,0:T(8,128)(2,1)S(1)} %copy-done.15, bf16[1280,1536]{1,0:T(8,128)(2,1)S(1)} %copy-done.15, s32[1280,8]{1,0:T(8,128)S(1)} %pad.14.clone.col_ref, s32[8,1280]{1,0:T(8,128)S(1)} %pad.15.row_ref), custom_call_target="tpu_custom_call" | custom-call | flops 8053063680 | bytes 5898240 | tf_op jit(solution)/shard_map/attention_forward/pallas_call | solution.py:80
  206.1 8.8 convolution_convert_fusion.2.q_ref.k_ref.v_ref
  214.9 3.4 slice.135
  218.7 9.0 convolution_convert_fusion.q_ref.k_ref.v_ref
  232.1 21.5 %attention_forward.5 = (bf16[1280,512]{1,0:T(8,128)(2,1)S(1)}, f32[4,8,1280]{2,1,0:T(8,128)S(1)}) custom-call(bf16[1280,1536]{1,0:T(8,128)(2,1)S(1)} %copy-done.17, bf16[1280,1536]{1,0:T(8,128)(2,1)S(1)} %copy-done.17, bf16[1280,1536]{1,0:T(8,128)(2,1)S(1)} %copy-done.17, s32[1280,8]{1,0:T(8,128)S(1)} %pad.16.clone.col_ref, s32[8,1280]{1,0:T(8,128)S(1)} %pad.17.row_ref), custom_call_target="tpu_custom_call" | custom-call | flops 8053063680 | bytes 5898240 | tf_op jit(solution)/shard_map/attention_forward/pallas_call | solution.py:80
  254.7 21.5 %attention_forward.4 = (bf16[1280,512]{1,0:T(8,128)(2,1)S(1)}, f32[4,8,1280]{2,1,0:T(8,128)S(1)}) custom-call(bf16[1280,1536]{1,0:T(8,128)(2,1)S(1)} %copy-done.13, bf16[1280,1536]{1,0:T(8,128)(2,1)S(1)} %copy-done.13, bf16[1280,1536]{1,0:T(8,128)(2,1)S(1)} %copy-done.13, s32[1280,8]{1,0:T(8,128)S(1)} %pad.16.clone.col_ref, s32[8,1280]{1,0:T(8,128)S(1)} %pad.17.row_ref), custom_call_target="tpu_custom_call" | custom-call | flops 8053063680 | bytes 5898240 | tf_op jit(solution)/shard_map/attention_forward/pallas_call | solution.py:80
  286.8 5.4 fusion.64
  295.4 21.7 %add_convert_fusion = (bf16[1920,2048]{1,0:T(8,128)(2,1)}, bf16[1920,2048]{1,0:T(8,128)(2,1)}) fusion(bf16[1920,1024]{1,0:T(8,128)(2,1)S(1)} %add_convert_fusion.3, bf16[1024,2048]{1,0:T(8,128)(2,1)} %bitcast.351), kind=kOutput, calls=%fused_computation.2 | convolution fusion | flops 8123842560 | bytes 23855104 | tf_op jit(solution)/shard_map/dot_general | solution.py:23
  317.1 18.8 %add_convert_fusion.1 = (bf16[1920,2048]{1,0:T(8,128)(2,1)}, bf16[1920,2048]{1,0:T(8,128)(2,1)}) fusion(bf16[1920,1024]{1,0:T(8,128)(2,1)S(1)} %add_convert_fusion.3, bf16[1024,2048]{1,0:T(8,128)(2,1)S(1)} %bitcast.350), kind=kOutput, calls=%fused_computation.5 | convolution fusion | flops 8123842560 | bytes 23855104 | tf_op jit(solution)/shard_map/dot_general | solution.py:23
  340.3 15.1 %fusion.49 = f32[1920,1024]{1,0:T(8,128)} fusion(bf16[1920,2048]{1,0:T(8,128)(2,1)} %get-tuple-element.53, pred[]{:T(512)S(6)} %eq.30, bf16[2048,2048]{1,0:T(8,128)(2,1)} %all-gather.2.cloned.1.call-done), kind=kOutput, calls=%fused_computation.162 | convolution fusion | flops 8055160832 | bytes 24117248 | tf_op jit(solution)/shard_map/dot_general | solution.py:27
  355.4 20.4 %fusion.71 = (f32[1920]{0:T(1024)S(1)}, f32[1920,1024]{1,0:T(8,128)S(1)}) fusion(f32[1920,1024]{1,0:T(8,128)} %fusion.49, bf16[1920,2048]{1,0:T(8,128)(2,1)} %get-tuple-element.56, pred[]{:T(512)S(6)} %eq.31, bf16[2048,2048]{1,0:T(8,128)(2,1)} %all-gather.2.cloned.1.call-done), kind=kOutput, calls=%fused_computation.254 | convolution fusion | flops 8059090944 | bytes 31989248 | tf_op jit(solution)/shard_map/dot_general | solution.py:27
  378.0 4.9 fusion.24
  382.8 3.7 fusion.22
  386.6 14.4 %convolution_convert_fusion.6 = bf16[1024,2048]{1,0:T(8,128)(2,1)S(1)} fusion(bf16[1920,1024]{1,0:T(8,128)(2,1)S(1)} %get-tuple-element.134, bf16[1920,2048]{1,0:T(8,128)(2,1)} %get-tuple-element.56), kind=kOutput, calls=%fused_computation.83 | convolution fusion | flops 8055160832 | bytes 15990784 | tf_op jit(solution)/shard_map/dot_general | solution.py:31
  401.0 11.6 %convolution_convert_fusion.7 = bf16[1024,2048]{1,0:T(8,128)(2,1)S(1)} fusion(bf16[1920,1024]{1,0:T(8,128)(2,1)S(1)} %get-tuple-element.134, bf16[1920,2048]{1,0:T(8,128)(2,1)} %get-tuple-element.53), kind=kOutput, calls=%fused_computation.84 | convolution fusion | flops 8055160832 | bytes 15990784 | tf_op jit(solution)/shard_map/dot_general | solution.py:31
  417.6 14.5 %multiply_convert_fusion = bf16[1920,2048]{1,0:T(8,128)(2,1)} fusion(bf16[1920,2048]{1,0:T(8,128)(2,1)} %get-tuple-element.60, bf16[1920,1024]{1,0:T(8,128)(2,1)S(1)} %copy-done.45, pred[]{:T(512)S(6)} %eq.31, bf16[2048,2048]{1,0:T(8,128)(2,1)} %all-gather.2.cloned.1.call-done), kind=kOutput, calls=%fused_computation | convolution fusion | flops 8066957312 | bytes 28049408 | tf_op jit(solution)/shard_map/dot_general | solution.py:23
  432.1 16.8 %multiply_convert_fusion.1 = bf16[1920,2048]{1,0:T(8,128)(2,1)} fusion(bf16[1920,2048]{1,0:T(8,128)(2,1)} %get-tuple-element.58, bf16[1920,1024]{1,0:T(8,128)(2,1)} %copy-done.44, pred[]{:T(512)S(6)} %eq.30, bf16[2048,2048]{1,0:T(8,128)(2,1)} %all-gather.2.cloned.1.call-done), kind=kOutput, calls=%fused_computation.1 | convolution fusion | flops 8066957312 | bytes 28049408 | tf_op jit(solution)/shard_map/dot_general | solution.py:23
  460.6 12.0 %convolution_convert_fusion.4 = bf16[1024,2048]{1,0:T(8,128)(2,1)S(1)} fusion(bf16[1920,1024]{1,0:T(8,128)(2,1)S(1)} %copy-done.47, bf16[1920,2048]{1,0:T(8,128)(2,1)} %multiply_convert_fusion), kind=kOutput, calls=%fused_computation.81 | convolution fusion | flops 8055160832 | bytes 15990784 | tf_op jit(solution)/shard_map/dot_general | solution.py:31
  475.2 9.8 %convolution_convert_fusion.5 = bf16[1024,2048]{1,0:T(8,128)(2,1)S(1)} fusion(bf16[1920,1024]{1,0:T(8,128)(2,1)S(1)} %copy-done.47, bf16[1920,2048]{1,0:T(8,128)(2,1)S(1)} %bitcast.363), kind=kOutput, calls=%fused_computation.82 | convolution fusion | flops 8055160832 | bytes 15990784 | tf_op jit(solution)/shard_map/dot_general | solution.py:31
  487.3 15.9 %collective-permute-done.9 = bf16[4,64,2048]{2,1,0:T(8,128)(2,1)S(1)} collective-permute-done((bf16[4,64,2048]{2,1,0:T(8,128)(2,1)S(1)}, bf16[4,64,2048]{2,1,0:T(8,128)(2,1)S(1)}, u32[]{:S(2)}, u32[]{:S(2)}) %collective-permute-start.9) | collective-permute-done | bytes 1048608 | tf_op jit(solution)/shard_map/ppermute | solution.py:399
  503.2 3.9 collective-permute-done.5
  513.0 12.9 %fusion.73 = f32[1920,1024]{1,0:T(8,128)} fusion(bf16[1920,2048]{1,0:T(8,128)(2,1)} %multiply_convert_fusion, bf16[1024,2048]{1,0:T(8,128)(2,1)S(1)} %bitcast.352), kind=kOutput, calls=%fused_computation.256 | convolution fusion | flops 8053063680 | bytes 19922944 | tf_op jit(solution)/shard_map/dot_general | solution.py:27
  526.0 21.2 %multiply_reduce_fusion = (f32[1024]{0:T(1024)}, f32[1920]{0:T(1024)S(1)}, f32[1920]{0:T(1024)S(1)}, f32[1024]{0:T(1024)}, f32[1920,1024]{1,0:T(8,128)}) fusion(f32[1920,1024]{1,0:T(8,128)} %copy-done.20, f32[1920]{0:T(1024)S(1)} %copy-done.74, f32[1920]{0:T(1024)S(1)} %copy-done.71, f32[1024]{0:T(1024)S(1)} %bitcast.333, f32[1920,1024]{1,0:T(8,128)} %fusion.73, ...), kind=kOutput, calls=%fused_computation.45 | convolution fusion | flops 8072718336 | bytes 35694592 | tf_op jit(solution)/shard_map/dot_general | solution.py:27
  547.2 11.5 %multiply_reduce_fusion.1 = (f32[1024]{0:T(1024)}, f32[1920]{0:T(1024)S(1)}, f32[1920]{0:T(1024)S(1)}, f32[1024]{0:T(1024)}, f32[1920,1024]{1,0:T(8,128)S(1)}) fusion(f32[1920,1024]{1,0:T(8,128)S(1)} %bitcast.283, f32[1920]{0:T(1024)S(1)} %copy-done.69, f32[1920]{0:T(1024)S(1)} %copy-done.65, f32[1024]{0:T(1024)S(1)} %bitcast.327, ...), kind=kLoop, calls=%fused_computation.46 | loop fusion | flops 35383552 | bytes 35467264 | tf_op jit(solution)/shard_map/reduce_sum | solution.py:217
  584.3 26.9 %attention_backward.3 = bf16[1280,1536]{1,0:T(8,128)(2,1)S(1)} custom-call(bf16[1280,1536]{1,0:T(8,128)(2,1)S(1)} %copy-done.18, bf16[1280,1536]{1,0:T(8,128)(2,1)S(1)} %copy-done.18, bf16[1280,1536]{1,0:T(8,128)(2,1)S(1)} %copy-done.18, bf16[1280,512]{1,0:T(8,128)(2,1)S(1)} %convolution_convert_fusion.9.do_ref, bf16[1280,512]{1,0:T(8,128)(2,1)S(1)} %copy-done.6, ...), custom_call_target="tpu_custom_call" | custom-call | flops 20132659200 | bytes 11796480 | tf_op jit(solution)/shard_map/attention_backward/pallas_call | solution.py:171
  611.2 4.5 convolution_convert_fusion.8
  626.3 52.5 %collective-permute-done.15 = bf16[640,512]{1,0:T(8,128)(2,1)S(1)} collective-permute-done((bf16[640,512]{1,0:T(8,128)(2,1)S(1)}, bf16[640,512]{1,0:T(8,128)(2,1)S(1)}, u32[]{:S(2)}, u32[]{:S(2)}) %collective-permute-start.15) | collective-permute-done | bytes 655392 | tf_op jit(solution)/shard_map/ppermute | solution.py:399
  680.2 26.6 %attention_backward.4 = bf16[1280,1536]{1,0:T(8,128)(2,1)S(1)} custom-call(bf16[1280,1536]{1,0:T(8,128)(2,1)S(1)} %copy-done.16, bf16[1280,1536]{1,0:T(8,128)(2,1)S(1)} %copy-done.16, bf16[1280,1536]{1,0:T(8,128)(2,1)S(1)} %copy-done.16, bf16[1280,512]{1,0:T(8,128)(2,1)S(1)} %pad_maximum_fusion.6.do_ref, bf16[1280,512]{1,0:T(8,128)(2,1)S(1)} %copy-done.4, ...), custom_call_target="tpu_custom_call" | custom-call | flops 20132659200 | bytes 11796480 | tf_op jit(solution)/shard_map/attention_backward/pallas_call | solution.py:171
  708.9 6.2 fusion.75
  716.5 19.9 %collective-permute-done.17 = bf16[4,64,512]{2,1,0:T(8,128)(2,1)S(1)} collective-permute-done((bf16[4,64,512]{2,1,0:T(8,128)(2,1)}, bf16[4,64,512]{2,1,0:T(8,128)(2,1)S(1)}, u32[]{:S(2)}, u32[]{:S(2)}) %collective-permute-start.17) | collective-permute-done | bytes 262176 | tf_op jit(solution)/shard_map/ppermute | solution.py:399
  746.8 26.6 %attention_backward.5 = bf16[1280,1536]{1,0:T(8,128)(2,1)S(1)} custom-call(bf16[1280,1536]{1,0:T(8,128)(2,1)S(1)} %copy-done.14, bf16[1280,1536]{1,0:T(8,128)(2,1)S(1)} %copy-done.14, bf16[1280,1536]{1,0:T(8,128)(2,1)S(1)} %copy-done.14, bf16[1280,512]{1,0:T(8,128)(2,1)S(1)} %convolution_convert_fusion.10.do_ref, bf16[1280,512]{1,0:T(8,128)(2,1)S(1)} %copy-done.10, ...), custom_call_target="tpu_custom_call" | custom-call | flops 20132659200 | bytes 11796480 | tf_op jit(solution)/shard_map/attention_backward/pallas_call | solution.py:171
  775.3 7.0 pad_maximum_fusion
  782.3 12.7 %convolution_convert_fusion.3 = bf16[1024,1536]{1,0:T(8,128)(2,1)S(1)} fusion(bf16[2560,1024]{1,0:T(8,128)(2,1)} %copy-done.35, bf16[2560,1536]{1,0:T(8,128)(2,1)} %pad_maximum_fusion), kind=kOutput, calls=%fused_computation.80 | convolution fusion | flops 8054636544 | bytes 16252928 | tf_op jit(solution)/shard_map/dot_general | solution.py:31
  806.1 6.1 collective-permute-done.35
  813.9 8.2 collective-permute-done.36
  826.3 7.2 collective-permute-done.23
  835.1 4.5 fusion.74
  839.7 4.3 fusion.72
  844.1 6.7 fusion.18
  857.0 8.6 fusion.17
  883.7 5.1 collective-permute-done.29
  888.8 6.6 collective-permute-done.30
  896.3 9.9 %collective-permute-done.26 = bf16[640,1024]{1,0:T(8,128)(2,1)} collective-permute-done((bf16[640,1024]{1,0:T(8,128)(2,1)}, bf16[640,1024]{1,0:T(8,128)(2,1)}, u32[]{:S(2)}, u32[]{:S(2)}) %collective-permute-start.26) | collective-permute-done | bytes 1310752 | tf_op jit(solution)/shard_map/ppermute | solution.py:399
  909.3 3.7 maximum_bitcast_fusion
  (432 shorter events, 169.7 us)
Async XLA Ops:
  7.2 333.1 %all-gather.2.cloned.1.call-start = ((), (), s32[]{:S(2)}) async-start(), calls=%async_computation | async-start | bytes 8650752 | tf_op jit(solution)/shard_map/all_gather | solution.py:517
  165.7 118.4 %copy-start.77 = (f32[1,1024]{1,0:T(1,128)}, f32[1,1024]{1,0:T(1,128)S(1)}, u32[]{:S(2)}) copy-start(f32[1,1024]{1,0:T(1,128)S(1)} %get-tuple-element.180) | copy-start | bytes 12292
  165.7 127.5 %copy-start.80 = (f32[1,1024]{1,0:T(1,128)}, f32[1,1024]{1,0:T(1,128)S(1)}, u32[]{:S(2)}) copy-start(f32[1,1024]{1,0:T(1,128)S(1)} %get-tuple-element.182) | copy-start | bytes 12292
  205.6 73.1 %collective-permute-start = (bf16[640,512]{1,0:T(8,128)(2,1)}, bf16[640,512]{1,0:T(8,128)(2,1)S(1)}, u32[]{:S(2)}, u32[]{:S(2)}) collective-permute-start(bf16[640,512]{1,0:T(8,128)(2,1)} %get-tuple-element.157), channel_id=1, source_target_pairs={{0,1},{1,0},{2,3},{3,2},{4,5},{5,4},{6,7},{7,6},{8,9},{9,8},{10,11... | collective-permute-start | bytes 1966088 | tf_op jit(solution)/shard_map/ppermute | solution.py:399
  279.1 57.3 %collective-permute-start.2 = (bf16[640,1024]{1,0:T(8,128)(2,1)S(1)}, bf16[640,1024]{1,0:T(8,128)(2,1)S(1)}, u32[]{:S(2)}, u32[]{:S(2)}) collective-permute-start(bf16[640,1024]{1,0:T(8,128)(2,1)S(1)} %get-tuple-element.145), channel_id=1, source_target_pairs={{0,1},{1,0},{2,3},{3,2},{4,5},{5,4},{6,7},{7,6},{8,9},{9,8},{10,11... | collective-permute-start | bytes 3932168 | tf_op jit(solution)/shard_map/ppermute | solution.py:399
  414.1 37.6 %collective-permute-start.4 = (bf16[4,2,64,2048]{3,2,1,0:T(8,128)(2,1)}, bf16[4,2,64,2048]{3,2,1,0:T(8,128)(2,1)}, u32[]{:S(2)}, u32[]{:S(2)}) collective-permute-start(bf16[4,2,64,2048]{3,2,1,0:T(8,128)(2,1)} %dynamic-slice_bitcast_fusion.2), channel_id=1, source_target_pairs={{0,2},{2,0},{1,3},{3,1},{4,6},{6,4},{5,7},{7,5},{8,10},{10,8},{9,1... | collective-permute-start | bytes 6291464 | tf_op jit(solution)/shard_map/ppermute | solution.py:399
  415.8 41.7 %collective-permute-start.3 = (bf16[4,2,64,2048]{3,2,1,0:T(8,128)(2,1)}, bf16[4,2,64,2048]{3,2,1,0:T(8,128)(2,1)}, u32[]{:S(2)}, u32[]{:S(2)}) collective-permute-start(bf16[4,2,64,2048]{3,2,1,0:T(8,128)(2,1)} %dynamic-slice_bitcast_fusion.3), channel_id=1, source_target_pairs={{0,2},{2,0},{1,3},{3,1},{4,6},{6,4},{5,7},{7,5},{8,10},{10,8},{9,1... | collective-permute-start | bytes 6291464 | tf_op jit(solution)/shard_map/ppermute | solution.py:399
  416.2 33.9 %collective-permute-start.1 = (bf16[640,1024]{1,0:T(8,128)(2,1)S(1)}, bf16[640,1024]{1,0:T(8,128)(2,1)S(1)}, u32[]{:S(2)}, u32[]{:S(2)}) collective-permute-start(bf16[640,1024]{1,0:T(8,128)(2,1)S(1)} %dynamic-slice_bitcast_fusion.6), channel_id=1, source_target_pairs={{0,1},{1,0},{2,3},{3,2},{4,5},{5,4},{6,7},{7,6},{8,9},{9,8},{10,11... | collective-permute-start | bytes 3932168 | tf_op jit(solution)/shard_map/ppermute | solution.py:399
  454.4 32.9 %collective-permute-start.6 = (bf16[4,64,2048]{2,1,0:T(8,128)(2,1)S(1)}, bf16[4,64,2048]{2,1,0:T(8,128)(2,1)S(1)}, u32[]{:S(2)}, u32[]{:S(2)}) collective-permute-start(bf16[4,64,2048]{2,1,0:T(8,128)(2,1)S(1)} %get-tuple-element.151), channel_id=1, source_target_pairs={{0,1},{1,0},{4,5},{5,4},{2,3},{3,2},{6,7},{7,6},{8,9},{9,8},{12,13... | collective-permute-start | bytes 3145736 | tf_op jit(solution)/shard_map/ppermute | solution.py:399
  455.2 48.0 %collective-permute-start.9 = (bf16[4,64,2048]{2,1,0:T(8,128)(2,1)S(1)}, bf16[4,64,2048]{2,1,0:T(8,128)(2,1)S(1)}, u32[]{:S(2)}, u32[]{:S(2)}) collective-permute-start(bf16[4,64,2048]{2,1,0:T(8,128)(2,1)S(1)} %get-tuple-element.152), channel_id=1, source_target_pairs={{0,5},{1,4},{4,1},{5,0},{2,7},{3,6},{6,3},{7,2},{8,13},{9,12},{12,... | collective-permute-start | bytes 3145736 | tf_op jit(solution)/shard_map/ppermute | solution.py:399
  460.0 47.1 %collective-permute-start.5 = (bf16[4,64,2048]{2,1,0:T(8,128)(2,1)S(1)}, bf16[4,64,2048]{2,1,0:T(8,128)(2,1)S(1)}, u32[]{:S(2)}, u32[]{:S(2)}) collective-permute-start(bf16[4,64,2048]{2,1,0:T(8,128)(2,1)S(1)} %dynamic-slice_bitcast_fusion.13), channel_id=1, source_target_pairs={{0,4},{1,5},{4,0},{5,1},{2,6},{3,7},{6,2},{7,3},{8,12},{9,13},{12,... | collective-permute-start | bytes 3145736 | tf_op jit(solution)/shard_map/ppermute | solution.py:399
  475.2 90.7 %collective-permute-start.8 = (bf16[4,2,64,2048]{3,2,1,0:T(8,128)(2,1)}, bf16[4,2,64,2048]{3,2,1,0:T(8,128)(2,1)}, u32[]{:S(2)}, u32[]{:S(2)}) collective-permute-start(bf16[4,2,64,2048]{3,2,1,0:T(8,128)(2,1)} %dynamic-slice_bitcast_fusion), channel_id=1, source_target_pairs={{0,2},{2,0},{1,3},{3,1},{4,6},{6,4},{5,7},{7,5},{8,10},{10,8},{9,1... | collective-permute-start | bytes 6291464 | tf_op jit(solution)/shard_map/ppermute | solution.py:399
  486.8 81.5 %collective-permute-start.7 = (bf16[4,2,64,2048]{3,2,1,0:T(8,128)(2,1)}, bf16[4,2,64,2048]{3,2,1,0:T(8,128)(2,1)}, u32[]{:S(2)}, u32[]{:S(2)}) collective-permute-start(bf16[4,2,64,2048]{3,2,1,0:T(8,128)(2,1)} %dynamic-slice_bitcast_fusion.1), channel_id=1, source_target_pairs={{0,2},{2,0},{1,3},{3,1},{4,6},{6,4},{5,7},{7,5},{8,10},{10,8},{9,1... | collective-permute-start | bytes 6291464 | tf_op jit(solution)/shard_map/ppermute | solution.py:399
  508.6 54.2 %collective-permute-start.20 = (bf16[64,2048]{1,0:T(8,128)(2,1)}, bf16[64,2048]{1,0:T(8,128)(2,1)}, u32[]{:S(2)}, u32[]{:S(2)}) collective-permute-start(bf16[64,2048]{1,0:T(8,128)(2,1)} %get-tuple-element.162), channel_id=1, source_target_pairs={{0,8},{8,0},{16,24},{24,16},{1,9},{9,1},{17,25},{25,17},{2,10},{10... | collective-permute-start | bytes 786440 | tf_op jit(solution)/shard_map/ppermute | solution.py:399
  509.1 53.7 %collective-permute-start.21 = (bf16[64,2048]{1,0:T(8,128)(2,1)S(1)}, bf16[64,2048]{1,0:T(8,128)(2,1)}, u32[]{:S(2)}, u32[]{:S(2)}) collective-permute-start(bf16[64,2048]{1,0:T(8,128)(2,1)S(1)} %get-tuple-element.164), channel_id=1, source_target_pairs={{0,16},{8,24},{16,0},{24,8},{1,17},{9,25},{17,1},{25,9},{2,18},{10... | collective-permute-start | bytes 786440 | tf_op jit(solution)/shard_map/ppermute | solution.py:399
  510.3 52.5 %collective-permute-start.22 = (bf16[64,2048]{1,0:T(8,128)(2,1)S(1)}, bf16[64,2048]{1,0:T(8,128)(2,1)}, u32[]{:S(2)}, u32[]{:S(2)}) collective-permute-start(bf16[64,2048]{1,0:T(8,128)(2,1)S(1)} %get-tuple-element.163), channel_id=1, source_target_pairs={{0,24},{8,16},{16,8},{24,0},{1,25},{9,17},{17,9},{25,1},{2,26},{10... | collective-permute-start | bytes 786440 | tf_op jit(solution)/shard_map/ppermute | solution.py:399
  582.9 37.7 %collective-permute-start.11 = (bf16[4,2,64,512]{3,2,1,0:T(8,128)(2,1)}, bf16[4,2,64,512]{3,2,1,0:T(8,128)(2,1)}, u32[]{:S(2)}, u32[]{:S(2)}) collective-permute-start(bf16[4,2,64,512]{3,2,1,0:T(8,128)(2,1)} %dynamic-slice_bitcast_fusion.18), channel_id=1, source_target_pairs={{0,2},{2,0},{1,3},{3,1},{4,6},{6,4},{5,7},{7,5},{8,10},{10,8},{9,1... | collective-permute-start | bytes 1572872 | tf_op jit(solution)/shard_map/ppermute | solution.py:399
  583.7 39.2 %collective-permute-start.10 = (bf16[4,2,64,512]{3,2,1,0:T(8,128)(2,1)}, bf16[4,2,64,512]{3,2,1,0:T(8,128)(2,1)}, u32[]{:S(2)}, u32[]{:S(2)}) collective-permute-start(bf16[4,2,64,512]{3,2,1,0:T(8,128)(2,1)} %dynamic-slice_bitcast_fusion.19), channel_id=1, source_target_pairs={{0,2},{2,0},{1,3},{3,1},{4,6},{6,4},{5,7},{7,5},{8,10},{10,8},{9,1... | collective-permute-start | bytes 1572872 | tf_op jit(solution)/shard_map/ppermute | solution.py:399
  615.9 130.4 %collective-permute-start.14 = (bf16[4,2,64,1536]{3,2,1,0:T(8,128)(2,1)S(1)}, bf16[4,2,64,1536]{3,2,1,0:T(8,128)(2,1)S(1)}, u32[]{:S(2)}, u32[]{:S(2)}) collective-permute-start(bf16[4,2,64,1536]{3,2,1,0:T(8,128)(2,1)S(1)} %dynamic-slice_bitcast_fusion.4), channel_id=1, source_target_pairs={{0,2},{2,0},{1,3},{3,1},{4,6},{6,4},{5,7},{7,5},{8,10},{10,8},{9,1... | collective-permute-start | bytes 4718600 | tf_op jit(solution)/shard_map/ppermute | solution.py:399
  616.0 122.5 %collective-permute-start.13 = (bf16[4,64,2048]{2,1,0:T(8,128)(2,1)}, bf16[4,64,2048]{2,1,0:T(8,128)(2,1)}, u32[]{:S(2)}, u32[]{:S(2)}) collective-permute-start(bf16[4,64,2048]{2,1,0:T(8,128)(2,1)} %get-tuple-element.149), channel_id=1, source_target_pairs={{0,1},{1,0},{4,5},{5,4},{2,3},{3,2},{6,7},{7,6},{8,9},{9,8},{12,13... | collective-permute-start | bytes 3145736 | tf_op jit(solution)/shard_map/ppermute | solution.py:399
  617.0 121.6 %collective-permute-start.16 = (bf16[4,64,2048]{2,1,0:T(8,128)(2,1)}, bf16[4,64,2048]{2,1,0:T(8,128)(2,1)}, u32[]{:S(2)}, u32[]{:S(2)}) collective-permute-start(bf16[4,64,2048]{2,1,0:T(8,128)(2,1)} %get-tuple-element.150), channel_id=1, source_target_pairs={{0,5},{1,4},{4,1},{5,0},{2,7},{3,6},{6,3},{7,2},{8,13},{9,12},{12,... | collective-permute-start | bytes 3145736 | tf_op jit(solution)/shard_map/ppermute | solution.py:399
  620.6 58.2 %collective-permute-start.15 = (bf16[640,512]{1,0:T(8,128)(2,1)S(1)}, bf16[640,512]{1,0:T(8,128)(2,1)S(1)}, u32[]{:S(2)}, u32[]{:S(2)}) collective-permute-start(bf16[640,512]{1,0:T(8,128)(2,1)S(1)} %convolution_convert_fusion.14), channel_id=1, source_target_pairs={{0,1},{1,0},{2,3},{3,2},{4,5},{5,4},{6,7},{7,6},{8,9},{9,8},{10,11... | collective-permute-start | bytes 1966088 | tf_op jit(solution)/shard_map/ppermute | solution.py:399
  622.9 83.9 %collective-permute-start.18 = (bf16[4,64,512]{2,1,0:T(8,128)(2,1)S(1)}, bf16[4,64,512]{2,1,0:T(8,128)(2,1)S(1)}, u32[]{:S(2)}, u32[]{:S(2)}) collective-permute-start(bf16[4,64,512]{2,1,0:T(8,128)(2,1)S(1)} %get-tuple-element.168), channel_id=1, source_target_pairs={{0,1},{1,0},{4,5},{5,4},{2,3},{3,2},{6,7},{7,6},{8,9},{9,8},{12,13... | collective-permute-start | bytes 786440 | tf_op jit(solution)/shard_map/ppermute | solution.py:399
  678.8 29.4 %collective-permute-start.19 = (bf16[4,64,512]{2,1,0:T(8,128)(2,1)S(1)}, bf16[4,64,512]{2,1,0:T(8,128)(2,1)S(1)}, u32[]{:S(2)}, u32[]{:S(2)}) collective-permute-start(bf16[4,64,512]{2,1,0:T(8,128)(2,1)S(1)} %get-tuple-element.169), channel_id=1, source_target_pairs={{0,5},{1,4},{4,1},{5,0},{2,7},{3,6},{6,3},{7,2},{8,13},{9,12},{12,... | collective-permute-start | bytes 786440 | tf_op jit(solution)/shard_map/ppermute | solution.py:399
  706.8 33.6 %collective-permute-start.12 = (bf16[4,64,2048]{2,1,0:T(8,128)(2,1)S(1)}, bf16[4,64,2048]{2,1,0:T(8,128)(2,1)S(1)}, u32[]{:S(2)}, u32[]{:S(2)}) collective-permute-start(bf16[4,64,2048]{2,1,0:T(8,128)(2,1)S(1)} %dynamic-slice_bitcast_fusion.9), channel_id=1, source_target_pairs={{0,4},{1,5},{4,0},{5,1},{2,6},{3,7},{6,2},{7,3},{8,12},{9,13},{12,... | collective-permute-start | bytes 3145736 | tf_op jit(solution)/shard_map/ppermute | solution.py:399
  708.2 28.2 %collective-permute-start.17 = (bf16[4,64,512]{2,1,0:T(8,128)(2,1)}, bf16[4,64,512]{2,1,0:T(8,128)(2,1)S(1)}, u32[]{:S(2)}, u32[]{:S(2)}) collective-permute-start(bf16[4,64,512]{2,1,0:T(8,128)(2,1)} %dynamic-slice_bitcast_fusion.28), channel_id=1, source_target_pairs={{0,4},{1,5},{4,0},{5,1},{2,6},{3,7},{6,2},{7,3},{8,12},{9,13},{12,... | collective-permute-start | bytes 786440 | tf_op jit(solution)/shard_map/ppermute | solution.py:399
  736.3 87.6 %collective-permute-start.25 = (bf16[640,1024]{1,0:T(8,128)(2,1)}, bf16[640,1024]{1,0:T(8,128)(2,1)}, u32[]{:S(2)}, u32[]{:S(2)}) collective-permute-start(bf16[640,1024]{1,0:T(8,128)(2,1)} %dynamic-slice_convert_fusion.1), channel_id=1, source_target_pairs={{0,1},{1,0},{2,3},{3,2},{4,5},{5,4},{6,7},{7,6},{8,9},{9,8},{10,11... | collective-permute-start | bytes 3932168 | tf_op jit(solution)/shard_map/ppermute | solution.py:399
  738.5 61.2 %collective-permute-start.32 = (bf16[64,512]{1,0:T(8,128)(2,1)S(1)}, bf16[64,512]{1,0:T(8,128)(2,1)S(1)}, u32[]{:S(2)}, u32[]{:S(2)}) collective-permute-start(bf16[64,512]{1,0:T(8,128)(2,1)S(1)} %get-tuple-element.170), channel_id=1, source_target_pairs={{0,8},{8,0},{16,24},{24,16},{1,9},{9,1},{17,25},{25,17},{2,10},{10... | collective-permute-start | bytes 196616 | tf_op jit(solution)/shard_map/ppermute | solution.py:399
  738.6 61.2 %collective-permute-start.33 = (bf16[64,512]{1,0:T(8,128)(2,1)S(1)}, bf16[64,512]{1,0:T(8,128)(2,1)S(1)}, u32[]{:S(2)}, u32[]{:S(2)}) collective-permute-start(bf16[64,512]{1,0:T(8,128)(2,1)S(1)} %get-tuple-element.172), channel_id=1, source_target_pairs={{0,16},{8,24},{16,0},{24,8},{1,17},{9,25},{17,1},{25,9},{2,18},{10... | collective-permute-start | bytes 196616 | tf_op jit(solution)/shard_map/ppermute | solution.py:399
  740.5 59.3 %collective-permute-start.34 = (bf16[64,512]{1,0:T(8,128)(2,1)S(1)}, bf16[64,512]{1,0:T(8,128)(2,1)S(1)}, u32[]{:S(2)}, u32[]{:S(2)}) collective-permute-start(bf16[64,512]{1,0:T(8,128)(2,1)S(1)} %get-tuple-element.171), channel_id=1, source_target_pairs={{0,24},{8,16},{16,8},{24,0},{1,25},{9,17},{17,9},{25,1},{2,26},{10... | collective-permute-start | bytes 196616 | tf_op jit(solution)/shard_map/ppermute | solution.py:399
  795.5 38.0 %collective-permute-start.24 = (bf16[4,2,64,1536]{3,2,0,1:T(8,128)(2,1)S(1)}, bf16[4,2,64,1536]{3,2,0,1:T(8,128)(2,1)S(1)}, u32[]{:S(2)}, u32[]{:S(2)}) collective-permute-start(bf16[4,2,64,1536]{3,2,0,1:T(8,128)(2,1)S(1)} %bitcast.308), channel_id=1, source_target_pairs={{0,2},{2,0},{1,3},{3,1},{4,6},{6,4},{5,7},{7,5},{8,10},{10,8},{9,1... | collective-permute-start | bytes 4718600 | tf_op jit(solution)/shard_map/ppermute | solution.py:399
  800.6 11.6 %collective-permute-start.35 = (bf16[64,2048]{1,0:T(8,128)(2,1)S(1)}, bf16[64,2048]{1,0:T(8,128)(2,1)S(1)}, u32[]{:S(2)}, u32[]{:S(2)}) collective-permute-start(bf16[64,2048]{1,0:T(8,128)(2,1)S(1)} %get-tuple-element.159), channel_id=1, source_target_pairs={{0,8},{8,0},{16,24},{24,16},{1,9},{9,1},{17,25},{25,17},{2,10},{10... | collective-permute-start | bytes 786440 | tf_op jit(solution)/shard_map/ppermute | solution.py:399
  800.6 21.4 %collective-permute-start.36 = (bf16[64,2048]{1,0:T(8,128)(2,1)S(1)}, bf16[64,2048]{1,0:T(8,128)(2,1)S(1)}, u32[]{:S(2)}, u32[]{:S(2)}) collective-permute-start(bf16[64,2048]{1,0:T(8,128)(2,1)S(1)} %get-tuple-element.161), channel_id=1, source_target_pairs={{0,16},{8,24},{16,0},{24,8},{1,17},{9,25},{17,1},{25,9},{2,18},{10... | collective-permute-start | bytes 786440 | tf_op jit(solution)/shard_map/ppermute | solution.py:399
  802.5 19.5 %collective-permute-start.37 = (bf16[64,2048]{1,0:T(8,128)(2,1)S(1)}, bf16[64,2048]{1,0:T(8,128)(2,1)S(1)}, u32[]{:S(2)}, u32[]{:S(2)}) collective-permute-start(bf16[64,2048]{1,0:T(8,128)(2,1)S(1)} %get-tuple-element.160), channel_id=1, source_target_pairs={{0,24},{8,16},{16,8},{24,0},{1,25},{9,17},{17,9},{25,1},{2,26},{10... | collective-permute-start | bytes 786440 | tf_op jit(solution)/shard_map/ppermute | solution.py:399
  812.2 21.3 %collective-permute-start.23 = (bf16[4,64,1536]{2,1,0:T(8,128)(2,1)S(1)}, bf16[4,64,1536]{2,1,0:T(8,128)(2,1)S(1)}, u32[]{:S(2)}, u32[]{:S(2)}) collective-permute-start(bf16[4,64,1536]{2,1,0:T(8,128)(2,1)S(1)} %get-tuple-element.154), channel_id=1, source_target_pairs={{0,5},{1,4},{4,1},{5,0},{2,7},{3,6},{6,3},{7,2},{8,13},{9,12},{12,... | collective-permute-start | bytes 2359304 | tf_op jit(solution)/shard_map/ppermute | solution.py:399
  823.0 52.8 %collective-permute-start.28 = (bf16[4,64,1536]{2,1,0:T(8,128)(2,1)}, bf16[4,64,1536]{2,1,0:T(8,128)(2,1)}, u32[]{:S(2)}, u32[]{:S(2)}) collective-permute-start(bf16[4,64,1536]{2,1,0:T(8,128)(2,1)} %get-tuple-element.153), channel_id=1, source_target_pairs={{0,1},{1,0},{4,5},{5,4},{2,3},{3,2},{6,7},{7,6},{8,9},{9,8},{12,13... | collective-permute-start | bytes 2359304 | tf_op jit(solution)/shard_map/ppermute | solution.py:399
  850.9 14.7 %collective-permute-start.38 = (f32[8,1024]{1,0:T(8,128)S(1)}, f32[8,1024]{1,0:T(8,128)S(1)}, u32[]{:S(2)}, u32[]{:S(2)}) collective-permute-start(f32[8,1024]{1,0:T(8,128)S(1)} %concatenate.39), channel_id=1, source_target_pairs={{0,1},{1,0},{4,5},{5,4},{2,3},{3,2},{6,7},{7,6},{8,9},{9,8},{12,13... | collective-permute-start | bytes 98312 | tf_op jit(solution)/shard_map/ppermute | solution.py:399
  852.0 13.6 %collective-permute-start.39 = (f32[8,1024]{1,0:T(8,128)S(1)}, f32[8,1024]{1,0:T(8,128)S(1)}, u32[]{:S(2)}, u32[]{:S(2)}) collective-permute-start(f32[8,1024]{1,0:T(8,128)S(1)} %concatenate.39), channel_id=1, source_target_pairs={{0,4},{1,5},{4,0},{5,1},{2,6},{3,7},{6,2},{7,3},{8,12},{9,13},{12,... | collective-permute-start | bytes 98312 | tf_op jit(solution)/shard_map/ppermute | solution.py:399
  853.2 12.4 %collective-permute-start.40 = (f32[8,1024]{1,0:T(8,128)S(1)}, f32[8,1024]{1,0:T(8,128)S(1)}, u32[]{:S(2)}, u32[]{:S(2)}) collective-permute-start(f32[8,1024]{1,0:T(8,128)S(1)} %concatenate.39), channel_id=1, source_target_pairs={{0,5},{1,4},{4,1},{5,0},{2,7},{3,6},{6,3},{7,2},{8,13},{9,12},{12,... | collective-permute-start | bytes 98312 | tf_op jit(solution)/shard_map/ppermute | solution.py:399
  855.7 20.0 %collective-permute-start.27 = (bf16[4,64,1536]{2,1,0:T(8,128)(2,1)S(1)}, bf16[4,64,1536]{2,1,0:T(8,128)(2,1)}, u32[]{:S(2)}, u32[]{:S(2)}) collective-permute-start(bf16[4,64,1536]{2,1,0:T(8,128)(2,1)S(1)} %dynamic-slice_bitcast_fusion.16), channel_id=1, source_target_pairs={{0,4},{1,5},{4,0},{5,1},{2,6},{3,7},{6,2},{7,3},{8,12},{9,13},{12,... | collective-permute-start | bytes 2359304 | tf_op jit(solution)/shard_map/ppermute | solution.py:399
  865.6 4.8 collective-permute-start.41
  865.7 4.9 collective-permute-start.42
  867.6 5.7 collective-permute-start.43
  873.3 2.4 collective-permute-start.44
  874.7 31.5 %collective-permute-start.26 = (bf16[640,1024]{1,0:T(8,128)(2,1)}, bf16[640,1024]{1,0:T(8,128)(2,1)}, u32[]{:S(2)}, u32[]{:S(2)}) collective-permute-start(bf16[640,1024]{1,0:T(8,128)(2,1)} %fusion.42), channel_id=1, source_target_pairs={{0,1},{1,0},{2,3},{3,2},{4,5},{5,4},{6,7},{7,6},{8,9},{9,8},{10,11... | collective-permute-start | bytes 3932168 | tf_op jit(solution)/shard_map/ppermute | solution.py:399
  878.0 10.8 %collective-permute-start.29 = (bf16[64,1536]{1,0:T(8,128)(2,1)S(1)}, bf16[64,1536]{1,0:T(8,128)(2,1)S(1)}, u32[]{:S(2)}, u32[]{:S(2)}) collective-permute-start(bf16[64,1536]{1,0:T(8,128)(2,1)S(1)} %get-tuple-element.165), channel_id=1, source_target_pairs={{0,8},{8,0},{16,24},{24,16},{1,9},{9,1},{17,25},{25,17},{2,10},{10... | collective-permute-start | bytes 589832 | tf_op jit(solution)/shard_map/ppermute | solution.py:399
  878.1 17.3 %collective-permute-start.30 = (bf16[64,1536]{1,0:T(8,128)(2,1)S(1)}, bf16[64,1536]{1,0:T(8,128)(2,1)S(1)}, u32[]{:S(2)}, u32[]{:S(2)}) collective-permute-start(bf16[64,1536]{1,0:T(8,128)(2,1)S(1)} %get-tuple-element.167), channel_id=1, source_target_pairs={{0,16},{8,24},{16,0},{24,8},{1,17},{9,25},{17,1},{25,9},{2,18},{10... | collective-permute-start | bytes 589832 | tf_op jit(solution)/shard_map/ppermute | solution.py:399
  881.2 14.2 %collective-permute-start.31 = (bf16[64,1536]{1,0:T(8,128)(2,1)S(1)}, bf16[64,1536]{1,0:T(8,128)(2,1)S(1)}, u32[]{:S(2)}, u32[]{:S(2)}) collective-permute-start(bf16[64,1536]{1,0:T(8,128)(2,1)S(1)} %get-tuple-element.166), channel_id=1, source_target_pairs={{0,24},{8,16},{16,8},{24,0},{1,25},{9,17},{17,9},{25,1},{2,26},{10... | collective-permute-start | bytes 589832 | tf_op jit(solution)/shard_map/ppermute | solution.py:399
  (109 other events, 1312.2 us)
Sparse Core Ops, SparseCore 0:
  206.2 77.1 all-gather.1

commit v6 on v4

--- a/solution.py
+++ b/solution.py
@@ -277,8 +277,8 @@
         partner = {"tp": apart(x, k)}
         crossed.append(copy(segments, segments_out.at[k - 1], partner))
         for n in range(moved):
-            source = tokens.at[n * tp + apart(x, k)]
-            crossed.append(copy(source, tokens_out.at[n * (tp - 1) + k - 1], partner))
+            target = tokens_out.at[n * (tp - 1) + k - 1]
+            crossed.append(copy(tokens.at[n * tp + apart(x, k)], target, partner))
 
     def part(number, t, at_y, span):
         weight, low, rows = chunks[number]
@@ -489,12 +489,12 @@
     def outgoing(values):
         return [block_at(values, 0, n * tp + (here ^ k)) for n in range(whole) for k in range(1, tp)]
 
-    def tree_rows(values, came):
+    def whole_trees(values, came):
         rows = []
         for n in range(whole):
             near = [block_at(values, 0, n * tp + here)]
             rows.append(in_place_order(near + came[n * (tp - 1) : (n + 1) * (tp - 1)]))
-        return lax.optimization_barrier(jnp.concatenate(rows + [values[m] for m in shared], axis=0))
+        return rows
 
     def rows_back(values):
         trees = values.reshape(micro, own_rows, width)
@@ -511,12 +511,17 @@
         return lax.dynamic_slice_in_dim(values, (here ^ k) * own_rows, own_rows)
 
     shard_qkv = w_qkv.reshape(w_qkv.shape[0], -1)
-    (full_qkv, full_out, full_up, full_down), seg_came, tokens_came = gather_weights(
-        [shard_qkv, w_out.T, w_up, w_down.T], [4, 1, 4, 4], tokens[:, 0], segments[:, 0]
+    (full_qkv, full_out, full_up), seg_came, tokens_came = gather_weights(
+        [shard_qkv, w_out.T, w_up], [4, 1, 4], tokens[:, 0], segments[:, 0]
     )
+    down = lax.all_gather(
+        after(w_down.T, full_qkv[0]), ("tp", "z", "y", "core"), axis=0, tiled=True
+    ).reshape(tp, width, -1)
+    full_down = [pick([down[s] for s in halves], here ^ t) for t in halves]
     seg_came = [segments[:, 0]] + seg_came
     seg_all = jnp.concatenate([pick(seg_came, here ^ s) for s in halves], axis=1)
-    x = tree_rows(tokens[:, 0], tokens_came).astype(f32)
+    rows = whole_trees(tokens[:, 0], tokens_came) + [tokens[m, 0] for m in shared]
+    x = lax.optimization_barrier(jnp.concatenate(rows, axis=0)).astype(f32)
     whole_tables = []
     for n in range(whole):
         seg = pick([seg_all[n * tp + s] for s in halves], here)
@@ -525,8 +530,9 @@
     share_tables = [segment_tables(seg_all[m], parents[m, 0]) for m in shared]
 
     normed = norm_forward(x, norm_gains[0], norm_biases[0]).astype(bf16)
+    normed_whole = normed[:split]
     share_qkv = [dot_nn(normed[split:], w).astype(bf16) for w in full_qkv]
-    whole_qkv = [dot_nn(normed[:split], w).astype(bf16) for w in full_qkv] if whole else []
+    whole_qkv = [dot_nn(normed_whole, w).astype(bf16) for w in full_qkv] if whole else []
     share_calls = []
     for n in range(share_count):
         cut = slice(n * own_rows, (n + 1) * own_rows)
@@ -561,11 +567,17 @@
         values, bent = lax.optimization_barrier((values.astype(bf16), bent.astype(bf16)))
         hidden.append(values)
         slope.append(bent)
+    normed_shared = []
+    for n in range(share_count):
+        start = split + n * own_rows
+        near = after(normed[start : start + own_rows], hidden[0])
+        normed_shared.append(in_place_order(exchange_tp([near] * tp)))
     branch_f = sum(dot_nt(hidden[t], full_down[t]) for t in halves)
     out = (residual + norm_forward(branch_f, norm_gains[3], norm_biases[3])).astype(bf16)
     out_rows = rows_back(out)
 
-    grad_out = tree_rows(cotangent, cotangent_came).astype(f32)
+    grad_out = whole_trees(cotangent, cotangent_came) + [cotangent[m] for m in shared]
+    grad_out = lax.optimization_barrier(jnp.concatenate(grad_out, axis=0)).astype(f32)
     grad_branch_f, sums_3 = norm_backward(branch_f, norm_gains[3], grad_out)
     grad_branch_f = grad_branch_f.astype(bf16)
     core_down = [scatter_core(dot_tn(grad_branch_f, hidden[t]).astype(bf16)) for t in halves]
@@ -576,8 +588,9 @@
     straight_down, across_down = scatter_plane(core_down)
     dw_up = [dot_tn(normed_f, grad_up[t]).astype(bf16) for t in halves]
     core_up = [scatter_core(part) for part in dw_up]
-    ready = [*dw_up, *straight_down]
-    grad_normed_f = sum(dot_nt(after(grad_up[t], *ready), full_up[t]) for t in halves)
+    grad_up = [after(values, *dw_up) for values in grad_up]
+    grad_up[1:] = [after(values, *straight_down) for values in grad_up[1:]]
+    grad_normed_f = sum(dot_nt(grad_up[t], full_up[t]) for t in halves)
     grad_part, sums_2 = norm_backward(residual, norm_gains[2], grad_normed_f)
     grad_residual = grad_out + grad_part
 
@@ -593,37 +606,56 @@
         share_do.append(in_place_order(exchange_tp([part[cut] for part in share_grad])))
     core_out = [scatter_core(dot_tn(grad_branch_a, part).astype(bf16)) for part in attended]
     grad_qkv = [[] for _ in halves]
-    share_parts = [[] for _ in halves]
 
     def whole_backward(t, *others):
         for n in range(whole):
             qkv, att, lse = saved[n, t]
-            do = whole_grad[t][n * tree_len : (n + 1) * tree_len]
+            do = after(whole_grad[t][n * tree_len : (n + 1) * tree_len], *share_grad)
             made = attention_backward(qkv, after(do, *others), att, lse, *whole_tables[n])
             grad_qkv[t].append(made)
         return grad_qkv[t]
 
     made = []
+    dw_qkv = [None] * tp
     for t in range(1, tp):
         made += whole_backward(t)
+        if whole:
+            dw_qkv[t] = dot_tn(normed_whole, jnp.concatenate(grad_qkv[t], axis=0)).astype(bf16)
+        else:
+            dw_qkv[t] = jnp.zeros(full_qkv[t].shape, bf16)
+    core_qkv = [None] + [scatter_core(part) for part in dw_qkv[1:]]
+    grad_shared = []
+    own_part = []
     for n in range(share_count):
         qkv, att, lse = saved[n]
-        do = after(share_do[n], z_down, *made)
+        do = after(share_do[n], *made)
         dx = attention_backward(qkv, do, att, lse, *share_tables[n])
         made = [dx]
-        parts = exchange_tp([share_rows(dx, k) for k in halves])
-        for t in halves:
-            share_parts[t].append(parts[t])
-    made = whole_backward(0, *core_out, *straight_up, *made)
+        grad_shared.append(dx)
+    whole_backward(0, *core_out, *straight_up, *core_qkv[1:], *made)
+    for n in range(share_count):
+        part = dot_nt(grad_shared[n], full_qkv[0])
+        pieces = exchange_tp([share_rows(part, 0)] + [share_rows(part, k).astype(bf16) for k in halves[1:]])
+        own_part.append(sum([piece.astype(f32) for piece in pieces[1:]], pieces[0]))
     straight_out, across_out = scatter_plane(core_out)
-    ready = [*across_up, *straight_out, *across_out, *made]
-    grad_qkv = [after(jnp.concatenate(grad_qkv[t] + share_parts[t], axis=0), *ready) for t in halves]
+    ready = [*across_up, z_down]
+    owned = [after(rows, *ready) for rows in grad_shared]
     z_up = scatter_z(total(straight_up + across_up))
     z_out = scatter_z(total(straight_out + across_out))
-    dw_qkv = [dot_tn(normed, grad_qkv[t]).astype(bf16) for t in halves]
-    straight_qkv, across_qkv = scatter_plane([scatter_core(part) for part in dw_qkv])
+    owned = [dot_tn(rows, grad) for rows, grad in zip(normed_shared, owned)]
+    if whole:
+        owned.append(dot_tn(normed_whole, jnp.concatenate(grad_qkv[0], axis=0)))
+    dw_qkv[0] = sum(owned).astype(bf16)
+    core_qkv[0] = scatter_core(dw_qkv[0])
+    straight_qkv, across_qkv = scatter_plane(core_qkv)
     z_qkv = scatter_z(total(straight_qkv + across_qkv))
-    grad_normed = sum(dot_nt(after(grad_qkv[t], *dw_qkv), full_qkv[t]) for t in halves)
+    ready = [dw_qkv[0], *across_qkv, *straight_out, *across_out]
+    grad_normed = list(own_part)
+    if whole:
+        trees = [after(jnp.concatenate(grad_qkv[t], axis=0), *ready) for t in halves]
+        trees[1:] = [after(rows, core_qkv[0]) for rows in trees[1:]]
+        grad_normed = [sum(dot_nt(trees[t], full_qkv[t]) for t in halves)] + grad_normed
+    grad_normed = jnp.concatenate(grad_normed, axis=0)
     grad_part, sums_0 = norm_backward(x, norm_gains[0], grad_normed)
     input_rows = rows_back(grad_residual + grad_part)
     sums = jnp.concatenate([sums_0, sums_1, sums_2, sums_3])

time: 911 us -> 845 us (0.928)
  waiting for transfers between devices: 166 us -> 113 us
  Pallas kernels: 288 us -> 253 us
  between operations: 2.99 us -> 16.3 us
    ppermute x46 -> x47, waiting for transfers between devices: 166 us -> 113 us  [send(): return lax.ppermute(values, axes, [(s, s ^ distance) for s in range(count)])]
    pallas_call x1, Pallas kernels: 143 us -> 108 us  [gather_weights(): pl.pallas_call(functools.partial(gather_kernel, chunks, len(shards), move...]
    dot_general x8 -> x9, matrix products: 70.1 us -> 65.9 us  [dot_tn(): lax.dot_general(a, b, (((0,), (0,)), ((), ())), preferred_element_type=f32)]
    reduce_sum x2 -> x3, other arithmetic: 18 us -> 21.6 us  [norm_backward(): jnp.sum(grad * xhat, axis=0)]
    ppermute x46 -> x47, starting transfers between devices: 59 us -> 56.8 us  [send(): return lax.ppermute(values, axes, [(s, s ^ distance) for s in range(count)])]
    dot_general x8 -> x9, matrix products: 90.2 us -> 89.5 us  [dot_nt(): lax.dot_general(a, b, (((1,), (1,)), ((), ())), preferred_element_type=f32)]
    unnamed x202 -> x210, local copies, waits for them, and re-layouts: 19.2 us -> 18.8 us
  transfers between devices with their start and end apart: 46 -> 48, of which waited for: 17 -> 15; matrix products, arithmetic and copies ran while one was open for 26% -> 30% of each run, Pallas kernels for 14% -> 17%
where the time goes in v6:
time: 845 us; the launch traced here: 836 us
  matrix products  255 us (30%)
  Pallas kernels  253 us (30%)
  waiting for transfers between devices  113 us (13%)
  other arithmetic  94.4 us (11%)
  starting transfers between devices  56.8 us (7%)
  local copies, waits for them, and re-layouts  46.8 us (6%)
  between operations  16.3 us (2%)
    ppermute x47, waiting for transfers between devices, send(): return lax.ppermute(values, axes, [(s, s ^ distance) for s in range(count)])  113 us
    pallas_call x1, Pallas kernels, gather_weights(): pl.pallas_call(functools.partial(gather_kernel, chunks, len(shards), move...  108 us
    dot_general x12, matrix products, dot_nn(): lax.dot_general(a, b, (((1,), (0,)), ((), ())), preferred_element_type=f32)  99.6 us
    dot_general x9, matrix products, dot_nt(): lax.dot_general(a, b, (((1,), (1,)), ((), ())), preferred_element_type=f32)  89.5 us
    pallas_call x3, Pallas kernels, attention_backward(): pl.pallas_call(attention_backward_kernel, name='attention_backward', out_...  80 us
    dot_general x9, matrix products, dot_tn(): lax.dot_general(a, b, (((0,), (0,)), ((), ())), preferred_element_type=f32)  65.9 us
    pallas_call x3, Pallas kernels, attention_forward(): pl.pallas_call(attention_forward_kernel, name='attention_forward', out_sh...  64.8 us
    ppermute x47, starting transfers between devices, send(): return lax.ppermute(values, axes, [(s, s ^ distance) for s in range(count)])  56.8 us
  transfers between devices with their start and end apart: 48, of which 15 were waited for; matrix products, arithmetic and copies ran while one was open for 30% of the time, Pallas kernels for 17%

profile of v6, /device:TPU:0, one launch (start us, length us, event | category | flops | bytes accessed | tf_op | source)
XLA Modules:
  0.0 835.9 jit_solution(10075906192471392775)
XLA Ops:
  11.6 108.2 %gather_weights.1 = (bf16[4,2,2,64,1536]{4,3,2,1,0:T(8,128)(2,1)}, bf16[4,2,2,64,1536]{4,3,2,1,0:T(8,128)(2,1)}, bf16[4,2,2,64,512]{4,3,2,1,0:T(8,128)(2,1)}, bf...) custom-call(bf16[64,1536]{1,0:T(8,128)(2,1)} %bitcast.309, ...), custom_call_target="tpu_custom_call" | custom-call | bytes 33554432 | tf_op jit(solution)/shard_map/gather_weights/pallas_call | solution.py:373
  127.8 3.5 convolution_convert_fusion.8
  131.8 8.8 %convolution_convert_fusion.q_ref.k_ref.v_ref = bf16[1280,1536]{1,0:T(8,128)(2,1)} fusion(bf16[1024,1536]{1,0:T(8,128)(2,1)} %bitcast.349, bf16[1920,1024]{1,0:T(8,128)(2,1)} %copy-done.24), kind=kOutput, calls=%fused_computation.49 | convolution fusion | flops 4028497920 | bytes 9699328 | tf_op jit(solution)/shard_map/dot_general | solution.py:23
  143.6 21.5 %attention_forward.5 = (bf16[1280,512]{1,0:T(8,128)(2,1)S(1)}, f32[4,8,1280]{2,1,0:T(8,128)S(1)}) custom-call(bf16[1280,1536]{1,0:T(8,128)(2,1)S(1)} %copy-done.8, bf16[1280,1536]{1,0:T(8,128)(2,1)S(1)} %copy-done.8, bf16[1280,1536]{1,0:T(8,128)(2,1)S(1)} %copy-done.8, s32[1280,8]{1,0:T(8,128)S(1)} %pad.14.clone.col_ref, s32[8,1280]{1,0:T(8,128)S(1)} %pad.15.row_ref), custom_call_target="tpu_custom_call" | custom-call | flops 8053063680 | bytes 5898240 | tf_op jit(solution)/shard_map/attention_forward/pallas_call | solution.py:80
  170.0 6.9 convolution_convert_fusion.1.q_ref.k_ref.v_ref
  176.9 21.8 %attention_forward.3 = (bf16[1280,512]{1,0:T(8,128)(2,1)S(1)}, f32[4,8,1280]{2,1,0:T(8,128)S(1)}) custom-call(bf16[1280,1536]{1,0:T(8,128)(2,1)S(1)} %convolution_convert_fusion.1.q_ref.k_ref.v_ref, bf16[1280,1536]{1,0:T(8,128)(2,1)S(1)} %convolution_convert_fusion.1.q_ref.k_ref.v_ref, bf16[1280,1536]{1,0:T(8,128)(2,1)S(1)} %convolution_convert_fusion.1.q_ref.k_ref.v_ref, ...), custom_call_target="tpu_custom_call" | custom-call | flops 8053063680 | bytes 5898240 | tf_op jit(solution)/shard_map/attention_forward/pallas_call | solution.py:80
  198.8 4.6 broadcast_select_fusion.3
  203.7 21.5 %attention_forward.4 = (bf16[1280,512]{1,0:T(8,128)(2,1)S(1)}, f32[4,8,1280]{2,1,0:T(8,128)S(1)}) custom-call(bf16[1280,1536]{1,0:T(8,128)(2,1)S(1)} %pad_maximum_fusion.2.q_ref.k_ref.v_ref, bf16[1280,1536]{1,0:T(8,128)(2,1)S(1)} %pad_maximum_fusion.2.q_ref.k_ref.v_ref, bf16[1280,1536]{1,0:T(8,128)(2,1)S(1)} %pad_maximum_fusion.2.q_ref.k_ref.v_ref, ...), custom_call_target="tpu_custom_call" | custom-call | flops 8053063680 | bytes 5898240 | tf_op jit(solution)/shard_map/attention_forward/pallas_call | solution.py:80
  229.5 12.9 %collective-permute-done.1 = bf16[640,512]{1,0:T(8,128)(2,1)S(1)} collective-permute-done((bf16[640,512]{1,0:T(8,128)(2,1)S(1)}, bf16[640,512]{1,0:T(8,128)(2,1)S(1)}, u32[]{:S(2)}, u32[]{:S(2)}) %collective-permute-start.1) | collective-permute-done | bytes 655392 | tf_op jit(solution)/shard_map/ppermute | solution.py:399
  259.8 21.8 %add_convert_fusion.1 = (bf16[1920,2048]{1,0:T(8,128)(2,1)}, bf16[1920,2048]{1,0:T(8,128)(2,1)}) fusion(bf16[1920,1024]{1,0:T(8,128)(2,1)S(1)} %add_convert_fusion.3, bf16[1024,2048]{1,0:T(8,128)(2,1)} %bitcast.343), kind=kOutput, calls=%fused_computation.5 | convolution fusion | flops 8123842560 | bytes 23855104 | tf_op jit(solution)/shard_map/dot_general | solution.py:23
  282.1 18.3 %add_convert_fusion = (bf16[1920,2048]{1,0:T(8,128)(2,1)}, bf16[1920,2048]{1,0:T(8,128)(2,1)}) fusion(bf16[1920,1024]{1,0:T(8,128)(2,1)S(1)} %add_convert_fusion.3, bf16[1024,2048]{1,0:T(8,128)(2,1)S(1)} %bitcast.342), kind=kOutput, calls=%fused_computation.2 | convolution fusion | flops 8123842560 | bytes 23855104 | tf_op jit(solution)/shard_map/dot_general | solution.py:23
  304.2 7.3 collective-permute-done.17
  313.2 15.5 %fusion.50 = f32[1920,1024]{1,0:T(8,128)} fusion(bf16[1920,2048]{1,0:T(8,128)(2,1)} %get-tuple-element.55, pred[]{:T(512)S(6)} %eq.30, bf16[2048,2048]{1,0:T(8,128)(2,1)} %all-gather.2.cloned.1.call-done), kind=kOutput, calls=%fused_computation.163 | convolution fusion | flops 8055160832 | bytes 24117248 | tf_op jit(solution)/shard_map/dot_general | solution.py:27
  328.6 20.2 %fusion.75 = (f32[1920]{0:T(1024)S(1)}, f32[1920,1024]{1,0:T(8,128)S(1)}) fusion(f32[1920,1024]{1,0:T(8,128)} %fusion.50, bf16[1920,2048]{1,0:T(8,128)(2,1)} %get-tuple-element.58, pred[]{:T(512)S(6)} %eq.31, bf16[2048,2048]{1,0:T(8,128)(2,1)} %all-gather.2.cloned.1.call-done), kind=kOutput, calls=%fused_computation.255 | convolution fusion | flops 8059090944 | bytes 31989248 | tf_op jit(solution)/shard_map/dot_general | solution.py:27
  351.0 5.0 fusion.21
  356.1 3.7 fusion.19
  359.8 14.1 %convolution_convert_fusion.5 = bf16[1024,2048]{1,0:T(8,128)(2,1)S(1)} fusion(bf16[1920,1024]{1,0:T(8,128)(2,1)S(1)} %get-tuple-element.140, bf16[1920,2048]{1,0:T(8,128)(2,1)} %get-tuple-element.55), kind=kOutput, calls=%fused_computation.77 | convolution fusion | flops 8055160832 | bytes 15990784 | tf_op jit(solution)/shard_map/dot_general | solution.py:31
  373.9 11.3 %convolution_convert_fusion.4 = bf16[1024,2048]{1,0:T(8,128)(2,1)S(1)} fusion(bf16[1920,1024]{1,0:T(8,128)(2,1)S(1)} %get-tuple-element.140, bf16[1920,2048]{1,0:T(8,128)(2,1)} %get-tuple-element.58), kind=kOutput, calls=%fused_computation.76 | convolution fusion | flops 8055160832 | bytes 15990784 | tf_op jit(solution)/shard_map/dot_general | solution.py:31
  390.7 14.7 %multiply_convert_fusion.1 = bf16[1920,2048]{1,0:T(8,128)(2,1)} fusion(bf16[1920,2048]{1,0:T(8,128)(2,1)} %get-tuple-element.60, bf16[1920,1024]{1,0:T(8,128)(2,1)S(1)} %copy-done.37, pred[]{:T(512)S(6)} %eq.30, bf16[2048,2048]{1,0:T(8,128)(2,1)} %all-gather.2.cloned.1.call-done), kind=kOutput, calls=%fused_computation.1 | convolution fusion | flops 8066957312 | bytes 28049408 | tf_op jit(solution)/shard_map/dot_general | solution.py:23
  405.4 14.5 %multiply_convert_fusion = bf16[1920,2048]{1,0:T(8,128)(2,1)} fusion(bf16[1920,2048]{1,0:T(8,128)(2,1)} %get-tuple-element.62, bf16[1920,1024]{1,0:T(8,128)(2,1)S(1)} %copy-done.37, pred[]{:T(512)S(6)} %eq.31, bf16[2048,2048]{1,0:T(8,128)(2,1)} %all-gather.2.cloned.1.call-done), kind=kOutput, calls=%fused_computation | convolution fusion | flops 8066957312 | bytes 28049408 | tf_op jit(solution)/shard_map/dot_general | solution.py:23
  419.9 3.4 fusion.44
  428.2 11.7 %convolution_convert_fusion.3 = bf16[1024,2048]{1,0:T(8,128)(2,1)S(1)} fusion(bf16[1920,1024]{1,0:T(8,128)(2,1)S(1)} %copy-done.39, bf16[1920,2048]{1,0:T(8,128)(2,1)} %multiply_convert_fusion.1), kind=kOutput, calls=%fused_computation.75 | convolution fusion | flops 8055160832 | bytes 15990784 | tf_op jit(solution)/shard_map/dot_general | solution.py:31
  439.9 10.0 %convolution_convert_fusion.2 = bf16[1024,2048]{1,0:T(8,128)(2,1)S(1)} fusion(bf16[1920,1024]{1,0:T(8,128)(2,1)S(1)} %copy-done.39, bf16[1920,2048]{1,0:T(8,128)(2,1)S(1)} %bitcast.356), kind=kOutput, calls=%fused_computation.74 | convolution fusion | flops 8055160832 | bytes 15990784 | tf_op jit(solution)/shard_map/dot_general | solution.py:31
  453.7 12.6 %fusion.77 = f32[1920,1024]{1,0:T(8,128)} fusion(bf16[1920,2048]{1,0:T(8,128)(2,1)} %multiply_convert_fusion.1, bf16[1024,2048]{1,0:T(8,128)(2,1)S(1)} %bitcast.344), kind=kOutput, calls=%fused_computation.257 | convolution fusion | flops 8053063680 | bytes 19922944 | tf_op jit(solution)/shard_map/dot_general | solution.py:27
  470.1 7.1 collective-permute-done.10
  477.2 21.4 %collective-permute-done.7 = bf16[4,64,2048]{2,1,0:T(8,128)(2,1)S(1)} collective-permute-done((bf16[4,64,2048]{2,1,0:T(8,128)(2,1)S(1)}, bf16[4,64,2048]{2,1,0:T(8,128)(2,1)S(1)}, u32[]{:S(2)}, u32[]{:S(2)}) %collective-permute-start.7) | collective-permute-done | bytes 1048608 | tf_op jit(solution)/shard_map/ppermute | solution.py:399
  500.4 21.2 %multiply_reduce_fusion = (f32[1024]{0:T(1024)}, f32[1920]{0:T(1024)S(1)}, f32[1920]{0:T(1024)S(1)}, f32[1024]{0:T(1024)}, f32[1920,1024]{1,0:T(8,128)}) fusion(f32[1920,1024]{1,0:T(8,128)} %copy-done.13, f32[1920]{0:T(1024)S(1)} %copy-done.66, f32[1920]{0:T(1024)S(1)} %copy-done.64, f32[1024]{0:T(1024)S(1)} %bitcast.325, f32[1920,1024]{1,0:T(8,128)} %fusion.77, ...), kind=kOutput, calls=%fused_computation.39 | convolution fusion | flops 8072718336 | bytes 35694592 | tf_op jit(solution)/shard_map/dot_general | solution.py:27
  521.6 11.6 %multiply_reduce_fusion.1 = (f32[1024]{0:T(1024)}, f32[1920]{0:T(1024)S(1)}, f32[1920]{0:T(1024)S(1)}, f32[1024]{0:T(1024)}, f32[1920,1024]{1,0:T(8,128)S(1)}) fusion(f32[1920,1024]{1,0:T(8,128)S(1)} %bitcast.277, f32[1920]{0:T(1024)S(1)} %copy-done.62, f32[1920]{0:T(1024)S(1)} %copy-done.58, f32[1024]{0:T(1024)S(1)} %bitcast.319, ...), kind=kLoop, calls=%fused_computation.40 | loop fusion | flops 35383552 | bytes 35467264 | tf_op jit(solution)/shard_map/reduce_sum | solution.py:217
  537.8 3.9 multiply_convert_fusion.4
  544.5 13.9 %collective-permute-done.20 = bf16[64,2048]{1,0:T(8,128)(2,1)S(1)} collective-permute-done((bf16[64,2048]{1,0:T(8,128)(2,1)S(1)}, bf16[64,2048]{1,0:T(8,128)(2,1)S(1)}, u32[]{:S(2)}, u32[]{:S(2)}) %collective-permute-start.20) | collective-permute-done | bytes 262176 | tf_op jit(solution)/shard_map/ppermute | solution.py:399
  584.2 26.8 %attention_backward.3 = bf16[1280,1536]{1,0:T(8,128)(2,1)S(1)} custom-call(bf16[1280,1536]{1,0:T(8,128)(2,1)S(1)} %copy-done.9, bf16[1280,1536]{1,0:T(8,128)(2,1)S(1)} %copy-done.9, bf16[1280,1536]{1,0:T(8,128)(2,1)S(1)} %copy-done.9, bf16[1280,512]{1,0:T(8,128)(2,1)S(1)} %convolution_convert_fusion.9.do_ref, bf16[1280,512]{1,0:T(8,128)(2,1)S(1)} %get-tuple-element.52.o_ref, ...), custom_call_target="tpu_custom_call" | custom-call | flops 20132659200 | bytes 11796480 | tf_op jit(solution)/shard_map/attention_backward/pallas_call | solution.py:171
  611.0 4.5 convolution_convert_fusion.6
  625.8 26.6 %attention_backward.4 = bf16[1280,1536]{1,0:T(8,128)(2,1)S(1)} custom-call(bf16[1280,1536]{1,0:T(8,128)(2,1)S(1)} %copy-done.1, bf16[1280,1536]{1,0:T(8,128)(2,1)S(1)} %copy-done.1, bf16[1280,1536]{1,0:T(8,128)(2,1)S(1)} %copy-done.1, bf16[1280,512]{1,0:T(8,128)(2,1)S(1)} %pad_maximum_fusion.5.do_ref, bf16[1280,512]{1,0:T(8,128)(2,1)S(1)} %copy-done.3, ...), custom_call_target="tpu_custom_call" | custom-call | flops 20132659200 | bytes 11796480 | tf_op jit(solution)/shard_map/attention_backward/pallas_call | solution.py:171
  653.2 6.3 fusion.79
  671.0 26.6 %attention_backward.5 = bf16[1280,1536]{1,0:T(8,128)(2,1)S(1)} custom-call(bf16[1280,1536]{1,0:T(8,128)(2,1)S(1)} %copy-done.11, bf16[1280,1536]{1,0:T(8,128)(2,1)S(1)} %copy-done.11, bf16[1280,1536]{1,0:T(8,128)(2,1)S(1)} %copy-done.11, bf16[1280,512]{1,0:T(8,128)(2,1)S(1)} %convolution_convert_fusion.10.do_ref, bf16[1280,512]{1,0:T(8,128)(2,1)S(1)} %copy-done.5, ...), custom_call_target="tpu_custom_call" | custom-call | flops 20132659200 | bytes 11796480 | tf_op jit(solution)/shard_map/attention_backward/pallas_call | solution.py:171
  697.7 4.5 fusion.35
  702.2 5.1 add_convert_fusion.4
  717.7 5.7 collective-permute-done.39
  724.8 12.2 %collective-permute-done.38 = bf16[64,2048]{1,0:T(8,128)(2,1)S(1)} collective-permute-done((bf16[64,2048]{1,0:T(8,128)(2,1)S(1)}, bf16[64,2048]{1,0:T(8,128)(2,1)S(1)}, u32[]{:S(2)}, u32[]{:S(2)}) %collective-permute-start.38) | collective-permute-done | bytes 262176 | tf_op jit(solution)/shard_map/ppermute | solution.py:399
  745.6 4.5 fusion.78
  750.2 4.4 fusion.76
  754.7 5.0 fusion.15
  763.5 7.7 fusion.14
  772.7 12.6 %collective-permute-start.44 = (f32[8,1024]{1,0:T(8,128)S(1)}, f32[8,1024]{1,0:T(8,128)S(1)}, u32[]{:S(2)}, u32[]{:S(2)}) collective-permute-start(f32[8,1024]{1,0:T(8,128)S(1)} %add_add_fusion.1), channel_id=1, source_target_pairs={{0,16},{8,24},{16,0},{24,8},{1,17},{9,25},{17,1},{25,9},{2,18},{10... | collective-permute-start | bytes 98312 | tf_op jit(solution)/shard_map/ppermute | solution.py:399
  799.1 4.1 collective-permute-done.33
  803.2 9.7 %collective-permute-done.32 = bf16[64,1536]{1,0:T(8,128)(2,1)S(1)} collective-permute-done((bf16[64,1536]{1,0:T(8,128)(2,1)S(1)}, bf16[64,1536]{1,0:T(8,128)(2,1)S(1)}, u32[]{:S(2)}, u32[]{:S(2)}) %collective-permute-start.32) | collective-permute-done | bytes 196640 | tf_op jit(solution)/shard_map/ppermute | solution.py:399
  813.8 8.2 collective-permute-done.28
  825.1 3.7 maximum_bitcast_fusion
  (417 shorter events, 168.5 us)
Async XLA Ops:
  7.2 306.0 %all-gather.2.cloned.1.call-start = ((), (), s32[]{:S(2)}) async-start(), calls=%async_computation | async-start | bytes 8650752 | tf_op jit(solution)/shard_map/all_gather | solution.py:517
  131.3 67.5 %collective-permute-start = (bf16[640,1536]{1,0:T(8,128)(2,1)}, bf16[640,1536]{1,0:T(8,128)(2,1)}, u32[]{:S(2)}, u32[]{:S(2)}) collective-permute-start(bf16[640,1536]{1,0:T(8,128)(2,1)} %convolution_convert_fusion.8), channel_id=1, source_target_pairs={{0,1},{1,0},{2,3},{3,2},{4,5},{5,4},{6,7},{7,6},{8,9},{9,8},{10,11... | collective-permute-start | bytes 5898248 | tf_op jit(solution)/shard_map/ppermute | solution.py:399
  225.3 17.1 %collective-permute-start.1 = (bf16[640,512]{1,0:T(8,128)(2,1)S(1)}, bf16[640,512]{1,0:T(8,128)(2,1)S(1)}, u32[]{:S(2)}, u32[]{:S(2)}) collective-permute-start(bf16[640,512]{1,0:T(8,128)(2,1)S(1)} %get-tuple-element.164), channel_id=1, source_target_pairs={{0,1},{1,0},{2,3},{3,2},{4,5},{5,4},{6,7},{7,6},{8,9},{9,8},{10,11... | collective-permute-start | bytes 1966088 | tf_op jit(solution)/shard_map/ppermute | solution.py:399
  242.7 57.7 %collective-permute-start.3 = (bf16[640,1024]{1,0:T(8,128)(2,1)S(1)}, bf16[640,1024]{1,0:T(8,128)(2,1)S(1)}, u32[]{:S(2)}, u32[]{:S(2)}) collective-permute-start(bf16[640,1024]{1,0:T(8,128)(2,1)S(1)} %get-tuple-element.148), channel_id=1, source_target_pairs={{0,1},{1,0},{2,3},{3,2},{4,5},{5,4},{6,7},{7,6},{8,9},{9,8},{10,11... | collective-permute-start | bytes 3932168 | tf_op jit(solution)/shard_map/ppermute | solution.py:399
  281.6 29.9 %collective-permute-start.17 = (bf16[640,1024]{1,0:T(8,128)(2,1)S(1)}, bf16[640,1024]{1,0:T(8,128)(2,1)S(1)}, u32[]{:S(2)}, u32[]{:S(2)}) collective-permute-start(bf16[640,1024]{1,0:T(8,128)(2,1)S(1)} %copy-done.27), channel_id=1, source_target_pairs={{0,1},{1,0},{2,3},{3,2},{4,5},{5,4},{6,7},{7,6},{8,9},{9,8},{10,11... | collective-permute-start | bytes 3932168 | tf_op jit(solution)/shard_map/ppermute | solution.py:399
  386.5 33.3 %collective-permute-start.2 = (bf16[640,1024]{1,0:T(8,128)(2,1)S(1)}, bf16[640,1024]{1,0:T(8,128)(2,1)}, u32[]{:S(2)}, u32[]{:S(2)}) collective-permute-start(bf16[640,1024]{1,0:T(8,128)(2,1)S(1)} %dynamic-slice_bitcast_fusion.6), channel_id=1, source_target_pairs={{0,1},{1,0},{2,3},{3,2},{4,5},{5,4},{6,7},{7,6},{8,9},{9,8},{10,11... | collective-permute-start | bytes 3932168 | tf_op jit(solution)/shard_map/ppermute | solution.py:399
  388.5 34.7 %collective-permute-start.4 = (bf16[4,2,64,2048]{3,2,1,0:T(8,128)(2,1)}, bf16[4,2,64,2048]{3,2,1,0:T(8,128)(2,1)}, u32[]{:S(2)}, u32[]{:S(2)}) collective-permute-start(bf16[4,2,64,2048]{3,2,1,0:T(8,128)(2,1)} %dynamic-slice_bitcast_fusion.3), channel_id=1, source_target_pairs={{0,2},{2,0},{1,3},{3,1},{4,6},{6,4},{5,7},{7,5},{8,10},{10,8},{9,1... | collective-permute-start | bytes 6291464 | tf_op jit(solution)/shard_map/ppermute | solution.py:399
  390.0 35.4 %collective-permute-start.5 = (bf16[4,2,64,2048]{3,2,1,0:T(8,128)(2,1)}, bf16[4,2,64,2048]{3,2,1,0:T(8,128)(2,1)}, u32[]{:S(2)}, u32[]{:S(2)}) collective-permute-start(bf16[4,2,64,2048]{3,2,1,0:T(8,128)(2,1)} %dynamic-slice_bitcast_fusion.2), channel_id=1, source_target_pairs={{0,2},{2,0},{1,3},{3,1},{4,6},{6,4},{5,7},{7,5},{8,10},{10,8},{9,1... | collective-permute-start | bytes 6291464 | tf_op jit(solution)/shard_map/ppermute | solution.py:399
  450.2 27.0 %collective-permute-start.10 = (bf16[4,64,2048]{2,1,0:T(8,128)(2,1)S(1)}, bf16[4,64,2048]{2,1,0:T(8,128)(2,1)S(1)}, u32[]{:S(2)}, u32[]{:S(2)}) collective-permute-start(bf16[4,64,2048]{2,1,0:T(8,128)(2,1)S(1)} %get-tuple-element.159), channel_id=1, source_target_pairs={{0,5},{1,4},{4,1},{5,0},{2,7},{3,6},{6,3},{7,2},{8,13},{9,12},{12,... | collective-permute-start | bytes 3145736 | tf_op jit(solution)/shard_map/ppermute | solution.py:399
  452.6 46.0 %collective-permute-start.7 = (bf16[4,64,2048]{2,1,0:T(8,128)(2,1)S(1)}, bf16[4,64,2048]{2,1,0:T(8,128)(2,1)S(1)}, u32[]{:S(2)}, u32[]{:S(2)}) collective-permute-start(bf16[4,64,2048]{2,1,0:T(8,128)(2,1)S(1)} %get-tuple-element.158), channel_id=1, source_target_pairs={{0,1},{1,0},{4,5},{5,4},{2,3},{3,2},{6,7},{7,6},{8,9},{9,8},{12,13... | collective-permute-start | bytes 3145736 | tf_op jit(solution)/shard_map/ppermute | solution.py:399
  453.2 45.4 %collective-permute-start.6 = (bf16[4,64,2048]{2,1,0:T(8,128)(2,1)S(1)}, bf16[4,64,2048]{2,1,0:T(8,128)(2,1)S(1)}, u32[]{:S(2)}, u32[]{:S(2)}) collective-permute-start(bf16[4,64,2048]{2,1,0:T(8,128)(2,1)S(1)} %dynamic-slice_bitcast_fusion.13), channel_id=1, source_target_pairs={{0,4},{1,5},{4,0},{5,1},{2,6},{3,7},{6,2},{7,3},{8,12},{9,13},{12,... | collective-permute-start | bytes 3145736 | tf_op jit(solution)/shard_map/ppermute | solution.py:399
  468.0 91.3 %collective-permute-start.8 = (bf16[4,2,64,2048]{3,2,1,0:T(8,128)(2,1)}, bf16[4,2,64,2048]{3,2,1,0:T(8,128)(2,1)}, u32[]{:S(2)}, u32[]{:S(2)}) collective-permute-start(bf16[4,2,64,2048]{3,2,1,0:T(8,128)(2,1)} %dynamic-slice_bitcast_fusion.1), channel_id=1, source_target_pairs={{0,2},{2,0},{1,3},{3,1},{4,6},{6,4},{5,7},{7,5},{8,10},{10,8},{9,1... | collective-permute-start | bytes 6291464 | tf_op jit(solution)/shard_map/ppermute | solution.py:399
  469.6 91.9 %collective-permute-start.9 = (bf16[4,2,64,2048]{3,2,1,0:T(8,128)(2,1)}, bf16[4,2,64,2048]{3,2,1,0:T(8,128)(2,1)}, u32[]{:S(2)}, u32[]{:S(2)}) collective-permute-start(bf16[4,2,64,2048]{3,2,1,0:T(8,128)(2,1)} %dynamic-slice_bitcast_fusion), channel_id=1, source_target_pairs={{0,2},{2,0},{1,3},{3,1},{4,6},{6,4},{5,7},{7,5},{8,10},{10,8},{9,1... | collective-permute-start | bytes 6291464 | tf_op jit(solution)/shard_map/ppermute | solution.py:399
  533.3 11.1 %collective-permute-start.21 = (bf16[64,2048]{1,0:T(8,128)(2,1)S(1)}, bf16[64,2048]{1,0:T(8,128)(2,1)S(1)}, u32[]{:S(2)}, u32[]{:S(2)}) collective-permute-start(bf16[64,2048]{1,0:T(8,128)(2,1)S(1)} %get-tuple-element.170), channel_id=1, source_target_pairs={{0,24},{8,16},{16,8},{24,0},{1,25},{9,17},{17,9},{25,1},{2,26},{10... | collective-permute-start | bytes 786440 | tf_op jit(solution)/shard_map/ppermute | solution.py:399
  534.8 23.5 %collective-permute-start.20 = (bf16[64,2048]{1,0:T(8,128)(2,1)S(1)}, bf16[64,2048]{1,0:T(8,128)(2,1)S(1)}, u32[]{:S(2)}, u32[]{:S(2)}) collective-permute-start(bf16[64,2048]{1,0:T(8,128)(2,1)S(1)} %get-tuple-element.171), channel_id=1, source_target_pairs={{0,16},{8,24},{16,0},{24,8},{1,17},{9,25},{17,1},{25,9},{2,18},{10... | collective-permute-start | bytes 786440 | tf_op jit(solution)/shard_map/ppermute | solution.py:399
  535.4 22.9 %collective-permute-start.19 = (bf16[64,2048]{1,0:T(8,128)(2,1)S(1)}, bf16[64,2048]{1,0:T(8,128)(2,1)S(1)}, u32[]{:S(2)}, u32[]{:S(2)}) collective-permute-start(bf16[64,2048]{1,0:T(8,128)(2,1)S(1)} %get-tuple-element.169), channel_id=1, source_target_pairs={{0,8},{8,0},{16,24},{24,16},{1,9},{9,1},{17,25},{25,17},{2,10},{10... | collective-permute-start | bytes 786440 | tf_op jit(solution)/shard_map/ppermute | solution.py:399
  577.5 45.5 %collective-permute-start.16 = (bf16[640,512]{1,0:T(8,128)(2,1)}, bf16[640,512]{1,0:T(8,128)(2,1)}, u32[]{:S(2)}, u32[]{:S(2)}) collective-permute-start(bf16[640,512]{1,0:T(8,128)(2,1)} %convolution_convert_fusion.13), channel_id=1, source_target_pairs={{0,1},{1,0},{2,3},{3,2},{4,5},{5,4},{6,7},{7,6},{8,9},{9,8},{10,11... | collective-permute-start | bytes 1966088 | tf_op jit(solution)/shard_map/ppermute | solution.py:399
  579.8 40.7 %collective-permute-start.11 = (bf16[4,2,64,512]{3,2,1,0:T(8,128)(2,1)}, bf16[4,2,64,512]{3,2,1,0:T(8,128)(2,1)S(1)}, u32[]{:S(2)}, u32[]{:S(2)}) collective-permute-start(bf16[4,2,64,512]{3,2,1,0:T(8,128)(2,1)} %dynamic-slice_bitcast_fusion.19), channel_id=1, source_target_pairs={{0,2},{2,0},{1,3},{3,1},{4,6},{6,4},{5,7},{7,5},{8,10},{10,8},{9,1... | collective-permute-start | bytes 1572872 | tf_op jit(solution)/shard_map/ppermute | solution.py:399
  580.6 37.4 %collective-permute-start.12 = (bf16[4,2,64,512]{3,2,1,0:T(8,128)(2,1)}, bf16[4,2,64,512]{3,2,1,0:T(8,128)(2,1)S(1)}, u32[]{:S(2)}, u32[]{:S(2)}) collective-permute-start(bf16[4,2,64,512]{3,2,1,0:T(8,128)(2,1)} %dynamic-slice_bitcast_fusion.18), channel_id=1, source_target_pairs={{0,2},{2,0},{1,3},{3,1},{4,6},{6,4},{5,7},{7,5},{8,10},{10,8},{9,1... | collective-permute-start | bytes 1572872 | tf_op jit(solution)/shard_map/ppermute | solution.py:399
  581.1 82.4 %collective-permute-start.18 = (bf16[4,64,2048]{2,1,0:T(8,128)(2,1)}, bf16[4,64,2048]{2,1,0:T(8,128)(2,1)}, u32[]{:S(2)}, u32[]{:S(2)}) collective-permute-start(bf16[4,64,2048]{2,1,0:T(8,128)(2,1)} %get-tuple-element.157), channel_id=1, source_target_pairs={{0,5},{1,4},{4,1},{5,0},{2,7},{3,6},{6,3},{7,2},{8,13},{9,12},{12,... | collective-permute-start | bytes 3145736 | tf_op jit(solution)/shard_map/ppermute | solution.py:399
  582.6 82.4 %collective-permute-start.14 = (bf16[4,64,2048]{2,1,0:T(8,128)(2,1)}, bf16[4,64,2048]{2,1,0:T(8,128)(2,1)}, u32[]{:S(2)}, u32[]{:S(2)}) collective-permute-start(bf16[4,64,2048]{2,1,0:T(8,128)(2,1)} %get-tuple-element.156), channel_id=1, source_target_pairs={{0,1},{1,0},{4,5},{5,4},{2,3},{3,2},{6,7},{7,6},{8,9},{9,8},{12,13... | collective-permute-start | bytes 3145736 | tf_op jit(solution)/shard_map/ppermute | solution.py:399
  618.8 46.2 %collective-permute-start.13 = (bf16[4,64,2048]{2,1,0:T(8,128)(2,1)}, bf16[4,64,2048]{2,1,0:T(8,128)(2,1)}, u32[]{:S(2)}, u32[]{:S(2)}) collective-permute-start(bf16[4,64,2048]{2,1,0:T(8,128)(2,1)} %dynamic-slice_bitcast_fusion.9), channel_id=1, source_target_pairs={{0,4},{1,5},{4,0},{5,1},{2,6},{3,7},{6,2},{7,3},{8,12},{9,13},{12,... | collective-permute-start | bytes 3145736 | tf_op jit(solution)/shard_map/ppermute | solution.py:399
  620.5 31.9 %collective-permute-start.25 = (bf16[4,64,512]{2,1,0:T(8,128)(2,1)S(1)}, bf16[4,64,512]{2,1,0:T(8,128)(2,1)S(1)}, u32[]{:S(2)}, u32[]{:S(2)}) collective-permute-start(bf16[4,64,512]{2,1,0:T(8,128)(2,1)S(1)} %get-tuple-element.176), channel_id=1, source_target_pairs={{0,5},{1,4},{4,1},{5,0},{2,7},{3,6},{6,3},{7,2},{8,13},{9,12},{12,... | collective-permute-start | bytes 786440 | tf_op jit(solution)/shard_map/ppermute | solution.py:399
  623.0 29.5 %collective-permute-start.24 = (bf16[4,64,512]{2,1,0:T(8,128)(2,1)S(1)}, bf16[4,64,512]{2,1,0:T(8,128)(2,1)S(1)}, u32[]{:S(2)}, u32[]{:S(2)}) collective-permute-start(bf16[4,64,512]{2,1,0:T(8,128)(2,1)S(1)} %get-tuple-element.175), channel_id=1, source_target_pairs={{0,1},{1,0},{4,5},{5,4},{2,3},{3,2},{6,7},{7,6},{8,9},{9,8},{12,13... | collective-permute-start | bytes 786440 | tf_op jit(solution)/shard_map/ppermute | solution.py:399
  652.4 18.2 %collective-permute-start.15 = (bf16[4,2,64,1536]{3,2,1,0:T(8,128)(2,1)}, bf16[4,2,64,1536]{3,2,1,0:T(8,128)(2,1)S(1)}, u32[]{:S(2)}, u32[]{:S(2)}) collective-permute-start(bf16[4,2,64,1536]{3,2,1,0:T(8,128)(2,1)} %dynamic-slice_bitcast_fusion.4), channel_id=1, source_target_pairs={{0,2},{2,0},{1,3},{3,1},{4,6},{6,4},{5,7},{7,5},{8,10},{10,8},{9,1... | collective-permute-start | bytes 4718600 | tf_op jit(solution)/shard_map/ppermute | solution.py:399
  652.5 8.9 %collective-permute-start.23 = (bf16[4,64,512]{2,1,0:T(8,128)(2,1)}, bf16[4,64,512]{2,1,0:T(8,128)(2,1)S(1)}, u32[]{:S(2)}, u32[]{:S(2)}) collective-permute-start(bf16[4,64,512]{2,1,0:T(8,128)(2,1)} %dynamic-slice_bitcast_fusion.25), channel_id=1, source_target_pairs={{0,4},{1,5},{4,0},{5,1},{2,6},{3,7},{6,2},{7,3},{8,12},{9,13},{12,... | collective-permute-start | bytes 786440 | tf_op jit(solution)/shard_map/ppermute | solution.py:399
  661.4 77.0 %collective-permute-start.27 = (bf16[640,1024]{1,0:T(8,128)(2,1)S(1)}, bf16[640,1024]{1,0:T(8,128)(2,1)}, u32[]{:S(2)}, u32[]{:S(2)}) collective-permute-start(bf16[640,1024]{1,0:T(8,128)(2,1)S(1)} %dynamic-slice_convert_fusion.1), channel_id=1, source_target_pairs={{0,1},{1,0},{2,3},{3,2},{4,5},{5,4},{6,7},{7,6},{8,9},{9,8},{10,11... | collective-permute-start | bytes 3932168 | tf_op jit(solution)/shard_map/ppermute | solution.py:399
  663.5 48.0 %collective-permute-start.36 = (bf16[64,512]{1,0:T(8,128)(2,1)S(1)}, bf16[64,512]{1,0:T(8,128)(2,1)S(1)}, u32[]{:S(2)}, u32[]{:S(2)}) collective-permute-start(bf16[64,512]{1,0:T(8,128)(2,1)S(1)} %get-tuple-element.178), channel_id=1, source_target_pairs={{0,24},{8,16},{16,8},{24,0},{1,25},{9,17},{17,9},{25,1},{2,26},{10... | collective-permute-start | bytes 196616 | tf_op jit(solution)/shard_map/ppermute | solution.py:399
  665.0 46.5 %collective-permute-start.35 = (bf16[64,512]{1,0:T(8,128)(2,1)S(1)}, bf16[64,512]{1,0:T(8,128)(2,1)S(1)}, u32[]{:S(2)}, u32[]{:S(2)}) collective-permute-start(bf16[64,512]{1,0:T(8,128)(2,1)S(1)} %get-tuple-element.179), channel_id=1, source_target_pairs={{0,16},{8,24},{16,0},{24,8},{1,17},{9,25},{17,1},{25,9},{2,18},{10... | collective-permute-start | bytes 196616 | tf_op jit(solution)/shard_map/ppermute | solution.py:399
  665.0 46.5 %collective-permute-start.34 = (bf16[64,512]{1,0:T(8,128)(2,1)S(1)}, bf16[64,512]{1,0:T(8,128)(2,1)S(1)}, u32[]{:S(2)}, u32[]{:S(2)}) collective-permute-start(bf16[64,512]{1,0:T(8,128)(2,1)S(1)} %get-tuple-element.177), channel_id=1, source_target_pairs={{0,8},{8,0},{16,24},{24,16},{1,9},{9,1},{17,25},{25,17},{2,10},{10... | collective-permute-start | bytes 196616 | tf_op jit(solution)/shard_map/ppermute | solution.py:399
  707.7 35.5 %collective-permute-start.26 = (bf16[4,2,64,1536]{3,2,0,1:T(8,128)(2,1)S(1)}, bf16[4,2,64,1536]{3,2,0,1:T(8,128)(2,1)S(1)}, u32[]{:S(2)}, u32[]{:S(2)}) collective-permute-start(bf16[4,2,64,1536]{3,2,0,1:T(8,128)(2,1)S(1)} %bitcast.300), channel_id=1, source_target_pairs={{0,2},{2,0},{1,3},{3,1},{4,6},{6,4},{5,7},{7,5},{8,10},{10,8},{9,1... | collective-permute-start | bytes 4718600 | tf_op jit(solution)/shard_map/ppermute | solution.py:399
  712.3 11.1 %collective-permute-start.39 = (bf16[64,2048]{1,0:T(8,128)(2,1)S(1)}, bf16[64,2048]{1,0:T(8,128)(2,1)S(1)}, u32[]{:S(2)}, u32[]{:S(2)}) collective-permute-start(bf16[64,2048]{1,0:T(8,128)(2,1)S(1)} %get-tuple-element.167), channel_id=1, source_target_pairs={{0,24},{8,16},{16,8},{24,0},{1,25},{9,17},{17,9},{25,1},{2,26},{10... | collective-permute-start | bytes 786440 | tf_op jit(solution)/shard_map/ppermute | solution.py:399
  713.8 23.2 %collective-permute-start.38 = (bf16[64,2048]{1,0:T(8,128)(2,1)S(1)}, bf16[64,2048]{1,0:T(8,128)(2,1)S(1)}, u32[]{:S(2)}, u32[]{:S(2)}) collective-permute-start(bf16[64,2048]{1,0:T(8,128)(2,1)S(1)} %get-tuple-element.168), channel_id=1, source_target_pairs={{0,16},{8,24},{16,0},{24,8},{1,17},{9,25},{17,1},{25,9},{2,18},{10... | collective-permute-start | bytes 786440 | tf_op jit(solution)/shard_map/ppermute | solution.py:399
  714.0 23.0 %collective-permute-start.37 = (bf16[64,2048]{1,0:T(8,128)(2,1)S(1)}, bf16[64,2048]{1,0:T(8,128)(2,1)S(1)}, u32[]{:S(2)}, u32[]{:S(2)}) collective-permute-start(bf16[64,2048]{1,0:T(8,128)(2,1)S(1)} %get-tuple-element.166), channel_id=1, source_target_pairs={{0,8},{8,0},{16,24},{24,16},{1,9},{9,1},{17,25},{25,17},{2,10},{10... | collective-permute-start | bytes 786440 | tf_op jit(solution)/shard_map/ppermute | solution.py:399
  723.4 19.7 %collective-permute-start.22 = (bf16[4,64,1536]{2,1,0:T(8,128)(2,1)S(1)}, bf16[4,64,1536]{2,1,0:T(8,128)(2,1)S(1)}, u32[]{:S(2)}, u32[]{:S(2)}) collective-permute-start(bf16[4,64,1536]{2,1,0:T(8,128)(2,1)S(1)} %get-tuple-element.161), channel_id=1, source_target_pairs={{0,5},{1,4},{4,1},{5,0},{2,7},{3,6},{6,3},{7,2},{8,13},{9,12},{12,... | collective-permute-start | bytes 2359304 | tf_op jit(solution)/shard_map/ppermute | solution.py:399
  737.9 53.2 %collective-permute-start.30 = (bf16[4,64,1536]{2,1,0:T(8,128)(2,1)}, bf16[4,64,1536]{2,1,0:T(8,128)(2,1)}, u32[]{:S(2)}, u32[]{:S(2)}) collective-permute-start(bf16[4,64,1536]{2,1,0:T(8,128)(2,1)} %get-tuple-element.160), channel_id=1, source_target_pairs={{0,1},{1,0},{4,5},{5,4},{2,3},{3,2},{6,7},{7,6},{8,9},{9,8},{12,13... | collective-permute-start | bytes 2359304 | tf_op jit(solution)/shard_map/ppermute | solution.py:399
  759.9 11.3 %collective-permute-start.42 = (f32[8,1024]{1,0:T(8,128)S(1)}, f32[8,1024]{1,0:T(8,128)S(1)}, u32[]{:S(2)}, u32[]{:S(2)}) collective-permute-start(f32[8,1024]{1,0:T(8,128)S(1)} %concatenate.39), channel_id=1, source_target_pairs={{0,5},{1,4},{4,1},{5,0},{2,7},{3,6},{6,3},{7,2},{8,13},{9,12},{12,... | collective-permute-start | bytes 98312 | tf_op jit(solution)/shard_map/ppermute | solution.py:399
  760.1 11.1 %collective-permute-start.41 = (f32[8,1024]{1,0:T(8,128)S(1)}, f32[8,1024]{1,0:T(8,128)S(1)}, u32[]{:S(2)}, u32[]{:S(2)}) collective-permute-start(f32[8,1024]{1,0:T(8,128)S(1)} %concatenate.39), channel_id=1, source_target_pairs={{0,4},{1,5},{4,0},{5,1},{2,6},{3,7},{6,2},{7,3},{8,12},{9,13},{12,... | collective-permute-start | bytes 98312 | tf_op jit(solution)/shard_map/ppermute | solution.py:399
  760.8 10.4 %collective-permute-start.40 = (f32[8,1024]{1,0:T(8,128)S(1)}, f32[8,1024]{1,0:T(8,128)S(1)}, u32[]{:S(2)}, u32[]{:S(2)}) collective-permute-start(f32[8,1024]{1,0:T(8,128)S(1)} %concatenate.39), channel_id=1, source_target_pairs={{0,1},{1,0},{4,5},{5,4},{2,3},{3,2},{6,7},{7,6},{8,9},{9,8},{12,13... | collective-permute-start | bytes 98312 | tf_op jit(solution)/shard_map/ppermute | solution.py:399
  763.5 27.6 %collective-permute-start.29 = (bf16[4,64,1536]{2,1,0:T(8,128)(2,1)}, bf16[4,64,1536]{2,1,0:T(8,128)(2,1)}, u32[]{:S(2)}, u32[]{:S(2)}) collective-permute-start(bf16[4,64,1536]{2,1,0:T(8,128)(2,1)} %dynamic-slice_bitcast_fusion.16), channel_id=1, source_target_pairs={{0,4},{1,5},{4,0},{5,1},{2,6},{3,7},{6,2},{7,3},{8,12},{9,13},{12,... | collective-permute-start | bytes 2359304 | tf_op jit(solution)/shard_map/ppermute | solution.py:399
  771.2 14.2 %collective-permute-start.45 = (f32[8,1024]{1,0:T(8,128)S(1)}, f32[8,1024]{1,0:T(8,128)S(1)}, u32[]{:S(2)}, u32[]{:S(2)}) collective-permute-start(f32[8,1024]{1,0:T(8,128)S(1)} %add_add_fusion.1), channel_id=1, source_target_pairs={{0,24},{8,16},{16,8},{24,0},{1,25},{9,17},{17,9},{25,1},{2,26},{10... | collective-permute-start | bytes 98312 | tf_op jit(solution)/shard_map/ppermute | solution.py:399
  772.7 14.8 %collective-permute-start.44 = (f32[8,1024]{1,0:T(8,128)S(1)}, f32[8,1024]{1,0:T(8,128)S(1)}, u32[]{:S(2)}, u32[]{:S(2)}) collective-permute-start(f32[8,1024]{1,0:T(8,128)S(1)} %add_add_fusion.1), channel_id=1, source_target_pairs={{0,16},{8,24},{16,0},{24,8},{1,17},{9,25},{17,1},{25,9},{2,18},{10... | collective-permute-start | bytes 98312 | tf_op jit(solution)/shard_map/ppermute | solution.py:399
  785.3 3.9 collective-permute-start.43
  789.2 1.8 collective-permute-start.46
  790.5 31.5 %collective-permute-start.28 = (bf16[640,1024]{1,0:T(8,128)(2,1)}, bf16[640,1024]{1,0:T(8,128)(2,1)}, u32[]{:S(2)}, u32[]{:S(2)}) collective-permute-start(bf16[640,1024]{1,0:T(8,128)(2,1)} %fusion.43), channel_id=1, source_target_pairs={{0,1},{1,0},{2,3},{3,2},{4,5},{5,4},{6,7},{7,6},{8,9},{9,8},{10,11... | collective-permute-start | bytes 3932168 | tf_op jit(solution)/shard_map/ppermute | solution.py:399
  793.4 9.8 %collective-permute-start.33 = (bf16[64,1536]{1,0:T(8,128)(2,1)S(1)}, bf16[64,1536]{1,0:T(8,128)(2,1)S(1)}, u32[]{:S(2)}, u32[]{:S(2)}) collective-permute-start(bf16[64,1536]{1,0:T(8,128)(2,1)S(1)} %get-tuple-element.173), channel_id=1, source_target_pairs={{0,24},{8,16},{16,8},{24,0},{1,25},{9,17},{17,9},{25,1},{2,26},{10... | collective-permute-start | bytes 589832 | tf_op jit(solution)/shard_map/ppermute | solution.py:399
  795.0 17.9 %collective-permute-start.32 = (bf16[64,1536]{1,0:T(8,128)(2,1)S(1)}, bf16[64,1536]{1,0:T(8,128)(2,1)S(1)}, u32[]{:S(2)}, u32[]{:S(2)}) collective-permute-start(bf16[64,1536]{1,0:T(8,128)(2,1)S(1)} %get-tuple-element.174), channel_id=1, source_target_pairs={{0,16},{8,24},{16,0},{24,8},{1,17},{9,25},{17,1},{25,9},{2,18},{10... | collective-permute-start | bytes 589832 | tf_op jit(solution)/shard_map/ppermute | solution.py:399
  795.3 17.6 %collective-permute-start.31 = (bf16[64,1536]{1,0:T(8,128)(2,1)S(1)}, bf16[64,1536]{1,0:T(8,128)(2,1)S(1)}, u32[]{:S(2)}, u32[]{:S(2)}) collective-permute-start(bf16[64,1536]{1,0:T(8,128)(2,1)S(1)} %get-tuple-element.172), channel_id=1, source_target_pairs={{0,8},{8,0},{16,24},{24,16},{1,9},{9,1},{17,25},{25,17},{2,10},{10... | collective-permute-start | bytes 589832 | tf_op jit(solution)/shard_map/ppermute | solution.py:399
  (102 other events, 1222.1 us)
Sparse Core Ops, SparseCore 0:
  131.9 84.4 all-gather.1

commit v7 on v6

--- a/solution.py
+++ b/solution.py
@@ -219,10 +219,11 @@
 
 def gelu_and_slope(values):
     square = values * values
-    bent = jnp.tanh(gelu_scale * values * (1.0 + gelu_cubic * square))
+    bent = jnp.tanh(values * (gelu_scale + gelu_scale * gelu_cubic * square))
     half = 0.5 + 0.5 * bent
-    slope = half + 2.0 * gelu_scale * values * half * (1.0 - half) * (1.0 + 3.0 * gelu_cubic * square)
-    return values * half, slope
+    made = values * half
+    slope = half + made * (1.0 - half) * (2.0 * gelu_scale + 6.0 * gelu_scale * gelu_cubic * square)
+    return made, slope
 
 
 def apart(position, distance):
@@ -254,9 +255,13 @@
     pl.semaphore_wait(barrier, len(partners))
 
     half = depth // 2
-    first = pl.ds(z // half * half, half)
-    second = pl.ds(half - z // half * half, half)
+    everything = pl.ds(0, depth)
     started = []
+
+    def spans(number):
+        if number % 3:
+            return everything, None
+        return pl.ds(z // half * half, half), pl.ds(half - z // half * half, half)
 
     def copy(source, target, partner):
         slot = len(started)
@@ -299,27 +304,33 @@
         crossed.append(over(number, t, t, at_y, span, {"core": 1 - core}))
 
     def plane_start(number, keep, sent):
+        first, second = spans(number)
         keep.wait()
-        for k in range(1, half):
+        for k in range(1, half if second is not None else depth):
             sent[k - 1].wait_recv()
         over_x = [over(number, 0, k, y, first, {"tp": apart(x, k)}) for k in range(1, tp)]
+        last = [(over(number, 0, 0, y, first, {"y": 1 - y}), 0, 1 - y, first)]
+        to_core(number, 0, y, first)
+        if second is None:
+            return over_x, None, last
         for k in range(half, depth):
             sent[k - 1].wait_recv()
         over_y = over(number, 0, 0, y, second, {"y": 1 - y})
-        last = [(over(number, 0, 0, y, first, {"y": 1 - y}), 0, 1 - y, first)]
         for k in range(1, tp):
             made = over(number, 0, k, y, second, {"tp": apart(x, k)})
             last.append((made, k, y, second))
-        to_core(number, 0, y, first)
         to_core(number, 0, y, second)
         return over_x, over_y, last
 
     def plane_turn(number, over_x, over_y, last):
+        first, second = spans(number)
         for k in range(1, tp):
             over_x[k - 1].wait_recv()
             made = over(number, k, k, y, first, {"y": 1 - y})
             last.append((made, k, 1 - y, first))
             to_core(number, k, y, first)
+        if second is None:
+            return last
         over_y.wait_recv()
         for k in range(1, tp):
             made = over(number, 0, k, 1 - y, second, {"tp": apart(x, k)})
@@ -439,19 +450,32 @@
     return (block_at(blocks, 2, core).astype(f32) + came.astype(f32)).astype(bf16)
 
 
-def scatter_plane(parts):
+def scatter_plane(parts, pieces=1):
     y = lax.axis_index("y")
-    straight, across = [block_at(parts[0], 1, y)], []
-    for t in range(len(parts)):
-        for j in range(2):
-            if t or j:
-                came = send(block_at(parts[t], 1, y ^ j), ("y", "tp"), j * len(parts) + t)
-                (across if t and j else straight).append(came)
+    straight, across = [[] for _ in range(pieces)], [[] for _ in range(pieces)]
+    size = parts[0].shape[0] // pieces
+    for piece in range(pieces):
+        rows = [part[piece * size : (piece + 1) * size] for part in parts]
+        straight[piece].append(block_at(rows[0], 1, y))
+        for t in range(len(parts)):
+            for j in range(2):
+                if t or j:
+                    came = send(block_at(rows[t], 1, y ^ j), ("y", "tp"), j * len(parts) + t)
+                    (across if t and j else straight)[piece].append(came)
     return straight, across
 
 
-def total(pieces):
-    return sum([piece.astype(f32) for piece in pieces[1:]], pieces[0].astype(f32)).astype(bf16)
+def flat(pieces):
+    return [value for piece in pieces for value in piece]
+
+
+def total(straight, across):
+    sums = []
+    for near, far in zip(straight, across):
+        pieces = near + far
+        made = sum([piece.astype(f32) for piece in pieces[1:]], pieces[0].astype(f32))
+        sums.append(made.astype(bf16))
+    return jnp.concatenate(sums, axis=0)
 
 
 def scatter_z(part):
@@ -540,19 +564,25 @@
     whole_out = [[] for _ in halves]
     share_out = [[] for _ in halves]
     saved = {}
-    for n in range(whole):
-        for t in halves:
-            qkv = whole_qkv[t][n * tree_len : (n + 1) * tree_len]
+    def whole_forward(t, *others):
+        for n in range(whole):
+            qkv = after(whole_qkv[t][n * tree_len : (n + 1) * tree_len], *others)
             out, lse = attention_forward(qkv, *whole_tables[n])
             saved[n, t] = (qkv, out, lse)
             whole_out[t].append(out)
+
+    whole_forward(0)
     share_calls = [after(call, *whole_out[0]) for call in share_calls]
+    made = []
     for n in range(share_count):
         out, lse = attention_forward(share_calls[n], *share_tables[n])
         saved[n] = (share_calls[n], out, lse)
+        made.append(out)
         parts = exchange_tp([share_rows(out, k) for k in halves])
         for t in halves:
             share_out[t].append(parts[t])
+    for t in range(1, tp):
+        whole_forward(t, *made)
     attended = [jnp.concatenate(whole_out[t] + share_out[t], axis=0) for t in halves]
     cotangent = after(cotangent[:, 0], *attended)
     cotangent_came = [send(piece, "tp", n % (tp - 1) + 1) for n, piece in enumerate(outgoing(cotangent))]
@@ -567,12 +597,12 @@
         values, bent = lax.optimization_barrier((values.astype(bf16), bent.astype(bf16)))
         hidden.append(values)
         slope.append(bent)
+    branch_f = sum(dot_nt(hidden[t], full_down[t]) for t in halves)
     normed_shared = []
     for n in range(share_count):
         start = split + n * own_rows
-        near = after(normed[start : start + own_rows], hidden[0])
+        near = after(normed[start : start + own_rows], branch_f)
         normed_shared.append(in_place_order(exchange_tp([near] * tp)))
-    branch_f = sum(dot_nt(hidden[t], full_down[t]) for t in halves)
     out = (residual + norm_forward(branch_f, norm_gains[3], norm_biases[3])).astype(bf16)
     out_rows = rows_back(out)
 
@@ -585,18 +615,20 @@
         (dot_nn(grad_branch_f, full_down[t]) * slope[t].astype(f32)).astype(bf16) for t in halves
     ]
     grad_up = [after(values, *core_down) for values in grad_up]
-    straight_down, across_down = scatter_plane(core_down)
-    dw_up = [dot_tn(normed_f, grad_up[t]).astype(bf16) for t in halves]
+    straight_down, across_down = scatter_plane(core_down, 2)
+    dw_up = [dot_tn(normed_f, grad_up[0]).astype(bf16)]
+    ready = [*dw_up, *straight_down[0]]
+    dw_up += [dot_tn(after(normed_f, *ready), grad_up[t]).astype(bf16) for t in halves[1:]]
     core_up = [scatter_core(part) for part in dw_up]
-    grad_up = [after(values, *dw_up) for values in grad_up]
-    grad_up[1:] = [after(values, *straight_down) for values in grad_up[1:]]
+    grad_up = [after(values, *dw_up, *straight_down[1]) for values in grad_up]
+    grad_up[1:] = [after(values, *across_down[0]) for values in grad_up[1:]]
     grad_normed_f = sum(dot_nt(grad_up[t], full_up[t]) for t in halves)
     grad_part, sums_2 = norm_backward(residual, norm_gains[2], grad_normed_f)
     grad_residual = grad_out + grad_part
 
     grad_branch_a, sums_1 = norm_backward(branch_a, norm_gains[1], grad_residual)
-    grad_branch_a = after(grad_branch_a.astype(bf16), *core_up, *across_down)
-    z_down = scatter_z(total(straight_down + across_down))
+    grad_branch_a = after(grad_branch_a.astype(bf16), *core_up, *across_down[1])
+    z_down = scatter_z(after(total(straight_down, across_down), grad_branch_a))
     straight_up, across_up = scatter_plane(core_up)
     share_grad = [dot_nn(grad_branch_a[split:], w).astype(bf16) for w in full_out]
     whole_grad = [dot_nn(grad_branch_a[:split], w).astype(bf16) for w in full_out] if whole else []
@@ -618,7 +650,7 @@
     made = []
     dw_qkv = [None] * tp
     for t in range(1, tp):
-        made += whole_backward(t)
+        made += whole_backward(t, z_down)
         if whole:
             dw_qkv[t] = dot_tn(normed_whole, jnp.concatenate(grad_qkv[t], axis=0)).astype(bf16)
         else:
@@ -632,24 +664,24 @@
         dx = attention_backward(qkv, do, att, lse, *share_tables[n])
         made = [dx]
         grad_shared.append(dx)
-    whole_backward(0, *core_out, *straight_up, *core_qkv[1:], *made)
+    whole_backward(0, *core_out, *flat(straight_up), *core_qkv[1:], *made)
     for n in range(share_count):
         part = dot_nt(grad_shared[n], full_qkv[0])
         pieces = exchange_tp([share_rows(part, 0)] + [share_rows(part, k).astype(bf16) for k in halves[1:]])
         own_part.append(sum([piece.astype(f32) for piece in pieces[1:]], pieces[0]))
     straight_out, across_out = scatter_plane(core_out)
-    ready = [*across_up, z_down]
+    ready = flat(across_up)
     owned = [after(rows, *ready) for rows in grad_shared]
-    z_up = scatter_z(total(straight_up + across_up))
-    z_out = scatter_z(total(straight_out + across_out))
+    z_out = scatter_z(total(straight_out, across_out))
     owned = [dot_tn(rows, grad) for rows, grad in zip(normed_shared, owned)]
     if whole:
         owned.append(dot_tn(normed_whole, jnp.concatenate(grad_qkv[0], axis=0)))
     dw_qkv[0] = sum(owned).astype(bf16)
     core_qkv[0] = scatter_core(dw_qkv[0])
+    z_up = scatter_z(after(total(straight_up, across_up), dw_qkv[0]))
     straight_qkv, across_qkv = scatter_plane(core_qkv)
-    z_qkv = scatter_z(total(straight_qkv + across_qkv))
-    ready = [dw_qkv[0], *across_qkv, *straight_out, *across_out]
+    z_qkv = scatter_z(total(straight_qkv, across_qkv))
+    ready = [dw_qkv[0], *flat(across_qkv), *flat(straight_out), *flat(across_out)]
     grad_normed = list(own_part)
     if whole:
         trees = [after(jnp.concatenate(grad_qkv[t], axis=0), *ready) for t in halves]
@@ -657,8 +689,9 @@
         grad_normed = [sum(dot_nt(trees[t], full_qkv[t]) for t in halves)] + grad_normed
     grad_normed = jnp.concatenate(grad_normed, axis=0)
     grad_part, sums_0 = norm_backward(x, norm_gains[0], grad_normed)
-    input_rows = rows_back(grad_residual + grad_part)
-    sums = jnp.concatenate([sums_0, sums_1, sums_2, sums_3])
+    grad_x = grad_residual + grad_part
+    input_rows = rows_back(grad_x)
+    sums = after(jnp.concatenate([sums_0, sums_1, sums_2, sums_3]), grad_x)
     sums = sum_everywhere(sums).reshape(4, 2, width)
     return (
         out_rows,

time: 845 us -> 865 us (1.024)
  Pallas kernels: 253 us -> 264 us
  waiting for transfers between devices: 113 us -> 124 us
    pallas_call x1, Pallas kernels: 108 us -> 119 us  [gather_weights(): pl.pallas_call(functools.partial(gather_kernel, chunks, len(shards), move...]
    ppermute x47 -> x50, waiting for transfers between devices: 113 us -> 124 us  [send(): return lax.ppermute(values, axes, [(s, s ^ distance) for s in range(count)])]
    ppermute x47 -> x50, starting transfers between devices: 56.8 us -> 49.3 us  [send(): return lax.ppermute(values, axes, [(s, s ^ distance) for s in range(count)])]
    unnamed x210 -> x220, local copies, waits for them, and re-layouts: 18.8 us -> 20.2 us
  transfers between devices with their start and end apart: 48 -> 51, of which waited for: 15 -> 20; matrix products, arithmetic and copies ran while one was open for 30% -> 36% of each run, Pallas kernels for 17% -> 17%
where the time goes in v7:
time: 865 us; the launch traced here: 855 us
  Pallas kernels  264 us (31%)
  matrix products  260 us (30%)
  waiting for transfers between devices  124 us (14%)
  other arithmetic  88.9 us (10%)
  local copies, waits for them, and re-layouts  52.5 us (6%)
  starting transfers between devices  49.3 us (6%)
  between operations  16.5 us (2%)
    ppermute x50, waiting for transfers between devices, send(): return lax.ppermute(values, axes, [(s, s ^ distance) for s in range(count)])  124 us
    pallas_call x1, Pallas kernels, gather_weights(): pl.pallas_call(functools.partial(gather_kernel, chunks, len(shards), move...  119 us
    dot_general x12, matrix products, dot_nn(): lax.dot_general(a, b, (((1,), (0,)), ((), ())), preferred_element_type=f32)  97.3 us
    dot_general x9, matrix products, dot_nt(): lax.dot_general(a, b, (((1,), (1,)), ((), ())), preferred_element_type=f32)  92.7 us
    pallas_call x3, Pallas kernels, attention_backward(): pl.pallas_call(attention_backward_kernel, name='attention_backward', out_...  80 us
    dot_general x9, matrix products, dot_tn(): lax.dot_general(a, b, (((0,), (0,)), ((), ())), preferred_element_type=f32)  70.5 us
    pallas_call x3, Pallas kernels, attention_forward(): pl.pallas_call(attention_forward_kernel, name='attention_forward', out_sh...  64.6 us
    ppermute x50, starting transfers between devices, send(): return lax.ppermute(values, axes, [(s, s ^ distance) for s in range(count)])  49.3 us
  transfers between devices with their start and end apart: 51, of which 20 were waited for; matrix products, arithmetic and copies ran while one was open for 36% of the time, Pallas kernels for 17%

profile of v7, /device:TPU:0, one launch (start us, length us, event | category | flops | bytes accessed | tf_op | source)
XLA Modules:
  0.0 855.3 jit_solution(4742066797940387801)
XLA Ops:
  10.1 119.3 %gather_weights.1 = (bf16[4,2,2,64,1536]{4,3,2,1,0:T(8,128)(2,1)}, bf16[4,2,2,64,1536]{4,3,2,1,0:T(8,128)(2,1)}, bf16[4,2,2,64,512]{4,3,2,1,0:T(8,128)(2,1)}, bf...) custom-call(bf16[64,1536]{1,0:T(8,128)(2,1)} %bitcast.320, ...), custom_call_target="tpu_custom_call" | custom-call | bytes 33554432 | tf_op jit(solution)/shard_map/gather_weights/pallas_call | solution.py:384
  138.3 3.5 convolution_convert_fusion.8
  142.4 5.7 convolution_convert_fusion.q_ref.k_ref.v_ref
  148.7 8.9 %convolution_convert_fusion.1.q_ref.k_ref.v_ref = bf16[1280,1536]{1,0:T(8,128)(2,1)} fusion(bf16[1024,1536]{1,0:T(8,128)(2,1)} %bitcast.356, bf16[1920,1024]{1,0:T(8,128)(2,1)} %copy-done.26), kind=kOutput, calls=%fused_computation.52 | convolution fusion | flops 4028497920 | bytes 9699328 | tf_op jit(solution)/shard_map/dot_general | solution.py:23
  162.9 21.5 %attention_forward.3 = (bf16[1280,512]{1,0:T(8,128)(2,1)S(1)}, f32[4,8,1280]{2,1,0:T(8,128)S(1)}) custom-call(bf16[1280,1536]{1,0:T(8,128)(2,1)S(1)} %copy-done.10, bf16[1280,1536]{1,0:T(8,128)(2,1)S(1)} %copy-done.10, bf16[1280,1536]{1,0:T(8,128)(2,1)S(1)} %copy-done.10, s32[1280,8]{1,0:T(8,128)S(1)} %pad.14.clone.col_ref, s32[8,1280]{1,0:T(8,128)S(1)} %pad.15.row_ref), custom_call_target="tpu_custom_call" | custom-call | flops 8053063680 | bytes 5898240 | tf_op jit(solution)/shard_map/attention_forward/pallas_call | solution.py:80
  184.4 21.7 %collective-permute-done = bf16[640,1536]{1,0:T(8,128)(2,1)} collective-permute-done((bf16[640,1536]{1,0:T(8,128)(2,1)}, bf16[640,1536]{1,0:T(8,128)(2,1)}, u32[]{:S(2)}, u32[]{:S(2)}) %collective-permute-start) | collective-permute-done | bytes 1966112 | tf_op jit(solution)/shard_map/ppermute | solution.py:410
  206.1 4.2 broadcast_select_fusion.3
  210.6 21.7 %attention_forward.4 = (bf16[1280,512]{1,0:T(8,128)(2,1)S(1)}, f32[4,8,1280]{2,1,0:T(8,128)S(1)}) custom-call(bf16[1280,1536]{1,0:T(8,128)(2,1)S(1)} %pad_maximum_fusion.2.q_ref.k_ref.v_ref, bf16[1280,1536]{1,0:T(8,128)(2,1)S(1)} %pad_maximum_fusion.2.q_ref.k_ref.v_ref, bf16[1280,1536]{1,0:T(8,128)(2,1)S(1)} %pad_maximum_fusion.2.q_ref.k_ref.v_ref, ...), custom_call_target="tpu_custom_call" | custom-call | flops 8053063680 | bytes 5898240 | tf_op jit(solution)/shard_map/attention_forward/pallas_call | solution.py:80
  234.4 21.4 %attention_forward.5 = (bf16[1280,512]{1,0:T(8,128)(2,1)S(1)}, f32[4,8,1280]{2,1,0:T(8,128)S(1)}) custom-call(bf16[1280,1536]{1,0:T(8,128)(2,1)S(1)} %copy-done.12, bf16[1280,1536]{1,0:T(8,128)(2,1)S(1)} %copy-done.12, bf16[1280,1536]{1,0:T(8,128)(2,1)S(1)} %copy-done.12, s32[1280,8]{1,0:T(8,128)S(1)} %pad.14.clone.col_ref, s32[8,1280]{1,0:T(8,128)S(1)} %pad.15.row_ref), custom_call_target="tpu_custom_call" | custom-call | flops 8053063680 | bytes 5898240 | tf_op jit(solution)/shard_map/attention_forward/pallas_call | solution.py:80
  275.4 20.6 %add_convert_fusion = (bf16[1920,2048]{1,0:T(8,128)(2,1)}, bf16[1920,2048]{1,0:T(8,128)(2,1)}) fusion(bf16[1920,1024]{1,0:T(8,128)(2,1)S(1)} %add_convert_fusion.3, bf16[1024,2048]{1,0:T(8,128)(2,1)} %bitcast.354), kind=kOutput, calls=%fused_computation.2 | convolution fusion | flops 8112046080 | bytes 23855104 | tf_op jit(solution)/shard_map/dot_general | solution.py:23
  296.0 16.9 %add_convert_fusion.1 = (bf16[1920,2048]{1,0:T(8,128)(2,1)}, bf16[1920,2048]{1,0:T(8,128)(2,1)}) fusion(bf16[1920,1024]{1,0:T(8,128)(2,1)S(1)} %add_convert_fusion.3, bf16[1024,2048]{1,0:T(8,128)(2,1)S(1)} %bitcast.353), kind=kOutput, calls=%fused_computation.6 | convolution fusion | flops 8112046080 | bytes 23855104 | tf_op jit(solution)/shard_map/dot_general | solution.py:23
  316.7 15.5 %fusion.54 = f32[1920,1024]{1,0:T(8,128)} fusion(bf16[1920,2048]{1,0:T(8,128)(2,1)} %get-tuple-element.62, pred[]{:T(512)S(6)} %eq.30, bf16[2048,2048]{1,0:T(8,128)(2,1)} %all-gather.2.cloned.1.call-done), kind=kOutput, calls=%fused_computation.163 | convolution fusion | flops 8055160832 | bytes 24117248 | tf_op jit(solution)/shard_map/dot_general | solution.py:27
  332.3 20.2 %fusion.81 = (f32[1920]{0:T(1024)S(1)}, f32[1920,1024]{1,0:T(8,128)S(1)}) fusion(f32[1920,1024]{1,0:T(8,128)} %fusion.54, bf16[1920,2048]{1,0:T(8,128)(2,1)} %get-tuple-element.65, pred[]{:T(512)S(6)} %eq.31, bf16[2048,2048]{1,0:T(8,128)(2,1)} %all-gather.2.cloned.1.call-done), kind=kOutput, calls=%fused_computation.265 | convolution fusion | flops 8059090944 | bytes 31989248 | tf_op jit(solution)/shard_map/dot_general | solution.py:27
  354.6 5.0 fusion.25
  359.7 3.7 fusion.23
  363.4 14.1 %convolution_convert_fusion.4 = bf16[1024,2048]{1,0:T(8,128)(2,1)S(1)} fusion(bf16[1920,1024]{1,0:T(8,128)(2,1)S(1)} %get-tuple-element.154, bf16[1920,2048]{1,0:T(8,128)(2,1)} %get-tuple-element.65), kind=kOutput, calls=%fused_computation.78 | convolution fusion | flops 8055160832 | bytes 15990784 | tf_op jit(solution)/shard_map/dot_general | solution.py:31
  377.6 11.4 %convolution_convert_fusion.5 = bf16[1024,2048]{1,0:T(8,128)(2,1)S(1)} fusion(bf16[1920,1024]{1,0:T(8,128)(2,1)S(1)} %get-tuple-element.154, bf16[1920,2048]{1,0:T(8,128)(2,1)} %get-tuple-element.62), kind=kOutput, calls=%fused_computation.79 | convolution fusion | flops 8055160832 | bytes 15990784 | tf_op jit(solution)/shard_map/dot_general | solution.py:31
  394.8 14.7 %multiply_convert_fusion = bf16[1920,2048]{1,0:T(8,128)(2,1)} fusion(bf16[1920,2048]{1,0:T(8,128)(2,1)} %get-tuple-element.70, bf16[1920,1024]{1,0:T(8,128)(2,1)S(1)} %copy-done.37, pred[]{:T(512)S(6)} %eq.31, bf16[2048,2048]{1,0:T(8,128)(2,1)} %all-gather.2.cloned.1.call-done), kind=kOutput, calls=%fused_computation | convolution fusion | flops 8066957312 | bytes 28049408 | tf_op jit(solution)/shard_map/dot_general | solution.py:23
  409.5 16.4 %multiply_convert_fusion.1 = bf16[1920,2048]{1,0:T(8,128)(2,1)} fusion(bf16[1920,2048]{1,0:T(8,128)(2,1)} %get-tuple-element.67, bf16[1920,1024]{1,0:T(8,128)(2,1)} %copy-done.36, pred[]{:T(512)S(6)} %eq.30, bf16[2048,2048]{1,0:T(8,128)(2,1)} %all-gather.2.cloned.1.call-done), kind=kOutput, calls=%fused_computation.1 | convolution fusion | flops 8066957312 | bytes 28049408 | tf_op jit(solution)/shard_map/dot_general | solution.py:23
  430.0 16.6 %collective-permute-done.23 = bf16[640,1024]{1,0:T(8,128)(2,1)} collective-permute-done((bf16[640,1024]{1,0:T(8,128)(2,1)S(1)}, bf16[640,1024]{1,0:T(8,128)(2,1)}, u32[]{:S(2)}, u32[]{:S(2)}) %collective-permute-start.23) | collective-permute-done | bytes 1310752 | tf_op jit(solution)/shard_map/ppermute | solution.py:410
  459.9 9.9 %convolution_convert_fusion.3 = bf16[1024,2048]{1,0:T(8,128)(2,1)S(1)} fusion(bf16[1920,1024]{1,0:T(8,128)(2,1)S(1)} %copy-done.39, bf16[1920,2048]{1,0:T(8,128)(2,1)S(1)} %bitcast.367), kind=kOutput, calls=%fused_computation.77 | convolution fusion | flops 8055160832 | bytes 15990784 | tf_op jit(solution)/shard_map/dot_general | solution.py:31
  473.9 9.1 %collective-permute-done.7 = bf16[2,64,2048]{2,1,0:T(8,128)(2,1)S(1)} collective-permute-done((bf16[2,64,2048]{2,1,0:T(8,128)(2,1)S(1)}, bf16[2,64,2048]{2,1,0:T(8,128)(2,1)S(1)}, u32[]{:S(2)}, u32[]{:S(2)}) %collective-permute-start.7) | collective-permute-done | bytes 524320 | tf_op jit(solution)/shard_map/ppermute | solution.py:410
  483.0 10.8 %collective-permute-done.10 = bf16[2,64,2048]{2,1,0:T(8,128)(2,1)S(1)} collective-permute-done((bf16[2,64,2048]{2,1,0:T(8,128)(2,1)S(1)}, bf16[2,64,2048]{2,1,0:T(8,128)(2,1)S(1)}, u32[]{:S(2)}, u32[]{:S(2)}) %collective-permute-start.10) | collective-permute-done | bytes 524320 | tf_op jit(solution)/shard_map/ppermute | solution.py:410
  494.2 13.1 %convolution_convert_fusion.2 = bf16[1024,2048]{1,0:T(8,128)(2,1)} fusion(bf16[1920,1024]{1,0:T(8,128)(2,1)S(1)} %copy-done.39, bf16[1920,2048]{1,0:T(8,128)(2,1)} %multiply_convert_fusion), kind=kOutput, calls=%fused_computation.76 | convolution fusion | flops 8055160832 | bytes 15990784 | tf_op jit(solution)/shard_map/dot_general | solution.py:31
  507.9 11.1 %fusion.83 = f32[1920,1024]{1,0:T(8,128)} fusion(bf16[1920,2048]{1,0:T(8,128)(2,1)S(1)} %bitcast.369, bf16[1024,2048]{1,0:T(8,128)(2,1)S(1)} %bitcast.355), kind=kOutput, calls=%fused_computation.267 | convolution fusion | flops 8053063680 | bytes 19922944 | tf_op jit(solution)/shard_map/dot_general | solution.py:27
  519.0 21.0 %multiply_reduce_fusion = (f32[1024]{0:T(1024)}, f32[1920]{0:T(1024)S(1)}, f32[1920]{0:T(1024)S(1)}, f32[1024]{0:T(1024)}, f32[1920,1024]{1,0:T(8,128)}) fusion(f32[1920,1024]{1,0:T(8,128)} %copy-done.15, f32[1920]{0:T(1024)S(1)} %copy-done.67, f32[1920]{0:T(1024)S(1)} %copy-done.65, f32[1024]{0:T(1024)S(1)} %bitcast.336, f32[1920,1024]{1,0:T(8,128)} %fusion.83, ...), kind=kOutput, calls=%fused_computation.41 | convolution fusion | flops 8072718336 | bytes 35694592 | tf_op jit(solution)/shard_map/dot_general | solution.py:27
  540.0 3.4 dynamic-slice_bitcast_fusion
  543.5 11.0 %multiply_reduce_fusion.1 = (f32[1024]{0:T(1024)}, f32[1920]{0:T(1024)S(1)}, f32[1920]{0:T(1024)S(1)}, f32[1024]{0:T(1024)}, f32[1920,1024]{1,0:T(8,128)S(1)}) fusion(f32[1920,1024]{1,0:T(8,128)S(1)} %bitcast.286, f32[1920]{0:T(1024)S(1)} %copy-done.63, f32[1920]{0:T(1024)S(1)} %copy-done.59, f32[1024]{0:T(1024)S(1)} %bitcast.330, ...), kind=kLoop, calls=%fused_computation.42 | loop fusion | flops 35383552 | bytes 35467264 | tf_op jit(solution)/shard_map/reduce_sum | solution.py:217
  586.6 8.8 %collective-permute-done.18 = bf16[64,2048]{1,0:T(8,128)(2,1)S(1)} collective-permute-done((bf16[64,2048]{1,0:T(8,128)(2,1)S(1)}, bf16[64,2048]{1,0:T(8,128)(2,1)S(1)}, u32[]{:S(2)}, u32[]{:S(2)}) %collective-permute-start.18) | collective-permute-done | bytes 262176 | tf_op jit(solution)/shard_map/ppermute | solution.py:410
  595.9 11.9 %collective-permute-done.19 = bf16[64,2048]{1,0:T(8,128)(2,1)S(1)} collective-permute-done((bf16[64,2048]{1,0:T(8,128)(2,1)S(1)}, bf16[64,2048]{1,0:T(8,128)(2,1)S(1)}, u32[]{:S(2)}, u32[]{:S(2)}) %collective-permute-start.19) | collective-permute-done | bytes 262176 | tf_op jit(solution)/shard_map/ppermute | solution.py:410
  609.7 26.8 %attention_backward.3 = bf16[1280,1536]{1,0:T(8,128)(2,1)S(1)} custom-call(bf16[1280,1536]{1,0:T(8,128)(2,1)S(1)} %copy-done.13, bf16[1280,1536]{1,0:T(8,128)(2,1)S(1)} %copy-done.13, bf16[1280,1536]{1,0:T(8,128)(2,1)S(1)} %copy-done.13, bf16[1280,512]{1,0:T(8,128)(2,1)S(1)} %convolution_convert_fusion.9.do_ref, bf16[1280,512]{1,0:T(8,128)(2,1)S(1)} %copy-done.5, ...), custom_call_target="tpu_custom_call" | custom-call | flops 20132659200 | bytes 11796480 | tf_op jit(solution)/shard_map/attention_backward/pallas_call | solution.py:171
  636.5 4.5 convolution_convert_fusion.6
  650.4 26.6 %attention_backward.4 = bf16[1280,1536]{1,0:T(8,128)(2,1)S(1)} custom-call(bf16[1280,1536]{1,0:T(8,128)(2,1)S(1)} %copy-done.1, bf16[1280,1536]{1,0:T(8,128)(2,1)S(1)} %copy-done.1, bf16[1280,1536]{1,0:T(8,128)(2,1)S(1)} %copy-done.1, bf16[1280,512]{1,0:T(8,128)(2,1)S(1)} %pad_maximum_fusion.5.do_ref, bf16[1280,512]{1,0:T(8,128)(2,1)S(1)} %copy-done.3, ...), custom_call_target="tpu_custom_call" | custom-call | flops 20132659200 | bytes 11796480 | tf_op jit(solution)/shard_map/attention_backward/pallas_call | solution.py:171
  678.4 6.3 fusion.85
  694.0 26.6 %attention_backward.5 = bf16[1280,1536]{1,0:T(8,128)(2,1)S(1)} custom-call(bf16[1280,1536]{1,0:T(8,128)(2,1)S(1)} %copy-done.11, bf16[1280,1536]{1,0:T(8,128)(2,1)S(1)} %copy-done.11, bf16[1280,1536]{1,0:T(8,128)(2,1)S(1)} %copy-done.11, bf16[1280,512]{1,0:T(8,128)(2,1)S(1)} %convolution_convert_fusion.10.do_ref, bf16[1280,512]{1,0:T(8,128)(2,1)S(1)} %copy-done.7, ...), custom_call_target="tpu_custom_call" | custom-call | flops 20132659200 | bytes 11796480 | tf_op jit(solution)/shard_map/attention_backward/pallas_call | solution.py:171
  720.7 6.2 fusion.39
  726.9 6.4 add_convert_fusion.4
  747.2 6.1 collective-permute-done.40
  757.2 9.4 %collective-permute-done.41 = bf16[64,2048]{1,0:T(8,128)(2,1)S(1)} collective-permute-done((bf16[64,2048]{1,0:T(8,128)(2,1)S(1)}, bf16[64,2048]{1,0:T(8,128)(2,1)S(1)}, u32[]{:S(2)}, u32[]{:S(2)}) %collective-permute-start.41) | collective-permute-done | bytes 262176 | tf_op jit(solution)/shard_map/ppermute | solution.py:410
  769.0 6.2 fusion.84
  775.2 7.6 fusion.82
  782.9 5.0 fusion.19
  788.0 5.3 fusion.18
  810.7 3.3 collective-permute-done.32
  821.1 5.1 collective-permute-done.34
  827.7 6.3 collective-permute-done.35
  834.9 6.3 collective-permute-done.31
  844.3 3.7 maximum_bitcast_fusion
  (441 shorter events, 177.6 us)
Async XLA Ops:
  7.2 309.5 %all-gather.2.cloned.1.call-start = ((), (), s32[]{:S(2)}) async-start(), calls=%async_computation | async-start | bytes 8650752 | tf_op jit(solution)/shard_map/all_gather | solution.py:541
  141.8 64.3 %collective-permute-start = (bf16[640,1536]{1,0:T(8,128)(2,1)}, bf16[640,1536]{1,0:T(8,128)(2,1)}, u32[]{:S(2)}, u32[]{:S(2)}) collective-permute-start(bf16[640,1536]{1,0:T(8,128)(2,1)} %convolution_convert_fusion.8), channel_id=1, source_target_pairs={{0,1},{1,0},{2,3},{3,2},{4,5},{5,4},{6,7},{7,6},{8,9},{9,8},{10,11... | collective-permute-start | bytes 5898248 | tf_op jit(solution)/shard_map/ppermute | solution.py:410
  233.5 24.8 %collective-permute-start.1 = (bf16[640,512]{1,0:T(8,128)(2,1)S(1)}, bf16[640,512]{1,0:T(8,128)(2,1)S(1)}, u32[]{:S(2)}, u32[]{:S(2)}) collective-permute-start(bf16[640,512]{1,0:T(8,128)(2,1)S(1)} %get-tuple-element.180), channel_id=1, source_target_pairs={{0,1},{1,0},{2,3},{3,2},{4,5},{5,4},{6,7},{7,6},{8,9},{9,8},{10,11... | collective-permute-start | bytes 1966088 | tf_op jit(solution)/shard_map/ppermute | solution.py:410
  258.7 54.2 %collective-permute-start.3 = (bf16[640,1024]{1,0:T(8,128)(2,1)S(1)}, bf16[640,1024]{1,0:T(8,128)(2,1)S(1)}, u32[]{:S(2)}, u32[]{:S(2)}) collective-permute-start(bf16[640,1024]{1,0:T(8,128)(2,1)S(1)} %get-tuple-element.162), channel_id=1, source_target_pairs={{0,1},{1,0},{2,3},{3,2},{4,5},{5,4},{6,7},{7,6},{8,9},{9,8},{10,11... | collective-permute-start | bytes 3932168 | tf_op jit(solution)/shard_map/ppermute | solution.py:410
  389.1 37.9 %collective-permute-start.2 = (bf16[640,1024]{1,0:T(8,128)(2,1)S(1)}, bf16[640,1024]{1,0:T(8,128)(2,1)}, u32[]{:S(2)}, u32[]{:S(2)}) collective-permute-start(bf16[640,1024]{1,0:T(8,128)(2,1)S(1)} %dynamic-slice_bitcast_fusion.6), channel_id=1, source_target_pairs={{0,1},{1,0},{2,3},{3,2},{4,5},{5,4},{6,7},{7,6},{8,9},{9,8},{10,11... | collective-permute-start | bytes 3932168 | tf_op jit(solution)/shard_map/ppermute | solution.py:410
  390.3 56.3 %collective-permute-start.23 = (bf16[640,1024]{1,0:T(8,128)(2,1)S(1)}, bf16[640,1024]{1,0:T(8,128)(2,1)}, u32[]{:S(2)}, u32[]{:S(2)}) collective-permute-start(bf16[640,1024]{1,0:T(8,128)(2,1)S(1)} %copy-done.29), channel_id=1, source_target_pairs={{0,1},{1,0},{2,3},{3,2},{4,5},{5,4},{6,7},{7,6},{8,9},{9,8},{10,11... | collective-permute-start | bytes 3932168 | tf_op jit(solution)/shard_map/ppermute | solution.py:410
  394.2 55.6 %collective-permute-start.4 = (bf16[4,2,64,2048]{3,2,1,0:T(8,128)(2,1)}, bf16[4,2,64,2048]{3,2,1,0:T(8,128)(2,1)}, u32[]{:S(2)}, u32[]{:S(2)}) collective-permute-start(bf16[4,2,64,2048]{3,2,1,0:T(8,128)(2,1)} %dynamic-slice_bitcast_fusion.3), channel_id=1, source_target_pairs={{0,2},{2,0},{1,3},{3,1},{4,6},{6,4},{5,7},{7,5},{8,10},{10,8},{9,1... | collective-permute-start | bytes 6291464 | tf_op jit(solution)/shard_map/ppermute | solution.py:410
  394.2 60.3 %collective-permute-start.5 = (bf16[4,2,64,2048]{3,2,1,0:T(8,128)(2,1)}, bf16[4,2,64,2048]{3,2,1,0:T(8,128)(2,1)}, u32[]{:S(2)}, u32[]{:S(2)}) collective-permute-start(bf16[4,2,64,2048]{3,2,1,0:T(8,128)(2,1)} %dynamic-slice_bitcast_fusion.2), channel_id=1, source_target_pairs={{0,2},{2,0},{1,3},{3,1},{4,6},{6,4},{5,7},{7,5},{8,10},{10,8},{9,1... | collective-permute-start | bytes 6291464 | tf_op jit(solution)/shard_map/ppermute | solution.py:410
  452.3 19.4 %collective-permute-start.6 = (bf16[2,64,2048]{2,1,0:T(8,128)(2,1)S(1)}, bf16[2,64,2048]{2,1,0:T(8,128)(2,1)S(1)}, u32[]{:S(2)}, u32[]{:S(2)}) collective-permute-start(bf16[2,64,2048]{2,1,0:T(8,128)(2,1)S(1)} %dynamic-slice_bitcast_fusion.22), channel_id=1, source_target_pairs={{0,4},{1,5},{4,0},{5,1},{2,6},{3,7},{6,2},{7,3},{8,12},{9,13},{12,... | collective-permute-start | bytes 1572872 | tf_op jit(solution)/shard_map/ppermute | solution.py:410
  452.4 54.9 %collective-permute-start.8 = (bf16[2,64,2048]{2,1,0:T(8,128)(2,1)S(1)}, bf16[2,64,2048]{2,1,0:T(8,128)(2,1)S(1)}, u32[]{:S(2)}, u32[]{:S(2)}) collective-permute-start(bf16[2,64,2048]{2,1,0:T(8,128)(2,1)S(1)} %dynamic-slice_bitcast_fusion.19), channel_id=1, source_target_pairs={{0,4},{1,5},{4,0},{5,1},{2,6},{3,7},{6,2},{7,3},{8,12},{9,13},{12,... | collective-permute-start | bytes 1572872 | tf_op jit(solution)/shard_map/ppermute | solution.py:410
  456.9 50.4 %collective-permute-start.9 = (bf16[2,64,2048]{2,1,0:T(8,128)(2,1)S(1)}, bf16[2,64,2048]{2,1,0:T(8,128)(2,1)S(1)}, u32[]{:S(2)}, u32[]{:S(2)}) collective-permute-start(bf16[2,64,2048]{2,1,0:T(8,128)(2,1)S(1)} %get-tuple-element.188), channel_id=1, source_target_pairs={{0,1},{1,0},{4,5},{5,4},{2,3},{3,2},{6,7},{7,6},{8,9},{9,8},{12,13... | collective-permute-start | bytes 1572872 | tf_op jit(solution)/shard_map/ppermute | solution.py:410
  458.2 24.8 %collective-permute-start.7 = (bf16[2,64,2048]{2,1,0:T(8,128)(2,1)S(1)}, bf16[2,64,2048]{2,1,0:T(8,128)(2,1)S(1)}, u32[]{:S(2)}, u32[]{:S(2)}) collective-permute-start(bf16[2,64,2048]{2,1,0:T(8,128)(2,1)S(1)} %get-tuple-element.190), channel_id=1, source_target_pairs={{0,1},{1,0},{4,5},{5,4},{2,3},{3,2},{6,7},{7,6},{8,9},{9,8},{12,13... | collective-permute-start | bytes 1572872 | tf_op jit(solution)/shard_map/ppermute | solution.py:410
  459.2 34.7 %collective-permute-start.10 = (bf16[2,64,2048]{2,1,0:T(8,128)(2,1)S(1)}, bf16[2,64,2048]{2,1,0:T(8,128)(2,1)S(1)}, u32[]{:S(2)}, u32[]{:S(2)}) collective-permute-start(bf16[2,64,2048]{2,1,0:T(8,128)(2,1)S(1)} %get-tuple-element.191), channel_id=1, source_target_pairs={{0,5},{1,4},{4,1},{5,0},{2,7},{3,6},{6,3},{7,2},{8,13},{9,12},{12,... | collective-permute-start | bytes 1572872 | tf_op jit(solution)/shard_map/ppermute | solution.py:410
  471.7 35.7 %collective-permute-start.13 = (bf16[2,64,2048]{2,1,0:T(8,128)(2,1)S(1)}, bf16[2,64,2048]{2,1,0:T(8,128)(2,1)S(1)}, u32[]{:S(2)}, u32[]{:S(2)}) collective-permute-start(bf16[2,64,2048]{2,1,0:T(8,128)(2,1)S(1)} %get-tuple-element.189), channel_id=1, source_target_pairs={{0,5},{1,4},{4,1},{5,0},{2,7},{3,6},{6,3},{7,2},{8,13},{9,12},{12,... | collective-permute-start | bytes 1572872 | tf_op jit(solution)/shard_map/ppermute | solution.py:410
  483.0 75.4 %collective-permute-start.11 = (bf16[4,2,64,2048]{3,2,1,0:T(8,128)(2,1)}, bf16[4,2,64,2048]{3,2,1,0:T(8,128)(2,1)}, u32[]{:S(2)}, u32[]{:S(2)}) collective-permute-start(bf16[4,2,64,2048]{3,2,1,0:T(8,128)(2,1)} %dynamic-slice_bitcast_fusion.1), channel_id=1, source_target_pairs={{0,2},{2,0},{1,3},{3,1},{4,6},{6,4},{5,7},{7,5},{8,10},{10,8},{9,1... | collective-permute-start | bytes 6291464 | tf_op jit(solution)/shard_map/ppermute | solution.py:410
  543.4 21.5 %collective-permute-start.12 = (bf16[4,2,64,2048]{3,2,1,0:T(8,128)(2,1)}, bf16[4,2,64,2048]{3,2,1,0:T(8,128)(2,1)}, u32[]{:S(2)}, u32[]{:S(2)}) collective-permute-start(bf16[4,2,64,2048]{3,2,1,0:T(8,128)(2,1)} %dynamic-slice_bitcast_fusion), channel_id=1, source_target_pairs={{0,2},{2,0},{1,3},{3,1},{4,6},{6,4},{5,7},{7,5},{8,10},{10,8},{9,1... | collective-permute-start | bytes 6291464 | tf_op jit(solution)/shard_map/ppermute | solution.py:410
  563.1 124.3 %collective-permute-start.16 = (bf16[4,64,2048]{2,1,0:T(8,128)(2,1)}, bf16[4,64,2048]{2,1,0:T(8,128)(2,1)}, u32[]{:S(2)}, u32[]{:S(2)}) collective-permute-start(bf16[4,64,2048]{2,1,0:T(8,128)(2,1)} %dynamic-slice_bitcast_fusion.9), channel_id=1, source_target_pairs={{0,4},{1,5},{4,0},{5,1},{2,6},{3,7},{6,2},{7,3},{8,12},{9,13},{12,... | collective-permute-start | bytes 3145736 | tf_op jit(solution)/shard_map/ppermute | solution.py:410
  580.4 66.6 %collective-permute-start.22 = (bf16[640,512]{1,0:T(8,128)(2,1)}, bf16[640,512]{1,0:T(8,128)(2,1)}, u32[]{:S(2)}, u32[]{:S(2)}) collective-permute-start(bf16[640,512]{1,0:T(8,128)(2,1)} %convolution_convert_fusion.13), channel_id=1, source_target_pairs={{0,1},{1,0},{2,3},{3,2},{4,5},{5,4},{6,7},{7,6},{8,9},{9,8},{10,11... | collective-permute-start | bytes 1966088 | tf_op jit(solution)/shard_map/ppermute | solution.py:410
  581.5 13.8 %collective-permute-start.18 = (bf16[64,2048]{1,0:T(8,128)(2,1)S(1)}, bf16[64,2048]{1,0:T(8,128)(2,1)S(1)}, u32[]{:S(2)}, u32[]{:S(2)}) collective-permute-start(bf16[64,2048]{1,0:T(8,128)(2,1)S(1)} %get-tuple-element.185), channel_id=1, source_target_pairs={{0,8},{8,0},{16,24},{24,16},{1,9},{9,1},{17,25},{25,17},{2,10},{10... | collective-permute-start | bytes 786440 | tf_op jit(solution)/shard_map/ppermute | solution.py:410
  581.6 13.8 %collective-permute-start.20 = (bf16[64,2048]{1,0:T(8,128)(2,1)S(1)}, bf16[64,2048]{1,0:T(8,128)(2,1)S(1)}, u32[]{:S(2)}, u32[]{:S(2)}) collective-permute-start(bf16[64,2048]{1,0:T(8,128)(2,1)S(1)} %get-tuple-element.186), channel_id=1, source_target_pairs={{0,24},{8,16},{16,8},{24,0},{1,25},{9,17},{17,9},{25,1},{2,26},{10... | collective-permute-start | bytes 786440 | tf_op jit(solution)/shard_map/ppermute | solution.py:410
  581.9 25.9 %collective-permute-start.19 = (bf16[64,2048]{1,0:T(8,128)(2,1)S(1)}, bf16[64,2048]{1,0:T(8,128)(2,1)S(1)}, u32[]{:S(2)}, u32[]{:S(2)}) collective-permute-start(bf16[64,2048]{1,0:T(8,128)(2,1)S(1)} %get-tuple-element.187), channel_id=1, source_target_pairs={{0,16},{8,24},{16,0},{24,8},{1,17},{9,25},{17,1},{25,9},{2,18},{10... | collective-permute-start | bytes 786440 | tf_op jit(solution)/shard_map/ppermute | solution.py:410
  595.4 45.9 %collective-permute-start.15 = (bf16[4,2,64,512]{3,2,1,0:T(8,128)(2,1)}, bf16[4,2,64,512]{3,2,1,0:T(8,128)(2,1)S(1)}, u32[]{:S(2)}, u32[]{:S(2)}) collective-permute-start(bf16[4,2,64,512]{3,2,1,0:T(8,128)(2,1)} %dynamic-slice_bitcast_fusion.14), channel_id=1, source_target_pairs={{0,2},{2,0},{1,3},{3,1},{4,6},{6,4},{5,7},{7,5},{8,10},{10,8},{9,1... | collective-permute-start | bytes 1572872 | tf_op jit(solution)/shard_map/ppermute | solution.py:410
  595.4 49.6 %collective-permute-start.14 = (bf16[4,2,64,512]{3,2,1,0:T(8,128)(2,1)}, bf16[4,2,64,512]{3,2,1,0:T(8,128)(2,1)S(1)}, u32[]{:S(2)}, u32[]{:S(2)}) collective-permute-start(bf16[4,2,64,512]{3,2,1,0:T(8,128)(2,1)} %dynamic-slice_bitcast_fusion.15), channel_id=1, source_target_pairs={{0,2},{2,0},{1,3},{3,1},{4,6},{6,4},{5,7},{7,5},{8,10},{10,8},{9,1... | collective-permute-start | bytes 1572872 | tf_op jit(solution)/shard_map/ppermute | solution.py:410
  607.8 81.2 %collective-permute-start.17 = (bf16[4,64,2048]{2,1,0:T(8,128)(2,1)}, bf16[4,64,2048]{2,1,0:T(8,128)(2,1)}, u32[]{:S(2)}, u32[]{:S(2)}) collective-permute-start(bf16[4,64,2048]{2,1,0:T(8,128)(2,1)} %get-tuple-element.170), channel_id=1, source_target_pairs={{0,1},{1,0},{4,5},{5,4},{2,3},{3,2},{6,7},{7,6},{8,9},{9,8},{12,13... | collective-permute-start | bytes 3145736 | tf_op jit(solution)/shard_map/ppermute | solution.py:410
  642.0 45.3 %collective-permute-start.24 = (bf16[4,64,2048]{2,1,0:T(8,128)(2,1)}, bf16[4,64,2048]{2,1,0:T(8,128)(2,1)}, u32[]{:S(2)}, u32[]{:S(2)}) collective-permute-start(bf16[4,64,2048]{2,1,0:T(8,128)(2,1)} %get-tuple-element.171), channel_id=1, source_target_pairs={{0,5},{1,4},{4,1},{5,0},{2,7},{3,6},{6,3},{7,2},{8,13},{9,12},{12,... | collective-permute-start | bytes 3145736 | tf_op jit(solution)/shard_map/ppermute | solution.py:410
  644.9 32.0 %collective-permute-start.27 = (bf16[4,64,512]{2,1,0:T(8,128)(2,1)}, bf16[4,64,512]{2,1,0:T(8,128)(2,1)S(1)}, u32[]{:S(2)}, u32[]{:S(2)}) collective-permute-start(bf16[4,64,512]{2,1,0:T(8,128)(2,1)} %get-tuple-element.195), channel_id=1, source_target_pairs={{0,1},{1,0},{4,5},{5,4},{2,3},{3,2},{6,7},{7,6},{8,9},{9,8},{12,13... | collective-permute-start | bytes 786440 | tf_op jit(solution)/shard_map/ppermute | solution.py:410
  647.0 31.0 %collective-permute-start.28 = (bf16[4,64,512]{2,1,0:T(8,128)(2,1)}, bf16[4,64,512]{2,1,0:T(8,128)(2,1)S(1)}, u32[]{:S(2)}, u32[]{:S(2)}) collective-permute-start(bf16[4,64,512]{2,1,0:T(8,128)(2,1)} %get-tuple-element.196), channel_id=1, source_target_pairs={{0,5},{1,4},{4,1},{5,0},{2,7},{3,6},{6,3},{7,2},{8,13},{9,12},{12,... | collective-permute-start | bytes 786440 | tf_op jit(solution)/shard_map/ppermute | solution.py:410
  677.0 16.6 %collective-permute-start.21 = (bf16[4,2,64,1536]{3,2,1,0:T(8,128)(2,1)S(1)}, bf16[4,2,64,1536]{3,2,1,0:T(8,128)(2,1)S(1)}, u32[]{:S(2)}, u32[]{:S(2)}) collective-permute-start(bf16[4,2,64,1536]{3,2,1,0:T(8,128)(2,1)S(1)} %dynamic-slice_bitcast_fusion.4), channel_id=1, source_target_pairs={{0,2},{2,0},{1,3},{3,1},{4,6},{6,4},{5,7},{7,5},{8,10},{10,8},{9,1... | collective-permute-start | bytes 4718600 | tf_op jit(solution)/shard_map/ppermute | solution.py:410
  678.0 8.1 collective-permute-start.26
  686.1 58.2 %collective-permute-start.30 = (bf16[640,1024]{1,0:T(8,128)(2,1)}, bf16[640,1024]{1,0:T(8,128)(2,1)}, u32[]{:S(2)}, u32[]{:S(2)}) collective-permute-start(bf16[640,1024]{1,0:T(8,128)(2,1)} %dynamic-slice_convert_fusion.1), channel_id=1, source_target_pairs={{0,1},{1,0},{2,3},{3,2},{4,5},{5,4},{6,7},{7,6},{8,9},{9,8},{10,11... | collective-permute-start | bytes 3932168 | tf_op jit(solution)/shard_map/ppermute | solution.py:410
  687.4 50.4 %collective-permute-start.37 = (bf16[64,512]{1,0:T(8,128)(2,1)S(1)}, bf16[64,512]{1,0:T(8,128)(2,1)S(1)}, u32[]{:S(2)}, u32[]{:S(2)}) collective-permute-start(bf16[64,512]{1,0:T(8,128)(2,1)S(1)} %get-tuple-element.197), channel_id=1, source_target_pairs={{0,8},{8,0},{16,24},{24,16},{1,9},{9,1},{17,25},{25,17},{2,10},{10... | collective-permute-start | bytes 196616 | tf_op jit(solution)/shard_map/ppermute | solution.py:410
  687.5 50.3 %collective-permute-start.39 = (bf16[64,512]{1,0:T(8,128)(2,1)S(1)}, bf16[64,512]{1,0:T(8,128)(2,1)S(1)}, u32[]{:S(2)}, u32[]{:S(2)}) collective-permute-start(bf16[64,512]{1,0:T(8,128)(2,1)S(1)} %get-tuple-element.198), channel_id=1, source_target_pairs={{0,24},{8,16},{16,8},{24,0},{1,25},{9,17},{17,9},{25,1},{2,26},{10... | collective-permute-start | bytes 196616 | tf_op jit(solution)/shard_map/ppermute | solution.py:410
  689.0 48.8 %collective-permute-start.38 = (bf16[64,512]{1,0:T(8,128)(2,1)S(1)}, bf16[64,512]{1,0:T(8,128)(2,1)S(1)}, u32[]{:S(2)}, u32[]{:S(2)}) collective-permute-start(bf16[64,512]{1,0:T(8,128)(2,1)S(1)} %get-tuple-element.199), channel_id=1, source_target_pairs={{0,16},{8,24},{16,0},{24,8},{1,17},{9,25},{17,1},{25,9},{2,18},{10... | collective-permute-start | bytes 196616 | tf_op jit(solution)/shard_map/ppermute | solution.py:410
  733.7 33.8 %collective-permute-start.29 = (bf16[4,2,64,1536]{3,2,0,1:T(8,128)(2,1)S(1)}, bf16[4,2,64,1536]{3,2,0,1:T(8,128)(2,1)S(1)}, u32[]{:S(2)}, u32[]{:S(2)}) collective-permute-start(bf16[4,2,64,1536]{3,2,0,1:T(8,128)(2,1)S(1)} %bitcast.311), channel_id=1, source_target_pairs={{0,2},{2,0},{1,3},{3,1},{4,6},{6,4},{5,7},{7,5},{8,10},{10,8},{9,1... | collective-permute-start | bytes 4718600 | tf_op jit(solution)/shard_map/ppermute | solution.py:410
  739.5 28.0 %collective-permute-start.25 = (bf16[4,64,1536]{2,1,0:T(8,128)(2,1)S(1)}, bf16[4,64,1536]{2,1,0:T(8,128)(2,1)S(1)}, u32[]{:S(2)}, u32[]{:S(2)}) collective-permute-start(bf16[4,64,1536]{2,1,0:T(8,128)(2,1)S(1)} %get-tuple-element.177), channel_id=1, source_target_pairs={{0,5},{1,4},{4,1},{5,0},{2,7},{3,6},{6,3},{7,2},{8,13},{9,12},{12,... | collective-permute-start | bytes 2359304 | tf_op jit(solution)/shard_map/ppermute | solution.py:410
  741.6 11.7 %collective-permute-start.40 = (bf16[64,2048]{1,0:T(8,128)(2,1)S(1)}, bf16[64,2048]{1,0:T(8,128)(2,1)S(1)}, u32[]{:S(2)}, u32[]{:S(2)}) collective-permute-start(bf16[64,2048]{1,0:T(8,128)(2,1)S(1)} %get-tuple-element.182), channel_id=1, source_target_pairs={{0,8},{8,0},{16,24},{24,16},{1,9},{9,1},{17,25},{25,17},{2,10},{10... | collective-permute-start | bytes 786440 | tf_op jit(solution)/shard_map/ppermute | solution.py:410
  742.6 14.5 %collective-permute-start.42 = (bf16[64,2048]{1,0:T(8,128)(2,1)S(1)}, bf16[64,2048]{1,0:T(8,128)(2,1)S(1)}, u32[]{:S(2)}, u32[]{:S(2)}) collective-permute-start(bf16[64,2048]{1,0:T(8,128)(2,1)S(1)} %get-tuple-element.183), channel_id=1, source_target_pairs={{0,24},{8,16},{16,8},{24,0},{1,25},{9,17},{17,9},{25,1},{2,26},{10... | collective-permute-start | bytes 786440 | tf_op jit(solution)/shard_map/ppermute | solution.py:410
  744.3 22.3 %collective-permute-start.41 = (bf16[64,2048]{1,0:T(8,128)(2,1)S(1)}, bf16[64,2048]{1,0:T(8,128)(2,1)S(1)}, u32[]{:S(2)}, u32[]{:S(2)}) collective-permute-start(bf16[64,2048]{1,0:T(8,128)(2,1)S(1)} %get-tuple-element.184), channel_id=1, source_target_pairs={{0,16},{8,24},{16,0},{24,8},{1,17},{9,25},{17,1},{25,9},{2,18},{10... | collective-permute-start | bytes 786440 | tf_op jit(solution)/shard_map/ppermute | solution.py:410
  753.3 57.5 %collective-permute-start.33 = (bf16[4,64,1536]{2,1,0:T(8,128)(2,1)}, bf16[4,64,1536]{2,1,0:T(8,128)(2,1)}, u32[]{:S(2)}, u32[]{:S(2)}) collective-permute-start(bf16[4,64,1536]{2,1,0:T(8,128)(2,1)} %get-tuple-element.176), channel_id=1, source_target_pairs={{0,1},{1,0},{4,5},{5,4},{2,3},{3,2},{6,7},{7,6},{8,9},{9,8},{12,13... | collective-permute-start | bytes 2359304 | tf_op jit(solution)/shard_map/ppermute | solution.py:410
  793.4 5.0 collective-permute-start.45
  797.0 17.0 %collective-permute-start.32 = (bf16[4,64,1536]{2,1,0:T(8,128)(2,1)S(1)}, bf16[4,64,1536]{2,1,0:T(8,128)(2,1)}, u32[]{:S(2)}, u32[]{:S(2)}) collective-permute-start(bf16[4,64,1536]{2,1,0:T(8,128)(2,1)S(1)} %dynamic-slice_bitcast_fusion.12), channel_id=1, source_target_pairs={{0,4},{1,5},{4,0},{5,1},{2,6},{3,7},{6,2},{7,3},{8,12},{9,13},{12,... | collective-permute-start | bytes 2359304 | tf_op jit(solution)/shard_map/ppermute | solution.py:410
  799.9 6.4 collective-permute-start.48
  801.6 4.9 collective-permute-start.47
  801.6 5.0 collective-permute-start.46
  809.7 31.5 %collective-permute-start.31 = (bf16[640,1024]{1,0:T(8,128)(2,1)}, bf16[640,1024]{1,0:T(8,128)(2,1)}, u32[]{:S(2)}, u32[]{:S(2)}) collective-permute-start(bf16[640,1024]{1,0:T(8,128)(2,1)} %fusion.47), channel_id=1, source_target_pairs={{0,1},{1,0},{2,3},{3,2},{4,5},{5,4},{6,7},{7,6},{8,9},{9,8},{10,11... | collective-permute-start | bytes 3932168 | tf_op jit(solution)/shard_map/ppermute | solution.py:410
  816.3 9.9 %collective-permute-start.34 = (bf16[64,1536]{1,0:T(8,128)(2,1)S(1)}, bf16[64,1536]{1,0:T(8,128)(2,1)S(1)}, u32[]{:S(2)}, u32[]{:S(2)}) collective-permute-start(bf16[64,1536]{1,0:T(8,128)(2,1)S(1)} %get-tuple-element.192), channel_id=1, source_target_pairs={{0,8},{8,0},{16,24},{24,16},{1,9},{9,1},{17,25},{25,17},{2,10},{10... | collective-permute-start | bytes 589832 | tf_op jit(solution)/shard_map/ppermute | solution.py:410
  816.4 11.3 %collective-permute-start.36 = (bf16[64,1536]{1,0:T(8,128)(2,1)S(1)}, bf16[64,1536]{1,0:T(8,128)(2,1)S(1)}, u32[]{:S(2)}, u32[]{:S(2)}) collective-permute-start(bf16[64,1536]{1,0:T(8,128)(2,1)S(1)} %get-tuple-element.193), channel_id=1, source_target_pairs={{0,24},{8,16},{16,8},{24,0},{1,25},{9,17},{17,9},{25,1},{2,26},{10... | collective-permute-start | bytes 589832 | tf_op jit(solution)/shard_map/ppermute | solution.py:410
  818.1 15.9 %collective-permute-start.35 = (bf16[64,1536]{1,0:T(8,128)(2,1)S(1)}, bf16[64,1536]{1,0:T(8,128)(2,1)S(1)}, u32[]{:S(2)}, u32[]{:S(2)}) collective-permute-start(bf16[64,1536]{1,0:T(8,128)(2,1)S(1)} %get-tuple-element.194), channel_id=1, source_target_pairs={{0,16},{8,24},{16,0},{24,8},{1,17},{9,25},{17,1},{25,9},{2,18},{10... | collective-permute-start | bytes 589832 | tf_op jit(solution)/shard_map/ppermute | solution.py:410
  (110 other events, 1575.4 us)
Sparse Core Ops, SparseCore 0:
  129.6 91.6 all-gather.1

commit v8 on v7

--- a/solution.py
+++ b/solution.py
@@ -255,13 +255,9 @@
     pl.semaphore_wait(barrier, len(partners))
 
     half = depth // 2
-    everything = pl.ds(0, depth)
+    first = pl.ds(z // half * half, half)
+    second = pl.ds(half - z // half * half, half)
     started = []
-
-    def spans(number):
-        if number % 3:
-            return everything, None
-        return pl.ds(z // half * half, half), pl.ds(half - z // half * half, half)
 
     def copy(source, target, partner):
         slot = len(started)
@@ -304,33 +300,27 @@
         crossed.append(over(number, t, t, at_y, span, {"core": 1 - core}))
 
     def plane_start(number, keep, sent):
-        first, second = spans(number)
         keep.wait()
-        for k in range(1, half if second is not None else depth):
+        for k in range(1, half):
             sent[k - 1].wait_recv()
         over_x = [over(number, 0, k, y, first, {"tp": apart(x, k)}) for k in range(1, tp)]
-        last = [(over(number, 0, 0, y, first, {"y": 1 - y}), 0, 1 - y, first)]
-        to_core(number, 0, y, first)
-        if second is None:
-            return over_x, None, last
         for k in range(half, depth):
             sent[k - 1].wait_recv()
         over_y = over(number, 0, 0, y, second, {"y": 1 - y})
+        last = [(over(number, 0, 0, y, first, {"y": 1 - y}), 0, 1 - y, first)]
         for k in range(1, tp):
             made = over(number, 0, k, y, second, {"tp": apart(x, k)})
             last.append((made, k, y, second))
+        to_core(number, 0, y, first)
         to_core(number, 0, y, second)
         return over_x, over_y, last
 
     def plane_turn(number, over_x, over_y, last):
-        first, second = spans(number)
         for k in range(1, tp):
             over_x[k - 1].wait_recv()
             made = over(number, k, k, y, first, {"y": 1 - y})
             last.append((made, k, 1 - y, first))
             to_core(number, k, y, first)
-        if second is None:
-            return last
         over_y.wait_recv()
         for k in range(1, tp):
             made = over(number, 0, k, 1 - y, second, {"tp": apart(x, k)})
@@ -469,6 +459,15 @@
     return [value for piece in pieces for value in piece]
 
 
+def over_y(part):
+    y = lax.axis_index("y")
+    return block_at(part, 1, y), send(block_at(part, 1, 1 - y), "y", 1)
+
+
+def over_tp(pairs):
+    return [send(total([list(pair)], [[]]), "tp", t + 1) for t, pair in enumerate(pairs)]
+
+
 def total(straight, across):
     sums = []
     for near, far in zip(straight, across):
@@ -478,11 +477,12 @@
     return jnp.concatenate(sums, axis=0)
 
 
-def scatter_z(part):
+def scatter_z(part, *late):
     z = lax.axis_index("z")
     made = block_at(part, 0, z).astype(f32)
     for k in range(1, part.shape[0]):
-        made = made + send(block_at(part, 0, z ^ k), "z", k).astype(f32)
+        came = send(block_at(part, 0, z ^ k), "z", k)
+        made = made + (after(came, *late) if late else came).astype(f32)
     return made
 
 
@@ -564,25 +564,19 @@
     whole_out = [[] for _ in halves]
     share_out = [[] for _ in halves]
     saved = {}
-    def whole_forward(t, *others):
-        for n in range(whole):
-            qkv = after(whole_qkv[t][n * tree_len : (n + 1) * tree_len], *others)
+    for n in range(whole):
+        for t in halves:
+            qkv = whole_qkv[t][n * tree_len : (n + 1) * tree_len]
             out, lse = attention_forward(qkv, *whole_tables[n])
             saved[n, t] = (qkv, out, lse)
             whole_out[t].append(out)
-
-    whole_forward(0)
     share_calls = [after(call, *whole_out[0]) for call in share_calls]
-    made = []
     for n in range(share_count):
         out, lse = attention_forward(share_calls[n], *share_tables[n])
         saved[n] = (share_calls[n], out, lse)
-        made.append(out)
         parts = exchange_tp([share_rows(out, k) for k in halves])
         for t in halves:
             share_out[t].append(parts[t])
-    for t in range(1, tp):
-        whole_forward(t, *made)
     attended = [jnp.concatenate(whole_out[t] + share_out[t], axis=0) for t in halves]
     cotangent = after(cotangent[:, 0], *attended)
     cotangent_came = [send(piece, "tp", n % (tp - 1) + 1) for n, piece in enumerate(outgoing(cotangent))]
@@ -597,12 +591,12 @@
         values, bent = lax.optimization_barrier((values.astype(bf16), bent.astype(bf16)))
         hidden.append(values)
         slope.append(bent)
-    branch_f = sum(dot_nt(hidden[t], full_down[t]) for t in halves)
-    normed_shared = []
+    crossing = []
     for n in range(share_count):
         start = split + n * own_rows
-        near = after(normed[start : start + own_rows], branch_f)
-        normed_shared.append(in_place_order(exchange_tp([near] * tp)))
+        near = after(normed[start : start + own_rows], hidden[0])
+        crossing.append(exchange_tp([near] * tp))
+    branch_f = sum(dot_nt(hidden[t], full_down[t]) for t in halves)
     out = (residual + norm_forward(branch_f, norm_gains[3], norm_biases[3])).astype(bf16)
     out_rows = rows_back(out)
 
@@ -628,15 +622,14 @@
 
     grad_branch_a, sums_1 = norm_backward(branch_a, norm_gains[1], grad_residual)
     grad_branch_a = after(grad_branch_a.astype(bf16), *core_up, *across_down[1])
-    z_down = scatter_z(after(total(straight_down, across_down), grad_branch_a))
-    straight_up, across_up = scatter_plane(core_up)
+    up_y = {t: over_y(core_up[t]) for t in reversed(halves)}
+    up_x = over_tp([up_y[t] for t in halves[1:]])
     share_grad = [dot_nn(grad_branch_a[split:], w).astype(bf16) for w in full_out]
     whole_grad = [dot_nn(grad_branch_a[:split], w).astype(bf16) for w in full_out] if whole else []
     share_do = []
     for n in range(share_count):
         cut = slice(n * own_rows, (n + 1) * own_rows)
         share_do.append(in_place_order(exchange_tp([part[cut] for part in share_grad])))
-    core_out = [scatter_core(dot_tn(grad_branch_a, part).astype(bf16)) for part in attended]
     grad_qkv = [[] for _ in halves]
 
     def whole_backward(t, *others):
@@ -649,39 +642,49 @@
 
     made = []
     dw_qkv = [None] * tp
+    down = total(straight_down, across_down)
     for t in range(1, tp):
-        made += whole_backward(t, z_down)
+        made += whole_backward(t)
         if whole:
             dw_qkv[t] = dot_tn(normed_whole, jnp.concatenate(grad_qkv[t], axis=0)).astype(bf16)
         else:
             dw_qkv[t] = jnp.zeros(full_qkv[t].shape, bf16)
+    z_down = scatter_z(down, *made)
     core_qkv = [None] + [scatter_core(part) for part in dw_qkv[1:]]
+    late_grad = after(grad_branch_a, *made)
+    core_out = [scatter_core(dot_tn(late_grad, part).astype(bf16)) for part in attended]
     grad_shared = []
     own_part = []
+    early_y = [up_y[t][1] for t in halves[1:]]
     for n in range(share_count):
         qkv, att, lse = saved[n]
-        do = after(share_do[n], *made)
+        do = after(share_do[n], *made, *early_y)
         dx = attention_backward(qkv, do, att, lse, *share_tables[n])
         made = [dx]
         grad_shared.append(dx)
-    whole_backward(0, *core_out, *flat(straight_up), *core_qkv[1:], *made)
+    whole_backward(0, *core_out, *up_x, up_y[0][1], *core_qkv[1:], *made)
     for n in range(share_count):
         part = dot_nt(grad_shared[n], full_qkv[0])
         pieces = exchange_tp([share_rows(part, 0)] + [share_rows(part, k).astype(bf16) for k in halves[1:]])
         own_part.append(sum([piece.astype(f32) for piece in pieces[1:]], pieces[0]))
-    straight_out, across_out = scatter_plane(core_out)
-    ready = flat(across_up)
+    qkv_y = {t: over_y(core_qkv[t]) for t in halves[1:]}
+    out_y = {t: over_y(core_out[t]) for t in reversed(halves)}
+    ready = [qkv_y[t][1] for t in halves[1:]]
     owned = [after(rows, *ready) for rows in grad_shared]
-    z_out = scatter_z(total(straight_out, across_out))
+    qkv_x = over_tp([qkv_y[t] for t in halves[1:]])
+    out_x = over_tp([out_y[t] for t in halves[1:]])
+    near = in_place_order
+    normed_shared = [near([pieces[0]] + [after(piece, *made) for piece in pieces[1:]]) for pieces in crossing]
     owned = [dot_tn(rows, grad) for rows, grad in zip(normed_shared, owned)]
     if whole:
         owned.append(dot_tn(normed_whole, jnp.concatenate(grad_qkv[0], axis=0)))
     dw_qkv[0] = sum(owned).astype(bf16)
     core_qkv[0] = scatter_core(dw_qkv[0])
-    z_up = scatter_z(after(total(straight_up, across_up), dw_qkv[0]))
-    straight_qkv, across_qkv = scatter_plane(core_qkv)
-    z_qkv = scatter_z(total(straight_qkv, across_qkv))
-    ready = [dw_qkv[0], *flat(across_qkv), *flat(straight_out), *flat(across_out)]
+    z_up_part = after(total([[*up_y[0], *up_x]], [[]]), dw_qkv[0])
+    z_out_part = after(total([[*out_y[0], *out_x]], [[]]), dw_qkv[0])
+    qkv_y[0] = over_y(core_qkv[0])
+    z_qkv = scatter_z(total([[*qkv_y[0], *qkv_x]], [[]]))
+    ready = [dw_qkv[0]]
     grad_normed = list(own_part)
     if whole:
         trees = [after(jnp.concatenate(grad_qkv[t], axis=0), *ready) for t in halves]
@@ -691,6 +694,8 @@
     grad_part, sums_0 = norm_backward(x, norm_gains[0], grad_normed)
     grad_x = grad_residual + grad_part
     input_rows = rows_back(grad_x)
+    z_up = scatter_z(z_up_part, grad_x)
+    z_out = scatter_z(z_out_part, grad_x)
     sums = after(jnp.concatenate([sums_0, sums_1, sums_2, sums_3]), grad_x)
     sums = sum_everywhere(sums).reshape(4, 2, width)
     return (

time: 865 us -> 860 us (level)
  Pallas kernels: 264 us -> 253 us
  other arithmetic: 88.9 us -> 98.4 us
    pallas_call x1, Pallas kernels: 119 us -> 108 us  [gather_weights(): pl.pallas_call(functools.partial(gather_kernel, chunks, len(shards), move...]
    dynamic_slice x2 -> x12, local copies, waits for them, and re-layouts: 0.32 us -> 9.87 us  [block_at(): return lax.dynamic_index_in_dim(values, index, axis, keepdims=False)]
    squeeze x23 -> x17, local copies, waits for them, and re-layouts: 16.1 us -> 7.41 us  [block_at(): return lax.dynamic_index_in_dim(values, index, axis, keepdims=False)]
    unnamed x220 -> x224, local copies, waits for them, and re-layouts: 20.2 us -> 20.6 us
  transfers between devices with their start and end apart: 51 -> 51, of which waited for: 20 -> 11; matrix products, arithmetic and copies ran while one was open for 36% -> 43% of each run, Pallas kernels for 17% -> 17%
where the time goes in v8:
time: 860 us; the launch traced here: 856 us
  matrix products  259 us (30%)
  Pallas kernels  253 us (29%)
  waiting for transfers between devices  125 us (15%)
  other arithmetic  98.4 us (11%)
  local copies, waits for them, and re-layouts  53 us (6%)
  starting transfers between devices  51.5 us (6%)
  between operations  16.4 us (2%)
    ppermute x50, waiting for transfers between devices, send(): return lax.ppermute(values, axes, [(s, s ^ distance) for s in range(count)])  125 us
    pallas_call x1, Pallas kernels, gather_weights(): pl.pallas_call(functools.partial(gather_kernel, chunks, len(shards), move...  108 us
    dot_general x12, matrix products, dot_nn(): lax.dot_general(a, b, (((1,), (0,)), ((), ())), preferred_element_type=f32)  98.2 us
    dot_general x9, matrix products, dot_nt(): lax.dot_general(a, b, (((1,), (1,)), ((), ())), preferred_element_type=f32)  88.3 us
    pallas_call x3, Pallas kernels, attention_backward(): pl.pallas_call(attention_backward_kernel, name='attention_backward', out_...  80 us
    dot_general x9, matrix products, dot_tn(): lax.dot_general(a, b, (((0,), (0,)), ((), ())), preferred_element_type=f32)  72.4 us
    pallas_call x3, Pallas kernels, attention_forward(): pl.pallas_call(attention_forward_kernel, name='attention_forward', out_sh...  64.7 us
    ppermute x50, starting transfers between devices, send(): return lax.ppermute(values, axes, [(s, s ^ distance) for s in range(count)])  51.5 us
  transfers between devices with their start and end apart: 51, of which 11 were waited for; matrix products, arithmetic and copies ran while one was open for 43% of the time, Pallas kernels for 17%

profile of v8, /device:TPU:0, one launch (start us, length us, event | category | flops | bytes accessed | tf_op | source)
XLA Modules:
  0.0 856.0 jit_solution(4319681854761807956)
XLA Ops:
  11.6 108.2 %gather_weights.1 = (bf16[4,2,2,64,1536]{4,3,2,1,0:T(8,128)(2,1)}, bf16[4,2,2,64,1536]{4,3,2,1,0:T(8,128)(2,1)}, bf16[4,2,2,64,512]{4,3,2,1,0:T(8,128)(2,1)}, bf...) custom-call(bf16[64,1536]{1,0:T(8,128)(2,1)} %bitcast.334, ...), custom_call_target="tpu_custom_call" | custom-call | bytes 33554432 | tf_op jit(solution)/shard_map/gather_weights/pallas_call | solution.py:374
  127.8 3.5 convolution_convert_fusion.8
  131.9 9.0 %convolution_convert_fusion.q_ref.k_ref.v_ref = bf16[1280,1536]{1,0:T(8,128)(2,1)} fusion(bf16[1024,1536]{1,0:T(8,128)(2,1)} %bitcast.371, bf16[1920,1024]{1,0:T(8,128)(2,1)} %copy-done.27), kind=kOutput, calls=%fused_computation.51 | convolution fusion | flops 4028497920 | bytes 9699328 | tf_op jit(solution)/shard_map/dot_general | solution.py:23
  140.9 5.7 convolution_convert_fusion.1.q_ref.k_ref.v_ref
  152.4 21.5 %attention_forward.5 = (bf16[1280,512]{1,0:T(8,128)(2,1)S(1)}, f32[4,8,1280]{2,1,0:T(8,128)S(1)}) custom-call(bf16[1280,1536]{1,0:T(8,128)(2,1)S(1)} %copy-done.12, bf16[1280,1536]{1,0:T(8,128)(2,1)S(1)} %copy-done.12, bf16[1280,1536]{1,0:T(8,128)(2,1)S(1)} %copy-done.12, s32[1280,8]{1,0:T(8,128)S(1)} %pad.14.clone.col_ref, s32[8,1280]{1,0:T(8,128)S(1)} %pad.15.row_ref), custom_call_target="tpu_custom_call" | custom-call | flops 8053063680 | bytes 5898240 | tf_op jit(solution)/shard_map/attention_forward/pallas_call | solution.py:80
  174.0 21.7 %attention_forward.3 = (bf16[1280,512]{1,0:T(8,128)(2,1)S(1)}, f32[4,8,1280]{2,1,0:T(8,128)S(1)}) custom-call(bf16[1280,1536]{1,0:T(8,128)(2,1)S(1)} %copy-done.10, bf16[1280,1536]{1,0:T(8,128)(2,1)S(1)} %copy-done.10, bf16[1280,1536]{1,0:T(8,128)(2,1)S(1)} %copy-done.10, s32[1280,8]{1,0:T(8,128)S(1)} %pad.14.clone.col_ref, s32[8,1280]{1,0:T(8,128)S(1)} %pad.15.row_ref), custom_call_target="tpu_custom_call" | custom-call | flops 8053063680 | bytes 5898240 | tf_op jit(solution)/shard_map/attention_forward/pallas_call | solution.py:80
  195.7 4.6 broadcast_select_fusion.3
  200.6 21.5 %attention_forward.4 = (bf16[1280,512]{1,0:T(8,128)(2,1)S(1)}, f32[4,8,1280]{2,1,0:T(8,128)S(1)}) custom-call(bf16[1280,1536]{1,0:T(8,128)(2,1)S(1)} %pad_maximum_fusion.2.q_ref.k_ref.v_ref, bf16[1280,1536]{1,0:T(8,128)(2,1)S(1)} %pad_maximum_fusion.2.q_ref.k_ref.v_ref, bf16[1280,1536]{1,0:T(8,128)(2,1)S(1)} %pad_maximum_fusion.2.q_ref.k_ref.v_ref, ...), custom_call_target="tpu_custom_call" | custom-call | flops 8053063680 | bytes 5898240 | tf_op jit(solution)/shard_map/attention_forward/pallas_call | solution.py:80
  226.4 12.9 %collective-permute-done.1 = bf16[640,512]{1,0:T(8,128)(2,1)S(1)} collective-permute-done((bf16[640,512]{1,0:T(8,128)(2,1)S(1)}, bf16[640,512]{1,0:T(8,128)(2,1)S(1)}, u32[]{:S(2)}, u32[]{:S(2)}) %collective-permute-start.1) | collective-permute-done | bytes 655392 | tf_op jit(solution)/shard_map/ppermute | solution.py:400
  256.5 20.7 %add_convert_fusion.1 = (bf16[1920,2048]{1,0:T(8,128)(2,1)}, bf16[1920,2048]{1,0:T(8,128)(2,1)}) fusion(bf16[1920,1024]{1,0:T(8,128)(2,1)S(1)} %add_convert_fusion.3, bf16[1024,2048]{1,0:T(8,128)(2,1)} %bitcast.367), kind=kOutput, calls=%fused_computation.6 | convolution fusion | flops 8112046080 | bytes 23855104 | tf_op jit(solution)/shard_map/dot_general | solution.py:23
  277.3 16.9 %add_convert_fusion = (bf16[1920,2048]{1,0:T(8,128)(2,1)}, bf16[1920,2048]{1,0:T(8,128)(2,1)}) fusion(bf16[1920,1024]{1,0:T(8,128)(2,1)S(1)} %add_convert_fusion.3, bf16[1024,2048]{1,0:T(8,128)(2,1)S(1)} %bitcast.369), kind=kOutput, calls=%fused_computation.2 | convolution fusion | flops 8112046080 | bytes 23855104 | tf_op jit(solution)/shard_map/dot_general | solution.py:23
  298.6 15.7 %fusion.57 = f32[1920,1024]{1,0:T(8,128)} fusion(bf16[1920,2048]{1,0:T(8,128)(2,1)} %get-tuple-element.70, pred[]{:T(512)S(6)} %eq.30, bf16[2048,2048]{1,0:T(8,128)(2,1)} %all-gather.2.cloned.1.call-done), kind=kOutput, calls=%fused_computation.175 | convolution fusion | flops 8055160832 | bytes 24117248 | tf_op jit(solution)/shard_map/dot_general | solution.py:27
  314.3 15.3 %fusion.96 = (f32[1920]{0:T(1024)S(1)}, f32[1920,1024]{1,0:T(8,128)}) fusion(f32[1920,1024]{1,0:T(8,128)} %fusion.57, bf16[1920,2048]{1,0:T(8,128)(2,1)} %get-tuple-element.73, pred[]{:T(512)S(6)} %eq.31, bf16[2048,2048]{1,0:T(8,128)(2,1)S(1)} %copy-done.89), kind=kOutput, calls=%fused_computation.297 | convolution fusion | flops 8059090944 | bytes 31989248 | tf_op jit(solution)/shard_map/dot_general | solution.py:27
  329.6 4.3 multiply_reduce_fusion.4
  335.1 4.9 fusion.25
  340.0 4.7 fusion.23
  344.7 14.2 %convolution_convert_fusion.5 = bf16[1024,2048]{1,0:T(8,128)(2,1)S(1)} fusion(bf16[1920,1024]{1,0:T(8,128)(2,1)} %get-tuple-element.168, bf16[1920,2048]{1,0:T(8,128)(2,1)} %get-tuple-element.70), kind=kOutput, calls=%fused_computation.79 | convolution fusion | flops 8055160832 | bytes 15990784 | tf_op jit(solution)/shard_map/dot_general | solution.py:31
  358.9 13.0 %convolution_convert_fusion.4 = bf16[1024,2048]{1,0:T(8,128)(2,1)S(1)} fusion(bf16[1920,1024]{1,0:T(8,128)(2,1)S(1)} %copy-done.36, bf16[1920,2048]{1,0:T(8,128)(2,1)} %get-tuple-element.73), kind=kOutput, calls=%fused_computation.78 | convolution fusion | flops 8055160832 | bytes 15990784 | tf_op jit(solution)/shard_map/dot_general | solution.py:31
  378.1 14.5 %multiply_convert_fusion = bf16[1920,2048]{1,0:T(8,128)(2,1)} fusion(bf16[1920,2048]{1,0:T(8,128)(2,1)} %get-tuple-element.78, bf16[1920,1024]{1,0:T(8,128)(2,1)S(1)} %copy-done.37, pred[]{:T(512)S(6)} %eq.31, bf16[2048,2048]{1,0:T(8,128)(2,1)} %all-gather.2.cloned.1.call-done), kind=kOutput, calls=%fused_computation | convolution fusion | flops 8066957312 | bytes 28049408 | tf_op jit(solution)/shard_map/dot_general | solution.py:23
  392.6 16.7 %multiply_convert_fusion.1 = bf16[1920,2048]{1,0:T(8,128)(2,1)} fusion(bf16[1920,2048]{1,0:T(8,128)(2,1)} %get-tuple-element.75, bf16[1920,1024]{1,0:T(8,128)(2,1)} %get-tuple-element.168, pred[]{:T(512)S(6)} %eq.30, bf16[2048,2048]{1,0:T(8,128)(2,1)} %all-gather.2.cloned.1.call-done), kind=kOutput, calls=%fused_computation.1 | convolution fusion | flops 8066957312 | bytes 28049408 | tf_op jit(solution)/shard_map/dot_general | solution.py:23
  414.5 3.1 fusion.28
  421.5 9.5 %convolution_convert_fusion.3 = bf16[1024,2048]{1,0:T(8,128)(2,1)S(1)} fusion(bf16[1920,1024]{1,0:T(8,128)(2,1)S(1)} %copy-done.39, bf16[1920,2048]{1,0:T(8,128)(2,1)S(1)} %bitcast.382), kind=kOutput, calls=%fused_computation.77 | convolution fusion | flops 8055160832 | bytes 15990784 | tf_op jit(solution)/shard_map/dot_general | solution.py:31
  440.2 6.7 collective-permute-done.10
  447.8 10.4 %collective-permute-done.7 = bf16[2,64,2048]{2,1,0:T(8,128)(2,1)S(1)} collective-permute-done((bf16[2,64,2048]{2,1,0:T(8,128)(2,1)S(1)}, bf16[2,64,2048]{2,1,0:T(8,128)(2,1)S(1)}, u32[]{:S(2)}, u32[]{:S(2)}) %collective-permute-start.7) | collective-permute-done | bytes 524320 | tf_op jit(solution)/shard_map/ppermute | solution.py:400
  459.1 13.6 %convolution_convert_fusion.2 = bf16[1024,2048]{1,0:T(8,128)(2,1)} fusion(bf16[1920,1024]{1,0:T(8,128)(2,1)S(1)} %copy-done.39, bf16[1920,2048]{1,0:T(8,128)(2,1)} %multiply_convert_fusion), kind=kOutput, calls=%fused_computation.76 | convolution fusion | flops 8055160832 | bytes 15990784 | tf_op jit(solution)/shard_map/dot_general | solution.py:31
  472.7 6.4 collective-permute-done.9
  479.4 12.8 %fusion.98 = f32[1920,1024]{1,0:T(8,128)} fusion(bf16[1920,2048]{1,0:T(8,128)(2,1)} %multiply_convert_fusion, bf16[1024,2048]{1,0:T(8,128)(2,1)S(1)} %bitcast.370), kind=kOutput, calls=%fused_computation.299 | convolution fusion | flops 8053063680 | bytes 19922944 | tf_op jit(solution)/shard_map/dot_general | solution.py:27
  492.2 18.4 %multiply_reduce_fusion = (f32[1024]{0:T(1024)}, f32[1920]{0:T(1024)S(1)}, f32[1920]{0:T(1024)S(1)}, f32[1024]{0:T(1024)}, f32[1920,1024]{1,0:T(8,128)}) fusion(f32[1920,1024]{1,0:T(8,128)S(1)} %bitcast.309, f32[1920]{0:T(1024)S(1)} %copy-done.69, f32[1920]{0:T(1024)S(1)} %copy-done.67, f32[1024]{0:T(1024)S(1)} %bitcast.351, f32[1920,1024]{1,0:T(8,128)} %fusion.98, ...), kind=kOutput, calls=%fused_computation.41 | convolution fusion | flops 8072718336 | bytes 35694592 | tf_op jit(solution)/shard_map/dot_general | solution.py:27
  518.2 10.2 %multiply_reduce_fusion.1 = (f32[1024]{0:T(1024)}, f32[1920]{0:T(1024)S(1)}, f32[1920]{0:T(1024)S(1)}, f32[1024]{0:T(1024)}, f32[1920,1024]{1,0:T(8,128)S(1)}) fusion(f32[1920,1024]{1,0:T(8,128)S(1)} %bitcast.307, f32[1920]{0:T(1024)S(1)} %copy-done.65, f32[1920]{0:T(1024)S(1)} %copy-done.61, f32[1024]{0:T(1024)S(1)} %bitcast.345, ...), kind=kLoop, calls=%fused_computation.42 | loop fusion | flops 35383552 | bytes 35467264 | tf_op jit(solution)/shard_map/reduce_sum | solution.py:217
  547.3 26.8 %attention_backward.3 = bf16[1280,1536]{1,0:T(8,128)(2,1)S(1)} custom-call(bf16[1280,1536]{1,0:T(8,128)(2,1)S(1)} %copy-done.13, bf16[1280,1536]{1,0:T(8,128)(2,1)S(1)} %copy-done.13, bf16[1280,1536]{1,0:T(8,128)(2,1)S(1)} %copy-done.13, bf16[1280,512]{1,0:T(8,128)(2,1)S(1)} %convolution_convert_fusion.9.do_ref, bf16[1280,512]{1,0:T(8,128)(2,1)S(1)} %copy-done.5, ...), custom_call_target="tpu_custom_call" | custom-call | flops 20132659200 | bytes 11796480 | tf_op jit(solution)/shard_map/attention_backward/pallas_call | solution.py:171
  578.9 4.5 convolution_convert_fusion.6
  591.4 9.2 %collective-permute-done.20 = bf16[640,512]{1,0:T(8,128)(2,1)S(1)} collective-permute-done((bf16[640,512]{1,0:T(8,128)(2,1)S(1)}, bf16[640,512]{1,0:T(8,128)(2,1)S(1)}, u32[]{:S(2)}, u32[]{:S(2)}) %collective-permute-start.20) | collective-permute-done | bytes 655392 | tf_op jit(solution)/shard_map/ppermute | solution.py:400
  601.4 19.5 %collective-permute-done.32 = bf16[4,64,512]{2,1,0:T(8,128)(2,1)S(1)} collective-permute-done((bf16[4,64,512]{2,1,0:T(8,128)(2,1)S(1)}, bf16[4,64,512]{2,1,0:T(8,128)(2,1)S(1)}, u32[]{:S(2)}, u32[]{:S(2)}) %collective-permute-start.32) | collective-permute-done | bytes 262176 | tf_op jit(solution)/shard_map/ppermute | solution.py:400
  623.5 26.6 %attention_backward.4 = bf16[1280,1536]{1,0:T(8,128)(2,1)S(1)} custom-call(bf16[1280,1536]{1,0:T(8,128)(2,1)S(1)} %copy-done.1, bf16[1280,1536]{1,0:T(8,128)(2,1)S(1)} %copy-done.1, bf16[1280,1536]{1,0:T(8,128)(2,1)S(1)} %copy-done.1, bf16[1280,512]{1,0:T(8,128)(2,1)S(1)} %pad_maximum_fusion.5.do_ref, bf16[1280,512]{1,0:T(8,128)(2,1)S(1)} %copy-done.3, ...), custom_call_target="tpu_custom_call" | custom-call | flops 20132659200 | bytes 11796480 | tf_op jit(solution)/shard_map/attention_backward/pallas_call | solution.py:171
  650.2 7.6 fusion.100
  660.6 3.4 broadcast_select_fusion.5
  669.7 41.6 %collective-permute-done.17 = bf16[4,64,2048]{2,1,0:T(8,128)(2,1)S(1)} collective-permute-done((bf16[4,64,2048]{2,1,0:T(8,128)(2,1)S(1)}, bf16[4,64,2048]{2,1,0:T(8,128)(2,1)S(1)}, u32[]{:S(2)}, u32[]{:S(2)}) %collective-permute-start.17) | collective-permute-done | bytes 1048608 | tf_op jit(solution)/shard_map/ppermute | solution.py:400
  711.2 26.6 %attention_backward.5 = bf16[1280,1536]{1,0:T(8,128)(2,1)S(1)} custom-call(bf16[1280,1536]{1,0:T(8,128)(2,1)S(1)} %copy-done.11, bf16[1280,1536]{1,0:T(8,128)(2,1)S(1)} %copy-done.11, bf16[1280,1536]{1,0:T(8,128)(2,1)S(1)} %copy-done.11, bf16[1280,512]{1,0:T(8,128)(2,1)S(1)} %convolution_convert_fusion.10.do_ref, bf16[1280,512]{1,0:T(8,128)(2,1)S(1)} %copy-done.7, ...), custom_call_target="tpu_custom_call" | custom-call | flops 20132659200 | bytes 11796480 | tf_op jit(solution)/shard_map/attention_backward/pallas_call | solution.py:171
  740.3 6.2 fusion.42
  746.5 6.7 add_convert_fusion.4
  762.4 6.0 fusion.99
  772.1 7.7 fusion.97
  779.8 4.9 fusion.19
  784.8 5.3 fusion.18
  816.1 5.7 collective-permute-done.26
  829.5 3.9 collective-permute-done.30
  833.4 7.6 collective-permute-done.29
  845.0 3.7 maximum_bitcast_fusion
  (450 shorter events, 175.4 us)
Async XLA Ops:
  7.2 291.4 %all-gather.2.cloned.1.call-start = ((), (), s32[]{:S(2)}) async-start(), calls=%async_computation | async-start | bytes 8650752 | tf_op jit(solution)/shard_map/all_gather | solution.py:541
  131.3 64.4 %collective-permute-start = (bf16[640,1536]{1,0:T(8,128)(2,1)}, bf16[640,1536]{1,0:T(8,128)(2,1)}, u32[]{:S(2)}, u32[]{:S(2)}) collective-permute-start(bf16[640,1536]{1,0:T(8,128)(2,1)} %convolution_convert_fusion.8), channel_id=1, source_target_pairs={{0,1},{1,0},{2,3},{3,2},{4,5},{5,4},{6,7},{7,6},{8,9},{9,8},{10,11... | collective-permute-start | bytes 5898248 | tf_op jit(solution)/shard_map/ppermute | solution.py:400
  222.2 17.1 %collective-permute-start.1 = (bf16[640,512]{1,0:T(8,128)(2,1)S(1)}, bf16[640,512]{1,0:T(8,128)(2,1)S(1)}, u32[]{:S(2)}, u32[]{:S(2)}) collective-permute-start(bf16[640,512]{1,0:T(8,128)(2,1)S(1)} %get-tuple-element.196), channel_id=1, source_target_pairs={{0,1},{1,0},{2,3},{3,2},{4,5},{5,4},{6,7},{7,6},{8,9},{9,8},{10,11... | collective-permute-start | bytes 1966088 | tf_op jit(solution)/shard_map/ppermute | solution.py:400
  239.7 55.1 %collective-permute-start.3 = (bf16[640,1024]{1,0:T(8,128)(2,1)S(1)}, bf16[640,1024]{1,0:T(8,128)(2,1)S(1)}, u32[]{:S(2)}, u32[]{:S(2)}) collective-permute-start(bf16[640,1024]{1,0:T(8,128)(2,1)S(1)} %get-tuple-element.180), channel_id=1, source_target_pairs={{0,1},{1,0},{2,3},{3,2},{4,5},{5,4},{6,7},{7,6},{8,9},{9,8},{10,11... | collective-permute-start | bytes 3932168 | tf_op jit(solution)/shard_map/ppermute | solution.py:400
  294.2 365.1 %collective-permute-start.21 = (bf16[640,1024]{1,0:T(8,128)(2,1)}, bf16[640,1024]{1,0:T(8,128)(2,1)}, u32[]{:S(2)}, u32[]{:S(2)}) collective-permute-start(bf16[640,1024]{1,0:T(8,128)(2,1)} %slice.141), channel_id=1, source_target_pairs={{0,1},{1,0},{2,3},{3,2},{4,5},{5,4},{6,7},{7,6},{8,9},{9,8},{10,11... | collective-permute-start | bytes 3932168 | tf_op jit(solution)/shard_map/ppermute | solution.py:400
  372.1 37.3 %collective-permute-start.2 = (bf16[640,1024]{1,0:T(8,128)(2,1)S(1)}, bf16[640,1024]{1,0:T(8,128)(2,1)}, u32[]{:S(2)}, u32[]{:S(2)}) collective-permute-start(bf16[640,1024]{1,0:T(8,128)(2,1)S(1)} %dynamic-slice_bitcast_fusion.3), channel_id=1, source_target_pairs={{0,1},{1,0},{2,3},{3,2},{4,5},{5,4},{6,7},{7,6},{8,9},{9,8},{10,11... | collective-permute-start | bytes 3932168 | tf_op jit(solution)/shard_map/ppermute | solution.py:400
  375.2 42.6 %collective-permute-start.4 = (bf16[4,2,64,2048]{3,2,1,0:T(8,128)(2,1)}, bf16[4,2,64,2048]{3,2,1,0:T(8,128)(2,1)}, u32[]{:S(2)}, u32[]{:S(2)}) collective-permute-start(bf16[4,2,64,2048]{3,2,1,0:T(8,128)(2,1)} %dynamic-slice_bitcast_fusion.1), channel_id=1, source_target_pairs={{0,2},{2,0},{1,3},{3,1},{4,6},{6,4},{5,7},{7,5},{8,10},{10,8},{9,1... | collective-permute-start | bytes 6291464 | tf_op jit(solution)/shard_map/ppermute | solution.py:400
  376.8 36.3 %collective-permute-start.5 = (bf16[4,2,64,2048]{3,2,1,0:T(8,128)(2,1)}, bf16[4,2,64,2048]{3,2,1,0:T(8,128)(2,1)}, u32[]{:S(2)}, u32[]{:S(2)}) collective-permute-start(bf16[4,2,64,2048]{3,2,1,0:T(8,128)(2,1)} %dynamic-slice_bitcast_fusion), channel_id=1, source_target_pairs={{0,2},{2,0},{1,3},{3,1},{4,6},{6,4},{5,7},{7,5},{8,10},{10,8},{9,1... | collective-permute-start | bytes 6291464 | tf_op jit(solution)/shard_map/ppermute | solution.py:400
  431.1 15.8 %collective-permute-start.10 = (bf16[2,64,2048]{2,1,0:T(8,128)(2,1)S(1)}, bf16[2,64,2048]{2,1,0:T(8,128)(2,1)S(1)}, u32[]{:S(2)}, u32[]{:S(2)}) collective-permute-start(bf16[2,64,2048]{2,1,0:T(8,128)(2,1)S(1)} %get-tuple-element.211), channel_id=1, source_target_pairs={{0,5},{1,4},{4,1},{5,0},{2,7},{3,6},{6,3},{7,2},{8,13},{9,12},{12,... | collective-permute-start | bytes 1572872 | tf_op jit(solution)/shard_map/ppermute | solution.py:400
  432.9 25.3 %collective-permute-start.7 = (bf16[2,64,2048]{2,1,0:T(8,128)(2,1)S(1)}, bf16[2,64,2048]{2,1,0:T(8,128)(2,1)S(1)}, u32[]{:S(2)}, u32[]{:S(2)}) collective-permute-start(bf16[2,64,2048]{2,1,0:T(8,128)(2,1)S(1)} %get-tuple-element.210), channel_id=1, source_target_pairs={{0,1},{1,0},{4,5},{5,4},{2,3},{3,2},{6,7},{7,6},{8,9},{9,8},{12,13... | collective-permute-start | bytes 1572872 | tf_op jit(solution)/shard_map/ppermute | solution.py:400
  434.2 24.6 %collective-permute-start.6 = (bf16[2,64,2048]{2,1,0:T(8,128)(2,1)S(1)}, bf16[2,64,2048]{2,1,0:T(8,128)(2,1)S(1)}, u32[]{:S(2)}, u32[]{:S(2)}) collective-permute-start(bf16[2,64,2048]{2,1,0:T(8,128)(2,1)S(1)} %dynamic-slice_bitcast_fusion.14), channel_id=1, source_target_pairs={{0,4},{1,5},{4,0},{5,1},{2,6},{3,7},{6,2},{7,3},{8,12},{9,13},{12,... | collective-permute-start | bytes 1572872 | tf_op jit(solution)/shard_map/ppermute | solution.py:400
  434.9 37.7 %collective-permute-start.13 = (bf16[2,64,2048]{2,1,0:T(8,128)(2,1)S(1)}, bf16[2,64,2048]{2,1,0:T(8,128)(2,1)S(1)}, u32[]{:S(2)}, u32[]{:S(2)}) collective-permute-start(bf16[2,64,2048]{2,1,0:T(8,128)(2,1)S(1)} %get-tuple-element.209), channel_id=1, source_target_pairs={{0,5},{1,4},{4,1},{5,0},{2,7},{3,6},{6,3},{7,2},{8,13},{9,12},{12,... | collective-permute-start | bytes 1572872 | tf_op jit(solution)/shard_map/ppermute | solution.py:400
  446.9 32.1 %collective-permute-start.9 = (bf16[2,64,2048]{2,1,0:T(8,128)(2,1)S(1)}, bf16[2,64,2048]{2,1,0:T(8,128)(2,1)S(1)}, u32[]{:S(2)}, u32[]{:S(2)}) collective-permute-start(bf16[2,64,2048]{2,1,0:T(8,128)(2,1)S(1)} %get-tuple-element.208), channel_id=1, source_target_pairs={{0,1},{1,0},{4,5},{5,4},{2,3},{3,2},{6,7},{7,6},{8,9},{9,8},{12,13... | collective-permute-start | bytes 1572872 | tf_op jit(solution)/shard_map/ppermute | solution.py:400
  458.2 20.8 %collective-permute-start.8 = (bf16[2,64,2048]{2,1,0:T(8,128)(2,1)S(1)}, bf16[2,64,2048]{2,1,0:T(8,128)(2,1)S(1)}, u32[]{:S(2)}, u32[]{:S(2)}) collective-permute-start(bf16[2,64,2048]{2,1,0:T(8,128)(2,1)S(1)} %dynamic-slice_bitcast_fusion.11), channel_id=1, source_target_pairs={{0,4},{1,5},{4,0},{5,1},{2,6},{3,7},{6,2},{7,3},{8,12},{9,13},{12,... | collective-permute-start | bytes 1572872 | tf_op jit(solution)/shard_map/ppermute | solution.py:400
  458.7 73.0 %collective-permute-start.11 = (bf16[4,2,64,2048]{3,2,0,1:T(8,128)(2,1)}, bf16[4,2,64,2048]{3,2,0,1:T(8,128)(2,1)}, u32[]{:S(2)}, u32[]{:S(2)}) collective-permute-start(bf16[4,2,64,2048]{3,2,0,1:T(8,128)(2,1)} %bitcast.297), channel_id=1, source_target_pairs={{0,2},{2,0},{1,3},{3,1},{4,6},{6,4},{5,7},{7,5},{8,10},{10,8},{9,1... | collective-permute-start | bytes 6291464 | tf_op jit(solution)/shard_map/ppermute | solution.py:400
  515.0 22.7 %collective-permute-start.12 = (bf16[4,2,64,2048]{3,2,0,1:T(8,128)(2,1)}, bf16[4,2,64,2048]{3,2,0,1:T(8,128)(2,1)}, u32[]{:S(2)}, u32[]{:S(2)}) collective-permute-start(bf16[4,2,64,2048]{3,2,0,1:T(8,128)(2,1)} %bitcast.296), channel_id=1, source_target_pairs={{0,2},{2,0},{1,3},{3,1},{4,6},{6,4},{5,7},{7,5},{8,10},{10,8},{9,1... | collective-permute-start | bytes 6291464 | tf_op jit(solution)/shard_map/ppermute | solution.py:400
  516.1 67.7 %collective-permute-start.42 = (bf16[64,2048]{1,0:T(8,128)(2,1)}, bf16[64,2048]{1,0:T(8,128)(2,1)S(1)}, u32[]{:S(2)}, u32[]{:S(2)}) collective-permute-start(bf16[64,2048]{1,0:T(8,128)(2,1)} %get-tuple-element.200), channel_id=1, source_target_pairs={{0,24},{8,16},{16,8},{24,0},{1,25},{9,17},{17,9},{25,1},{2,26},{10... | collective-permute-start | bytes 786440 | tf_op jit(solution)/shard_map/ppermute | solution.py:400
  517.5 67.9 %collective-permute-start.41 = (bf16[64,2048]{1,0:T(8,128)(2,1)}, bf16[64,2048]{1,0:T(8,128)(2,1)S(1)}, u32[]{:S(2)}, u32[]{:S(2)}) collective-permute-start(bf16[64,2048]{1,0:T(8,128)(2,1)} %get-tuple-element.199), channel_id=1, source_target_pairs={{0,16},{8,24},{16,0},{24,8},{1,17},{9,25},{17,1},{25,9},{2,18},{10... | collective-permute-start | bytes 786440 | tf_op jit(solution)/shard_map/ppermute | solution.py:400
  531.7 55.2 %collective-permute-start.40 = (bf16[64,2048]{1,0:T(8,128)(2,1)}, bf16[64,2048]{1,0:T(8,128)(2,1)S(1)}, u32[]{:S(2)}, u32[]{:S(2)}) collective-permute-start(bf16[64,2048]{1,0:T(8,128)(2,1)} %get-tuple-element.198), channel_id=1, source_target_pairs={{0,8},{8,0},{16,24},{24,16},{1,9},{9,1},{17,25},{25,17},{2,10},{10... | collective-permute-start | bytes 786440 | tf_op jit(solution)/shard_map/ppermute | solution.py:400
  537.7 132.0 %collective-permute-start.18 = (bf16[4,64,2048]{2,1,0:T(8,128)(2,1)}, bf16[4,64,2048]{2,1,0:T(8,128)(2,1)}, u32[]{:S(2)}, u32[]{:S(2)}) collective-permute-start(bf16[4,64,2048]{2,1,0:T(8,128)(2,1)} %dynamic-slice_bitcast_fusion.4), channel_id=1, source_target_pairs={{0,4},{4,0},{1,5},{5,1},{2,6},{6,2},{3,7},{7,3},{8,12},{12,8},{9,1... | collective-permute-start | bytes 3145736 | tf_op jit(solution)/shard_map/ppermute | solution.py:400
  584.6 16.0 %collective-permute-start.20 = (bf16[640,512]{1,0:T(8,128)(2,1)S(1)}, bf16[640,512]{1,0:T(8,128)(2,1)S(1)}, u32[]{:S(2)}, u32[]{:S(2)}) collective-permute-start(bf16[640,512]{1,0:T(8,128)(2,1)S(1)} %copy-done.100), channel_id=1, source_target_pairs={{0,1},{1,0},{2,3},{3,2},{4,5},{5,4},{6,7},{7,6},{8,9},{9,8},{10,11... | collective-permute-start | bytes 1966088 | tf_op jit(solution)/shard_map/ppermute | solution.py:400
  590.2 32.2 %collective-permute-start.16 = (bf16[4,64,2048]{2,1,0:T(8,128)(2,1)S(1)}, bf16[4,64,2048]{2,1,0:T(8,128)(2,1)S(1)}, u32[]{:S(2)}, u32[]{:S(2)}) collective-permute-start(bf16[4,64,2048]{2,1,0:T(8,128)(2,1)S(1)} %dynamic-slice_bitcast_fusion.5), channel_id=1, source_target_pairs={{0,4},{4,0},{1,5},{5,1},{2,6},{6,2},{3,7},{7,3},{8,12},{12,8},{9,1... | collective-permute-start | bytes 3145736 | tf_op jit(solution)/shard_map/ppermute | solution.py:400
  591.0 75.2 %collective-permute-start.19 = (bf16[4,2,64,1536]{3,2,0,1:T(8,128)(2,1)}, bf16[4,2,64,1536]{3,2,0,1:T(8,128)(2,1)}, u32[]{:S(2)}, u32[]{:S(2)}) collective-permute-start(bf16[4,2,64,1536]{3,2,0,1:T(8,128)(2,1)} %bitcast.299), channel_id=1, source_target_pairs={{0,2},{2,0},{1,3},{3,1},{4,6},{6,4},{5,7},{7,5},{8,10},{10,8},{9,1... | collective-permute-start | bytes 4718600 | tf_op jit(solution)/shard_map/ppermute | solution.py:400
  600.6 20.3 %collective-permute-start.32 = (bf16[4,64,512]{2,1,0:T(8,128)(2,1)S(1)}, bf16[4,64,512]{2,1,0:T(8,128)(2,1)S(1)}, u32[]{:S(2)}, u32[]{:S(2)}) collective-permute-start(bf16[4,64,512]{2,1,0:T(8,128)(2,1)S(1)} %dynamic-slice_bitcast_fusion.19), channel_id=1, source_target_pairs={{0,4},{4,0},{1,5},{5,1},{2,6},{6,2},{3,7},{7,3},{8,12},{12,8},{9,1... | collective-permute-start | bytes 786440 | tf_op jit(solution)/shard_map/ppermute | solution.py:400
  620.9 43.1 %collective-permute-start.31 = (bf16[4,64,512]{2,1,0:T(8,128)(2,1)S(1)}, bf16[4,64,512]{2,1,0:T(8,128)(2,1)S(1)}, u32[]{:S(2)}, u32[]{:S(2)}) collective-permute-start(bf16[4,64,512]{2,1,0:T(8,128)(2,1)S(1)} %dynamic-slice_bitcast_fusion.20), channel_id=1, source_target_pairs={{0,4},{4,0},{1,5},{5,1},{2,6},{6,2},{3,7},{7,3},{8,12},{12,8},{9,1... | collective-permute-start | bytes 786440 | tf_op jit(solution)/shard_map/ppermute | solution.py:400
  622.3 42.7 %collective-permute-start.33 = (bf16[4,64,512]{2,1,0:T(8,128)(2,1)}, bf16[4,64,512]{2,1,0:T(8,128)(2,1)}, u32[]{:S(2)}, u32[]{:S(2)}) collective-permute-start(bf16[4,64,512]{2,1,0:T(8,128)(2,1)} %fusion.63), channel_id=1, source_target_pairs={{0,1},{1,0},{2,3},{3,2},{4,5},{5,4},{6,7},{7,6},{8,9},{9,8},{10,11... | collective-permute-start | bytes 786440 | tf_op jit(solution)/shard_map/ppermute | solution.py:400
  659.2 100.7 %collective-permute-start.24 = (bf16[640,1024]{1,0:T(8,128)(2,1)}, bf16[640,1024]{1,0:T(8,128)(2,1)S(1)}, u32[]{:S(2)}, u32[]{:S(2)}) collective-permute-start(bf16[640,1024]{1,0:T(8,128)(2,1)} %dynamic-slice_convert_fusion.1), channel_id=1, source_target_pairs={{0,1},{1,0},{2,3},{3,2},{4,5},{5,4},{6,7},{7,6},{8,9},{9,8},{10,11... | collective-permute-start | bytes 3932168 | tf_op jit(solution)/shard_map/ppermute | solution.py:400
  664.0 47.3 %collective-permute-start.17 = (bf16[4,64,2048]{2,1,0:T(8,128)(2,1)S(1)}, bf16[4,64,2048]{2,1,0:T(8,128)(2,1)S(1)}, u32[]{:S(2)}, u32[]{:S(2)}) collective-permute-start(bf16[4,64,2048]{2,1,0:T(8,128)(2,1)S(1)} %fusion.41), channel_id=1, source_target_pairs={{0,1},{1,0},{2,3},{3,2},{4,5},{5,4},{6,7},{7,6},{8,9},{9,8},{10,11... | collective-permute-start | bytes 3145736 | tf_op jit(solution)/shard_map/ppermute | solution.py:400
  668.2 78.2 %collective-permute-start.22 = (bf16[4,64,1536]{2,1,0:T(8,128)(2,1)S(1)}, bf16[4,64,1536]{2,1,0:T(8,128)(2,1)S(1)}, u32[]{:S(2)}, u32[]{:S(2)}) collective-permute-start(bf16[4,64,1536]{2,1,0:T(8,128)(2,1)S(1)} %dynamic-slice_bitcast_fusion.7), channel_id=1, source_target_pairs={{0,4},{4,0},{1,5},{5,1},{2,6},{6,2},{3,7},{7,3},{8,12},{12,8},{9,1... | collective-permute-start | bytes 2359304 | tf_op jit(solution)/shard_map/ppermute | solution.py:400
  753.5 14.9 %collective-permute-start.23 = (bf16[4,2,64,1536]{3,2,0,1:T(8,128)(2,1)S(1)}, bf16[4,2,64,1536]{3,2,0,1:T(8,128)(2,1)S(1)}, u32[]{:S(2)}, u32[]{:S(2)}) collective-permute-start(bf16[4,2,64,1536]{3,2,0,1:T(8,128)(2,1)S(1)} %bitcast.327), channel_id=1, source_target_pairs={{0,2},{2,0},{1,3},{3,1},{4,6},{6,4},{5,7},{7,5},{8,10},{10,8},{9,1... | collective-permute-start | bytes 4718600 | tf_op jit(solution)/shard_map/ppermute | solution.py:400
  754.7 61.4 %collective-permute-start.27 = (bf16[4,64,1536]{2,1,0:T(8,128)(2,1)}, bf16[4,64,1536]{2,1,0:T(8,128)(2,1)}, u32[]{:S(2)}, u32[]{:S(2)}) collective-permute-start(bf16[4,64,1536]{2,1,0:T(8,128)(2,1)} %fusion.47), channel_id=1, source_target_pairs={{0,1},{1,0},{2,3},{3,2},{4,5},{5,4},{6,7},{7,6},{8,9},{9,8},{10,11... | collective-permute-start | bytes 2359304 | tf_op jit(solution)/shard_map/ppermute | solution.py:400
  755.9 49.8 %collective-permute-start.36 = (bf16[64,512]{1,0:T(8,128)(2,1)S(1)}, bf16[64,512]{1,0:T(8,128)(2,1)S(1)}, u32[]{:S(2)}, u32[]{:S(2)}) collective-permute-start(bf16[64,512]{1,0:T(8,128)(2,1)S(1)} %get-tuple-element.216), channel_id=1, source_target_pairs={{0,24},{8,16},{16,8},{24,0},{1,25},{9,17},{17,9},{25,1},{2,26},{10... | collective-permute-start | bytes 196616 | tf_op jit(solution)/shard_map/ppermute | solution.py:400
  757.5 32.7 %collective-permute-start.39 = (bf16[64,2048]{1,0:T(8,128)(2,1)S(1)}, bf16[64,2048]{1,0:T(8,128)(2,1)S(1)}, u32[]{:S(2)}, u32[]{:S(2)}) collective-permute-start(bf16[64,2048]{1,0:T(8,128)(2,1)S(1)} %get-tuple-element.202), channel_id=1, source_target_pairs={{0,24},{8,16},{16,8},{24,0},{1,25},{9,17},{17,9},{25,1},{2,26},{10... | collective-permute-start | bytes 786440 | tf_op jit(solution)/shard_map/ppermute | solution.py:400
  759.9 32.4 %collective-permute-start.38 = (bf16[64,2048]{1,0:T(8,128)(2,1)S(1)}, bf16[64,2048]{1,0:T(8,128)(2,1)S(1)}, u32[]{:S(2)}, u32[]{:S(2)}) collective-permute-start(bf16[64,2048]{1,0:T(8,128)(2,1)S(1)} %get-tuple-element.203), channel_id=1, source_target_pairs={{0,16},{8,24},{16,0},{24,8},{1,17},{9,25},{17,1},{25,9},{2,18},{10... | collective-permute-start | bytes 786440 | tf_op jit(solution)/shard_map/ppermute | solution.py:400
  768.5 27.6 %collective-permute-start.37 = (bf16[64,2048]{1,0:T(8,128)(2,1)S(1)}, bf16[64,2048]{1,0:T(8,128)(2,1)}, u32[]{:S(2)}, u32[]{:S(2)}) collective-permute-start(bf16[64,2048]{1,0:T(8,128)(2,1)S(1)} %get-tuple-element.201), channel_id=1, source_target_pairs={{0,8},{8,0},{16,24},{24,16},{1,9},{9,1},{17,25},{25,17},{2,10},{10... | collective-permute-start | bytes 786440 | tf_op jit(solution)/shard_map/ppermute | solution.py:400
  791.0 10.4 %collective-permute-start.45 = (f32[8,1024]{1,0:T(8,128)S(1)}, f32[8,1024]{1,0:T(8,128)S(1)}, u32[]{:S(2)}, u32[]{:S(2)}) collective-permute-start(f32[8,1024]{1,0:T(8,128)S(1)} %concatenate.43), channel_id=1, source_target_pairs={{0,5},{1,4},{4,1},{5,0},{2,7},{3,6},{6,3},{7,2},{8,13},{9,12},{12,... | collective-permute-start | bytes 98312 | tf_op jit(solution)/shard_map/ppermute | solution.py:400
  793.1 10.1 %collective-permute-start.44 = (f32[8,1024]{1,0:T(8,128)S(1)}, f32[8,1024]{1,0:T(8,128)S(1)}, u32[]{:S(2)}, u32[]{:S(2)}) collective-permute-start(f32[8,1024]{1,0:T(8,128)S(1)} %concatenate.43), channel_id=1, source_target_pairs={{0,4},{1,5},{4,0},{5,1},{2,6},{3,7},{6,2},{7,3},{8,12},{9,13},{12,... | collective-permute-start | bytes 98312 | tf_op jit(solution)/shard_map/ppermute | solution.py:400
  796.0 8.3 collective-permute-start.43
  801.4 6.1 collective-permute-start.35
  803.2 5.6 collective-permute-start.34
  804.4 17.5 %collective-permute-start.26 = (bf16[4,64,1536]{2,1,0:T(8,128)(2,1)}, bf16[4,64,1536]{2,1,0:T(8,128)(2,1)}, u32[]{:S(2)}, u32[]{:S(2)}) collective-permute-start(bf16[4,64,1536]{2,1,0:T(8,128)(2,1)} %dynamic-slice_bitcast_fusion.6), channel_id=1, source_target_pairs={{0,4},{4,0},{1,5},{5,1},{2,6},{6,2},{3,7},{7,3},{8,12},{12,8},{9,1... | collective-permute-start | bytes 2359304 | tf_op jit(solution)/shard_map/ppermute | solution.py:400
  805.8 7.8 collective-permute-start.48
  807.5 6.9 collective-permute-start.47
  808.8 5.6 collective-permute-start.46
  813.6 28.3 %collective-permute-start.25 = (bf16[640,1024]{1,0:T(8,128)(2,1)}, bf16[640,1024]{1,0:T(8,128)(2,1)}, u32[]{:S(2)}, u32[]{:S(2)}) collective-permute-start(bf16[640,1024]{1,0:T(8,128)(2,1)} %fusion.50), channel_id=1, source_target_pairs={{0,1},{1,0},{2,3},{3,2},{4,5},{5,4},{6,7},{7,6},{8,9},{9,8},{10,11... | collective-permute-start | bytes 3932168 | tf_op jit(solution)/shard_map/ppermute | solution.py:400
  823.8 9.6 %collective-permute-start.30 = (bf16[64,1536]{1,0:T(8,128)(2,1)S(1)}, bf16[64,1536]{1,0:T(8,128)(2,1)S(1)}, u32[]{:S(2)}, u32[]{:S(2)}) collective-permute-start(bf16[64,1536]{1,0:T(8,128)(2,1)S(1)} %get-tuple-element.213), channel_id=1, source_target_pairs={{0,24},{8,16},{16,8},{24,0},{1,25},{9,17},{17,9},{25,1},{2,26},{10... | collective-permute-start | bytes 589832 | tf_op jit(solution)/shard_map/ppermute | solution.py:400
  825.1 15.9 %collective-permute-start.29 = (bf16[64,1536]{1,0:T(8,128)(2,1)S(1)}, bf16[64,1536]{1,0:T(8,128)(2,1)S(1)}, u32[]{:S(2)}, u32[]{:S(2)}) collective-permute-start(bf16[64,1536]{1,0:T(8,128)(2,1)S(1)} %get-tuple-element.214), channel_id=1, source_target_pairs={{0,16},{8,24},{16,0},{24,8},{1,17},{9,25},{17,1},{25,9},{2,18},{10... | collective-permute-start | bytes 589832 | tf_op jit(solution)/shard_map/ppermute | solution.py:400
  826.5 14.5 %collective-permute-start.28 = (bf16[64,1536]{1,0:T(8,128)(2,1)S(1)}, bf16[64,1536]{1,0:T(8,128)(2,1)S(1)}, u32[]{:S(2)}, u32[]{:S(2)}) collective-permute-start(bf16[64,1536]{1,0:T(8,128)(2,1)S(1)} %get-tuple-element.212), channel_id=1, source_target_pairs={{0,8},{8,0},{16,24},{24,16},{1,9},{9,1},{17,25},{25,17},{2,10},{10... | collective-permute-start | bytes 589832 | tf_op jit(solution)/shard_map/ppermute | solution.py:400
  (112 other events, 1335.6 us)
Sparse Core Ops, SparseCore 0:
  132.0 84.5 all-gather.1

commit v9 on v8

--- a/solution.py
+++ b/solution.py
@@ -622,8 +622,7 @@
 
     grad_branch_a, sums_1 = norm_backward(branch_a, norm_gains[1], grad_residual)
     grad_branch_a = after(grad_branch_a.astype(bf16), *core_up, *across_down[1])
-    up_y = {t: over_y(core_up[t]) for t in reversed(halves)}
-    up_x = over_tp([up_y[t] for t in halves[1:]])
+    up_y = {t: over_y(core_up[t]) for t in halves[1:]}
     share_grad = [dot_nn(grad_branch_a[split:], w).astype(bf16) for w in full_out]
     whole_grad = [dot_nn(grad_branch_a[:split], w).astype(bf16) for w in full_out] if whole else []
     share_do = []
@@ -652,17 +651,19 @@
     z_down = scatter_z(down, *made)
     core_qkv = [None] + [scatter_core(part) for part in dw_qkv[1:]]
     late_grad = after(grad_branch_a, *made)
+    up_x = over_tp([up_y[t] for t in halves[1:]])
     core_out = [scatter_core(dot_tn(late_grad, part).astype(bf16)) for part in attended]
     grad_shared = []
     own_part = []
-    early_y = [up_y[t][1] for t in halves[1:]]
     for n in range(share_count):
         qkv, att, lse = saved[n]
-        do = after(share_do[n], *made, *early_y)
+        do = after(share_do[n], *made)
         dx = attention_backward(qkv, do, att, lse, *share_tables[n])
         made = [dx]
         grad_shared.append(dx)
-    whole_backward(0, *core_out, *up_x, up_y[0][1], *core_qkv[1:], *made)
+    up_y[0] = over_y(after(core_up[0], *made))
+    last = whole_backward(0, *core_qkv[1:], *made) + made
+    core_out = [after(part, *last) for part in core_out]
     for n in range(share_count):
         part = dot_nt(grad_shared[n], full_qkv[0])
         pieces = exchange_tp([share_rows(part, 0)] + [share_rows(part, k).astype(bf16) for k in halves[1:]])
@@ -684,7 +685,7 @@
     z_out_part = after(total([[*out_y[0], *out_x]], [[]]), dw_qkv[0])
     qkv_y[0] = over_y(core_qkv[0])
     z_qkv = scatter_z(total([[*qkv_y[0], *qkv_x]], [[]]))
-    ready = [dw_qkv[0]]
+    ready = [dw_qkv[0], *up_x, up_y[0][1]]
     grad_normed = list(own_part)
     if whole:
         trees = [after(jnp.concatenate(grad_qkv[t], axis=0), *ready) for t in halves]

time: 860 us -> 796 us (0.926)
  waiting for transfers between devices: 125 us -> 56.6 us
    ppermute x50, waiting for transfers between devices: 125 us -> 56.6 us  [send(): return lax.ppermute(values, axes, [(s, s ^ distance) for s in range(count)])]
    unnamed x224 -> x222, local copies, waits for them, and re-layouts: 20.6 us -> 19.2 us
  transfers between devices with their start and end apart: 51 -> 51, of which waited for: 11 -> 10; matrix products, arithmetic and copies ran while one was open for 43% -> 48% of each run, Pallas kernels for 17% -> 18%
where the time goes in v9:
time: 796 us; the launch traced here: 793 us
  matrix products  257 us (32%)
  Pallas kernels  253 us (32%)
  other arithmetic  103 us (13%)
  waiting for transfers between devices  56.6 us (7%)
  local copies, waits for them, and re-layouts  55 us (7%)
  starting transfers between devices  51.7 us (6%)
  between operations  16.4 us (2%)
    pallas_call x1, Pallas kernels, gather_weights(): pl.pallas_call(functools.partial(gather_kernel, chunks, len(shards), move...  108 us
    dot_general x12, matrix products, dot_nn(): lax.dot_general(a, b, (((1,), (0,)), ((), ())), preferred_element_type=f32)  98 us
    dot_general x9, matrix products, dot_nt(): lax.dot_general(a, b, (((1,), (1,)), ((), ())), preferred_element_type=f32)  86.8 us
    pallas_call x3, Pallas kernels, attention_backward(): pl.pallas_call(attention_backward_kernel, name='attention_backward', out_...  80 us
    dot_general x9, matrix products, dot_tn(): lax.dot_general(a, b, (((0,), (0,)), ((), ())), preferred_element_type=f32)  72.4 us
    pallas_call x3, Pallas kernels, attention_forward(): pl.pallas_call(attention_forward_kernel, name='attention_forward', out_sh...  64.7 us
    ppermute x50, waiting for transfers between devices, send(): return lax.ppermute(values, axes, [(s, s ^ distance) for s in range(count)])  56.6 us
    ppermute x50, starting transfers between devices, send(): return lax.ppermute(values, axes, [(s, s ^ distance) for s in range(count)])  51.6 us
  transfers between devices with their start and end apart: 51, of which 10 were waited for; matrix products, arithmetic and copies ran while one was open for 48% of the time, Pallas kernels for 18%

profile of v9, /device:TPU:0, one launch (start us, length us, event | category | flops | bytes accessed | tf_op | source)
XLA Modules:
  0.0 792.6 jit_solution(9972967743815035519)
XLA Ops:
  11.6 108.2 %gather_weights.1 = (bf16[4,2,2,64,1536]{4,3,2,1,0:T(8,128)(2,1)}, bf16[4,2,2,64,1536]{4,3,2,1,0:T(8,128)(2,1)}, bf16[4,2,2,64,512]{4,3,2,1,0:T(8,128)(2,1)}, bf...) custom-call(bf16[64,1536]{1,0:T(8,128)(2,1)} %bitcast.337, ...), custom_call_target="tpu_custom_call" | custom-call | bytes 33554432 | tf_op jit(solution)/shard_map/gather_weights/pallas_call | solution.py:374
  127.8 3.5 convolution_convert_fusion.8
  131.9 9.0 %convolution_convert_fusion.q_ref.k_ref.v_ref = bf16[1280,1536]{1,0:T(8,128)(2,1)} fusion(bf16[1024,1536]{1,0:T(8,128)(2,1)} %bitcast.378, bf16[1920,1024]{1,0:T(8,128)(2,1)} %copy-done.28), kind=kOutput, calls=%fused_computation.51 | convolution fusion | flops 4028497920 | bytes 9699328 | tf_op jit(solution)/shard_map/dot_general | solution.py:23
  140.9 5.7 convolution_convert_fusion.1.q_ref.k_ref.v_ref
  152.4 21.5 %attention_forward.5 = (bf16[1280,512]{1,0:T(8,128)(2,1)S(1)}, f32[4,8,1280]{2,1,0:T(8,128)S(1)}) custom-call(bf16[1280,1536]{1,0:T(8,128)(2,1)S(1)} %copy-done.12, bf16[1280,1536]{1,0:T(8,128)(2,1)S(1)} %copy-done.12, bf16[1280,1536]{1,0:T(8,128)(2,1)S(1)} %copy-done.12, s32[1280,8]{1,0:T(8,128)S(1)} %pad.14.clone.col_ref, s32[8,1280]{1,0:T(8,128)S(1)} %pad.15.row_ref), custom_call_target="tpu_custom_call" | custom-call | flops 8053063680 | bytes 5898240 | tf_op jit(solution)/shard_map/attention_forward/pallas_call | solution.py:80
  174.0 21.7 %attention_forward.3 = (bf16[1280,512]{1,0:T(8,128)(2,1)S(1)}, f32[4,8,1280]{2,1,0:T(8,128)S(1)}) custom-call(bf16[1280,1536]{1,0:T(8,128)(2,1)S(1)} %copy-done.10, bf16[1280,1536]{1,0:T(8,128)(2,1)S(1)} %copy-done.10, bf16[1280,1536]{1,0:T(8,128)(2,1)S(1)} %copy-done.10, s32[1280,8]{1,0:T(8,128)S(1)} %pad.14.clone.col_ref, s32[8,1280]{1,0:T(8,128)S(1)} %pad.15.row_ref), custom_call_target="tpu_custom_call" | custom-call | flops 8053063680 | bytes 5898240 | tf_op jit(solution)/shard_map/attention_forward/pallas_call | solution.py:80
  195.8 4.6 broadcast_select_fusion.3
  200.6 21.5 %attention_forward.4 = (bf16[1280,512]{1,0:T(8,128)(2,1)S(1)}, f32[4,8,1280]{2,1,0:T(8,128)S(1)}) custom-call(bf16[1280,1536]{1,0:T(8,128)(2,1)S(1)} %pad_maximum_fusion.2.q_ref.k_ref.v_ref, bf16[1280,1536]{1,0:T(8,128)(2,1)S(1)} %pad_maximum_fusion.2.q_ref.k_ref.v_ref, bf16[1280,1536]{1,0:T(8,128)(2,1)S(1)} %pad_maximum_fusion.2.q_ref.k_ref.v_ref, ...), custom_call_target="tpu_custom_call" | custom-call | flops 8053063680 | bytes 5898240 | tf_op jit(solution)/shard_map/attention_forward/pallas_call | solution.py:80
  226.4 12.9 %collective-permute-done.1 = bf16[640,512]{1,0:T(8,128)(2,1)S(1)} collective-permute-done((bf16[640,512]{1,0:T(8,128)(2,1)S(1)}, bf16[640,512]{1,0:T(8,128)(2,1)S(1)}, u32[]{:S(2)}, u32[]{:S(2)}) %collective-permute-start.1) | collective-permute-done | bytes 655392 | tf_op jit(solution)/shard_map/ppermute | solution.py:400
  256.5 20.7 %add_convert_fusion.1 = (bf16[1920,2048]{1,0:T(8,128)(2,1)}, bf16[1920,2048]{1,0:T(8,128)(2,1)}) fusion(bf16[1920,1024]{1,0:T(8,128)(2,1)S(1)} %add_convert_fusion.3, bf16[1024,2048]{1,0:T(8,128)(2,1)} %bitcast.370), kind=kOutput, calls=%fused_computation.6 | convolution fusion | flops 8112046080 | bytes 23855104 | tf_op jit(solution)/shard_map/dot_general | solution.py:23
  277.3 16.9 %add_convert_fusion = (bf16[1920,2048]{1,0:T(8,128)(2,1)}, bf16[1920,2048]{1,0:T(8,128)(2,1)}) fusion(bf16[1920,1024]{1,0:T(8,128)(2,1)S(1)} %add_convert_fusion.3, bf16[1024,2048]{1,0:T(8,128)(2,1)S(1)} %bitcast.372), kind=kOutput, calls=%fused_computation.2 | convolution fusion | flops 8112046080 | bytes 23855104 | tf_op jit(solution)/shard_map/dot_general | solution.py:23
  298.5 15.7 %fusion.57 = f32[1920,1024]{1,0:T(8,128)} fusion(bf16[1920,2048]{1,0:T(8,128)(2,1)} %get-tuple-element.73, pred[]{:T(512)S(6)} %eq.30, bf16[2048,2048]{1,0:T(8,128)(2,1)} %all-gather.2.cloned.1.call-done), kind=kOutput, calls=%fused_computation.175 | convolution fusion | flops 8055160832 | bytes 24117248 | tf_op jit(solution)/shard_map/dot_general | solution.py:27
  314.2 15.3 %fusion.96 = (f32[1920]{0:T(1024)S(1)}, f32[1920,1024]{1,0:T(8,128)}) fusion(f32[1920,1024]{1,0:T(8,128)} %fusion.57, bf16[1920,2048]{1,0:T(8,128)(2,1)} %get-tuple-element.76, pred[]{:T(512)S(6)} %eq.31, bf16[2048,2048]{1,0:T(8,128)(2,1)S(1)} %copy-done.88), kind=kOutput, calls=%fused_computation.297 | convolution fusion | flops 8059090944 | bytes 31989248 | tf_op jit(solution)/shard_map/dot_general | solution.py:27
  329.6 4.3 multiply_reduce_fusion.4
  335.0 4.8 fusion.25
  339.9 4.7 fusion.23
  344.6 14.2 %convolution_convert_fusion.5 = bf16[1024,2048]{1,0:T(8,128)(2,1)S(1)} fusion(bf16[1920,1024]{1,0:T(8,128)(2,1)} %get-tuple-element.174, bf16[1920,2048]{1,0:T(8,128)(2,1)} %get-tuple-element.73), kind=kOutput, calls=%fused_computation.79 | convolution fusion | flops 8055160832 | bytes 15990784 | tf_op jit(solution)/shard_map/dot_general | solution.py:31
  358.8 13.1 %convolution_convert_fusion.4 = bf16[1024,2048]{1,0:T(8,128)(2,1)S(1)} fusion(bf16[1920,1024]{1,0:T(8,128)(2,1)S(1)} %copy-done.38, bf16[1920,2048]{1,0:T(8,128)(2,1)} %get-tuple-element.76), kind=kOutput, calls=%fused_computation.78 | convolution fusion | flops 8055160832 | bytes 15990784 | tf_op jit(solution)/shard_map/dot_general | solution.py:31
  378.0 14.5 %multiply_convert_fusion = bf16[1920,2048]{1,0:T(8,128)(2,1)} fusion(bf16[1920,2048]{1,0:T(8,128)(2,1)} %get-tuple-element.81, bf16[1920,1024]{1,0:T(8,128)(2,1)S(1)} %copy-done.39, pred[]{:T(512)S(6)} %eq.31, bf16[2048,2048]{1,0:T(8,128)(2,1)} %all-gather.2.cloned.1.call-done), kind=kOutput, calls=%fused_computation | convolution fusion | flops 8066957312 | bytes 28049408 | tf_op jit(solution)/shard_map/dot_general | solution.py:23
  392.5 16.6 %multiply_convert_fusion.1 = bf16[1920,2048]{1,0:T(8,128)(2,1)} fusion(bf16[1920,2048]{1,0:T(8,128)(2,1)} %get-tuple-element.78, bf16[1920,1024]{1,0:T(8,128)(2,1)} %get-tuple-element.174, pred[]{:T(512)S(6)} %eq.30, bf16[2048,2048]{1,0:T(8,128)(2,1)} %all-gather.2.cloned.1.call-done), kind=kOutput, calls=%fused_computation.1 | convolution fusion | flops 8066957312 | bytes 28049408 | tf_op jit(solution)/shard_map/dot_general | solution.py:23
  414.3 3.1 fusion.28
  421.3 10.0 %convolution_convert_fusion.3 = bf16[1024,2048]{1,0:T(8,128)(2,1)S(1)} fusion(bf16[1920,1024]{1,0:T(8,128)(2,1)S(1)} %copy-done.41, bf16[1920,2048]{1,0:T(8,128)(2,1)S(1)} %bitcast.385), kind=kOutput, calls=%fused_computation.77 | convolution fusion | flops 8055160832 | bytes 15990784 | tf_op jit(solution)/shard_map/dot_general | solution.py:31
  440.5 6.6 collective-permute-done.10
  448.0 10.4 %collective-permute-done.7 = bf16[2,64,2048]{2,1,0:T(8,128)(2,1)S(1)} collective-permute-done((bf16[2,64,2048]{2,1,0:T(8,128)(2,1)S(1)}, bf16[2,64,2048]{2,1,0:T(8,128)(2,1)S(1)}, u32[]{:S(2)}, u32[]{:S(2)}) %collective-permute-start.7) | collective-permute-done | bytes 524320 | tf_op jit(solution)/shard_map/ppermute | solution.py:400
  459.4 13.1 %convolution_convert_fusion.2 = bf16[1024,2048]{1,0:T(8,128)(2,1)} fusion(bf16[1920,1024]{1,0:T(8,128)(2,1)S(1)} %copy-done.41, bf16[1920,2048]{1,0:T(8,128)(2,1)} %multiply_convert_fusion), kind=kOutput, calls=%fused_computation.76 | convolution fusion | flops 8055160832 | bytes 15990784 | tf_op jit(solution)/shard_map/dot_general | solution.py:31
  472.5 6.8 collective-permute-done.9
  479.7 12.8 %fusion.98 = f32[1920,1024]{1,0:T(8,128)} fusion(bf16[1920,2048]{1,0:T(8,128)(2,1)} %multiply_convert_fusion, bf16[1024,2048]{1,0:T(8,128)(2,1)S(1)} %bitcast.373), kind=kOutput, calls=%fused_computation.299 | convolution fusion | flops 8053063680 | bytes 19922944 | tf_op jit(solution)/shard_map/dot_general | solution.py:27
  492.5 18.3 %multiply_reduce_fusion = (f32[1024]{0:T(1024)}, f32[1920]{0:T(1024)S(1)}, f32[1920]{0:T(1024)S(1)}, f32[1024]{0:T(1024)}, f32[1920,1024]{1,0:T(8,128)}) fusion(f32[1920,1024]{1,0:T(8,128)S(1)} %bitcast.309, f32[1920]{0:T(1024)S(1)} %copy-done.68, f32[1920]{0:T(1024)S(1)} %copy-done.66, f32[1024]{0:T(1024)S(1)} %bitcast.354, f32[1920,1024]{1,0:T(8,128)} %fusion.98, ...), kind=kOutput, calls=%fused_computation.41 | convolution fusion | flops 8072718336 | bytes 35694592 | tf_op jit(solution)/shard_map/dot_general | solution.py:27
  510.9 4.2 constant_dynamic-slice_fusion.9
  519.9 10.1 %multiply_reduce_fusion.1 = (f32[1024]{0:T(1024)}, f32[1920]{0:T(1024)S(1)}, f32[1920]{0:T(1024)S(1)}, f32[1024]{0:T(1024)}, f32[1920,1024]{1,0:T(8,128)S(1)}) fusion(f32[1920,1024]{1,0:T(8,128)S(1)} %bitcast.307, f32[1920]{0:T(1024)S(1)} %copy-done.64, f32[1920]{0:T(1024)S(1)} %copy-done.60, f32[1024]{0:T(1024)S(1)} %bitcast.348, ...), kind=kLoop, calls=%fused_computation.42 | loop fusion | flops 35383552 | bytes 35467264 | tf_op jit(solution)/shard_map/reduce_sum | solution.py:217
  530.0 4.5 multiply_convert_fusion.2
  548.2 26.8 %attention_backward.3 = bf16[1280,1536]{1,0:T(8,128)(2,1)S(1)} custom-call(bf16[1280,1536]{1,0:T(8,128)(2,1)S(1)} %copy-done.13, bf16[1280,1536]{1,0:T(8,128)(2,1)S(1)} %copy-done.13, bf16[1280,1536]{1,0:T(8,128)(2,1)S(1)} %copy-done.13, bf16[1280,512]{1,0:T(8,128)(2,1)S(1)} %convolution_convert_fusion.9.do_ref, bf16[1280,512]{1,0:T(8,128)(2,1)S(1)} %copy-done.5, ...), custom_call_target="tpu_custom_call" | custom-call | flops 20132659200 | bytes 11796480 | tf_op jit(solution)/shard_map/attention_backward/pallas_call | solution.py:171
  575.1 4.5 convolution_convert_fusion.6
  595.0 26.6 %attention_backward.4 = bf16[1280,1536]{1,0:T(8,128)(2,1)S(1)} custom-call(bf16[1280,1536]{1,0:T(8,128)(2,1)S(1)} %copy-done.1, bf16[1280,1536]{1,0:T(8,128)(2,1)S(1)} %copy-done.1, bf16[1280,1536]{1,0:T(8,128)(2,1)S(1)} %copy-done.1, bf16[1280,512]{1,0:T(8,128)(2,1)S(1)} %pad_maximum_fusion.5.do_ref, bf16[1280,512]{1,0:T(8,128)(2,1)S(1)} %copy-done.3, ...), custom_call_target="tpu_custom_call" | custom-call | flops 20132659200 | bytes 11796480 | tf_op jit(solution)/shard_map/attention_backward/pallas_call | solution.py:171
  621.6 6.3 fusion.100
  632.3 3.4 broadcast_select_fusion.5
  643.6 26.6 %attention_backward.5 = bf16[1280,1536]{1,0:T(8,128)(2,1)S(1)} custom-call(bf16[1280,1536]{1,0:T(8,128)(2,1)S(1)} %copy-done.11, bf16[1280,1536]{1,0:T(8,128)(2,1)S(1)} %copy-done.11, bf16[1280,1536]{1,0:T(8,128)(2,1)S(1)} %copy-done.11, bf16[1280,512]{1,0:T(8,128)(2,1)S(1)} %convolution_convert_fusion.10.do_ref, bf16[1280,512]{1,0:T(8,128)(2,1)S(1)} %copy-done.7, ...), custom_call_target="tpu_custom_call" | custom-call | flops 20132659200 | bytes 11796480 | tf_op jit(solution)/shard_map/attention_backward/pallas_call | solution.py:171
  671.0 6.2 fusion.42
  682.9 6.7 add_convert_fusion.4
  703.7 6.2 fusion.99
  710.0 7.3 fusion.97
  717.3 4.9 fusion.19
  722.3 5.3 fusion.18
  753.2 6.1 collective-permute-done.24
  766.9 3.9 collective-permute-done.28
  770.9 6.8 collective-permute-done.27
  778.5 3.1 fusion.32
  781.6 3.7 maximum_bitcast_fusion
  (449 shorter events, 172.4 us)
Async XLA Ops:
  7.2 291.4 %all-gather.2.cloned.1.call-start = ((), (), s32[]{:S(2)}) async-start(), calls=%async_computation | async-start | bytes 8650752 | tf_op jit(solution)/shard_map/all_gather | solution.py:541
  131.3 64.5 %collective-permute-start = (bf16[640,1536]{1,0:T(8,128)(2,1)}, bf16[640,1536]{1,0:T(8,128)(2,1)}, u32[]{:S(2)}, u32[]{:S(2)}) collective-permute-start(bf16[640,1536]{1,0:T(8,128)(2,1)} %convolution_convert_fusion.8), channel_id=1, source_target_pairs={{0,1},{1,0},{2,3},{3,2},{4,5},{5,4},{6,7},{7,6},{8,9},{9,8},{10,11... | collective-permute-start | bytes 5898248 | tf_op jit(solution)/shard_map/ppermute | solution.py:400
  222.3 17.1 %collective-permute-start.1 = (bf16[640,512]{1,0:T(8,128)(2,1)S(1)}, bf16[640,512]{1,0:T(8,128)(2,1)S(1)}, u32[]{:S(2)}, u32[]{:S(2)}) collective-permute-start(bf16[640,512]{1,0:T(8,128)(2,1)S(1)} %get-tuple-element.202), channel_id=1, source_target_pairs={{0,1},{1,0},{2,3},{3,2},{4,5},{5,4},{6,7},{7,6},{8,9},{9,8},{10,11... | collective-permute-start | bytes 1966088 | tf_op jit(solution)/shard_map/ppermute | solution.py:400
  239.7 55.0 %collective-permute-start.3 = (bf16[640,1024]{1,0:T(8,128)(2,1)S(1)}, bf16[640,1024]{1,0:T(8,128)(2,1)S(1)}, u32[]{:S(2)}, u32[]{:S(2)}) collective-permute-start(bf16[640,1024]{1,0:T(8,128)(2,1)S(1)} %get-tuple-element.186), channel_id=1, source_target_pairs={{0,1},{1,0},{2,3},{3,2},{4,5},{5,4},{6,7},{7,6},{8,9},{9,8},{10,11... | collective-permute-start | bytes 3932168 | tf_op jit(solution)/shard_map/ppermute | solution.py:400
  294.1 336.3 %collective-permute-start.16 = (bf16[640,1024]{1,0:T(8,128)(2,1)}, bf16[640,1024]{1,0:T(8,128)(2,1)}, u32[]{:S(2)}, u32[]{:S(2)}) collective-permute-start(bf16[640,1024]{1,0:T(8,128)(2,1)} %slice.141), channel_id=1, source_target_pairs={{0,1},{1,0},{2,3},{3,2},{4,5},{5,4},{6,7},{7,6},{8,9},{9,8},{10,11... | collective-permute-start | bytes 3932168 | tf_op jit(solution)/shard_map/ppermute | solution.py:400
  372.0 37.2 %collective-permute-start.2 = (bf16[640,1024]{1,0:T(8,128)(2,1)S(1)}, bf16[640,1024]{1,0:T(8,128)(2,1)}, u32[]{:S(2)}, u32[]{:S(2)}) collective-permute-start(bf16[640,1024]{1,0:T(8,128)(2,1)S(1)} %dynamic-slice_bitcast_fusion.3), channel_id=1, source_target_pairs={{0,1},{1,0},{2,3},{3,2},{4,5},{5,4},{6,7},{7,6},{8,9},{9,8},{10,11... | collective-permute-start | bytes 3932168 | tf_op jit(solution)/shard_map/ppermute | solution.py:400
  375.1 42.5 %collective-permute-start.4 = (bf16[4,2,64,2048]{3,2,1,0:T(8,128)(2,1)}, bf16[4,2,64,2048]{3,2,1,0:T(8,128)(2,1)}, u32[]{:S(2)}, u32[]{:S(2)}) collective-permute-start(bf16[4,2,64,2048]{3,2,1,0:T(8,128)(2,1)} %dynamic-slice_bitcast_fusion.1), channel_id=1, source_target_pairs={{0,2},{2,0},{1,3},{3,1},{4,6},{6,4},{5,7},{7,5},{8,10},{10,8},{9,1... | collective-permute-start | bytes 6291464 | tf_op jit(solution)/shard_map/ppermute | solution.py:400
  376.8 36.2 %collective-permute-start.5 = (bf16[4,2,64,2048]{3,2,1,0:T(8,128)(2,1)}, bf16[4,2,64,2048]{3,2,1,0:T(8,128)(2,1)}, u32[]{:S(2)}, u32[]{:S(2)}) collective-permute-start(bf16[4,2,64,2048]{3,2,1,0:T(8,128)(2,1)} %dynamic-slice_bitcast_fusion), channel_id=1, source_target_pairs={{0,2},{2,0},{1,3},{3,1},{4,6},{6,4},{5,7},{7,5},{8,10},{10,8},{9,1... | collective-permute-start | bytes 6291464 | tf_op jit(solution)/shard_map/ppermute | solution.py:400
  431.4 15.8 %collective-permute-start.10 = (bf16[2,64,2048]{2,1,0:T(8,128)(2,1)S(1)}, bf16[2,64,2048]{2,1,0:T(8,128)(2,1)S(1)}, u32[]{:S(2)}, u32[]{:S(2)}) collective-permute-start(bf16[2,64,2048]{2,1,0:T(8,128)(2,1)S(1)} %get-tuple-element.217), channel_id=1, source_target_pairs={{0,5},{1,4},{4,1},{5,0},{2,7},{3,6},{6,3},{7,2},{8,13},{9,12},{12,... | collective-permute-start | bytes 1572872 | tf_op jit(solution)/shard_map/ppermute | solution.py:400
  433.2 25.2 %collective-permute-start.7 = (bf16[2,64,2048]{2,1,0:T(8,128)(2,1)S(1)}, bf16[2,64,2048]{2,1,0:T(8,128)(2,1)S(1)}, u32[]{:S(2)}, u32[]{:S(2)}) collective-permute-start(bf16[2,64,2048]{2,1,0:T(8,128)(2,1)S(1)} %get-tuple-element.216), channel_id=1, source_target_pairs={{0,1},{1,0},{4,5},{5,4},{2,3},{3,2},{6,7},{7,6},{8,9},{9,8},{12,13... | collective-permute-start | bytes 1572872 | tf_op jit(solution)/shard_map/ppermute | solution.py:400
  434.4 24.5 %collective-permute-start.6 = (bf16[2,64,2048]{2,1,0:T(8,128)(2,1)S(1)}, bf16[2,64,2048]{2,1,0:T(8,128)(2,1)S(1)}, u32[]{:S(2)}, u32[]{:S(2)}) collective-permute-start(bf16[2,64,2048]{2,1,0:T(8,128)(2,1)S(1)} %dynamic-slice_bitcast_fusion.14), channel_id=1, source_target_pairs={{0,4},{1,5},{4,0},{5,1},{2,6},{3,7},{6,2},{7,3},{8,12},{9,13},{12,... | collective-permute-start | bytes 1572872 | tf_op jit(solution)/shard_map/ppermute | solution.py:400
  435.1 37.4 %collective-permute-start.13 = (bf16[2,64,2048]{2,1,0:T(8,128)(2,1)S(1)}, bf16[2,64,2048]{2,1,0:T(8,128)(2,1)S(1)}, u32[]{:S(2)}, u32[]{:S(2)}) collective-permute-start(bf16[2,64,2048]{2,1,0:T(8,128)(2,1)S(1)} %get-tuple-element.215), channel_id=1, source_target_pairs={{0,5},{1,4},{4,1},{5,0},{2,7},{3,6},{6,3},{7,2},{8,13},{9,12},{12,... | collective-permute-start | bytes 1572872 | tf_op jit(solution)/shard_map/ppermute | solution.py:400
  447.2 32.1 %collective-permute-start.9 = (bf16[2,64,2048]{2,1,0:T(8,128)(2,1)S(1)}, bf16[2,64,2048]{2,1,0:T(8,128)(2,1)S(1)}, u32[]{:S(2)}, u32[]{:S(2)}) collective-permute-start(bf16[2,64,2048]{2,1,0:T(8,128)(2,1)S(1)} %get-tuple-element.214), channel_id=1, source_target_pairs={{0,1},{1,0},{4,5},{5,4},{2,3},{3,2},{6,7},{7,6},{8,9},{9,8},{12,13... | collective-permute-start | bytes 1572872 | tf_op jit(solution)/shard_map/ppermute | solution.py:400
  458.4 20.8 %collective-permute-start.8 = (bf16[2,64,2048]{2,1,0:T(8,128)(2,1)S(1)}, bf16[2,64,2048]{2,1,0:T(8,128)(2,1)S(1)}, u32[]{:S(2)}, u32[]{:S(2)}) collective-permute-start(bf16[2,64,2048]{2,1,0:T(8,128)(2,1)S(1)} %dynamic-slice_bitcast_fusion.11), channel_id=1, source_target_pairs={{0,4},{1,5},{4,0},{5,1},{2,6},{3,7},{6,2},{7,3},{8,12},{9,13},{12,... | collective-permute-start | bytes 1572872 | tf_op jit(solution)/shard_map/ppermute | solution.py:400
  459.0 75.6 %collective-permute-start.11 = (bf16[4,2,64,2048]{3,2,0,1:T(8,128)(2,1)}, bf16[4,2,64,2048]{3,2,0,1:T(8,128)(2,1)}, u32[]{:S(2)}, u32[]{:S(2)}) collective-permute-start(bf16[4,2,64,2048]{3,2,0,1:T(8,128)(2,1)} %bitcast.297), channel_id=1, source_target_pairs={{0,2},{2,0},{1,3},{3,1},{4,6},{6,4},{5,7},{7,5},{8,10},{10,8},{9,1... | collective-permute-start | bytes 6291464 | tf_op jit(solution)/shard_map/ppermute | solution.py:400
  516.7 22.6 %collective-permute-start.12 = (bf16[4,2,64,2048]{3,2,0,1:T(8,128)(2,1)}, bf16[4,2,64,2048]{3,2,0,1:T(8,128)(2,1)}, u32[]{:S(2)}, u32[]{:S(2)}) collective-permute-start(bf16[4,2,64,2048]{3,2,0,1:T(8,128)(2,1)} %bitcast.296), channel_id=1, source_target_pairs={{0,2},{2,0},{1,3},{3,1},{4,6},{6,4},{5,7},{7,5},{8,10},{10,8},{9,1... | collective-permute-start | bytes 6291464 | tf_op jit(solution)/shard_map/ppermute | solution.py:400
  517.8 67.0 %collective-permute-start.42 = (bf16[64,2048]{1,0:T(8,128)(2,1)}, bf16[64,2048]{1,0:T(8,128)(2,1)S(1)}, u32[]{:S(2)}, u32[]{:S(2)}) collective-permute-start(bf16[64,2048]{1,0:T(8,128)(2,1)} %get-tuple-element.206), channel_id=1, source_target_pairs={{0,24},{8,16},{16,8},{24,0},{1,25},{9,17},{17,9},{25,1},{2,26},{10... | collective-permute-start | bytes 786440 | tf_op jit(solution)/shard_map/ppermute | solution.py:400
  519.1 65.7 %collective-permute-start.41 = (bf16[64,2048]{1,0:T(8,128)(2,1)}, bf16[64,2048]{1,0:T(8,128)(2,1)S(1)}, u32[]{:S(2)}, u32[]{:S(2)}) collective-permute-start(bf16[64,2048]{1,0:T(8,128)(2,1)} %get-tuple-element.205), channel_id=1, source_target_pairs={{0,16},{8,24},{16,0},{24,8},{1,17},{9,25},{17,1},{25,9},{2,18},{10... | collective-permute-start | bytes 786440 | tf_op jit(solution)/shard_map/ppermute | solution.py:400
  534.5 52.7 %collective-permute-start.40 = (bf16[64,2048]{1,0:T(8,128)(2,1)}, bf16[64,2048]{1,0:T(8,128)(2,1)S(1)}, u32[]{:S(2)}, u32[]{:S(2)}) collective-permute-start(bf16[64,2048]{1,0:T(8,128)(2,1)} %get-tuple-element.204), channel_id=1, source_target_pairs={{0,8},{8,0},{16,24},{24,16},{1,9},{9,1},{17,25},{25,17},{2,10},{10... | collective-permute-start | bytes 786440 | tf_op jit(solution)/shard_map/ppermute | solution.py:400
  547.3 45.4 %collective-permute-start.15 = (bf16[640,512]{1,0:T(8,128)(2,1)}, bf16[640,512]{1,0:T(8,128)(2,1)}, u32[]{:S(2)}, u32[]{:S(2)}) collective-permute-start(bf16[640,512]{1,0:T(8,128)(2,1)} %convolution_convert_fusion.13), channel_id=1, source_target_pairs={{0,1},{1,0},{2,3},{3,2},{4,5},{5,4},{6,7},{7,6},{8,9},{9,8},{10,11... | collective-permute-start | bytes 1966088 | tf_op jit(solution)/shard_map/ppermute | solution.py:400
  584.8 6.1 collective-permute-start.31
  584.9 7.6 collective-permute-start.29
  589.7 49.5 %collective-permute-start.14 = (bf16[4,2,64,1536]{3,2,0,1:T(8,128)(2,1)S(1)}, bf16[4,2,64,1536]{3,2,0,1:T(8,128)(2,1)}, u32[]{:S(2)}, u32[]{:S(2)}) collective-permute-start(bf16[4,2,64,1536]{3,2,0,1:T(8,128)(2,1)S(1)} %bitcast.329), channel_id=1, source_target_pairs={{0,2},{2,0},{1,3},{3,1},{4,6},{6,4},{5,7},{7,5},{8,10},{10,8},{9,1... | collective-permute-start | bytes 4718600 | tf_op jit(solution)/shard_map/ppermute | solution.py:400
  590.9 44.7 %collective-permute-start.18 = (bf16[4,64,2048]{2,1,0:T(8,128)(2,1)}, bf16[4,64,2048]{2,1,0:T(8,128)(2,1)}, u32[]{:S(2)}, u32[]{:S(2)}) collective-permute-start(bf16[4,64,2048]{2,1,0:T(8,128)(2,1)} %dynamic-slice_bitcast_fusion.5), channel_id=1, source_target_pairs={{0,4},{4,0},{1,5},{5,1},{2,6},{6,2},{3,7},{7,3},{8,12},{12,8},{9,1... | collective-permute-start | bytes 3145736 | tf_op jit(solution)/shard_map/ppermute | solution.py:400
  629.3 50.7 %collective-permute-start.22 = (bf16[640,1024]{1,0:T(8,128)(2,1)}, bf16[640,1024]{1,0:T(8,128)(2,1)}, u32[]{:S(2)}, u32[]{:S(2)}) collective-permute-start(bf16[640,1024]{1,0:T(8,128)(2,1)} %dynamic-slice_convert_fusion.1), channel_id=1, source_target_pairs={{0,1},{1,0},{2,3},{3,2},{4,5},{5,4},{6,7},{7,6},{8,9},{9,8},{10,11... | collective-permute-start | bytes 3932168 | tf_op jit(solution)/shard_map/ppermute | solution.py:400
  631.6 58.5 %collective-permute-start.20 = (bf16[4,64,2048]{2,1,0:T(8,128)(2,1)}, bf16[4,64,2048]{2,1,0:T(8,128)(2,1)}, u32[]{:S(2)}, u32[]{:S(2)}) collective-permute-start(bf16[4,64,2048]{2,1,0:T(8,128)(2,1)} %dynamic-slice_bitcast_fusion.4), channel_id=1, source_target_pairs={{0,4},{4,0},{1,5},{5,1},{2,6},{6,2},{3,7},{7,3},{8,12},{12,8},{9,1... | collective-permute-start | bytes 3145736 | tf_op jit(solution)/shard_map/ppermute | solution.py:400
  638.3 51.8 %collective-permute-start.19 = (bf16[4,64,2048]{2,1,0:T(8,128)(2,1)}, bf16[4,64,2048]{2,1,0:T(8,128)(2,1)}, u32[]{:S(2)}, u32[]{:S(2)}) collective-permute-start(bf16[4,64,2048]{2,1,0:T(8,128)(2,1)} %fusion.41), channel_id=1, source_target_pairs={{0,1},{1,0},{2,3},{3,2},{4,5},{5,4},{6,7},{7,6},{8,9},{9,8},{10,11... | collective-permute-start | bytes 3145736 | tf_op jit(solution)/shard_map/ppermute | solution.py:400
  642.3 40.6 %collective-permute-start.17 = (bf16[4,64,1536]{2,1,0:T(8,128)(2,1)}, bf16[4,64,1536]{2,1,0:T(8,128)(2,1)}, u32[]{:S(2)}, u32[]{:S(2)}) collective-permute-start(bf16[4,64,1536]{2,1,0:T(8,128)(2,1)} %dynamic-slice_bitcast_fusion.7), channel_id=1, source_target_pairs={{0,4},{4,0},{1,5},{5,1},{2,6},{6,2},{3,7},{7,3},{8,12},{12,8},{9,1... | collective-permute-start | bytes 2359304 | tf_op jit(solution)/shard_map/ppermute | solution.py:400
  670.3 9.0 %collective-permute-start.32 = (bf16[4,64,512]{2,1,0:T(8,128)(2,1)S(1)}, bf16[4,64,512]{2,1,0:T(8,128)(2,1)S(1)}, u32[]{:S(2)}, u32[]{:S(2)}) collective-permute-start(bf16[4,64,512]{2,1,0:T(8,128)(2,1)S(1)} %dynamic-slice_bitcast_fusion.19), channel_id=1, source_target_pairs={{0,4},{4,0},{1,5},{5,1},{2,6},{6,2},{3,7},{7,3},{8,12},{12,8},{9,1... | collective-permute-start | bytes 786440 | tf_op jit(solution)/shard_map/ppermute | solution.py:400
  679.3 10.7 %collective-permute-start.30 = (bf16[4,64,512]{2,1,0:T(8,128)(2,1)S(1)}, bf16[4,64,512]{2,1,0:T(8,128)(2,1)S(1)}, u32[]{:S(2)}, u32[]{:S(2)}) collective-permute-start(bf16[4,64,512]{2,1,0:T(8,128)(2,1)S(1)} %dynamic-slice_bitcast_fusion.20), channel_id=1, source_target_pairs={{0,4},{4,0},{1,5},{5,1},{2,6},{6,2},{3,7},{7,3},{8,12},{12,8},{9,1... | collective-permute-start | bytes 786440 | tf_op jit(solution)/shard_map/ppermute | solution.py:400
  680.0 9.9 %collective-permute-start.33 = (bf16[4,64,512]{2,1,0:T(8,128)(2,1)S(1)}, bf16[4,64,512]{2,1,0:T(8,128)(2,1)S(1)}, u32[]{:S(2)}, u32[]{:S(2)}) collective-permute-start(bf16[4,64,512]{2,1,0:T(8,128)(2,1)S(1)} %fusion.63), channel_id=1, source_target_pairs={{0,1},{1,0},{2,3},{3,2},{4,5},{5,4},{6,7},{7,6},{8,9},{9,8},{10,11... | collective-permute-start | bytes 786440 | tf_op jit(solution)/shard_map/ppermute | solution.py:400
  689.9 10.2 %collective-permute-start.21 = (bf16[4,2,64,1536]{3,2,0,1:T(8,128)(2,1)S(1)}, bf16[4,2,64,1536]{3,2,0,1:T(8,128)(2,1)S(1)}, u32[]{:S(2)}, u32[]{:S(2)}) collective-permute-start(bf16[4,2,64,1536]{3,2,0,1:T(8,128)(2,1)S(1)} %bitcast.330), channel_id=1, source_target_pairs={{0,2},{2,0},{1,3},{3,1},{4,6},{6,4},{5,7},{7,5},{8,10},{10,8},{9,1... | collective-permute-start | bytes 4718600 | tf_op jit(solution)/shard_map/ppermute | solution.py:400
  694.9 58.3 %collective-permute-start.25 = (bf16[4,64,1536]{2,1,0:T(8,128)(2,1)}, bf16[4,64,1536]{2,1,0:T(8,128)(2,1)}, u32[]{:S(2)}, u32[]{:S(2)}) collective-permute-start(bf16[4,64,1536]{2,1,0:T(8,128)(2,1)} %fusion.47), channel_id=1, source_target_pairs={{0,1},{1,0},{2,3},{3,2},{4,5},{5,4},{6,7},{7,6},{8,9},{9,8},{10,11... | collective-permute-start | bytes 2359304 | tf_op jit(solution)/shard_map/ppermute | solution.py:400
  696.0 47.1 %collective-permute-start.36 = (bf16[64,512]{1,0:T(8,128)(2,1)S(1)}, bf16[64,512]{1,0:T(8,128)(2,1)S(1)}, u32[]{:S(2)}, u32[]{:S(2)}) collective-permute-start(bf16[64,512]{1,0:T(8,128)(2,1)S(1)} %get-tuple-element.222), channel_id=1, source_target_pairs={{0,24},{8,16},{16,8},{24,0},{1,25},{9,17},{17,9},{25,1},{2,26},{10... | collective-permute-start | bytes 196616 | tf_op jit(solution)/shard_map/ppermute | solution.py:400
  697.6 30.1 %collective-permute-start.39 = (bf16[64,2048]{1,0:T(8,128)(2,1)S(1)}, bf16[64,2048]{1,0:T(8,128)(2,1)S(1)}, u32[]{:S(2)}, u32[]{:S(2)}) collective-permute-start(bf16[64,2048]{1,0:T(8,128)(2,1)S(1)} %get-tuple-element.208), channel_id=1, source_target_pairs={{0,24},{8,16},{16,8},{24,0},{1,25},{9,17},{17,9},{25,1},{2,26},{10... | collective-permute-start | bytes 786440 | tf_op jit(solution)/shard_map/ppermute | solution.py:400
  700.1 29.9 %collective-permute-start.38 = (bf16[64,2048]{1,0:T(8,128)(2,1)S(1)}, bf16[64,2048]{1,0:T(8,128)(2,1)S(1)}, u32[]{:S(2)}, u32[]{:S(2)}) collective-permute-start(bf16[64,2048]{1,0:T(8,128)(2,1)S(1)} %get-tuple-element.209), channel_id=1, source_target_pairs={{0,16},{8,24},{16,0},{24,8},{1,17},{9,25},{17,1},{25,9},{2,18},{10... | collective-permute-start | bytes 786440 | tf_op jit(solution)/shard_map/ppermute | solution.py:400
  700.1 33.5 %collective-permute-start.37 = (bf16[64,2048]{1,0:T(8,128)(2,1)S(1)}, bf16[64,2048]{1,0:T(8,128)(2,1)}, u32[]{:S(2)}, u32[]{:S(2)}) collective-permute-start(bf16[64,2048]{1,0:T(8,128)(2,1)S(1)} %get-tuple-element.207), channel_id=1, source_target_pairs={{0,8},{8,0},{16,24},{24,16},{1,9},{9,1},{17,25},{25,17},{2,10},{10... | collective-permute-start | bytes 786440 | tf_op jit(solution)/shard_map/ppermute | solution.py:400
  728.5 10.3 %collective-permute-start.45 = (f32[8,1024]{1,0:T(8,128)S(1)}, f32[8,1024]{1,0:T(8,128)S(1)}, u32[]{:S(2)}, u32[]{:S(2)}) collective-permute-start(f32[8,1024]{1,0:T(8,128)S(1)} %concatenate.43), channel_id=1, source_target_pairs={{0,5},{1,4},{4,1},{5,0},{2,7},{3,6},{6,3},{7,2},{8,13},{9,12},{12,... | collective-permute-start | bytes 98312 | tf_op jit(solution)/shard_map/ppermute | solution.py:400
  730.7 9.1 %collective-permute-start.44 = (f32[8,1024]{1,0:T(8,128)S(1)}, f32[8,1024]{1,0:T(8,128)S(1)}, u32[]{:S(2)}, u32[]{:S(2)}) collective-permute-start(f32[8,1024]{1,0:T(8,128)S(1)} %concatenate.43), channel_id=1, source_target_pairs={{0,4},{1,5},{4,0},{5,1},{2,6},{3,7},{6,2},{7,3},{8,12},{9,13},{12,... | collective-permute-start | bytes 98312 | tf_op jit(solution)/shard_map/ppermute | solution.py:400
  733.6 8.2 %collective-permute-start.43 = (f32[8,1024]{1,0:T(8,128)S(1)}, f32[8,1024]{1,0:T(8,128)S(1)}, u32[]{:S(2)}, u32[]{:S(2)}) collective-permute-start(f32[8,1024]{1,0:T(8,128)S(1)} %concatenate.43), channel_id=1, source_target_pairs={{0,1},{1,0},{4,5},{5,4},{2,3},{3,2},{6,7},{7,6},{8,9},{9,8},{12,13... | collective-permute-start | bytes 98312 | tf_op jit(solution)/shard_map/ppermute | solution.py:400
  741.8 17.4 %collective-permute-start.24 = (bf16[4,64,1536]{2,1,0:T(8,128)(2,1)}, bf16[4,64,1536]{2,1,0:T(8,128)(2,1)}, u32[]{:S(2)}, u32[]{:S(2)}) collective-permute-start(bf16[4,64,1536]{2,1,0:T(8,128)(2,1)} %dynamic-slice_bitcast_fusion.6), channel_id=1, source_target_pairs={{0,4},{4,0},{1,5},{5,1},{2,6},{6,2},{3,7},{7,3},{8,12},{12,8},{9,1... | collective-permute-start | bytes 2359304 | tf_op jit(solution)/shard_map/ppermute | solution.py:400
  743.2 7.7 collective-permute-start.48
  744.6 7.2 collective-permute-start.47
  745.0 6.9 collective-permute-start.46
  750.9 27.6 %collective-permute-start.23 = (bf16[640,1024]{1,0:T(8,128)(2,1)}, bf16[640,1024]{1,0:T(8,128)(2,1)}, u32[]{:S(2)}, u32[]{:S(2)}) collective-permute-start(bf16[640,1024]{1,0:T(8,128)(2,1)} %fusion.50), channel_id=1, source_target_pairs={{0,1},{1,0},{2,3},{3,2},{4,5},{5,4},{6,7},{7,6},{8,9},{9,8},{10,11... | collective-permute-start | bytes 3932168 | tf_op jit(solution)/shard_map/ppermute | solution.py:400
  761.2 9.6 %collective-permute-start.28 = (bf16[64,1536]{1,0:T(8,128)(2,1)S(1)}, bf16[64,1536]{1,0:T(8,128)(2,1)S(1)}, u32[]{:S(2)}, u32[]{:S(2)}) collective-permute-start(bf16[64,1536]{1,0:T(8,128)(2,1)S(1)} %get-tuple-element.219), channel_id=1, source_target_pairs={{0,24},{8,16},{16,8},{24,0},{1,25},{9,17},{17,9},{25,1},{2,26},{10... | collective-permute-start | bytes 589832 | tf_op jit(solution)/shard_map/ppermute | solution.py:400
  762.7 15.0 %collective-permute-start.27 = (bf16[64,1536]{1,0:T(8,128)(2,1)S(1)}, bf16[64,1536]{1,0:T(8,128)(2,1)S(1)}, u32[]{:S(2)}, u32[]{:S(2)}) collective-permute-start(bf16[64,1536]{1,0:T(8,128)(2,1)S(1)} %get-tuple-element.220), channel_id=1, source_target_pairs={{0,16},{8,24},{16,0},{24,8},{1,17},{9,25},{17,1},{25,9},{2,18},{10... | collective-permute-start | bytes 589832 | tf_op jit(solution)/shard_map/ppermute | solution.py:400
  763.1 14.5 %collective-permute-start.26 = (bf16[64,1536]{1,0:T(8,128)(2,1)S(1)}, bf16[64,1536]{1,0:T(8,128)(2,1)S(1)}, u32[]{:S(2)}, u32[]{:S(2)}) collective-permute-start(bf16[64,1536]{1,0:T(8,128)(2,1)S(1)} %get-tuple-element.218), channel_id=1, source_target_pairs={{0,8},{8,0},{16,24},{24,16},{1,9},{9,1},{17,25},{25,17},{2,10},{10... | collective-permute-start | bytes 589832 | tf_op jit(solution)/shard_map/ppermute | solution.py:400
  (111 other events, 1158.8 us)
Sparse Core Ops, SparseCore 0:
  132.0 84.4 all-gather.1

commit v10 on v9

--- a/solution.py
+++ b/solution.py
@@ -697,7 +697,7 @@
     input_rows = rows_back(grad_x)
     z_up = scatter_z(z_up_part, grad_x)
     z_out = scatter_z(z_out_part, grad_x)
-    sums = after(jnp.concatenate([sums_0, sums_1, sums_2, sums_3]), grad_x)
+    sums = after(jnp.concatenate([sums_0, sums_1, sums_2, sums_3]), qkv_y[0][1])
     sums = sum_everywhere(sums).reshape(4, 2, width)
     return (
         out_rows,

time: 796 us -> 830 us (1.043)
  waiting for transfers between devices: 56.6 us -> 90.7 us
    ppermute x50, waiting for transfers between devices: 56.6 us -> 90.7 us  [send(): return lax.ppermute(values, axes, [(s, s ^ distance) for s in range(count)])]
    unnamed x222 -> x228, local copies, waits for them, and re-layouts: 19.2 us -> 19.1 us
  transfers between devices with their start and end apart: 51 -> 51, of which waited for: 10 -> 11; matrix products, arithmetic and copies ran while one was open for 48% -> 46% of each run, Pallas kernels for 18% -> 18%
where the time goes in v10:
time: 830 us; the launch traced here: 826 us
  matrix products  257 us (31%)
  Pallas kernels  253 us (30%)
  other arithmetic  104 us (13%)
  waiting for transfers between devices  90.7 us (11%)
  local copies, waits for them, and re-layouts  53.4 us (6%)
  starting transfers between devices  50.9 us (6%)
  between operations  16.5 us (2%)
    pallas_call x1, Pallas kernels, gather_weights(): pl.pallas_call(functools.partial(gather_kernel, chunks, len(shards), move...  108 us
    dot_general x12, matrix products, dot_nn(): lax.dot_general(a, b, (((1,), (0,)), ((), ())), preferred_element_type=f32)  98.1 us
    ppermute x50, waiting for transfers between devices, send(): return lax.ppermute(values, axes, [(s, s ^ distance) for s in range(count)])  90.7 us
    dot_general x9, matrix products, dot_nt(): lax.dot_general(a, b, (((1,), (1,)), ((), ())), preferred_element_type=f32)  86.8 us
    pallas_call x3, Pallas kernels, attention_backward(): pl.pallas_call(attention_backward_kernel, name='attention_backward', out_...  80 us
    dot_general x9, matrix products, dot_tn(): lax.dot_general(a, b, (((0,), (0,)), ((), ())), preferred_element_type=f32)  72.4 us
    pallas_call x3, Pallas kernels, attention_forward(): pl.pallas_call(attention_forward_kernel, name='attention_forward', out_sh...  64.7 us
    ppermute x50, starting transfers between devices, send(): return lax.ppermute(values, axes, [(s, s ^ distance) for s in range(count)])  50.8 us
  transfers between devices with their start and end apart: 51, of which 11 were waited for; matrix products, arithmetic and copies ran while one was open for 46% of the time, Pallas kernels for 18%

profile of v10, /device:TPU:0, one launch (start us, length us, event | category | flops | bytes accessed | tf_op | source)
XLA Modules:
  0.0 825.8 jit_solution(9207885241187249163)
XLA Ops:
  11.6 108.2 %gather_weights.1 = (bf16[4,2,2,64,1536]{4,3,2,1,0:T(8,128)(2,1)}, bf16[4,2,2,64,1536]{4,3,2,1,0:T(8,128)(2,1)}, bf16[4,2,2,64,512]{4,3,2,1,0:T(8,128)(2,1)}, bf...) custom-call(bf16[64,1536]{1,0:T(8,128)(2,1)} %bitcast.337, ...), custom_call_target="tpu_custom_call" | custom-call | bytes 33554432 | tf_op jit(solution)/shard_map/gather_weights/pallas_call | solution.py:374
  127.8 3.5 convolution_convert_fusion.8
  131.9 9.0 %convolution_convert_fusion.q_ref.k_ref.v_ref = bf16[1280,1536]{1,0:T(8,128)(2,1)} fusion(bf16[1024,1536]{1,0:T(8,128)(2,1)} %bitcast.378, bf16[1920,1024]{1,0:T(8,128)(2,1)} %copy-done.29), kind=kOutput, calls=%fused_computation.51 | convolution fusion | flops 4028497920 | bytes 9699328 | tf_op jit(solution)/shard_map/dot_general | solution.py:23
  140.9 5.7 convolution_convert_fusion.1.q_ref.k_ref.v_ref
  152.4 21.5 %attention_forward.5 = (bf16[1280,512]{1,0:T(8,128)(2,1)S(1)}, f32[4,8,1280]{2,1,0:T(8,128)S(1)}) custom-call(bf16[1280,1536]{1,0:T(8,128)(2,1)S(1)} %copy-done.12, bf16[1280,1536]{1,0:T(8,128)(2,1)S(1)} %copy-done.12, bf16[1280,1536]{1,0:T(8,128)(2,1)S(1)} %copy-done.12, s32[1280,8]{1,0:T(8,128)S(1)} %pad.14.clone.col_ref, s32[8,1280]{1,0:T(8,128)S(1)} %pad.15.row_ref), custom_call_target="tpu_custom_call" | custom-call | flops 8053063680 | bytes 5898240 | tf_op jit(solution)/shard_map/attention_forward/pallas_call | solution.py:80
  174.0 21.7 %attention_forward.3 = (bf16[1280,512]{1,0:T(8,128)(2,1)S(1)}, f32[4,8,1280]{2,1,0:T(8,128)S(1)}) custom-call(bf16[1280,1536]{1,0:T(8,128)(2,1)S(1)} %copy-done.10, bf16[1280,1536]{1,0:T(8,128)(2,1)S(1)} %copy-done.10, bf16[1280,1536]{1,0:T(8,128)(2,1)S(1)} %copy-done.10, s32[1280,8]{1,0:T(8,128)S(1)} %pad.14.clone.col_ref, s32[8,1280]{1,0:T(8,128)S(1)} %pad.15.row_ref), custom_call_target="tpu_custom_call" | custom-call | flops 8053063680 | bytes 5898240 | tf_op jit(solution)/shard_map/attention_forward/pallas_call | solution.py:80
  195.8 4.6 broadcast_select_fusion.3
  200.6 21.5 %attention_forward.4 = (bf16[1280,512]{1,0:T(8,128)(2,1)S(1)}, f32[4,8,1280]{2,1,0:T(8,128)S(1)}) custom-call(bf16[1280,1536]{1,0:T(8,128)(2,1)S(1)} %pad_maximum_fusion.2.q_ref.k_ref.v_ref, bf16[1280,1536]{1,0:T(8,128)(2,1)S(1)} %pad_maximum_fusion.2.q_ref.k_ref.v_ref, bf16[1280,1536]{1,0:T(8,128)(2,1)S(1)} %pad_maximum_fusion.2.q_ref.k_ref.v_ref, ...), custom_call_target="tpu_custom_call" | custom-call | flops 8053063680 | bytes 5898240 | tf_op jit(solution)/shard_map/attention_forward/pallas_call | solution.py:80
  226.4 12.9 %collective-permute-done.1 = bf16[640,512]{1,0:T(8,128)(2,1)S(1)} collective-permute-done((bf16[640,512]{1,0:T(8,128)(2,1)S(1)}, bf16[640,512]{1,0:T(8,128)(2,1)S(1)}, u32[]{:S(2)}, u32[]{:S(2)}) %collective-permute-start.1) | collective-permute-done | bytes 655392 | tf_op jit(solution)/shard_map/ppermute | solution.py:400
  256.5 20.7 %add_convert_fusion.1 = (bf16[1920,2048]{1,0:T(8,128)(2,1)}, bf16[1920,2048]{1,0:T(8,128)(2,1)}) fusion(bf16[1920,1024]{1,0:T(8,128)(2,1)S(1)} %add_convert_fusion.3, bf16[1024,2048]{1,0:T(8,128)(2,1)} %bitcast.370), kind=kOutput, calls=%fused_computation.6 | convolution fusion | flops 8112046080 | bytes 23855104 | tf_op jit(solution)/shard_map/dot_general | solution.py:23
  277.3 16.9 %add_convert_fusion = (bf16[1920,2048]{1,0:T(8,128)(2,1)}, bf16[1920,2048]{1,0:T(8,128)(2,1)}) fusion(bf16[1920,1024]{1,0:T(8,128)(2,1)S(1)} %add_convert_fusion.3, bf16[1024,2048]{1,0:T(8,128)(2,1)S(1)} %bitcast.372), kind=kOutput, calls=%fused_computation.2 | convolution fusion | flops 8112046080 | bytes 23855104 | tf_op jit(solution)/shard_map/dot_general | solution.py:23
  298.5 15.7 %fusion.57 = f32[1920,1024]{1,0:T(8,128)} fusion(bf16[1920,2048]{1,0:T(8,128)(2,1)} %get-tuple-element.73, pred[]{:T(512)S(6)} %eq.30, bf16[2048,2048]{1,0:T(8,128)(2,1)} %all-gather.2.cloned.1.call-done), kind=kOutput, calls=%fused_computation.175 | convolution fusion | flops 8055160832 | bytes 24117248 | tf_op jit(solution)/shard_map/dot_general | solution.py:27
  314.3 15.3 %fusion.96 = (f32[1920]{0:T(1024)S(1)}, f32[1920,1024]{1,0:T(8,128)}) fusion(f32[1920,1024]{1,0:T(8,128)} %fusion.57, bf16[1920,2048]{1,0:T(8,128)(2,1)} %get-tuple-element.76, pred[]{:T(512)S(6)} %eq.31, bf16[2048,2048]{1,0:T(8,128)(2,1)S(1)} %copy-done.90), kind=kOutput, calls=%fused_computation.297 | convolution fusion | flops 8059090944 | bytes 31989248 | tf_op jit(solution)/shard_map/dot_general | solution.py:27
  329.6 4.3 multiply_reduce_fusion.4
  335.1 4.8 fusion.25
  339.9 4.7 fusion.23
  344.7 14.2 %convolution_convert_fusion.5 = bf16[1024,2048]{1,0:T(8,128)(2,1)S(1)} fusion(bf16[1920,1024]{1,0:T(8,128)(2,1)} %get-tuple-element.174, bf16[1920,2048]{1,0:T(8,128)(2,1)} %get-tuple-element.73), kind=kOutput, calls=%fused_computation.79 | convolution fusion | flops 8055160832 | bytes 15990784 | tf_op jit(solution)/shard_map/dot_general | solution.py:31
  358.8 13.1 %convolution_convert_fusion.4 = bf16[1024,2048]{1,0:T(8,128)(2,1)S(1)} fusion(bf16[1920,1024]{1,0:T(8,128)(2,1)S(1)} %copy-done.40, bf16[1920,2048]{1,0:T(8,128)(2,1)} %get-tuple-element.76), kind=kOutput, calls=%fused_computation.78 | convolution fusion | flops 8055160832 | bytes 15990784 | tf_op jit(solution)/shard_map/dot_general | solution.py:31
  378.0 14.5 %multiply_convert_fusion = bf16[1920,2048]{1,0:T(8,128)(2,1)} fusion(bf16[1920,2048]{1,0:T(8,128)(2,1)} %get-tuple-element.81, bf16[1920,1024]{1,0:T(8,128)(2,1)S(1)} %copy-done.41, pred[]{:T(512)S(6)} %eq.31, bf16[2048,2048]{1,0:T(8,128)(2,1)} %all-gather.2.cloned.1.call-done), kind=kOutput, calls=%fused_computation | convolution fusion | flops 8066957312 | bytes 28049408 | tf_op jit(solution)/shard_map/dot_general | solution.py:23
  392.6 16.7 %multiply_convert_fusion.1 = bf16[1920,2048]{1,0:T(8,128)(2,1)} fusion(bf16[1920,2048]{1,0:T(8,128)(2,1)} %get-tuple-element.78, bf16[1920,1024]{1,0:T(8,128)(2,1)} %get-tuple-element.174, pred[]{:T(512)S(6)} %eq.30, bf16[2048,2048]{1,0:T(8,128)(2,1)} %all-gather.2.cloned.1.call-done), kind=kOutput, calls=%fused_computation.1 | convolution fusion | flops 8066957312 | bytes 28049408 | tf_op jit(solution)/shard_map/dot_general | solution.py:23
  414.5 3.1 fusion.28
  421.4 10.0 %convolution_convert_fusion.3 = bf16[1024,2048]{1,0:T(8,128)(2,1)S(1)} fusion(bf16[1920,1024]{1,0:T(8,128)(2,1)S(1)} %copy-done.43, bf16[1920,2048]{1,0:T(8,128)(2,1)S(1)} %bitcast.385), kind=kOutput, calls=%fused_computation.77 | convolution fusion | flops 8055160832 | bytes 15990784 | tf_op jit(solution)/shard_map/dot_general | solution.py:31
  440.6 6.7 collective-permute-done.10
  448.1 10.5 %collective-permute-done.7 = bf16[2,64,2048]{2,1,0:T(8,128)(2,1)S(1)} collective-permute-done((bf16[2,64,2048]{2,1,0:T(8,128)(2,1)S(1)}, bf16[2,64,2048]{2,1,0:T(8,128)(2,1)S(1)}, u32[]{:S(2)}, u32[]{:S(2)}) %collective-permute-start.7) | collective-permute-done | bytes 524320 | tf_op jit(solution)/shard_map/ppermute | solution.py:400
  459.5 13.1 %convolution_convert_fusion.2 = bf16[1024,2048]{1,0:T(8,128)(2,1)} fusion(bf16[1920,1024]{1,0:T(8,128)(2,1)S(1)} %copy-done.43, bf16[1920,2048]{1,0:T(8,128)(2,1)} %multiply_convert_fusion), kind=kOutput, calls=%fused_computation.76 | convolution fusion | flops 8055160832 | bytes 15990784 | tf_op jit(solution)/shard_map/dot_general | solution.py:31
  472.6 6.8 collective-permute-done.9
  479.9 12.8 %fusion.98 = f32[1920,1024]{1,0:T(8,128)} fusion(bf16[1920,2048]{1,0:T(8,128)(2,1)} %multiply_convert_fusion, bf16[1024,2048]{1,0:T(8,128)(2,1)S(1)} %bitcast.373), kind=kOutput, calls=%fused_computation.299 | convolution fusion | flops 8053063680 | bytes 19922944 | tf_op jit(solution)/shard_map/dot_general | solution.py:27
  492.7 18.3 %multiply_reduce_fusion = (f32[1024]{0:T(1024)}, f32[1920]{0:T(1024)S(1)}, f32[1920]{0:T(1024)S(1)}, f32[1024]{0:T(1024)}, f32[1920,1024]{1,0:T(8,128)}) fusion(f32[1920,1024]{1,0:T(8,128)S(1)} %bitcast.309, f32[1920]{0:T(1024)S(1)} %copy-done.70, f32[1920]{0:T(1024)S(1)} %copy-done.68, f32[1024]{0:T(1024)S(1)} %bitcast.354, f32[1920,1024]{1,0:T(8,128)} %fusion.98, ...), kind=kOutput, calls=%fused_computation.41 | convolution fusion | flops 8072718336 | bytes 35694592 | tf_op jit(solution)/shard_map/dot_general | solution.py:27
  511.0 4.2 constant_dynamic-slice_fusion.9
  520.0 10.1 %multiply_reduce_fusion.1 = (f32[1024]{0:T(1024)}, f32[1920]{0:T(1024)S(1)}, f32[1920]{0:T(1024)S(1)}, f32[1024]{0:T(1024)}, f32[1920,1024]{1,0:T(8,128)S(1)}) fusion(f32[1920,1024]{1,0:T(8,128)S(1)} %bitcast.307, f32[1920]{0:T(1024)S(1)} %copy-done.66, f32[1920]{0:T(1024)S(1)} %copy-done.62, f32[1024]{0:T(1024)S(1)} %bitcast.348, ...), kind=kLoop, calls=%fused_computation.42 | loop fusion | flops 35383552 | bytes 35467264 | tf_op jit(solution)/shard_map/reduce_sum | solution.py:217
  530.2 4.5 multiply_convert_fusion.2
  548.4 26.8 %attention_backward.3 = bf16[1280,1536]{1,0:T(8,128)(2,1)S(1)} custom-call(bf16[1280,1536]{1,0:T(8,128)(2,1)S(1)} %copy-done.13, bf16[1280,1536]{1,0:T(8,128)(2,1)S(1)} %copy-done.13, bf16[1280,1536]{1,0:T(8,128)(2,1)S(1)} %copy-done.13, bf16[1280,512]{1,0:T(8,128)(2,1)S(1)} %convolution_convert_fusion.9.do_ref, bf16[1280,512]{1,0:T(8,128)(2,1)S(1)} %copy-done.5, ...), custom_call_target="tpu_custom_call" | custom-call | flops 20132659200 | bytes 11796480 | tf_op jit(solution)/shard_map/attention_backward/pallas_call | solution.py:171
  575.3 4.5 convolution_convert_fusion.6
  595.4 26.6 %attention_backward.4 = bf16[1280,1536]{1,0:T(8,128)(2,1)S(1)} custom-call(bf16[1280,1536]{1,0:T(8,128)(2,1)S(1)} %copy-done.1, bf16[1280,1536]{1,0:T(8,128)(2,1)S(1)} %copy-done.1, bf16[1280,1536]{1,0:T(8,128)(2,1)S(1)} %copy-done.1, bf16[1280,512]{1,0:T(8,128)(2,1)S(1)} %pad_maximum_fusion.5.do_ref, bf16[1280,512]{1,0:T(8,128)(2,1)S(1)} %copy-done.3, ...), custom_call_target="tpu_custom_call" | custom-call | flops 20132659200 | bytes 11796480 | tf_op jit(solution)/shard_map/attention_backward/pallas_call | solution.py:171
  621.9 6.3 fusion.100
  632.6 3.4 broadcast_select_fusion.5
  644.0 26.6 %attention_backward.5 = bf16[1280,1536]{1,0:T(8,128)(2,1)S(1)} custom-call(bf16[1280,1536]{1,0:T(8,128)(2,1)S(1)} %copy-done.11, bf16[1280,1536]{1,0:T(8,128)(2,1)S(1)} %copy-done.11, bf16[1280,1536]{1,0:T(8,128)(2,1)S(1)} %copy-done.11, bf16[1280,512]{1,0:T(8,128)(2,1)S(1)} %convolution_convert_fusion.10.do_ref, bf16[1280,512]{1,0:T(8,128)(2,1)S(1)} %copy-done.7, ...), custom_call_target="tpu_custom_call" | custom-call | flops 20132659200 | bytes 11796480 | tf_op jit(solution)/shard_map/attention_backward/pallas_call | solution.py:171
  671.4 6.2 fusion.42
  683.2 6.7 add_convert_fusion.4
  705.3 6.1 fusion.99
  711.4 7.5 fusion.97
  719.0 4.8 fusion.19
  723.9 3.9 fusion.18
  739.9 12.3 %collective-permute-done.24 = bf16[4,64,1536]{2,1,0:T(8,128)(2,1)} collective-permute-done((bf16[4,64,1536]{2,1,0:T(8,128)(2,1)S(1)}, bf16[4,64,1536]{2,1,0:T(8,128)(2,1)}, u32[]{:S(2)}, u32[]{:S(2)}) %collective-permute-start.24) | collective-permute-done | bytes 786464 | tf_op jit(solution)/shard_map/ppermute | solution.py:400
  757.3 23.4 %collective-permute-done.45 = f32[8,1024]{1,0:T(8,128)S(1)} collective-permute-done((f32[8,1024]{1,0:T(8,128)S(1)}, f32[8,1024]{1,0:T(8,128)S(1)}, u32[]{:S(2)}, u32[]{:S(2)}) %collective-permute-start.45) | collective-permute-done | bytes 32800 | tf_op jit(solution)/shard_map/ppermute | solution.py:400
  794.9 4.3 collective-permute-done.28
  799.2 10.5 %collective-permute-done.27 = bf16[64,1536]{1,0:T(8,128)(2,1)} collective-permute-done((bf16[64,1536]{1,0:T(8,128)(2,1)}, bf16[64,1536]{1,0:T(8,128)(2,1)}, u32[]{:S(2)}, u32[]{:S(2)}) %collective-permute-start.27) | collective-permute-done | bytes 196640 | tf_op jit(solution)/shard_map/ppermute | solution.py:400
  814.8 3.7 maximum_bitcast_fusion
  (455 shorter events, 176.1 us)
Async XLA Ops:
  7.2 291.4 %all-gather.2.cloned.1.call-start = ((), (), s32[]{:S(2)}) async-start(), calls=%async_computation | async-start | bytes 8650752 | tf_op jit(solution)/shard_map/all_gather | solution.py:541
  131.3 64.5 %collective-permute-start = (bf16[640,1536]{1,0:T(8,128)(2,1)}, bf16[640,1536]{1,0:T(8,128)(2,1)}, u32[]{:S(2)}, u32[]{:S(2)}) collective-permute-start(bf16[640,1536]{1,0:T(8,128)(2,1)} %convolution_convert_fusion.8), channel_id=1, source_target_pairs={{0,1},{1,0},{2,3},{3,2},{4,5},{5,4},{6,7},{7,6},{8,9},{9,8},{10,11... | collective-permute-start | bytes 5898248 | tf_op jit(solution)/shard_map/ppermute | solution.py:400
  222.3 17.1 %collective-permute-start.1 = (bf16[640,512]{1,0:T(8,128)(2,1)S(1)}, bf16[640,512]{1,0:T(8,128)(2,1)S(1)}, u32[]{:S(2)}, u32[]{:S(2)}) collective-permute-start(bf16[640,512]{1,0:T(8,128)(2,1)S(1)} %get-tuple-element.202), channel_id=1, source_target_pairs={{0,1},{1,0},{2,3},{3,2},{4,5},{5,4},{6,7},{7,6},{8,9},{9,8},{10,11... | collective-permute-start | bytes 1966088 | tf_op jit(solution)/shard_map/ppermute | solution.py:400
  239.7 55.0 %collective-permute-start.3 = (bf16[640,1024]{1,0:T(8,128)(2,1)S(1)}, bf16[640,1024]{1,0:T(8,128)(2,1)S(1)}, u32[]{:S(2)}, u32[]{:S(2)}) collective-permute-start(bf16[640,1024]{1,0:T(8,128)(2,1)S(1)} %get-tuple-element.186), channel_id=1, source_target_pairs={{0,1},{1,0},{2,3},{3,2},{4,5},{5,4},{6,7},{7,6},{8,9},{9,8},{10,11... | collective-permute-start | bytes 3932168 | tf_op jit(solution)/shard_map/ppermute | solution.py:400
  294.1 336.7 %collective-permute-start.16 = (bf16[640,1024]{1,0:T(8,128)(2,1)}, bf16[640,1024]{1,0:T(8,128)(2,1)}, u32[]{:S(2)}, u32[]{:S(2)}) collective-permute-start(bf16[640,1024]{1,0:T(8,128)(2,1)} %slice.141), channel_id=1, source_target_pairs={{0,1},{1,0},{2,3},{3,2},{4,5},{5,4},{6,7},{7,6},{8,9},{9,8},{10,11... | collective-permute-start | bytes 3932168 | tf_op jit(solution)/shard_map/ppermute | solution.py:400
  372.1 37.3 %collective-permute-start.2 = (bf16[640,1024]{1,0:T(8,128)(2,1)S(1)}, bf16[640,1024]{1,0:T(8,128)(2,1)}, u32[]{:S(2)}, u32[]{:S(2)}) collective-permute-start(bf16[640,1024]{1,0:T(8,128)(2,1)S(1)} %dynamic-slice_bitcast_fusion.3), channel_id=1, source_target_pairs={{0,1},{1,0},{2,3},{3,2},{4,5},{5,4},{6,7},{7,6},{8,9},{9,8},{10,11... | collective-permute-start | bytes 3932168 | tf_op jit(solution)/shard_map/ppermute | solution.py:400
  375.2 42.6 %collective-permute-start.4 = (bf16[4,2,64,2048]{3,2,1,0:T(8,128)(2,1)}, bf16[4,2,64,2048]{3,2,1,0:T(8,128)(2,1)}, u32[]{:S(2)}, u32[]{:S(2)}) collective-permute-start(bf16[4,2,64,2048]{3,2,1,0:T(8,128)(2,1)} %dynamic-slice_bitcast_fusion.1), channel_id=1, source_target_pairs={{0,2},{2,0},{1,3},{3,1},{4,6},{6,4},{5,7},{7,5},{8,10},{10,8},{9,1... | collective-permute-start | bytes 6291464 | tf_op jit(solution)/shard_map/ppermute | solution.py:400
  376.8 36.3 %collective-permute-start.5 = (bf16[4,2,64,2048]{3,2,1,0:T(8,128)(2,1)}, bf16[4,2,64,2048]{3,2,1,0:T(8,128)(2,1)}, u32[]{:S(2)}, u32[]{:S(2)}) collective-permute-start(bf16[4,2,64,2048]{3,2,1,0:T(8,128)(2,1)} %dynamic-slice_bitcast_fusion), channel_id=1, source_target_pairs={{0,2},{2,0},{1,3},{3,1},{4,6},{6,4},{5,7},{7,5},{8,10},{10,8},{9,1... | collective-permute-start | bytes 6291464 | tf_op jit(solution)/shard_map/ppermute | solution.py:400
  431.5 15.8 %collective-permute-start.10 = (bf16[2,64,2048]{2,1,0:T(8,128)(2,1)S(1)}, bf16[2,64,2048]{2,1,0:T(8,128)(2,1)S(1)}, u32[]{:S(2)}, u32[]{:S(2)}) collective-permute-start(bf16[2,64,2048]{2,1,0:T(8,128)(2,1)S(1)} %get-tuple-element.217), channel_id=1, source_target_pairs={{0,5},{1,4},{4,1},{5,0},{2,7},{3,6},{6,3},{7,2},{8,13},{9,12},{12,... | collective-permute-start | bytes 1572872 | tf_op jit(solution)/shard_map/ppermute | solution.py:400
  433.3 25.3 %collective-permute-start.7 = (bf16[2,64,2048]{2,1,0:T(8,128)(2,1)S(1)}, bf16[2,64,2048]{2,1,0:T(8,128)(2,1)S(1)}, u32[]{:S(2)}, u32[]{:S(2)}) collective-permute-start(bf16[2,64,2048]{2,1,0:T(8,128)(2,1)S(1)} %get-tuple-element.216), channel_id=1, source_target_pairs={{0,1},{1,0},{4,5},{5,4},{2,3},{3,2},{6,7},{7,6},{8,9},{9,8},{12,13... | collective-permute-start | bytes 1572872 | tf_op jit(solution)/shard_map/ppermute | solution.py:400
  434.6 24.5 %collective-permute-start.6 = (bf16[2,64,2048]{2,1,0:T(8,128)(2,1)S(1)}, bf16[2,64,2048]{2,1,0:T(8,128)(2,1)S(1)}, u32[]{:S(2)}, u32[]{:S(2)}) collective-permute-start(bf16[2,64,2048]{2,1,0:T(8,128)(2,1)S(1)} %dynamic-slice_bitcast_fusion.14), channel_id=1, source_target_pairs={{0,4},{1,5},{4,0},{5,1},{2,6},{3,7},{6,2},{7,3},{8,12},{9,13},{12,... | collective-permute-start | bytes 1572872 | tf_op jit(solution)/shard_map/ppermute | solution.py:400
  435.3 37.3 %collective-permute-start.13 = (bf16[2,64,2048]{2,1,0:T(8,128)(2,1)S(1)}, bf16[2,64,2048]{2,1,0:T(8,128)(2,1)S(1)}, u32[]{:S(2)}, u32[]{:S(2)}) collective-permute-start(bf16[2,64,2048]{2,1,0:T(8,128)(2,1)S(1)} %get-tuple-element.215), channel_id=1, source_target_pairs={{0,5},{1,4},{4,1},{5,0},{2,7},{3,6},{6,3},{7,2},{8,13},{9,12},{12,... | collective-permute-start | bytes 1572872 | tf_op jit(solution)/shard_map/ppermute | solution.py:400
  447.3 32.1 %collective-permute-start.9 = (bf16[2,64,2048]{2,1,0:T(8,128)(2,1)S(1)}, bf16[2,64,2048]{2,1,0:T(8,128)(2,1)S(1)}, u32[]{:S(2)}, u32[]{:S(2)}) collective-permute-start(bf16[2,64,2048]{2,1,0:T(8,128)(2,1)S(1)} %get-tuple-element.214), channel_id=1, source_target_pairs={{0,1},{1,0},{4,5},{5,4},{2,3},{3,2},{6,7},{7,6},{8,9},{9,8},{12,13... | collective-permute-start | bytes 1572872 | tf_op jit(solution)/shard_map/ppermute | solution.py:400
  458.6 20.9 %collective-permute-start.8 = (bf16[2,64,2048]{2,1,0:T(8,128)(2,1)S(1)}, bf16[2,64,2048]{2,1,0:T(8,128)(2,1)S(1)}, u32[]{:S(2)}, u32[]{:S(2)}) collective-permute-start(bf16[2,64,2048]{2,1,0:T(8,128)(2,1)S(1)} %dynamic-slice_bitcast_fusion.11), channel_id=1, source_target_pairs={{0,4},{1,5},{4,0},{5,1},{2,6},{3,7},{6,2},{7,3},{8,12},{9,13},{12,... | collective-permute-start | bytes 1572872 | tf_op jit(solution)/shard_map/ppermute | solution.py:400
  459.1 75.6 %collective-permute-start.11 = (bf16[4,2,64,2048]{3,2,0,1:T(8,128)(2,1)}, bf16[4,2,64,2048]{3,2,0,1:T(8,128)(2,1)}, u32[]{:S(2)}, u32[]{:S(2)}) collective-permute-start(bf16[4,2,64,2048]{3,2,0,1:T(8,128)(2,1)} %bitcast.297), channel_id=1, source_target_pairs={{0,2},{2,0},{1,3},{3,1},{4,6},{6,4},{5,7},{7,5},{8,10},{10,8},{9,1... | collective-permute-start | bytes 6291464 | tf_op jit(solution)/shard_map/ppermute | solution.py:400
  516.8 22.6 %collective-permute-start.12 = (bf16[4,2,64,2048]{3,2,0,1:T(8,128)(2,1)}, bf16[4,2,64,2048]{3,2,0,1:T(8,128)(2,1)}, u32[]{:S(2)}, u32[]{:S(2)}) collective-permute-start(bf16[4,2,64,2048]{3,2,0,1:T(8,128)(2,1)} %bitcast.296), channel_id=1, source_target_pairs={{0,2},{2,0},{1,3},{3,1},{4,6},{6,4},{5,7},{7,5},{8,10},{10,8},{9,1... | collective-permute-start | bytes 6291464 | tf_op jit(solution)/shard_map/ppermute | solution.py:400
  517.9 67.0 %collective-permute-start.42 = (bf16[64,2048]{1,0:T(8,128)(2,1)}, bf16[64,2048]{1,0:T(8,128)(2,1)S(1)}, u32[]{:S(2)}, u32[]{:S(2)}) collective-permute-start(bf16[64,2048]{1,0:T(8,128)(2,1)} %get-tuple-element.206), channel_id=1, source_target_pairs={{0,24},{8,16},{16,8},{24,0},{1,25},{9,17},{17,9},{25,1},{2,26},{10... | collective-permute-start | bytes 786440 | tf_op jit(solution)/shard_map/ppermute | solution.py:400
  519.3 65.8 %collective-permute-start.41 = (bf16[64,2048]{1,0:T(8,128)(2,1)}, bf16[64,2048]{1,0:T(8,128)(2,1)S(1)}, u32[]{:S(2)}, u32[]{:S(2)}) collective-permute-start(bf16[64,2048]{1,0:T(8,128)(2,1)} %get-tuple-element.205), channel_id=1, source_target_pairs={{0,16},{8,24},{16,0},{24,8},{1,17},{9,25},{17,1},{25,9},{2,18},{10... | collective-permute-start | bytes 786440 | tf_op jit(solution)/shard_map/ppermute | solution.py:400
  534.7 52.7 %collective-permute-start.40 = (bf16[64,2048]{1,0:T(8,128)(2,1)}, bf16[64,2048]{1,0:T(8,128)(2,1)S(1)}, u32[]{:S(2)}, u32[]{:S(2)}) collective-permute-start(bf16[64,2048]{1,0:T(8,128)(2,1)} %get-tuple-element.204), channel_id=1, source_target_pairs={{0,8},{8,0},{16,24},{24,16},{1,9},{9,1},{17,25},{25,17},{2,10},{10... | collective-permute-start | bytes 786440 | tf_op jit(solution)/shard_map/ppermute | solution.py:400
  547.4 45.4 %collective-permute-start.15 = (bf16[640,512]{1,0:T(8,128)(2,1)}, bf16[640,512]{1,0:T(8,128)(2,1)}, u32[]{:S(2)}, u32[]{:S(2)}) collective-permute-start(bf16[640,512]{1,0:T(8,128)(2,1)} %convolution_convert_fusion.13), channel_id=1, source_target_pairs={{0,1},{1,0},{2,3},{3,2},{4,5},{5,4},{6,7},{7,6},{8,9},{9,8},{10,11... | collective-permute-start | bytes 1966088 | tf_op jit(solution)/shard_map/ppermute | solution.py:400
  585.0 6.2 collective-permute-start.31
  585.0 7.6 collective-permute-start.29
  589.9 49.6 %collective-permute-start.14 = (bf16[4,2,64,1536]{3,2,0,1:T(8,128)(2,1)S(1)}, bf16[4,2,64,1536]{3,2,0,1:T(8,128)(2,1)}, u32[]{:S(2)}, u32[]{:S(2)}) collective-permute-start(bf16[4,2,64,1536]{3,2,0,1:T(8,128)(2,1)S(1)} %bitcast.329), channel_id=1, source_target_pairs={{0,2},{2,0},{1,3},{3,1},{4,6},{6,4},{5,7},{7,5},{8,10},{10,8},{9,1... | collective-permute-start | bytes 4718600 | tf_op jit(solution)/shard_map/ppermute | solution.py:400
  591.1 44.9 %collective-permute-start.18 = (bf16[4,64,2048]{2,1,0:T(8,128)(2,1)}, bf16[4,64,2048]{2,1,0:T(8,128)(2,1)}, u32[]{:S(2)}, u32[]{:S(2)}) collective-permute-start(bf16[4,64,2048]{2,1,0:T(8,128)(2,1)} %dynamic-slice_bitcast_fusion.5), channel_id=1, source_target_pairs={{0,4},{4,0},{1,5},{5,1},{2,6},{6,2},{3,7},{7,3},{8,12},{12,8},{9,1... | collective-permute-start | bytes 3145736 | tf_op jit(solution)/shard_map/ppermute | solution.py:400
  629.7 50.7 %collective-permute-start.22 = (bf16[640,1024]{1,0:T(8,128)(2,1)}, bf16[640,1024]{1,0:T(8,128)(2,1)}, u32[]{:S(2)}, u32[]{:S(2)}) collective-permute-start(bf16[640,1024]{1,0:T(8,128)(2,1)} %dynamic-slice_convert_fusion.1), channel_id=1, source_target_pairs={{0,1},{1,0},{2,3},{3,2},{4,5},{5,4},{6,7},{7,6},{8,9},{9,8},{10,11... | collective-permute-start | bytes 3932168 | tf_op jit(solution)/shard_map/ppermute | solution.py:400
  632.0 59.1 %collective-permute-start.20 = (bf16[4,64,2048]{2,1,0:T(8,128)(2,1)}, bf16[4,64,2048]{2,1,0:T(8,128)(2,1)}, u32[]{:S(2)}, u32[]{:S(2)}) collective-permute-start(bf16[4,64,2048]{2,1,0:T(8,128)(2,1)} %dynamic-slice_bitcast_fusion.4), channel_id=1, source_target_pairs={{0,4},{4,0},{1,5},{5,1},{2,6},{6,2},{3,7},{7,3},{8,12},{12,8},{9,1... | collective-permute-start | bytes 3145736 | tf_op jit(solution)/shard_map/ppermute | solution.py:400
  638.6 52.4 %collective-permute-start.19 = (bf16[4,64,2048]{2,1,0:T(8,128)(2,1)}, bf16[4,64,2048]{2,1,0:T(8,128)(2,1)}, u32[]{:S(2)}, u32[]{:S(2)}) collective-permute-start(bf16[4,64,2048]{2,1,0:T(8,128)(2,1)} %fusion.41), channel_id=1, source_target_pairs={{0,1},{1,0},{2,3},{3,2},{4,5},{5,4},{6,7},{7,6},{8,9},{9,8},{10,11... | collective-permute-start | bytes 3145736 | tf_op jit(solution)/shard_map/ppermute | solution.py:400
  642.6 40.6 %collective-permute-start.17 = (bf16[4,64,1536]{2,1,0:T(8,128)(2,1)}, bf16[4,64,1536]{2,1,0:T(8,128)(2,1)}, u32[]{:S(2)}, u32[]{:S(2)}) collective-permute-start(bf16[4,64,1536]{2,1,0:T(8,128)(2,1)} %dynamic-slice_bitcast_fusion.7), channel_id=1, source_target_pairs={{0,4},{4,0},{1,5},{5,1},{2,6},{6,2},{3,7},{7,3},{8,12},{12,8},{9,1... | collective-permute-start | bytes 2359304 | tf_op jit(solution)/shard_map/ppermute | solution.py:400
  670.6 9.0 %collective-permute-start.32 = (bf16[4,64,512]{2,1,0:T(8,128)(2,1)S(1)}, bf16[4,64,512]{2,1,0:T(8,128)(2,1)S(1)}, u32[]{:S(2)}, u32[]{:S(2)}) collective-permute-start(bf16[4,64,512]{2,1,0:T(8,128)(2,1)S(1)} %dynamic-slice_bitcast_fusion.19), channel_id=1, source_target_pairs={{0,4},{4,0},{1,5},{5,1},{2,6},{6,2},{3,7},{7,3},{8,12},{12,8},{9,1... | collective-permute-start | bytes 786440 | tf_op jit(solution)/shard_map/ppermute | solution.py:400
  679.6 10.7 %collective-permute-start.30 = (bf16[4,64,512]{2,1,0:T(8,128)(2,1)S(1)}, bf16[4,64,512]{2,1,0:T(8,128)(2,1)S(1)}, u32[]{:S(2)}, u32[]{:S(2)}) collective-permute-start(bf16[4,64,512]{2,1,0:T(8,128)(2,1)S(1)} %dynamic-slice_bitcast_fusion.20), channel_id=1, source_target_pairs={{0,4},{4,0},{1,5},{5,1},{2,6},{6,2},{3,7},{7,3},{8,12},{12,8},{9,1... | collective-permute-start | bytes 786440 | tf_op jit(solution)/shard_map/ppermute | solution.py:400
  680.4 10.0 %collective-permute-start.33 = (bf16[4,64,512]{2,1,0:T(8,128)(2,1)S(1)}, bf16[4,64,512]{2,1,0:T(8,128)(2,1)S(1)}, u32[]{:S(2)}, u32[]{:S(2)}) collective-permute-start(bf16[4,64,512]{2,1,0:T(8,128)(2,1)S(1)} %fusion.63), channel_id=1, source_target_pairs={{0,1},{1,0},{2,3},{3,2},{4,5},{5,4},{6,7},{7,6},{8,9},{9,8},{10,11... | collective-permute-start | bytes 786440 | tf_op jit(solution)/shard_map/ppermute | solution.py:400
  690.3 13.3 %collective-permute-start.21 = (bf16[4,2,64,1536]{3,2,0,1:T(8,128)(2,1)S(1)}, bf16[4,2,64,1536]{3,2,0,1:T(8,128)(2,1)S(1)}, u32[]{:S(2)}, u32[]{:S(2)}) collective-permute-start(bf16[4,2,64,1536]{3,2,0,1:T(8,128)(2,1)S(1)} %bitcast.330), channel_id=1, source_target_pairs={{0,2},{2,0},{1,3},{3,1},{4,6},{6,4},{5,7},{7,5},{8,10},{10,8},{9,1... | collective-permute-start | bytes 4718600 | tf_op jit(solution)/shard_map/ppermute | solution.py:400
  694.0 33.9 %collective-permute-start.36 = (bf16[64,512]{1,0:T(8,128)(2,1)}, bf16[64,512]{1,0:T(8,128)(2,1)S(1)}, u32[]{:S(2)}, u32[]{:S(2)}) collective-permute-start(bf16[64,512]{1,0:T(8,128)(2,1)} %get-tuple-element.222), channel_id=1, source_target_pairs={{0,24},{8,16},{16,8},{24,0},{1,25},{9,17},{17,9},{25,1},{2,26},{10... | collective-permute-start | bytes 196616 | tf_op jit(solution)/shard_map/ppermute | solution.py:400
  695.4 36.9 %collective-permute-start.35 = (bf16[64,512]{1,0:T(8,128)(2,1)}, bf16[64,512]{1,0:T(8,128)(2,1)}, u32[]{:S(2)}, u32[]{:S(2)}) collective-permute-start(bf16[64,512]{1,0:T(8,128)(2,1)} %get-tuple-element.223), channel_id=1, source_target_pairs={{0,16},{8,24},{16,0},{24,8},{1,17},{9,25},{17,1},{25,9},{2,18},{10... | collective-permute-start | bytes 196616 | tf_op jit(solution)/shard_map/ppermute | solution.py:400
  695.7 37.8 %collective-permute-start.34 = (bf16[64,512]{1,0:T(8,128)(2,1)}, bf16[64,512]{1,0:T(8,128)(2,1)}, u32[]{:S(2)}, u32[]{:S(2)}) collective-permute-start(bf16[64,512]{1,0:T(8,128)(2,1)} %get-tuple-element.221), channel_id=1, source_target_pairs={{0,8},{8,0},{16,24},{24,16},{1,9},{9,1},{17,25},{25,17},{2,10},{10... | collective-permute-start | bytes 196616 | tf_op jit(solution)/shard_map/ppermute | solution.py:400
  699.3 35.1 %collective-permute-start.39 = (bf16[64,2048]{1,0:T(8,128)(2,1)}, bf16[64,2048]{1,0:T(8,128)(2,1)}, u32[]{:S(2)}, u32[]{:S(2)}) collective-permute-start(bf16[64,2048]{1,0:T(8,128)(2,1)} %get-tuple-element.208), channel_id=1, source_target_pairs={{0,24},{8,16},{16,8},{24,0},{1,25},{9,17},{17,9},{25,1},{2,26},{10... | collective-permute-start | bytes 786440 | tf_op jit(solution)/shard_map/ppermute | solution.py:400
  703.6 32.3 %collective-permute-start.38 = (bf16[64,2048]{1,0:T(8,128)(2,1)}, bf16[64,2048]{1,0:T(8,128)(2,1)}, u32[]{:S(2)}, u32[]{:S(2)}) collective-permute-start(bf16[64,2048]{1,0:T(8,128)(2,1)} %get-tuple-element.209), channel_id=1, source_target_pairs={{0,16},{8,24},{16,0},{24,8},{1,17},{9,25},{17,1},{25,9},{2,18},{10... | collective-permute-start | bytes 786440 | tf_op jit(solution)/shard_map/ppermute | solution.py:400
  727.9 7.9 collective-permute-start.37
  732.3 52.9 %collective-permute-start.25 = (bf16[4,64,1536]{2,1,0:T(8,128)(2,1)}, bf16[4,64,1536]{2,1,0:T(8,128)(2,1)}, u32[]{:S(2)}, u32[]{:S(2)}) collective-permute-start(bf16[4,64,1536]{2,1,0:T(8,128)(2,1)} %fusion.47), channel_id=1, source_target_pairs={{0,1},{1,0},{2,3},{3,2},{4,5},{5,4},{6,7},{7,6},{8,9},{9,8},{10,11... | collective-permute-start | bytes 2359304 | tf_op jit(solution)/shard_map/ppermute | solution.py:400
  733.4 78.2 %collective-permute-start.23 = (bf16[640,1024]{1,0:T(8,128)(2,1)}, bf16[640,1024]{1,0:T(8,128)(2,1)}, u32[]{:S(2)}, u32[]{:S(2)}) collective-permute-start(bf16[640,1024]{1,0:T(8,128)(2,1)} %fusion.50), channel_id=1, source_target_pairs={{0,1},{1,0},{2,3},{3,2},{4,5},{5,4},{6,7},{7,6},{8,9},{9,8},{10,11... | collective-permute-start | bytes 3932168 | tf_op jit(solution)/shard_map/ppermute | solution.py:400
  734.4 17.8 %collective-permute-start.24 = (bf16[4,64,1536]{2,1,0:T(8,128)(2,1)S(1)}, bf16[4,64,1536]{2,1,0:T(8,128)(2,1)}, u32[]{:S(2)}, u32[]{:S(2)}) collective-permute-start(bf16[4,64,1536]{2,1,0:T(8,128)(2,1)S(1)} %dynamic-slice_bitcast_fusion.6), channel_id=1, source_target_pairs={{0,4},{4,0},{1,5},{5,1},{2,6},{6,2},{3,7},{7,3},{8,12},{12,8},{9,1... | collective-permute-start | bytes 2359304 | tf_op jit(solution)/shard_map/ppermute | solution.py:400
  752.2 28.4 %collective-permute-start.45 = (f32[8,1024]{1,0:T(8,128)S(1)}, f32[8,1024]{1,0:T(8,128)S(1)}, u32[]{:S(2)}, u32[]{:S(2)}) collective-permute-start(f32[8,1024]{1,0:T(8,128)S(1)} %concatenate.43), channel_id=1, source_target_pairs={{0,5},{1,4},{4,1},{5,0},{2,7},{3,6},{6,3},{7,2},{8,13},{9,12},{12,... | collective-permute-start | bytes 98312 | tf_op jit(solution)/shard_map/ppermute | solution.py:400
  754.2 26.5 %collective-permute-start.44 = (f32[8,1024]{1,0:T(8,128)S(1)}, f32[8,1024]{1,0:T(8,128)S(1)}, u32[]{:S(2)}, u32[]{:S(2)}) collective-permute-start(f32[8,1024]{1,0:T(8,128)S(1)} %concatenate.43), channel_id=1, source_target_pairs={{0,4},{1,5},{4,0},{5,1},{2,6},{3,7},{6,2},{7,3},{8,12},{9,13},{12,... | collective-permute-start | bytes 98312 | tf_op jit(solution)/shard_map/ppermute | solution.py:400
  754.8 25.9 %collective-permute-start.43 = (f32[8,1024]{1,0:T(8,128)S(1)}, f32[8,1024]{1,0:T(8,128)S(1)}, u32[]{:S(2)}, u32[]{:S(2)}) collective-permute-start(f32[8,1024]{1,0:T(8,128)S(1)} %concatenate.43), channel_id=1, source_target_pairs={{0,1},{1,0},{4,5},{5,4},{2,3},{3,2},{6,7},{7,6},{8,9},{9,8},{12,13... | collective-permute-start | bytes 98312 | tf_op jit(solution)/shard_map/ppermute | solution.py:400
  780.7 6.4 collective-permute-start.48
  789.2 10.0 %collective-permute-start.28 = (bf16[64,1536]{1,0:T(8,128)(2,1)}, bf16[64,1536]{1,0:T(8,128)(2,1)}, u32[]{:S(2)}, u32[]{:S(2)}) collective-permute-start(bf16[64,1536]{1,0:T(8,128)(2,1)} %get-tuple-element.219), channel_id=1, source_target_pairs={{0,24},{8,16},{16,8},{24,0},{1,25},{9,17},{17,9},{25,1},{2,26},{10... | collective-permute-start | bytes 589832 | tf_op jit(solution)/shard_map/ppermute | solution.py:400
  790.7 19.0 %collective-permute-start.27 = (bf16[64,1536]{1,0:T(8,128)(2,1)}, bf16[64,1536]{1,0:T(8,128)(2,1)}, u32[]{:S(2)}, u32[]{:S(2)}) collective-permute-start(bf16[64,1536]{1,0:T(8,128)(2,1)} %get-tuple-element.220), channel_id=1, source_target_pairs={{0,16},{8,24},{16,0},{24,8},{1,17},{9,25},{17,1},{25,9},{2,18},{10... | collective-permute-start | bytes 589832 | tf_op jit(solution)/shard_map/ppermute | solution.py:400
  791.5 18.2 %collective-permute-start.26 = (bf16[64,1536]{1,0:T(8,128)(2,1)}, bf16[64,1536]{1,0:T(8,128)(2,1)}, u32[]{:S(2)}, u32[]{:S(2)}) collective-permute-start(bf16[64,1536]{1,0:T(8,128)(2,1)} %get-tuple-element.218), channel_id=1, source_target_pairs={{0,8},{8,0},{16,24},{24,16},{1,9},{9,1},{17,25},{25,17},{2,10},{10... | collective-permute-start | bytes 589832 | tf_op jit(solution)/shard_map/ppermute | solution.py:400
  (114 other events, 1277.3 us)
Sparse Core Ops, SparseCore 0:
  132.0 84.4 all-gather.1
